TPU v7x, 128 devices: a whole 4x4x4 slice. The times are simulated.
128 devices in a mesh: tile: 32 (over x, y, core), slab: 4 (over z).
Axes of the slice: x: 4, y: 4, z: 4, core: 2. Of those that a mesh axis runs over, the one named last changes fastest.
Arguments:
- stored: float32 [128, 8, 256, 1024], P('tile', 'slab'), may hold values from -6 to 6
- offsets: int32 [2, 2, 128], P(None, None, ('tile', 'slab')), may hold values from 0 to 128
Outputs:
- surface: float32 [2, 128, 128, 1024], P(None, ('tile', 'slab'))
- peak: float32 [2, 128], P(None, ('tile', 'slab'))
All inputs are finite; a program needn't handle non-finite values.
Results may differ from a plain program's by a relative error of at most 0.0003.
Values sent between devices are 32-bit elements; how exact they have to be, the bound alone decides.
No kernel may reach another device: no remote copies, remote signals or barrier semaphores. Data moves between devices by JAX's collectives and lax.ppermute only.
A program may use at most 192 MiB of HBM per device.

v0:
```python
import math

import jax
import jax.numpy as jnp
from jax import lax
from jax.sharding import PartitionSpec as P

A = 128
GC = 7
ROUNDS = 2


FLOOR = 0.25
HIGH = lax.Precision.HIGHEST


def from_behind(x, axis, by):
    size = lax.axis_size(axis)
    pairs = [(i, i + by) for i in range(size) if 0 <= i + by < size]
    return lax.ppermute(x, axis, pairs)


def dft_table(length):
    index = jnp.arange(length, dtype=jnp.int32)
    angle = (index[:, None] * index[None, :] % length).astype(jnp.float32) * (
        2.0 * math.pi / length
    )
    return (jnp.cos(angle), jnp.sin(angle))


def complex_table(length, sign):
    cos_t, sin_t = dft_table(length)
    first = jnp.stack((cos_t, sign * sin_t), axis=1)
    second = jnp.stack((-sign * sin_t, cos_t), axis=1)
    return jnp.stack((first, second))


def twiddle_table(outer, inner):
    total = outer * inner
    rows = jnp.arange(outer, dtype=jnp.int32)
    cols = jnp.arange(inner, dtype=jnp.int32)
    angle = (rows[:, None] * cols[None, :] % total).astype(jnp.float32) * (2.0 * math.pi / total)
    return (jnp.cos(angle), jnp.sin(angle))


def spin(pair, table, sign):
    cos_t, sin_t = table
    real = pair[0]
    imag = pair[1]
    return jnp.stack((real * cos_t - sign * imag * sin_t, imag * cos_t + sign * real * sin_t))


def forward(strip, tabs):
    depth, across, along = strip.shape
    inner = along // 8
    shaped = strip.reshape(depth, across, 8, inner)
    pair = jnp.einsum("zanm,nek->ezakm", shaped, tabs["f_outer"][0], precision=HIGH)
    pair = spin(pair, tabs["twist"], -1.0)
    pair = jnp.einsum("czakm,cmej->ezakj", pair, tabs["f_inner"], precision=HIGH)
    pair = jnp.einsum("czakj,caeb->ezbkj", pair, tabs["f_across"], precision=HIGH)
    pair = jnp.einsum("czakj,czey->eyakj", pair, tabs["f_depth"], precision=HIGH)
    return pair * (1.0 / math.sqrt(depth * across * along))


def inverse_real(pair, tabs):
    depth, across, outer, inner = pair.shape[1:]
    pair = jnp.einsum("cyakj,cyez->ezakj", pair, tabs["b_depth"], precision=HIGH)
    pair = jnp.einsum("czbkj,cbea->ezakj", pair, tabs["b_across"], precision=HIGH)
    pair = jnp.einsum("czakj,cjem->ezakm", pair, tabs["b_inner"], precision=HIGH)
    pair = spin(pair, tabs["twist"], 1.0)
    result = jnp.einsum("czakm,ckn->zanm", pair, tabs["b_outer"][:, :, 0], precision=HIGH)
    return result.reshape(depth, across, outer * inner) * (
        1.0 / math.sqrt(depth * across * outer * inner)
    )


def on_device(stored, offsets):
    owned = lax.all_to_all(stored, "slab", split_axis=0, concat_axis=1, tiled=True)[0]
    depth, rows_band, along = owned.shape
    inner = along // 8
    tabs = {
        "f_outer": complex_table(8, -1.0),
        "f_inner": complex_table(inner, -1.0),
        "f_across": complex_table(A, -1.0),
        "f_depth": complex_table(depth, -1.0),
        "b_outer": complex_table(8, 1.0),
        "b_inner": complex_table(inner, 1.0),
        "b_across": complex_table(A, 1.0),
        "b_depth": complex_table(depth, 1.0),
        "twist": twiddle_table(8, inner),
    }
    count = lax.axis_size(("tile", "slab"))
    place = lax.axis_index(("tile", "slab"))
    surfaces = []
    for rnd in range(ROUNDS):
        own_strip = lax.dynamic_slice_in_dim(owned, offsets[rnd, 0, 0], A, 1)
        given_strip = lax.dynamic_slice_in_dim(owned, offsets[rnd, 1, 0], A, 1)
        if rnd == 0:
            valid = jnp.logical_and(place % GC != GC - 1, place + 1 < count)
        else:
            valid = place + GC < count
        spec_own = forward(own_strip, tabs)
        given_spec = forward(given_strip, tabs)
        if rnd == 0:
            spec_partner = from_behind(given_spec, ("tile", "slab"), -1)
        else:
            spec_partner = from_behind(given_spec, ("tile", "slab"), -GC)
        spec_partner = spec_partner * valid.astype(jnp.float32)
        cross_real = spec_own[0] * spec_partner[0] + spec_own[1] * spec_partner[1]
        cross_imag = spec_own[1] * spec_partner[0] - spec_own[0] * spec_partner[1]
        denom = jnp.maximum(jnp.sqrt(cross_real * cross_real + cross_imag * cross_imag), FLOOR)
        field = inverse_real(jnp.stack((cross_real / denom, cross_imag / denom)), tabs)
        surfaces.append(jnp.max(field, axis=0))
    surface = jnp.stack(surfaces)[:, None]
    peak = jnp.max(surface, axis=(2, 3))
    return (surface, peak)


def solution(mesh):
    return jax.shard_map(
        on_device,
        mesh=mesh,
        in_specs=(P("tile", "slab", None, None), P(None, None, ("tile", "slab"))),
        out_specs=(P(None, ("tile", "slab"), None, None), P(None, ("tile", "slab"))),
        check_vma=False,
    )
```

profile of v0, /device:TPU:56, one launch (start us, length us, event | category | flops | bytes accessed | tf_op | source)
XLA Modules:
  0.0 562.6 jit_solution(18440363426083800554)
XLA Ops:
  0.6 5.7 %all-to-all-start = ((f32[4,2,256,1024]{3,2,1,0:T(8,128)}), f32[4,2,256,1024]{3,2,1,0:T(8,128)}, u32[]{:S(2)}, u32[]{:S(2)}) async-start(f32[4,2,256,1024]{3,2,1,0:T(8,128)} %param.2), calls=%async_computation | async-start | bytes 16777216 | tf_op jit(solution)/shard_map/all_to_all | solution.py:78
  6.4 0.0 copy-done.12
  6.4 0.7 fusion.164
  14.7 0.1 fusion.154
  14.7 0.1 broadcast_multiply_fusion.4
  14.8 0.1 broadcast_multiply_fusion.3
  14.8 0.6 fusion.134
  15.5 0.3 fusion.125
  15.7 0.3 broadcast_multiply_fusion.2
  16.0 0.7 fusion.116
  16.7 83.4 %all-to-all-done = f32[4,2,256,1024]{3,2,1,0:T(8,128)} async-done(((f32[4,2,256,1024]{3,2,1,0:T(8,128)}), f32[4,2,256,1024]{3,2,1,0:T(8,128)}, u32[]{:S(2)}, u32[]{:S(2)}) %all-to-all-start) | async-done | bytes 8388640 | tf_op jit(solution)/shard_map/all_to_all | solution.py:78
  100.1 9.3 %constant_dynamic-slice_fusion.1 = (f32[8,128,1024]{2,1,0:T(8,128)S(1)}, f32[8,128,1024]{2,1,0:T(8,128)S(1)}, f32[8,128,1024]{2,1,0:T(8,128)}, f32[8,128,1024]{2,1,0:T(8,128)S(1)}) fusion(f32[8,256,1024]{2,1,0:T(8,128)} %bitcast.22, s32[]{:T(128)S(6)} %select_n.166, s32[]{:T(128)S(6)} %select_n.167, s32[]{:T(128)S(6)} %select_n.164, s32[]{:T(128)S(6)} %select_n.162), kind=kLoop, calls=%fused_computation.188 | loop fusion | bytes 33554448 | tf_op jit(solution)/shard_map/dynamic_slice | solution.py:96
  109.5 1.0 copy.147
  110.5 7.3 %convolution_bitcast_fusion = f32[2,8,128,8,128]{4,3,2,1,0:T(8,128)S(1)} fusion(f32[8,128,8,128,1]{3,2,1,0,4:T(8,128)S(1)} %bitcast.321, f32[8,1,8]{0,2,1:T(8,128)S(1)} %get-tuple-element.49, f32[8,1,8]{0,2,1:T(8,128)S(1)} %get-tuple-element.48), kind=kOutput, calls=%fused_computation.104 | convolution fusion | flops 201326720 | bytes 12583424 | tf_op jit(solution)/shard_map/zanm,nek->ezakm/dot_general | solution.py:57
  117.8 1.0 copy.145
  118.9 9.0 %convolution_bitcast_fusion.2 = f32[2,8,128,8,128]{4,3,2,1,0:T(8,128)} fusion(f32[8,128,8,128,1]{3,2,1,0,4:T(8,128)S(1)} %bitcast.322, f32[8,1,8]{0,2,1:T(8,128)S(1)} %get-tuple-element.49, f32[8,1,8]{0,2,1:T(8,128)S(1)} %get-tuple-element.48), kind=kOutput, calls=%fused_computation.106 | convolution fusion | flops 201326720 | bytes 12583424 | tf_op jit(solution)/shard_map/zanm,nek->ezakm/dot_general | solution.py:57
  127.9 1.0 copy.144
  128.9 8.8 %convolution_bitcast_fusion.3 = f32[2,8,128,8,128]{4,3,2,1,0:T(8,128)} fusion(f32[8,128,8,128,1]{3,2,1,0,4:T(8,128)S(1)} %bitcast.323, f32[8,1,8]{0,2,1:T(8,128)S(1)} %get-tuple-element.49, f32[8,1,8]{0,2,1:T(8,128)S(1)} %get-tuple-element.48), kind=kOutput, calls=%fused_computation.107 | convolution fusion | flops 201326720 | bytes 12583424 | tf_op jit(solution)/shard_map/zanm,nek->ezakm/dot_general | solution.py:57
  137.7 1.0 copy.146
  138.7 9.0 %convolution_bitcast_fusion.1 = f32[2,8,128,8,128]{4,3,2,1,0:T(8,128)} fusion(f32[8,128,8,128,1]{3,2,1,0,4:T(8,128)S(1)} %bitcast.320, f32[8,1,8]{0,2,1:T(8,128)S(1)} %get-tuple-element.49, f32[8,1,8]{0,2,1:T(8,128)S(1)} %get-tuple-element.48), kind=kOutput, calls=%fused_computation.105 | convolution fusion | flops 201326720 | bytes 12583424 | tf_op jit(solution)/shard_map/zanm,nek->ezakm/dot_general | solution.py:57
  147.7 28.1 %multiply_subtract_fusion.3 = (f32[1,8,128,8,128]{4,3,2,1,0:T(8,128)}, f32[1,8,128,8,128]{4,3,2,1,0:T(8,128)}, f32[1,8,128,8,128]{4,3,2,1,0:T(8,128)}, f32[1,8,1...) fusion(f32[2,8,128,8,128]{4,3,2,1,0:T(8,128)} %convolution_bitc, ...), kind=kLoop, calls=%fused_computation.81 | loop fusion | flops 25165824 | bytes 67117056 | tf_op jit(solution)/shard_map/sub | solution.py:50
  175.8 4.1 pad_maximum_fusion.1
  179.9 9.1 %fusion.36 = f32[2,128,8,128,8,1]{3,1,5,4,2,0:T(8,128)S(1)} fusion(f32[2,8,128,8,128]{4,3,2,1,0:T(8,128)S(1)} %pad_maximum_fusion.1, f32[1,128,2,128]{1,3,0,2:T(8,128)S(1)} %get-tuple-element.25, f32[1,128,2,128]{1,3,0,2:T(8,128)S(1)} %get-tuple-element.28), kind=kOutput, calls=%fused_computation.45 | convolution fusion | flops 6442516480 | bytes 17039360 | tf_op jit(solution)/shard_map/czakm,cmej->ezakj/dot_general | solution.py:59
  189.0 9.3 %fusion.91 = f32[2,8,128,8,128]{4,2,3,1,0:T(8,128)S(1)} fusion(f32[2,128,8,128,8,1]{3,1,5,4,2,0:T(8,128)S(1)} %fusion.36, f32[1,128,2,128]{1,3,0,2:T(8,128)S(1)} %get-tuple-element.25, f32[1,128,2,128]{1,3,0,2:T(8,128)S(1)} %get-tuple-element.28), kind=kOutput, calls=%fused_computation.101 | convolution fusion | flops 6442516480 | bytes 17039360 | tf_op jit(solution)/shard_map/czakj,caeb->ezbkj/dot_general | solution.py:60
  198.2 16.5 %bitcast_multiply_fusion.2 = f32[2,8,128,8,128]{4,1,3,2,0:T(8,128)} fusion(f32[2,8,128,8,128]{4,2,3,1,0:T(8,128)S(1)} %fusion.91, f32[1,8,2,8]{1,3,2,0:T(8,128)S(1)} %get-tuple-element.39, f32[1,8,2,8]{1,3,2,0:T(8,128)S(1)} %get-tuple-element.42), kind=kOutput, calls=%fused_computation.42 | convolution fusion | flops 404750592 | bytes 16778240 | tf_op jit(solution)/shard_map/czakj,czey->eyakj/dot_general | solution.py:61
  214.7 3.2 collective-permute-start
  218.0 0.6 fusion.152
  218.6 4.1 pad_maximum_fusion.4
  222.7 9.1 %fusion.25 = f32[2,128,8,128,8,1]{3,1,5,4,2,0:T(8,128)S(1)} fusion(f32[2,8,128,8,128]{4,3,2,1,0:T(8,128)S(1)} %pad_maximum_fusion.4, f32[1,128,2,128]{1,3,0,2:T(8,128)S(1)} %get-tuple-element.25, f32[1,128,2,128]{1,3,0,2:T(8,128)S(1)} %get-tuple-element.28), kind=kOutput, calls=%fused_computation.32 | convolution fusion | flops 6442516480 | bytes 17039360 | tf_op jit(solution)/shard_map/czakm,cmej->ezakj/dot_general | solution.py:59
  231.8 9.3 %fusion.97 = f32[2,8,128,8,128]{4,2,3,1,0:T(8,128)S(1)} fusion(f32[2,128,8,128,8,1]{3,1,5,4,2,0:T(8,128)S(1)} %fusion.25, f32[1,128,2,128]{1,3,0,2:T(8,128)S(1)} %get-tuple-element.25, f32[1,128,2,128]{1,3,0,2:T(8,128)S(1)} %get-tuple-element.28), kind=kOutput, calls=%fused_computation.103 | convolution fusion | flops 6442516480 | bytes 17039360 | tf_op jit(solution)/shard_map/czakj,caeb->ezbkj/dot_general | solution.py:60
  241.1 16.5 %bitcast_multiply_fusion = f32[2,8,128,8,128]{4,1,3,2,0:T(8,128)} fusion(f32[2,8,128,8,128]{4,2,3,1,0:T(8,128)S(1)} %fusion.97, f32[1,8,2,8]{1,3,2,0:T(8,128)S(1)} %get-tuple-element.39, f32[1,8,2,8]{1,3,2,0:T(8,128)S(1)} %get-tuple-element.42), kind=kOutput, calls=%fused_computation.29 | convolution fusion | flops 404750592 | bytes 16778240 | tf_op jit(solution)/shard_map/czakj,czey->eyakj/dot_general | solution.py:61
  257.6 2.7 collective-permute-start.1
  260.4 0.8 pad_maximum_fusion
  261.2 1.4 copy-done.1
  262.6 3.0 pad_maximum_fusion.3
  265.6 9.1 %fusion.40 = f32[2,128,8,128,8,1]{3,1,5,4,2,0:T(8,128)S(1)} fusion(f32[2,8,128,8,128]{4,3,2,1,0:T(8,128)S(1)} %pad_maximum_fusion, f32[1,128,2,128]{1,3,0,2:T(8,128)S(1)} %get-tuple-element.25, f32[1,128,2,128]{1,3,0,2:T(8,128)S(1)} %get-tuple-element.28), kind=kOutput, calls=%fused_computation.50 | convolution fusion | flops 6442516480 | bytes 17039360 | tf_op jit(solution)/shard_map/czakm,cmej->ezakj/dot_general | solution.py:59
  274.7 9.2 %fusion.88 = f32[2,8,128,8,128]{4,2,3,1,0:T(8,128)S(1)} fusion(f32[2,128,8,128,8,1]{3,1,5,4,2,0:T(8,128)S(1)} %fusion.40, f32[1,128,2,128]{1,3,0,2:T(8,128)S(1)} %get-tuple-element.25, f32[1,128,2,128]{1,3,0,2:T(8,128)S(1)} %get-tuple-element.28), kind=kOutput, calls=%fused_computation.100 | convolution fusion | flops 6442516480 | bytes 17039360 | tf_op jit(solution)/shard_map/czakj,caeb->ezbkj/dot_general | solution.py:60
  284.0 9.3 %fusion.29 = f32[2,128,8,128,8,1]{3,1,5,4,2,0:T(8,128)S(1)} fusion(f32[2,8,128,8,128]{4,3,2,1,0:T(8,128)S(1)} %pad_maximum_fusion.3, f32[1,128,2,128]{1,3,0,2:T(8,128)S(1)} %get-tuple-element.25, f32[1,128,2,128]{1,3,0,2:T(8,128)S(1)} %get-tuple-element.28), kind=kOutput, calls=%fused_computation.37 | convolution fusion | flops 6442516480 | bytes 17039360 | tf_op jit(solution)/shard_map/czakm,cmej->ezakj/dot_general | solution.py:59
  293.3 10.4 %fusion.94 = f32[2,8,128,8,128]{4,2,3,1,0:T(8,128)} fusion(f32[2,128,8,128,8,1]{3,1,5,4,2,0:T(8,128)S(1)} %fusion.29, f32[1,128,2,128]{1,3,0,2:T(8,128)S(1)} %get-tuple-element.25, f32[1,128,2,128]{1,3,0,2:T(8,128)S(1)} %get-tuple-element.28), kind=kOutput, calls=%fused_computation.102 | convolution fusion | flops 6442516480 | bytes 17039360 | tf_op jit(solution)/shard_map/czakj,caeb->ezbkj/dot_general | solution.py:60
  303.7 14.9 %bitcast_multiply_fusion.3 = f32[2,8,128,8,128]{4,1,3,2,0:T(8,128)S(1)} fusion(f32[2,8,128,8,128]{4,2,3,1,0:T(8,128)S(1)} %fusion.88, f32[1,8,2,8]{1,3,2,0:T(8,128)S(1)} %get-tuple-element.39, f32[1,8,2,8]{1,3,2,0:T(8,128)S(1)} %get-tuple-element.42), kind=kOutput, calls=%fused_computation.47 | convolution fusion | flops 404750592 | bytes 16778240 | tf_op jit(solution)/shard_map/czakj,czey->eyakj/dot_general | solution.py:61
  318.5 17.2 %bitcast_multiply_fusion.1 = f32[2,8,128,8,128]{4,1,3,2,0:T(8,128)S(1)} fusion(f32[2,8,128,8,128]{4,2,3,1,0:T(8,128)} %fusion.94, f32[1,8,2,8]{1,3,2,0:T(8,128)S(1)} %get-tuple-element.39, f32[1,8,2,8]{1,3,2,0:T(8,128)S(1)} %get-tuple-element.42), kind=kOutput, calls=%fused_computation.34 | convolution fusion | flops 404750592 | bytes 16778240 | tf_op jit(solution)/shard_map/czakj,czey->eyakj/dot_general | solution.py:61
  335.7 62.8 %collective-permute-done = f32[2,8,128,8,128]{4,1,3,2,0:T(8,128)} collective-permute-done((f32[2,8,128,8,128]{4,1,3,2,0:T(8,128)}, f32[2,8,128,8,128]{4,1,3,2,0:T(8,128)}, u32[]{:S(2)}, u32[]{:S(2)}) %collective-permute-start) | collective-permute-done | bytes 8388640 | tf_op jit(solution)/shard_map/ppermute | solution.py:20
  398.5 8.5 %broadcast_multiply_fusion.1 = f32[2,8,128,8,128]{4,1,3,2,0:T(8,128)} fusion(f32[2,8,128,8,128]{4,1,3,2,0:T(8,128)} %collective-permute-done, f32[]{:T(128)S(6)} %convert_element_type.135), kind=kLoop, calls=%fused_computation.89 | loop fusion | flops 2097152 | bytes 16777220 | tf_op jit(solution)/shard_map/mul | solution.py:108
  407.0 6.3 %fusion.61 = (f32[1,8,128,8,128]{4,1,3,2,0:T(8,128)S(1)}, f32[1,8,128,8,128]{4,1,3,2,0:T(8,128)S(1)}, f32[1,8,128,8,128]{4,1,3,2,0:T(8,128)}) fusion(f32[2,8,128,8,128]{4,1,3,2,0:T(8,128)} %broadcast_multiply_fusion.1, f32[2,8,128,8,128]{4,1,3,2,0:T(8,128)S(1)} %bitcast_multiply_fusion.3), kind=kLoop, calls=%fused_computation.87 | loop fusion | flops 11534336 | bytes 29360128 | tf_op jit(solution)/shard_map/div | solution.py:112
  413.4 4.0 fusion.60
  417.4 0.0 copy-start.4
  417.4 8.1 %fusion.76 = f32[2,8,128,8,128,1]{4,1,3,2,0,5:T(8,128)S(1)} fusion(f32[1,8,128,8,128]{4,1,3,2,0:T(8,128)S(1)} %fusion.60, f32[1,8,128,8,128]{4,1,3,2,0:T(8,128)S(1)} %get-tuple-element.5, f32[1,8,2,8]{1,3,2,0:T(8,128)S(1)} %copy-done.8, f32[1,8,2,8]{1,3,2,0:T(8,128)S(1)} %copy-done.7), kind=kOutput, calls=%fused_computation.96 | convolution fusion | flops 404750592 | bytes 16778240 | tf_op jit(solution)/shard_map/cyakj,cyez->ezakj/dot_general | solution.py:67
  425.5 12.7 %fusion.70 = f32[2,8,128,8,128,1]{4,2,0,3,1,5:T(8,128)S(1)} fusion(f32[2,8,128,8,128,1]{4,1,3,2,0,5:T(8,128)S(1)} %fusion.76, f32[1,128,2,128]{1,3,2,0:T(8,128)S(1)} %copy-done.5, f32[1,128,2,128]{1,3,2,0:T(8,128)S(1)} %copy-done.4), kind=kOutput, calls=%fused_computation.94 | convolution fusion | flops 6442516480 | bytes 17039360 | tf_op jit(solution)/shard_map/czbkj,cbea->ezakj/dot_general | solution.py:68
  438.1 12.4 %fusion.82 = f32[2,8,128,8,128]{4,3,2,1,0:T(8,128)S(1)} fusion(f32[2,8,128,8,128,1]{4,2,0,3,1,5:T(8,128)S(1)} %fusion.70, f32[1,128,2,128]{1,3,2,0:T(8,128)S(1)} %copy-done.5, f32[1,128,2,128]{1,3,2,0:T(8,128)S(1)} %copy-done.4), kind=kOutput, calls=%fused_computation.98 | convolution fusion | flops 6442516480 | bytes 17039360 | tf_op jit(solution)/shard_map/czakj,cjem->ezakm/dot_general | solution.py:69
  450.6 41.0 %collective-permute-done.1 = f32[2,8,128,8,128]{4,1,3,2,0:T(8,128)} collective-permute-done((f32[2,8,128,8,128]{4,1,3,2,0:T(8,128)}, f32[2,8,128,8,128]{4,1,3,2,0:T(8,128)}, u32[]{:S(2)}, u32[]{:S(2)}) %collective-permute-start.1) | collective-permute-done | bytes 8388640 | tf_op jit(solution)/shard_map/ppermute | solution.py:20
  491.6 8.5 %broadcast_multiply_fusion = f32[2,8,128,8,128]{4,1,3,2,0:T(8,128)} fusion(f32[2,8,128,8,128]{4,1,3,2,0:T(8,128)} %collective-permute-done.1, f32[]{:T(128)S(6)} %convert_element_type.136), kind=kLoop, calls=%fused_computation.77 | loop fusion | flops 2097152 | bytes 16777220 | tf_op jit(solution)/shard_map/mul | solution.py:108
  500.1 6.3 %fusion.59 = (f32[1,8,128,8,128]{4,1,3,2,0:T(8,128)S(1)}, f32[1,8,128,8,128]{4,1,3,2,0:T(8,128)S(1)}, f32[1,8,128,8,128]{4,1,3,2,0:T(8,128)}) fusion(f32[2,8,128,8,128]{4,1,3,2,0:T(8,128)} %broadcast_multiply_fusion, f32[2,8,128,8,128]{4,1,3,2,0:T(8,128)S(1)} %bitcast_multiply_fusion.1), kind=kLoop, calls=%fused_computation.75 | loop fusion | flops 11534336 | bytes 29360128 | tf_op jit(solution)/shard_map/div | solution.py:112
  506.4 4.0 fusion.58
  510.3 8.1 %fusion.79 = f32[2,8,128,8,128,1]{4,1,3,2,0,5:T(8,128)S(1)} fusion(f32[1,8,128,8,128]{4,1,3,2,0:T(8,128)S(1)} %fusion.58, f32[1,8,128,8,128]{4,1,3,2,0:T(8,128)S(1)} %get-tuple-element.2, f32[1,8,2,8]{1,3,2,0:T(8,128)S(1)} %copy-done.8, f32[1,8,2,8]{1,3,2,0:T(8,128)S(1)} %copy-done.7), kind=kOutput, calls=%fused_computation.97 | convolution fusion | flops 404750592 | bytes 16778240 | tf_op jit(solution)/shard_map/cyakj,cyez->ezakj/dot_general | solution.py:67
  518.4 12.7 %fusion.73 = f32[2,8,128,8,128,1]{4,2,0,3,1,5:T(8,128)S(1)} fusion(f32[2,8,128,8,128,1]{4,1,3,2,0,5:T(8,128)S(1)} %fusion.79, f32[1,128,2,128]{1,3,2,0:T(8,128)S(1)} %copy-done.5, f32[1,128,2,128]{1,3,2,0:T(8,128)S(1)} %copy-done.4), kind=kOutput, calls=%fused_computation.95 | convolution fusion | flops 6442516480 | bytes 17039360 | tf_op jit(solution)/shard_map/czbkj,cbea->ezakj/dot_general | solution.py:68
  531.1 12.3 %fusion.85 = f32[2,8,128,8,128]{4,3,2,1,0:T(8,128)S(1)} fusion(f32[2,8,128,8,128,1]{4,2,0,3,1,5:T(8,128)S(1)} %fusion.73, f32[1,128,2,128]{1,3,2,0:T(8,128)S(1)} %copy-done.5, f32[1,128,2,128]{1,3,2,0:T(8,128)S(1)} %copy-done.4), kind=kOutput, calls=%fused_computation.99 | convolution fusion | flops 6442516480 | bytes 17039360 | tf_op jit(solution)/shard_map/czakj,cjem->ezakm/dot_general | solution.py:69
  543.4 4.7 multiply_subtract_fusion
  548.2 6.1 %fusion.56 = f32[8,128,128]{2,0,1:T(8,128)S(1)} fusion(f32[1,8,128,8,128]{4,3,2,1,0:T(8,128)} %get-tuple-element.9, f32[1,8,128,8,128]{4,3,2,1,0:T(8,128)S(1)} %get-tuple-element.8, f32[1,8,2,8]{1,3,2,0:T(8,128)S(1)} %copy-done.8, f32[1,8,2,8]{1,3,2,0:T(8,128)S(1)} %copy-done.7), kind=kOutput, calls=%fused_computation.67 | convolution fusion | flops 205390080 | bytes 8913920 | tf_op jit(solution)/shard_map/czakm,ckn->zanm/dot_general | solution.py:71
  554.3 0.1 stack.91
  554.4 6.7 %fusion.57 = f32[8,128,128]{2,0,1:T(8,128)S(1)} fusion(f32[1,8,128,8,128]{4,3,2,1,0:T(8,128)} %get-tuple-element.30, f32[1,8,128,8,128]{4,3,2,1,0:T(8,128)} %get-tuple-element.31, f32[1,8,2,8]{1,3,2,0:T(8,128)S(1)} %copy-done.8, f32[1,8,2,8]{1,3,2,0:T(8,128)S(1)} %copy-done.7), kind=kOutput, calls=%fused_computation.69 | convolution fusion | flops 205390080 | bytes 8913920 | tf_op jit(solution)/shard_map/czakm,ckn->zanm/dot_general | solution.py:71
  561.0 0.1 stack.86
  561.2 0.0 copy-start.6
  561.2 0.8 reduce_max.37
  562.1 0.1 copy-done.6
  (23 shorter events, 0.1 us)
Async XLA Ops:
  0.6 5.7 %copy-start.12 = (s32[2,2,1]{1,2,0:T(1,128)S(1)}, s32[2,2,1]{1,2,0:T(1,128)}, u32[]{:S(2)}) copy-start(s32[2,2,1]{1,2,0:T(1,128)} %param.3) | copy-start | bytes 52
  0.6 99.5 %all-to-all-start = ((f32[4,2,256,1024]{3,2,1,0:T(8,128)}), f32[4,2,256,1024]{3,2,1,0:T(8,128)}, u32[]{:S(2)}, u32[]{:S(2)}) async-start(f32[4,2,256,1024]{3,2,1,0:T(8,128)} %param.2), calls=%async_computation | async-start | bytes 16777216 | tf_op jit(solution)/shard_map/all_to_all | solution.py:78
  14.8 132.9 %copy-start.9 = (f32[8,128]{1,0:T(8,128)}, f32[8,128]{1,0:T(8,128)S(1)}, u32[]{:S(2)}) copy-start(f32[8,128]{1,0:T(8,128)S(1)} %get-tuple-element.51) | copy-start | bytes 12292
  110.5 7.3 %copy-start = (f32[8,128,1024]{2,1,0:T(8,128)S(1)}, f32[8,128,1024]{2,1,0:T(8,128)}, u32[]{:S(2)}) copy-start(f32[8,128,1024]{2,1,0:T(8,128)} %get-tuple-element.22) | copy-start | bytes 12582916
  214.7 183.8 %collective-permute-start = (f32[2,8,128,8,128]{4,1,3,2,0:T(8,128)}, f32[2,8,128,8,128]{4,1,3,2,0:T(8,128)}, u32[]{:S(2)}, u32[]{:S(2)}) collective-permute-start(f32[2,8,128,8,128]{4,1,3,2,0:T(8,128)} %bitcast_multiply_fusion.2), channel_id=1, source_target_pairs={{1,0},{2,1},{3,2},{4,3},{5,4},{6,5},{7,6},{8,7},{9,8},{10,9},{11,1... | collective-permute-start | bytes 25165832 | tf_op jit(solution)/shard_map/ppermute | solution.py:20
  241.1 19.3 %copy-start.2 = (f32[1,8,128,8,128]{4,3,2,1,0:T(8,128)S(1)}, f32[1,8,128,8,128]{4,3,2,1,0:T(8,128)}, u32[]{:S(2)}) copy-start(f32[1,8,128,8,128]{4,3,2,1,0:T(8,128)} %get-tuple-element.36) | copy-start | bytes 12582916
  241.1 19.3 %copy-start.3 = (f32[1,8,128,8,128]{4,3,2,1,0:T(8,128)S(1)}, f32[1,8,128,8,128]{4,3,2,1,0:T(8,128)}, u32[]{:S(2)}) copy-start(f32[1,8,128,8,128]{4,3,2,1,0:T(8,128)} %get-tuple-element.37) | copy-start | bytes 12582916
  257.6 233.9 %collective-permute-start.1 = (f32[2,8,128,8,128]{4,1,3,2,0:T(8,128)}, f32[2,8,128,8,128]{4,1,3,2,0:T(8,128)}, u32[]{:S(2)}, u32[]{:S(2)}) collective-permute-start(f32[2,8,128,8,128]{4,1,3,2,0:T(8,128)} %bitcast_multiply_fusion), channel_id=1, source_target_pairs={{7,0},{8,1},{9,2},{10,3},{11,4},{12,5},{13,6},{14,7},{15,8},{16,9}... | collective-permute-start | bytes 25165832 | tf_op jit(solution)/shard_map/ppermute | solution.py:20
  260.4 2.2 copy-start.1
  413.3 4.0 copy-start.7
  413.4 4.0 copy-start.8
  417.4 8.1 %copy-start.4 = (f32[1,128,2,128]{1,3,2,0:T(8,128)S(1)}, f32[1,128,2,128]{1,3,2,0:T(8,128)}, u32[]{:S(2)}) copy-start(f32[1,128,2,128]{1,3,2,0:T(8,128)} %get-tuple-element.24) | copy-start | bytes 393220
  417.4 8.1 %copy-start.5 = (f32[1,128,2,128]{1,3,2,0:T(8,128)S(1)}, f32[1,128,2,128]{1,3,2,0:T(8,128)}, u32[]{:S(2)}) copy-start(f32[1,128,2,128]{1,3,2,0:T(8,128)} %get-tuple-element.29) | copy-start | bytes 393220
  531.1 12.3 %copy-start.10 = (f32[8,128]{1,0:T(8,128)S(1)}, f32[8,128]{1,0:T(8,128)}, u32[]{:S(2)}) copy-start(f32[8,128]{1,0:T(8,128)} %copy-done.9) | copy-start | bytes 12292
  531.1 12.3 %copy-start.11 = (f32[8,128]{1,0:T(8,128)S(1)}, f32[8,128]{1,0:T(8,128)}, u32[]{:S(2)}) copy-start(f32[8,128]{1,0:T(8,128)} %fusion.152) | copy-start | bytes 12292
  561.2 1.0 copy-start.6
where the time goes:
time: 571 us; the launch traced here: 563 us
  matrix products  253 us (44%)
  waiting for transfers between devices  187 us (33%)
  other arithmetic  85.8 us (15%)
  local copies, waits for them, and re-layouts  15.8 us (3%)
  starting transfers between devices  11.7 us (2%)
  between operations  9.21 us (2%)
    ppermute x2, waiting for transfers between devices, from_behind(): return lax.ppermute(x, axis, pairs)  104 us
    all_to_all x1, waiting for transfers between devices, on_device(): lax.all_to_all(stored, 'slab', split_axis=0, concat_axis=1, tiled=True)[0]  83.4 us
    dot_general x4, matrix products, forward(): jnp.einsum('czakj,czey->eyakj', pair, tabs['f_depth'], precision=HIGH)  65.1 us
    dot_general x4, matrix products, forward(): jnp.einsum('czakj,caeb->ezbkj', pair, tabs['f_across'], precision=HIGH)  38.1 us
    dot_general x4, matrix products, forward(): jnp.einsum('czakm,cmej->ezakj', pair, tabs['f_inner'], precision=HIGH)  36.6 us
    dot_general x4, matrix products, forward(): jnp.einsum('zanm,nek->ezakm', shaped, tabs['f_outer'][0], precision=HIGH)  34.1 us
    sub x2, other arithmetic, spin(): real * cos_t - sign * imag * sin_t  32.8 us
    dot_general x2, matrix products, inverse_real(): jnp.einsum('czbkj,cbea->ezakj', pair, tabs['b_across'], precision=HIGH)  25.3 us
  transfers between devices with their start and end apart: 3, of which 3 were waited for; matrix products, arithmetic and copies ran while one was open for 30% of the time, Pallas kernels for 0%

commit v1 on v0

v1 whole, which is shorter than its diff:
```python
import functools
import math

import jax
import jax.numpy as jnp
from jax import lax
from jax.experimental import pallas as pl
from jax.experimental.pallas import tpu as pltpu
from jax.sharding import PartitionSpec as P

GC = 7
ROUNDS = 2
A = 128
L = 1024
Z = 8
FLOOR = 0.25
BF = jnp.bfloat16
F32 = jnp.float32
HALF = math.sqrt(0.5)


def split(x):
    hi = x.astype(BF)
    lo = (x - hi.astype(F32)).astype(BF)
    return hi, lo


def split_table(x):
    hi = lax.reduce_precision(x, exponent_bits=8, mantissa_bits=7)
    return hi.astype(BF), (x - hi).astype(BF)


def three_rows(x):
    hi, lo = split_table(x)
    return jnp.concatenate((hi, hi, lo), axis=0)


def three_cols(x):
    hi, lo = split_table(x)
    return jnp.concatenate((hi, hi, lo), axis=1)


def trig(index, total):
    angle = (index % total).astype(F32) * (2.0 * math.pi / total)
    return jnp.cos(angle), jnp.sin(angle)


def iota(length):
    return lax.optimization_barrier(jnp.arange(length, dtype=jnp.int32))


def along_tables():
    rows = iota(512)[:, None]
    m = iota(256)[None, :]
    n4 = rows[:256]
    m4 = m[:, :128]
    nyquist = (1 - 2 * (n4 % 2)).astype(F32)
    first = m4 == 0
    c0, s0 = trig(n4 * (4 * m4), L)
    c2, s2 = trig(n4 * (4 * m4 + 2), L)
    c1, s1 = trig(rows * (2 * m + 1), L)
    im0 = jnp.where(first, nyquist, -s0)
    scale = 1.0 / L
    fwd = (
        three_rows(scale * jnp.concatenate((c0, im0), axis=1)),
        three_rows(scale * jnp.concatenate((c2, -s2), axis=1)),
        three_rows(scale * jnp.concatenate((c1, -s1), axis=1)),
    )
    return fwd


def back_tables():
    cols = iota(512)[None, :]
    m = iota(256)[:, None]
    n4 = cols[:, :256]
    m4 = m[:128]
    nyquist = (1 - 2 * (n4 % 2)).astype(F32)
    first = m4 == 0
    c0, s0 = trig(n4 * (4 * m4), L)
    c2, s2 = trig(n4 * (4 * m4 + 2), L)
    c1, s1 = trig(cols * (2 * m + 1), L)
    scale = 1.0 / L
    re0 = jnp.where(first, scale, 2.0 * scale * c0)
    im0 = jnp.where(first, scale * nyquist, -2.0 * scale * s0)
    odd = 2.0 * scale * jnp.concatenate((c1[:128], -s1[:128], c1[128:], -s1[128:]), axis=0)
    return (
        three_rows(jnp.concatenate((re0, im0), axis=0)),
        three_rows(2.0 * scale * jnp.concatenate((c2, -s2), axis=0)),
        three_rows(odd),
    )


def across_forward(offset):
    v = iota(A)[:, None]
    r = iota(A)[None, :]
    c, s = trig((r - offset + A) * v, A)
    top = jnp.concatenate((c, s), axis=1)
    low = jnp.concatenate((-s, c), axis=1)
    return three_cols(jnp.concatenate((top, low), axis=0))


def across_back():
    v = iota(A)[None, :]
    a = iota(A)[:, None]
    c, s = trig(a * v, A)
    top = jnp.concatenate((c, -s), axis=1)
    low = jnp.concatenate((s, c), axis=1)
    return three_cols(jnp.concatenate((top, low), axis=0))


def edge_tables():
    lane = iota(A)
    i = lane[:, None]
    j = lane[None, :]
    inside = jnp.logical_and(i < Z, j < Z)
    c, s = trig(i * j, Z)
    c = jnp.where(inside, c, 0.0)
    s = jnp.where(inside, s, 0.0)
    fwd = jnp.concatenate(
        (jnp.concatenate((c, -s), axis=1), jnp.concatenate((s, c), axis=1)), axis=0
    )
    rev = jnp.concatenate(
        (jnp.concatenate((c, s), axis=1), jnp.concatenate((-s, c), axis=1)), axis=0
    )
    flip = ((i + j) % A == 0).astype(F32)
    return fwd, rev, flip


def dot3_left(x, table):
    hi, lo = split(x)
    return jnp.dot(jnp.concatenate((hi, lo, hi), axis=1), table, preferred_element_type=F32)


def dot3_right(table, x):
    hi, lo = split(x)
    return jnp.dot(table, jnp.concatenate((hi, lo, hi), axis=0), preferred_element_type=F32)


def choose(y_ref, offset):
    row = lax.broadcasted_iota(jnp.int32, (A, 512), 0)
    later = row >= offset
    real = jnp.where(later, y_ref[0, :A, :], y_ref[0, A:, :])
    imag = jnp.where(later, y_ref[1, :A, :], y_ref[1, A:, :])
    return jnp.concatenate((real, imag), axis=0)


def given_kernel(off_ref, x_ref, w0_ref, w2_ref, w1_ref, a_ref, y_ref, g0_ref, g1_ref):
    x = x_ref[0]
    low = x[:, :512]
    high = x[:, 512:]
    y0 = low + high
    d1 = dot3_left(low - high, w1_ref[...])
    y_ref[0, 0, :, 256:512] = d1[:, :256]
    y_ref[0, 1, :, 256:512] = d1[:, 256:]
    d0 = dot3_left(y0[:, :256] + y0[:, 256:], w0_ref[...])
    y_ref[0, 0, :, 0:128] = d0[:, :128]
    y_ref[0, 1, :, 0:128] = d0[:, 128:]
    d2 = dot3_left(y0[:, :256] - y0[:, 256:], w2_ref[...])
    y_ref[0, 0, :, 128:256] = d2[:, :128]
    y_ref[0, 1, :, 128:256] = d2[:, 128:]
    for out_ref, k in ((g0_ref, 0), (g1_ref, 1)):
        spec = dot3_right(a_ref[k], choose(y_ref.at[0], off_ref[k]))
        out_ref[0, 0] = spec[:A]
        out_ref[0, 1] = spec[A:]


def own_kernel(off_ref, y_ref, a_ref, g0_ref, g1_ref):
    for out_ref, k in ((g0_ref, 0), (g1_ref, 1)):
        spec = dot3_right(a_ref[k], choose(y_ref.at[0], off_ref[k]))
        out_ref[0, 0] = spec[:A]
        out_ref[0, 1] = spec[A:]


def whole(shape):
    return pl.BlockSpec(shape, lambda *_: (0,) * len(shape))


def forward_given(planes, offs, fwd, mats, interpret=False):
    depth = planes.shape[0]
    spec_shape = jax.ShapeDtypeStruct((depth, 2, A, 512), F32)
    spec_block = pl.BlockSpec((1, 2, A, 512), lambda z, *_: (z, 0, 0, 0))
    return pl.pallas_call(
        given_kernel,
        out_shape=(jax.ShapeDtypeStruct((depth, 2, 256, 512), F32), spec_shape, spec_shape),
        grid_spec=pltpu.PrefetchScalarGridSpec(
            num_scalar_prefetch=1,
            grid=(depth,),
            in_specs=[
                pl.BlockSpec((1, 256, L), lambda z, *_: (z, 0, 0)),
                whole((768, 256)),
                whole((768, 256)),
                whole((1536, 512)),
                whole((2, 256, 768)),
            ],
            out_specs=[pl.BlockSpec((1, 2, 256, 512), lambda z, *_: (z, 0, 0, 0)), spec_block, spec_block],
        ),
        cost_estimate=pl.CostEstimate(flops=depth * 900_000_000, bytes_accessed=depth * 3_200_000, transcendentals=0),
        interpret=interpret,
        name="forward_given",
    )(offs, planes, *fwd, mats)


def forward_own(y, offs, mats, interpret=False):
    depth = y.shape[0]
    spec_shape = jax.ShapeDtypeStruct((depth, 2, A, 512), F32)
    spec_block = pl.BlockSpec((1, 2, A, 512), lambda z, *_: (z, 0, 0, 0))
    return pl.pallas_call(
        own_kernel,
        out_shape=(spec_shape, spec_shape),
        grid_spec=pltpu.PrefetchScalarGridSpec(
            num_scalar_prefetch=1,
            grid=(depth,),
            in_specs=[
                pl.BlockSpec((1, 2, 256, 512), lambda z, *_: (z, 0, 0, 0)),
                whole((2, 256, 768)),
            ],
            out_specs=[spec_block, spec_block],
        ),
        cost_estimate=pl.CostEstimate(flops=depth * 400_000_000, bytes_accessed=depth * 2_000_000, transcendentals=0),
        interpret=interpret,
        name="forward_own",
    )(offs, y, mats)


def times_i(x, sign):
    return (-sign * x[1], sign * x[0])


def cadd(x, y):
    return (x[0] + y[0], x[1] + y[1])


def csub(x, y):
    return (x[0] - y[0], x[1] - y[1])


def eighth(x, sign):
    return ((x[0] - sign * x[1]) * HALF, (x[1] + sign * x[0]) * HALF)


def dft4(x, sign):
    a = cadd(x[0], x[2])
    b = csub(x[0], x[2])
    c = cadd(x[1], x[3])
    d = times_i(csub(x[1], x[3]), sign)
    return [cadd(a, c), cadd(b, d), csub(a, c), csub(b, d)]


def dft8(x, sign):
    even = dft4([x[0], x[2], x[4], x[6]], sign)
    odd = dft4([x[1], x[3], x[5], x[7]], sign)
    odd = [odd[0], eighth(odd[1], sign), times_i(odd[2], sign), times_i(eighth(odd[3], sign), sign)]
    return [cadd(even[k], odd[k]) for k in range(4)] + [csub(even[k], odd[k]) for k in range(4)]


def normalized(p, q):
    real = p[0] * q[0] + p[1] * q[1]
    imag = p[1] * q[0] - p[0] * q[1]
    scale = lax.rsqrt(jnp.maximum(real * real + imag * imag, FLOOR * FLOOR))
    return (real * scale, imag * scale)


def to_lanes(ref, part):
    lane = lax.broadcasted_iota(jnp.int32, (A, 128), 1)
    out = jnp.zeros((A, 128), F32)
    for z in range(Z):
        block = ref(z, part)
        if z:
            block = pltpu.roll(block, z, 1)
        out = jnp.where(lane == z, block, out)
    return out


def pair_kernel(pieces, *refs):
    own_refs = refs[:pieces]
    far_refs = refs[pieces : 2 * pieces]
    ab_ref, v0_ref, v2_ref, v1_ref, ef_ref, er_ref, flip_ref = refs[2 * pieces : 2 * pieces + 7]
    surf_ref, peak_ref, r_ref, qh_ref, ql_ref = refs[-5:]
    step = pl.program_id(0)

    def get(group, z, part, rows):
        return group[z % pieces][z // pieces, part, rows, :]

    def chunk(i, _):
        rows = pl.ds(pl.multiple_of(i * 8, 8), 8)
        own = dft8([(get(own_refs, z, 0, rows), get(own_refs, z, 1, rows)) for z in range(Z)], -1.0)
        far = dft8([(get(far_refs, z, 0, rows), get(far_refs, z, 1, rows)) for z in range(Z)], -1.0)
        back = dft8([normalized(own[u], far[u]) for u in range(Z)], 1.0)
        for z in range(Z):
            r_ref[rows, z * 128 : (z + 1) * 128] = back[z][0]
            r_ref[pl.ds(pl.multiple_of(i * 8 + A, 8), 8), z * 128 : (z + 1) * 128] = back[z][1]
        return 0

    lax.fori_loop(0, A // 8, chunk, 0)

    @pl.when(step == 0)
    def _():
        high = lax.Precision.HIGHEST
        every = slice(None)

        def edge(group):
            packed = jnp.concatenate(
                [to_lanes(lambda z, part: get(group, z, part, every), part) for part in range(2)], axis=1
            )
            here = jnp.dot(packed, ef_ref[...], precision=high, preferred_element_type=F32)
            turned = jnp.dot(packed, er_ref[...], precision=high, preferred_element_type=F32)
            there = jnp.dot(flip_ref[...], turned, precision=high, preferred_element_type=F32)
            hr, hi = here[:, :128], here[:, 128:]
            tr, ti = there[:, :128], there[:, 128:]
            return ((hr + tr) * 0.5, (hi - ti) * 0.5), ((hi + ti) * 0.5, (tr - hr) * 0.5)

        own_zero, own_last = edge(own_refs)
        far_zero, far_last = edge(far_refs)
        zero = normalized(own_zero, far_zero)
        last = normalized(own_last, far_last)
        both = jnp.concatenate((zero[0] - last[1], zero[1] + last[0]), axis=1)
        field = jnp.dot(both, er_ref[...], precision=high, preferred_element_type=F32)
        lane = lax.broadcasted_iota(jnp.int32, (A, 128), 1)
        for part in range(2):
            source = field[:, part * 128 : (part + 1) * 128]
            for z in range(Z):
                moved = pltpu.roll(source, 128 - z, 1) if z else source
                place = (slice(part * A, (part + 1) * A), slice(z * 128, (z + 1) * 128))
                r_ref[place] = jnp.where(lane == 0, moved, r_ref[place])

    for half in range(2):
        q = dot3_right(ab_ref[...], r_ref[:, half * 512 : (half + 1) * 512])
        hi, lo = split(q)
        for k in range(4):
            z = half * 4 + k
            for part in range(2):
                rows = slice(part * A, (part + 1) * A)
                qh_ref[step, z, :, part * 128 : (part + 1) * 128] = hi[rows, k * 128 : (k + 1) * 128]
                ql_ref[step, z, :, part * 128 : (part + 1) * 128] = lo[rows, k * 128 : (k + 1) * 128]

    @pl.when(step == 3)
    def _():
        def planes(i, _):
            two = pl.ds(i * 2, 2)

            def take(b):
                return qh_ref[b, two].reshape(2 * A, 256), ql_ref[b, two].reshape(2 * A, 256)

            h0, l0 = take(0)
            y00 = jnp.dot(jnp.concatenate((h0, l0, h0), axis=1), v0_ref[...], preferred_element_type=F32)
            h2, l2 = take(1)
            y01 = jnp.dot(jnp.concatenate((h2, l2, h2), axis=1), v2_ref[...], preferred_element_type=F32)
            h1, l1 = take(2)
            h3, l3 = take(3)
            y1 = jnp.dot(
                jnp.concatenate((h1, h3, l1, l3, h1, h3), axis=1), v1_ref[...], preferred_element_type=F32
            )
            y0 = jnp.concatenate((y00 + y01, y00 - y01), axis=1)
            top = jnp.concatenate((y0 + y1, y0 - y1), axis=1)
            top = jnp.maximum(top[:A], top[A:])

            @pl.when(i == 0)
            def _():
                surf_ref[0] = top

            @pl.when(i > 0)
            def _():
                surf_ref[0] = jnp.maximum(surf_ref[0], top)

            return 0

        lax.fori_loop(0, Z // 2, planes, 0)
        peak_ref[0] = jnp.broadcast_to(jnp.max(surf_ref[0]), (8, 128))


def pair(rnd, own, far, ab, back, edges, before, interpret=False):
    pieces = len(own)
    depth = Z // pieces
    block = pl.BlockSpec((depth, 2, A, 128), lambda w: (0, 0, 0, w))
    args = list(own) + list(far) + [ab, *back, *edges]
    in_specs = [block] * (2 * pieces) + [
        whole((256, 768)),
        whole((768, 256)),
        whole((768, 256)),
        whole((1536, 512)),
        whole((256, 256)),
        whole((256, 256)),
        whole((128, 128)),
    ]
    aliases = {}
    if before is not None:
        aliases = {len(args): 0, len(args) + 1: 1}
        args += list(before)
        in_specs += [pl.BlockSpec(memory_space=pl.ANY)] * 2
    return pl.pallas_call(
        functools.partial(pair_kernel, pieces),
        out_shape=(
            jax.ShapeDtypeStruct((ROUNDS, A, L), F32),
            jax.ShapeDtypeStruct((ROUNDS, 8, 128), F32),
        ),
        grid=(4,),
        in_specs=in_specs,
        out_specs=(
            pl.BlockSpec((1, A, L), lambda w: (rnd, 0, 0)),
            pl.BlockSpec((1, 8, 128), lambda w: (rnd, 0, 0)),
        ),
        scratch_shapes=[
            pltpu.VMEM((2 * A, Z * 128), F32),
            pltpu.VMEM((4, Z, A, 256), BF),
            pltpu.VMEM((4, Z, A, 256), BF),
        ],
        input_output_aliases=aliases,
        cost_estimate=pl.CostEstimate(flops=5_000_000_000, bytes_accessed=12_000_000, transcendentals=500_000),
        interpret=interpret,
        name=f"pair_{rnd}",
    )(*args)


def shift(x, by, size, ok):
    pairs = [(i + by, i) for i in range(size) if ok(i)]
    return lax.ppermute(x, ("tile", "slab"), pairs)


def on_device(stored, offsets):
    size = lax.axis_size(("tile", "slab"))
    owned = lax.all_to_all(stored, "slab", split_axis=0, concat_axis=1, tiled=True)[0]
    offs = offsets[:, :, 0]
    fwd = along_tables()
    back = back_tables()
    ab = across_back()
    edges = edge_tables()
    own_mats = jnp.stack([across_forward(offs[r, 0]) for r in range(ROUNDS)])
    given_mats = jnp.stack([across_forward(offs[r, 1]) for r in range(ROUNDS)])
    y, g0, g1 = forward_given(owned, offs[:, 1], fwd, given_mats)
    far0 = shift(g0, 1, size, lambda t: t % GC != GC - 1 and t + 1 < size)
    far1 = shift(g1, GC, size, lambda t: t + GC < size)
    own0, own1 = forward_own(y, offs[:, 0], own_mats)
    out = pair(0, [own0], [far0], ab, back, edges, None)
    surface, peak = pair(1, [own1], [far1], ab, back, edges, out)
    return surface[:, None], peak[:, 0, :1]


def solution(mesh):
    return jax.shard_map(
        on_device,
        mesh=mesh,
        in_specs=(P("tile", "slab", None, None), P(None, None, ("tile", "slab"))),
        out_specs=(P(None, ("tile", "slab"), None, None), P(None, ("tile", "slab"))),
        check_vma=False,
    )
```

time: 571 us -> 275 us (0.48); the launches traced: 563 us -> 275 us
  matrix products: 253 us -> 0 us
  other arithmetic: 85.8 us -> 21.5 us
  Pallas kernels: 0 us -> 57.5 us
  local copies, waits for them, and re-layouts: 15.8 us -> 2.63 us
  between operations: 9.21 us -> 0.82 us
  waiting for transfers between devices: 187 us -> 180 us
    dot_general x24 -> x0, matrix products: 253 us -> none  [the longest x4 65.1 us: forward(): jnp.einsum('czakj,czey->eyakj', pair, tabs['f_depth'], precision=HIGH)]
    pallas_call x0 -> x4, Pallas kernels: none -> 57.5 us  [the longest x2 30.9 us: pair(): pl.pallas_call(functools.partial(pair_kernel, pieces), out_shape=(jax.Sha...]
    sub x2 -> x0, other arithmetic: 32.8 us -> none  [spin(): real * cos_t - sign * imag * sin_t]
    div x4 -> x0, other arithmetic: 20.5 us -> none  [the longest x2 12.6 us: on_device(): cross_real / denom]
    mul x5 -> x2, other arithmetic: 17.4 us -> 0.02 us  [the longest x1 0.01 us: back_tables(): im0 = jnp.where(first, scale * nyquist, -2.0 * scale * s0)]
    another operation x6, other arithmetic: 13.3 us -> 2.01 us  [the longest x3 1.01 us: on_device(): given_mats = jnp.stack([across_forward(offs[r, 1]) for r in range(ROUNDS)])]
    dynamic_slice x1 -> x0, local copies, waits for them, and re-layouts: 9.33 us -> none  [on_device(): own_strip = lax.dynamic_slice_in_dim(owned, offsets[rnd, 0, 0], A, 1)]
    concatenate x0 -> x8, other arithmetic: none -> 7.36 us  [the longest x6 5.77 us: three_rows(): return jnp.concatenate((hi, hi, lo), axis=0)]
  transfers between devices with their start and end apart: 3 -> 3, of which waited for: 3 -> 3; matrix products, arithmetic and copies ran while one was open for 30% -> 8% of each run, Pallas kernels for 0% -> 10%
where the time goes in v1:
time: 275 us
  waiting for transfers between devices  180 us (65%)
  Pallas kernels  57.5 us (21%)
  other arithmetic  21.5 us (8%)
  starting transfers between devices  12 us (4%)
    ppermute x2, waiting for transfers between devices, shift(): return lax.ppermute(x, ('tile', 'slab'), pairs)  99.7 us
    all_to_all x1, waiting for transfers between devices, on_device(): lax.all_to_all(stored, 'slab', split_axis=0, concat_axis=1, tiled=True)[0]  80.6 us
    pallas_call x2, Pallas kernels, pair(): pl.pallas_call(functools.partial(pair_kernel, pieces), out_shape=(jax.Sha...  30.9 us
    pallas_call x1, Pallas kernels, forward_given(): pl.pallas_call(given_kernel, out_shape=(jax.ShapeDtypeStruct((depth, 2, 2...  15.9 us
    pallas_call x1, Pallas kernels, forward_own(): pl.pallas_call(own_kernel, out_shape=(spec_shape, spec_shape), grid_spec=...  10.8 us
    cos x4, other arithmetic, trig(): return (jnp.cos(angle), jnp.sin(angle))  6.5 us
    ppermute x2, starting transfers between devices, shift(): return lax.ppermute(x, ('tile', 'slab'), pairs)  6.19 us
    concatenate x6, other arithmetic, three_rows(): return jnp.concatenate((hi, hi, lo), axis=0)  5.77 us
  transfers between devices with their start and end apart: 3, of which 3 were waited for; matrix products, arithmetic and copies ran while one was open for 8% of the time, Pallas kernels for 10%

profile of v1, /device:TPU:56, one launch (start us, length us, event | category | flops | bytes accessed | tf_op | source)
XLA Modules:
  0.0 274.7 jit_solution(4054761604851190873)
XLA Ops:
  0.6 0.0 copy-start
  0.6 5.8 %all-to-all-start = ((f32[4,2,256,1024]{3,2,1,0:T(8,128)}), f32[4,2,256,1024]{3,2,1,0:T(8,128)}, u32[]{:S(2)}, u32[]{:S(2)}) async-start(f32[4,2,256,1024]{3,2,1,0:T(8,128)} %param.2), calls=%async_computation | async-start | bytes 16777216 | tf_op jit(solution)/shard_map/all_to_all | solution.py:421
  6.4 0.0 copy-done
  6.4 0.7 slice_reduce_fusion.1
  7.1 0.6 fusion.86
  7.7 2.5 subtract_add_fusion.1
  10.2 1.6 fusion.73
  11.9 1.1 fusion.55
  13.0 0.1 reduce-precision_convert_fusion.9
  13.1 0.8 pad_maximum_fusion.4.w0_ref
  13.9 0.8 pad_maximum_fusion.5.w2_ref
  14.7 0.1 reduce-precision_convert_fusion.6
  14.8 0.9 pad_maximum_fusion.2.a_ref
  15.8 2.1 fusion.21
  17.9 0.2 reduce-precision_convert_fusion.1
  18.1 1.3 pad_maximum_fusion.w1_ref
  19.4 80.6 %all-to-all-done = f32[4,2,256,1024]{3,2,1,0:T(8,128)} async-done(((f32[4,2,256,1024]{3,2,1,0:T(8,128)}), f32[4,2,256,1024]{3,2,1,0:T(8,128)}, u32[]{:S(2)}, u32[]{:S(2)}) %all-to-all-start) | async-done | bytes 8388640 | tf_op jit(solution)/shard_map/all_to_all | solution.py:421
  100.1 15.9 %forward_given.1 = (f32[8,2,256,512]{3,2,1,0:T(8,128)}, f32[8,2,128,512]{3,2,1,0:T(8,128)}, f32[8,2,128,512]{3,2,1,0:T(8,128)}) custom-call(s32[2]{0:T(128)} %get-tuple-element.24.off_ref, f32[8,256,1024]{2,1,0:T(8,128)} %bitcast.1.x_ref, bf16[768,256]{1,0:T(8,128)(2,1)} %pad_maximum_fusion.4.w0_ref, bf16[768,256]{1,0:T(8,128)(2,1)} %pad_maximum_fusion.5.w2_ref, ...), custom_call_target="tpu_custom_call" | custom-call | flops 7200000000 | bytes 25600000 | tf_op jit(solution)/shard_map/forward_given/pallas_call | solution.py:182
  115.9 3.1 %collective-permute-start.1 = (f32[8,2,128,512]{3,2,1,0:T(8,128)}, f32[8,2,128,512]{3,2,1,0:T(8,128)}, u32[]{:S(2)}, u32[]{:S(2)}) collective-permute-start(f32[8,2,128,512]{3,2,1,0:T(8,128)} %get-tuple-element.15), channel_id=1, source_target_pairs={{1,0},{2,1},{3,2},{4,3},{5,4},{6,5},{8,7},{9,8},{10,9},{11,10},{12... | collective-permute-start | bytes 12582920 | tf_op jit(solution)/shard_map/ppermute | solution.py:416
  119.0 3.1 %collective-permute-start = (f32[8,2,128,512]{3,2,1,0:T(8,128)}, f32[8,2,128,512]{3,2,1,0:T(8,128)}, u32[]{:S(2)}, u32[]{:S(2)}) collective-permute-start(f32[8,2,128,512]{3,2,1,0:T(8,128)} %get-tuple-element.13), channel_id=1, source_target_pairs={{7,0},{8,1},{9,2},{10,3},{11,4},{12,5},{13,6},{14,7},{15,8},{16,9}... | collective-permute-start | bytes 12582920 | tf_op jit(solution)/shard_map/ppermute | solution.py:416
  122.2 0.1 reduce-precision_convert_fusion.4
  122.3 0.8 pad_maximum_fusion.6.refs_2_
  123.1 1.1 fusion.54
  124.2 0.1 reduce-precision_convert_fusion.2
  124.3 0.8 pad_maximum_fusion.7.refs_3_
  125.1 0.8 pad_maximum_fusion.8.refs_4_
  125.9 0.8 fusion.9
  126.7 0.9 pad_maximum_fusion.3.a_ref
  127.7 2.1 fusion.20
  129.8 0.1 slice_negate_fusion.1
  129.9 0.2 reduce-precision_convert_fusion
  130.1 0.7 fusion.57.refs_8_
  130.8 1.3 pad_maximum_fusion.1.refs_5_
  132.1 10.8 %forward_own.1 = (f32[8,2,128,512]{3,2,1,0:T(8,128)}, f32[8,2,128,512]{3,2,1,0:T(8,128)}) custom-call(s32[2]{0:T(128)} %get-tuple-element.25.off_ref, f32[8,2,256,512]{3,2,1,0:T(8,128)} %get-tuple-element.11.y_ref, bf16[2,256,768]{2,1,0:T(8,128)(2,1)} %pad_maximum_fusion.3.a_ref), custom_call_target="tpu_custom_call" | custom-call | flops 3200000000 | bytes 16000000 | tf_op jit(solution)/shard_map/forward_own/pallas_call | solution.py:207
  142.9 67.0 %collective-permute-done.1.refs_1_ = f32[8,2,128,512]{3,2,1,0:T(8,128)} collective-permute-done((f32[8,2,128,512]{3,2,1,0:T(8,128)}, f32[8,2,128,512]{3,2,1,0:T(8,128)}, u32[]{:S(2)}, u32[]{:S(2)}) %collective-permute-start.1) | collective-permute-done | bytes 4194336 | tf_op jit(solution)/shard_map/ppermute | solution.py:416
  209.9 15.4 %pair_0.1 = (f32[2,128,1024]{2,1,0:T(8,128)}, f32[2,8,128]{2,1,0:T(8,128)}) custom-call(f32[8,2,128,512]{3,2,1,0:T(8,128)} %get-tuple-element.14.refs_0_, f32[8,2,128,512]{3,2,1,0:T(8,128)} %collective-permute-done.1.refs_1_, bf16[256,768]{1,0:T(8,128)(2,1)} %pad_maximum_fusion.6.refs_2_, bf16[768,256]{1,0:T(8,128)(2,1)} %pad_maximum_fusion.7.refs_3_, ...), custom_call_target="tpu_custom_call" | custom-call | flops 5000000000 | bytes 12000000 | tf_op jit(solution)/shard_map/pair_0/pallas_call | solution.py:390
  225.3 32.7 %collective-permute-done.refs_1_ = f32[8,2,128,512]{3,2,1,0:T(8,128)} collective-permute-done((f32[8,2,128,512]{3,2,1,0:T(8,128)}, f32[8,2,128,512]{3,2,1,0:T(8,128)}, u32[]{:S(2)}, u32[]{:S(2)}) %collective-permute-start) | collective-permute-done | bytes 4194336 | tf_op jit(solution)/shard_map/ppermute | solution.py:416
  258.0 15.4 %pair_1.1 = (f32[2,128,1024]{2,1,0:T(8,128)}, f32[2,8,128]{2,1,0:T(8,128)}) custom-call(f32[8,2,128,512]{3,2,1,0:T(8,128)} %get-tuple-element.12.refs_0_, f32[8,2,128,512]{3,2,1,0:T(8,128)} %collective-permute-done.refs_1_, bf16[256,768]{1,0:T(8,128)(2,1)} %pad_maximum_fusion.6.refs_2_, ...), custom_call_target="tpu_custom_call", output_to_operand_aliasing={{0}: (9, {}), {1}: (10, {})} | custom-call | flops 5000000000 | bytes 12000000 | tf_op jit(solution)/shard_map/pair_1/pallas_call | solution.py:390
  273.4 1.3 slice_reduce_fusion
  (17 shorter events, 0.2 us)
Async XLA Ops:
  0.6 5.8 %copy-start = (s32[2,2,1]{1,2,0:T(1,128)S(1)}, s32[2,2,1]{1,2,0:T(1,128)}, u32[]{:S(2)}) copy-start(s32[2,2,1]{1,2,0:T(1,128)} %param.3) | copy-start | bytes 52
  0.6 99.5 %all-to-all-start = ((f32[4,2,256,1024]{3,2,1,0:T(8,128)}), f32[4,2,256,1024]{3,2,1,0:T(8,128)}, u32[]{:S(2)}, u32[]{:S(2)}) async-start(f32[4,2,256,1024]{3,2,1,0:T(8,128)} %param.2), calls=%async_computation | async-start | bytes 16777216 | tf_op jit(solution)/shard_map/all_to_all | solution.py:421
  115.9 93.9 %collective-permute-start.1 = (f32[8,2,128,512]{3,2,1,0:T(8,128)}, f32[8,2,128,512]{3,2,1,0:T(8,128)}, u32[]{:S(2)}, u32[]{:S(2)}) collective-permute-start(f32[8,2,128,512]{3,2,1,0:T(8,128)} %get-tuple-element.15), channel_id=1, source_target_pairs={{1,0},{2,1},{3,2},{4,3},{5,4},{6,5},{8,7},{9,8},{10,9},{11,10},{12... | collective-permute-start | bytes 12582920 | tf_op jit(solution)/shard_map/ppermute | solution.py:416
  119.0 139.0 %collective-permute-start = (f32[8,2,128,512]{3,2,1,0:T(8,128)}, f32[8,2,128,512]{3,2,1,0:T(8,128)}, u32[]{:S(2)}, u32[]{:S(2)}) collective-permute-start(f32[8,2,128,512]{3,2,1,0:T(8,128)} %get-tuple-element.13), channel_id=1, source_target_pairs={{7,0},{8,1},{9,2},{10,3},{11,4},{12,5},{13,6},{14,7},{15,8},{16,9}... | collective-permute-start | bytes 12582920 | tf_op jit(solution)/shard_map/ppermute | solution.py:416

commit v2 on v0

v2 whole, which is shorter than its diff:
```python
import functools
import math

import jax
import jax.numpy as jnp
from jax import lax
from jax.experimental import pallas as pl
from jax.experimental.pallas import tpu as pltpu
from jax.sharding import PartitionSpec as P

GC = 7
ROUNDS = 2
A = 128
L = 1024
Z = 8
FLOOR = 0.25
BF = jnp.bfloat16
F32 = jnp.float32
HALF = math.sqrt(0.5)


def split(x):
    hi = x.astype(BF)
    lo = (x - hi.astype(F32)).astype(BF)
    return hi, lo


def split_table(x):
    hi = lax.reduce_precision(x, exponent_bits=8, mantissa_bits=7)
    return hi.astype(BF), (x - hi).astype(BF)


def three_rows(x):
    hi, lo = split_table(x)
    return jnp.concatenate((hi, hi, lo), axis=0)


def three_cols(x):
    hi, lo = split_table(x)
    return jnp.concatenate((hi, hi, lo), axis=1)


def trig(index, total):
    angle = (index % total).astype(F32) * (2.0 * math.pi / total)
    return jnp.cos(angle), jnp.sin(angle)


def iota(length):
    return lax.optimization_barrier(jnp.arange(length, dtype=jnp.int32))


def odd_tables():
    rows = iota(512)[:, None]
    m = iota(256)[None, :]
    c, s = trig(rows * (2 * m + 1), L)
    scale = 1.0 / L
    return three_rows(
        scale * jnp.concatenate((c[:, :128], -s[:, :128], c[:, 128:], -s[:, 128:]), axis=1)
    )


def even_tables():
    n = iota(256)[:, None]
    m = iota(A)[None, :]
    c0, s0 = trig(n * (4 * m), L)
    c2, s2 = trig(n * (4 * m + 2), L)
    last = (1 - 2 * (n % 2)).astype(F32)
    im0 = jnp.where(m == 0, last, -s0)
    scale = 1.0 / L
    return (
        three_rows(scale * jnp.concatenate((c0, im0), axis=1)),
        three_rows(scale * jnp.concatenate((c2, -s2), axis=1)),
    )


def odd_back():
    cols = iota(512)[None, :]
    m = iota(256)[:, None]
    c, s = trig(cols * (2 * m + 1), L)
    scale = 2.0 / L
    return jnp.stack(
        [three_rows(scale * jnp.concatenate((c[b : b + A], -s[b : b + A]), axis=0)) for b in (0, A)]
    )


def even_back():
    cols = iota(256)[None, :]
    m = iota(A)[:, None]
    c0, s0 = trig(cols * (4 * m), L)
    c2, s2 = trig(cols * (4 * m + 2), L)
    last = (1 - 2 * (cols % 2)).astype(F32)
    scale = 2.0 / L
    re0 = jnp.where(m == 0, 0.5 * scale, scale * c0)
    im0 = jnp.where(m == 0, 0.5 * scale * last, -scale * s0)
    return jnp.stack(
        (
            three_rows(jnp.concatenate((re0, im0), axis=0)),
            three_rows(scale * jnp.concatenate((c2, -s2), axis=0)),
        )
    )


def across_forward(offset):
    v = iota(A)[:, None]
    r = iota(A)[None, :]
    c, s = trig((r - offset + A) * v, A)
    top = jnp.concatenate((c, s), axis=1)
    low = jnp.concatenate((-s, c), axis=1)
    return three_cols(jnp.concatenate((top, low), axis=0))


def across_back():
    v = iota(A)[None, :]
    a = iota(A)[:, None]
    c, s = trig(a * v, A)
    top = jnp.concatenate((c, -s), axis=1)
    low = jnp.concatenate((s, c), axis=1)
    return three_cols(jnp.concatenate((top, low), axis=0))


def edge_tables():
    lane = iota(A)
    i = lane[:, None]
    j = lane[None, :]
    inside = jnp.logical_and(i < Z, j < Z)
    c, s = trig(i * j, Z)
    c = jnp.where(inside, c, 0.0)
    s = jnp.where(inside, s, 0.0)
    fwd = jnp.concatenate(
        (jnp.concatenate((c, -s), axis=1), jnp.concatenate((s, c), axis=1)), axis=0
    )
    rev = jnp.concatenate(
        (jnp.concatenate((c, s), axis=1), jnp.concatenate((-s, c), axis=1)), axis=0
    )
    flip = ((i + j) % A == 0).astype(F32)
    return fwd, rev, flip


def dot3_left(x, table):
    hi, lo = split(x)
    return jnp.dot(jnp.concatenate((hi, lo, hi), axis=1), table, preferred_element_type=F32)


def dot3_right(table, x):
    hi, lo = split(x)
    return jnp.dot(table, jnp.concatenate((hi, lo, hi), axis=0), preferred_element_type=F32)


def whole(shape):
    return pl.BlockSpec(shape, lambda *_: (0,) * len(shape))


def times_i(x, sign):
    return (-sign * x[1], sign * x[0])


def cadd(x, y):
    return (x[0] + y[0], x[1] + y[1])


def csub(x, y):
    return (x[0] - y[0], x[1] - y[1])


def eighth(x, sign):
    return ((x[0] - sign * x[1]) * HALF, (x[1] + sign * x[0]) * HALF)


def dft4(x, sign):
    a = cadd(x[0], x[2])
    b = csub(x[0], x[2])
    c = cadd(x[1], x[3])
    d = times_i(csub(x[1], x[3]), sign)
    return [cadd(a, c), cadd(b, d), csub(a, c), csub(b, d)]


def dft8(x, sign):
    even = dft4([x[0], x[2], x[4], x[6]], sign)
    odd = dft4([x[1], x[3], x[5], x[7]], sign)
    odd = [odd[0], eighth(odd[1], sign), times_i(odd[2], sign), times_i(eighth(odd[3], sign), sign)]
    return [cadd(even[k], odd[k]) for k in range(4)] + [csub(even[k], odd[k]) for k in range(4)]


def odd_kernel(order_ref, x_ref, w_ref, out_ref):
    x = x_ref[0].reshape(512, L)
    out_ref[0] = dot3_left(x[:, :512] - x[:, 512:], w_ref[...]).reshape(2, 256, 512)


def even_kernel(order_ref, x_ref, w0_ref, w2_ref, out_ref):
    x = x_ref[0].reshape(512, L)
    y = x[:, :512] + x[:, 512:]
    out_ref[0, :, :, :256] = dot3_left(y[:, :256] + y[:, 256:], w0_ref[...]).reshape(2, 256, 256)
    out_ref[0, :, :, 256:] = dot3_left(y[:, :256] - y[:, 256:], w2_ref[...]).reshape(2, 256, 256)


def along(kernel, name, stored, order, tables, interpret=False):
    tiles, planes = stored.shape[:2]
    return pl.pallas_call(
        kernel,
        out_shape=jax.ShapeDtypeStruct((tiles, planes, 256, 512), F32),
        grid_spec=pltpu.PrefetchScalarGridSpec(
            num_scalar_prefetch=1,
            grid=(tiles,),
            in_specs=[pl.BlockSpec((1, planes, 256, L), lambda i, order: (order[i], 0, 0, 0))]
            + [whole(t.shape) for t in tables],
            out_specs=pl.BlockSpec((1, planes, 256, 512), lambda i, order: (i, 0, 0, 0)),
        ),
        cost_estimate=pl.CostEstimate(flops=3_200_000_000, bytes_accessed=14_000_000, transcendentals=0),
        interpret=interpret,
        name=name,
    )(order, stored, *tables)


def across(y_ref, first, count, offset, table):
    later = lax.broadcasted_iota(jnp.int32, (A, 256), 0) >= offset
    picked = [jnp.where(later, y_ref[first + k, :A, :], y_ref[first + k, A:, :]) for k in range(count)]
    real = jnp.concatenate([p[:, :128] for p in picked], axis=1)
    imag = jnp.concatenate([p[:, 128:] for p in picked], axis=1)
    return dot3_right(table, jnp.concatenate((real, imag), axis=0))


def send_kernel(off_ref, y_ref, a_ref, g0_ref, g1_ref):
    for out_ref, k in ((g0_ref, 0), (g1_ref, 1)):
        out_ref[0] = across(y_ref, 0, 4, off_ref[k], a_ref[k])


def spectra(y, offs, mats, interpret=False):
    shape = jax.ShapeDtypeStruct((2, 256, Z * 128), F32)
    block = pl.BlockSpec((1, 256, 512), lambda w, h, *_: (w, 0, h))
    return pl.pallas_call(
        send_kernel,
        out_shape=(shape, shape),
        grid_spec=pltpu.PrefetchScalarGridSpec(
            num_scalar_prefetch=1,
            grid=(2, 2),
            in_specs=[pl.BlockSpec((4, 256, 256), lambda w, h, *_: (h, 0, w)), whole((2, 256, 768))],
            out_specs=(block, block),
        ),
        cost_estimate=pl.CostEstimate(flops=1_600_000_000, bytes_accessed=8_000_000, transcendentals=0),
        interpret=interpret,
        name="spectra",
    )(offs, y, mats)


def normalized(p, q, sign):
    real = p[0] * q[0] + p[1] * q[1]
    imag = p[1] * q[0] - p[0] * q[1]
    scale = lax.rsqrt(jnp.maximum(real * real + imag * imag, FLOOR * FLOOR))
    return (real * scale, imag * (scale * sign))


def to_lanes(ref, part):
    lane = lax.broadcasted_iota(jnp.int32, (A, 128), 1)
    out = jnp.zeros((A, 128), F32)
    for z in range(Z):
        block = ref[part * A : (part + 1) * A, z * 128 : (z + 1) * 128]
        if z:
            block = pltpu.roll(block, z, 1)
        out = jnp.where(lane == z, block, out)
    return out


def edge_fix(own_ref, far_ref, r_ref, ef_ref, er_ref, flip_ref, sign):
    high = lax.Precision.HIGHEST

    def edge(ref):
        packed = jnp.concatenate([to_lanes(ref, part) for part in range(2)], axis=1)
        here = jnp.dot(packed, ef_ref[...], precision=high, preferred_element_type=F32)
        turned = jnp.dot(packed, er_ref[...], precision=high, preferred_element_type=F32)
        there = jnp.dot(flip_ref[...], turned, precision=high, preferred_element_type=F32)
        hr, hi = here[:, :128], here[:, 128:]
        tr, ti = there[:, :128], there[:, 128:]
        return ((hr + tr) * 0.5, (hi - ti) * 0.5), ((hi + ti) * 0.5, (tr - hr) * 0.5)

    own_zero, own_last = edge(own_ref)
    far_zero, far_last = edge(far_ref)
    zero = normalized(own_zero, far_zero, sign)
    last = normalized(own_last, far_last, sign)
    both = jnp.concatenate((zero[0] - last[1], zero[1] + last[0]), axis=1)
    field = jnp.dot(both, er_ref[...], precision=high, preferred_element_type=F32)
    lane = lax.broadcasted_iota(jnp.int32, (A, 128), 1)
    for part in range(2):
        source = field[:, part * 128 : (part + 1) * 128]
        for z in range(Z):
            moved = pltpu.roll(source, 128 - z, 1) if z else source
            place = (slice(part * A, (part + 1) * A), slice(z * 128, (z + 1) * 128))
            r_ref[place] = jnp.where(lane == 0, moved, r_ref[place])


def pair_kernel(even, ints_ref, y_ref, far_ref, a_ref, ab_ref, v_ref, *refs):
    if even:
        ef_ref, er_ref, flip_ref, odd_ref, out_ref, own_ref, r_ref, acc_ref = refs
    else:
        out_ref, own_ref, r_ref = refs
    step = pl.program_id(0)
    sign = ints_ref[1].astype(F32)
    for half in range(2):
        own_ref[:, half * 512 : (half + 1) * 512] = across(y_ref, half * 4, 4, ints_ref[0], a_ref[...])

    def chunk(i, _):
        up = pl.ds(pl.multiple_of(i * 8, 8), 8)
        down = pl.ds(pl.multiple_of(i * 8 + A, 8), 8)

        def load(ref):
            return [(ref[up, z * 128 : (z + 1) * 128], ref[down, z * 128 : (z + 1) * 128]) for z in range(Z)]

        own = dft8(load(own_ref), -1.0)
        far = dft8(load(far_ref.at[0]), -1.0)
        back = dft8([normalized(own[u], far[u], sign) for u in range(Z)], 1.0)
        for z in range(Z):
            r_ref[up, z * 128 : (z + 1) * 128] = back[z][0]
            r_ref[down, z * 128 : (z + 1) * 128] = back[z][1]
        return 0

    lax.fori_loop(0, A // 8, chunk, 0)

    if even:
        @pl.when(step == 0)
        def _():
            edge_fix(own_ref, far_ref.at[0], r_ref, ef_ref, er_ref, flip_ref, sign)

    def parts():
        for half in range(2):
            q = dot3_right(ab_ref[...], r_ref[:, half * 512 : (half + 1) * 512])
            for k in range(0, 4, 2):
                rows = [
                    jnp.concatenate((q[:A, j * 128 : (j + 1) * 128], q[A:, j * 128 : (j + 1) * 128]), axis=1)
                    for j in (k, k + 1)
                ]
                yield half * 4 + k, dot3_left(jnp.concatenate(rows, axis=0), v_ref[0])

    @pl.when(step == 0)
    def _():
        target = acc_ref if even else out_ref
        for z, part in parts():
            target[z : z + 2] = part.reshape(2, A, -1)

    @pl.when(step == 1)
    def _():
        top = None
        for z, part in parts():
            if not even:
                out_ref[z : z + 2] += part.reshape(2, A, -1)
                continue
            first = acc_ref[z : z + 2].reshape(2 * A, 256)
            odd = odd_ref[z : z + 2].reshape(2 * A, 512)
            y = jnp.concatenate((first + part, first - part), axis=1)
            x = jnp.concatenate((y + odd, y - odd), axis=1)
            x = jnp.maximum(x[:A], x[A:])
            if z == 0:
                out_ref[...] = x
            else:
                out_ref[...] = jnp.maximum(out_ref[...], x)


def pair(rnd, even, ints, y, far, mat, ab, back, edges, odd, interpret=False):
    args = [y, far, mat, ab, back]
    in_specs = [
        pl.BlockSpec((Z, 256, 256), lambda w, *_: (0, 0, w)),
        pl.BlockSpec((1, 256, Z * 128), lambda w, *_: (w, 0, 0)),
        whole((256, 768)),
        whole((256, 768)),
        pl.BlockSpec((1, 768, back.shape[2]), lambda w, *_: (w, 0, 0)),
    ]
    scratch = [pltpu.VMEM((256, Z * 128), F32)] * 2
    out_shape = (Z, A, 512)
    if even:
        args += [*edges, odd]
        in_specs += [whole((256, 256)), whole((256, 256)), whole((128, 128)), whole((Z, A, 512))]
        scratch += [pltpu.VMEM((Z, A, 256), F32)]
        out_shape = (A, L)
    return pl.pallas_call(
        functools.partial(pair_kernel, even),
        out_shape=jax.ShapeDtypeStruct(out_shape, F32),
        grid_spec=pltpu.PrefetchScalarGridSpec(
            num_scalar_prefetch=1,
            grid=(2,),
            in_specs=in_specs,
            out_specs=whole(out_shape),
            scratch_shapes=scratch,
        ),
        cost_estimate=pl.CostEstimate(flops=3_000_000_000, bytes_accessed=10_000_000, transcendentals=500_000),
        interpret=interpret,
        name=("even" if even else "odd") + f"_{rnd}",
    )(ints, *args)


SLAB_OF = [t % 4 for t in range(128)]
TURN_ROW = [False] * 19
TURN_COLUMN = [False] * 7
MOVED = False


def moved(x, pairs):
    return lax.ppermute(x, ("tile", "slab"), pairs)


def lookup(table, place):
    return jnp.asarray(table, dtype=jnp.int32)[place]


def plan(size, slabs):
    home = list(range(size))
    at = [slabs * (t // slabs) + SLAB_OF[t] for t in home]
    holds = [0] * size
    for t in home:
        holds[at[t]] = t
    order = [holds[p] % slabs for p in home]
    turned = [[TURN_ROW[t // GC] for t in home], [TURN_COLUMN[t % GC] for t in home]]
    travel, result = [], []
    for rnd, step in enumerate((1, GC)):
        go, out = [], []
        for t in home:
            if t + step >= size or (rnd == 0 and t % GC == GC - 1):
                continue
            near, far = at[t], at[t + step]
            go.append((near, far) if turned[rnd][t] else (far, near))
            out.append((far if turned[rnd][t] else near, t))
        travel.append(go)
        result.append(out)
    return at, holds, order, turned, travel, result


def on_device(stored, offsets):
    size = lax.axis_size(("tile", "slab"))
    slabs = lax.axis_size("slab")
    place = lax.axis_index(("tile", "slab"))
    at, holds, order, turned, travel, result = plan(size, slabs)
    group = place // slabs
    sequence = jnp.asarray(order, dtype=jnp.int32).reshape(-1, slabs)[group]
    tile = lookup(holds, place)

    def gather(x):
        y = lax.all_to_all(x, "slab", split_axis=0, concat_axis=1, tiled=True)
        return y.reshape(Z, 256, 512)

    odd_src = along(odd_kernel, "along_odd", stored, sequence, (odd_tables(),))
    odd_all = gather(odd_src)
    offs = moved(offsets[:, :, 0], [(t, at[t]) for t in range(size)]) if MOVED else offsets[:, :, 0]
    turn = [lookup([int(f) for f in turned[r]], tile) for r in range(ROUNDS)]
    keep = [jnp.where(turn[r] == 1, offs[r, 1], offs[r, 0]) for r in range(ROUNDS)]
    send = [jnp.where(turn[r] == 1, offs[r, 0], offs[r, 1]) for r in range(ROUNDS)]
    ints = [jnp.stack((keep[r], 1 - 2 * turn[r])) for r in range(ROUNDS)]
    sends = jnp.stack(send)
    send_mats = jnp.stack([across_forward(o) for o in send])
    even_src = along(even_kernel, "along_even", stored, sequence, even_tables())
    odd_all, even_src, sends, send_mats = lax.optimization_barrier((odd_all, even_src, sends, send_mats))
    even_all = gather(even_src)
    odd_sent = spectra(odd_all, sends, send_mats)
    odd_far = [moved(odd_sent[r], travel[r]) for r in range(ROUNDS)]
    keep_mats = [across_forward(o) for o in keep]
    ab = across_back()
    edges = edge_tables()
    back_odd = odd_back()
    back_even = even_back()
    even_sent = spectra(even_all, sends, send_mats)
    even_sent, ints = lax.optimization_barrier((even_sent, ints))
    even_far = [moved(even_sent[r], travel[r]) for r in range(ROUNDS)]
    odd = [
        pair(r, False, ints[r], odd_all, odd_far[r], keep_mats[r], ab, back_odd, None, None)
        for r in range(ROUNDS)
    ]
    surfaces = []
    for r in range(ROUNDS):
        top = pair(r, True, ints[r], even_all, even_far[r], keep_mats[r], ab, back_even, edges, odd[r])
        surfaces.append(moved(top, result[r]) if MOVED else top)
    surface = jnp.stack(surfaces)[:, None]
    peak = jnp.max(surface, axis=(2, 3))
    return surface, peak


def solution(mesh):
    return jax.shard_map(
        on_device,
        mesh=mesh,
        in_specs=(P("tile", "slab", None, None), P(None, None, ("tile", "slab"))),
        out_specs=(P(None, ("tile", "slab"), None, None), P(None, ("tile", "slab"))),
        check_vma=False,
    )
```

time: 571 us -> 275 us (0.48)
  the two profiles are of different devices: /device:TPU:56 before, /device:TPU:22 now
where the time goes in v2:
time: 275 us; the launch traced here: 274 us
  waiting for transfers between devices  146 us (53%)
  Pallas kernels  77.4 us (28%)
  other arithmetic  28.1 us (10%)
  starting transfers between devices  18.8 us (7%)
  local copies, waits for them, and re-layouts  3.2 us (1%)
    all_to_all x2, waiting for transfers between devices, gather(): y = lax.all_to_all(x, 'slab', split_axis=0, concat_axis=1, tiled=True)  128 us
    pallas_call x4, Pallas kernels, pair(): pl.pallas_call(functools.partial(pair_kernel, even), out_shape=jax.ShapeD...  48 us
    ppermute x4, waiting for transfers between devices, moved(): return lax.ppermute(x, ('tile', 'slab'), pairs)  17.4 us
    pallas_call x2, Pallas kernels, along(): pl.pallas_call(kernel, out_shape=jax.ShapeDtypeStruct((tiles, planes, 256...  16.5 us
    pallas_call x2, Pallas kernels, spectra(): pl.pallas_call(send_kernel, out_shape=(shape, shape), grid_spec=pltpu.Pre...  12.9 us
    all_to_all x2, starting transfers between devices, gather(): y = lax.all_to_all(x, 'slab', split_axis=0, concat_axis=1, tiled=True)  10.3 us
    ppermute x4, starting transfers between devices, moved(): return lax.ppermute(x, ('tile', 'slab'), pairs)  8.46 us
  transfers between devices with their start and end apart: 6, of which 3 were waited for; matrix products, arithmetic and copies ran while one was open for 8% of the time, Pallas kernels for 20%

profile of v2, /device:TPU:22, one launch (start us, length us, event | category | flops | bytes accessed | tf_op | source)
XLA Modules:
  0.0 274.2 jit_solution(3165306779049725930)
XLA Ops:
  0.7 1.3 dynamic-slice_bitcast_fusion.order_ref
  2.0 2.1 fusion.25
  4.1 0.1 slice_negate_fusion.3
  4.1 0.2 reduce-precision_convert_fusion
  4.3 1.3 pad_maximum_fusion.w_ref
  5.6 8.9 %along_odd.1 = f32[4,2,256,512]{3,2,1,0:T(8,128)} custom-call(s32[4]{0:T(128)} %dynamic-slice_bitcast_fusion.order_ref, f32[4,2,256,1024]{3,2,1,0:T(8,128)} %x_ref.3, bf16[1536,512]{1,0:T(8,128)(2,1)} %pad_maximum_fusion.w_ref), custom_call_target="tpu_custom_call" | custom-call | flops 3200000000 | bytes 14000000 | tf_op jit(solution)/shard_map/along_odd/pallas_call | solution.py:198
  14.5 0.0 copy-start.1
  14.5 5.5 %all-to-all-start = ((f32[4,2,256,512]{3,2,1,0:T(8,128)}), f32[4,2,256,512]{3,2,1,0:T(8,128)}, u32[]{:S(2)}, u32[]{:S(2)}) async-start(f32[4,2,256,512]{3,2,1,0:T(8,128)} %along_odd.1), calls=%async_computation | async-start | bytes 8388608 | tf_op jit(solution)/shard_map/all_to_all | solution.py:434
  20.0 0.0 copy-done.1
  20.0 0.6 fusion.85
  20.6 1.8 pad_add_fusion.2.off_ref
  22.3 2.5 subtract_add_fusion.1
  24.8 1.6 fusion.66
  26.5 0.1 reduce-precision_convert_fusion.7
  26.7 1.1 fusion.59
  27.8 0.1 reduce-precision_convert_fusion.10
  27.9 0.8 pad_maximum_fusion.5.w0_ref
  28.7 0.8 pad_maximum_fusion.6.w2_ref
  29.5 0.9 pad_maximum_fusion.3.a_ref
  30.4 7.6 %along_even.1 = f32[4,2,256,512]{3,2,1,0:T(8,128)} custom-call(s32[4]{0:T(128)} %dynamic-slice_bitcast_fusion.order_ref, f32[4,2,256,1024]{3,2,1,0:T(8,128)} %x_ref.3, bf16[768,256]{1,0:T(8,128)(2,1)} %pad_maximum_fusion.5.w0_ref, bf16[768,256]{1,0:T(8,128)(2,1)} %pad_maximum_fusion.6.w2_ref), custom_call_target="tpu_custom_call" | custom-call | flops 3200000000 | bytes 14000000 | tf_op jit(solution)/shard_map/along_even/pallas_call | solution.py:198
  38.0 31.4 %all-to-all-done = f32[4,2,256,512]{3,2,1,0:T(8,128)} async-done(((f32[4,2,256,512]{3,2,1,0:T(8,128)}), f32[4,2,256,512]{3,2,1,0:T(8,128)}, u32[]{:S(2)}, u32[]{:S(2)}) %all-to-all-start) | async-done | bytes 4194336 | tf_op jit(solution)/shard_map/all_to_all | solution.py:434
  69.4 4.9 %all-to-all-start.1 = ((f32[4,2,256,512]{3,2,1,0:T(8,128)}), f32[4,2,256,512]{3,2,1,0:T(8,128)}, u32[]{:S(2)}, u32[]{:S(2)}) async-start(f32[4,2,256,512]{3,2,1,0:T(8,128)} %along_even.1), calls=%async_computation.1 | async-start | bytes 8388608 | tf_op jit(solution)/shard_map/all_to_all | solution.py:434
  74.3 0.8 pad_maximum_fusion.7.a_ref
  75.1 1.1 multiply_select_fusion.7
  76.3 0.1 reduce-precision_convert_fusion.4
  76.3 0.1 reduce-precision_convert_fusion.3
  76.4 2.1 fusion.23
  78.5 6.4 %spectra.3 = (f32[2,256,1024]{2,1,0:T(8,128)}, f32[2,256,1024]{2,1,0:T(8,128)}) custom-call(s32[2]{0:T(128)} %pad_add_fusion.2.off_ref, f32[8,256,512]{2,1,0:T(8,128)} %bitcast.1.y_ref, bf16[2,256,768]{2,1,0:T(8,128)(2,1)} %pad_maximum_fusion.3.a_ref), custom_call_target="tpu_custom_call" | custom-call | flops 1600000000 | bytes 8000000 | tf_op jit(solution)/shard_map/spectra/pallas_call | solution.py:230
  85.0 1.3 collective-permute-start.1
  86.3 0.8 pad_maximum_fusion.8.ab_ref
  87.1 4.0 %collective-permute-start.3 = (f32[2,256,1024]{2,1,0:T(8,128)}, f32[2,256,1024]{2,1,0:T(8,128)}, u32[]{:S(2)}, u32[]{:S(2)}) collective-permute-start(f32[2,256,1024]{2,1,0:T(8,128)} %get-tuple-element.25), channel_id=1, source_target_pairs={{7,0},{8,1},{9,2},{10,3},{11,4},{12,5},{13,6},{14,7},{15,8},{16,9}... | collective-permute-start | bytes 6291464 | tf_op jit(solution)/shard_map/ppermute | solution.py:395
  91.1 1.9 pad_add_fusion
  93.0 97.0 %all-to-all-done.1 = f32[4,2,256,512]{3,2,1,0:T(8,128)} async-done(((f32[4,2,256,512]{3,2,1,0:T(8,128)}), f32[4,2,256,512]{3,2,1,0:T(8,128)}, u32[]{:S(2)}, u32[]{:S(2)}) %all-to-all-start.1) | async-done | bytes 4194336 | tf_op jit(solution)/shard_map/all_to_all | solution.py:434
  190.0 6.5 %spectra.2 = (f32[2,256,1024]{2,1,0:T(8,128)}, f32[2,256,1024]{2,1,0:T(8,128)}) custom-call(s32[2]{0:T(128)} %pad_add_fusion.2.off_ref, f32[8,256,512]{2,1,0:T(8,128)} %bitcast.9.y_ref, bf16[2,256,768]{2,1,0:T(8,128)(2,1)} %pad_maximum_fusion.3.a_ref), custom_call_target="tpu_custom_call" | custom-call | flops 1600000000 | bytes 8000000 | tf_op jit(solution)/shard_map/spectra/pallas_call | solution.py:230
  196.5 1.3 collective-permute-start
  197.8 0.1 slice_negate_fusion.1
  197.9 1.9 collective-permute-start.2
  199.8 0.8 pad_maximum_fusion.9.a_ref
  200.6 0.1 reduce-precision_convert_fusion.2
  200.7 0.1 reduce-precision_convert_fusion.1
  200.8 0.8 fusion.12
  201.6 0.1 maximum_bitcast_fusion
  201.7 0.1 maximum_bitcast_fusion.1
  201.7 0.9 pad_maximum_fusion.4.v_ref
  202.7 1.3 pad_maximum_fusion.1.v_ref
  204.0 0.7 fusion.61.refs_2_
  204.8 0.0 collective-permute-done.1.far_ref
  204.8 11.1 %odd_0.1.refs_3_ = f32[8,128,512]{2,1,0:T(8,128)} custom-call(s32[2]{0:T(128)} %get-tuple-element.19.ints_ref, f32[8,256,512]{2,1,0:T(8,128)} %bitcast.1.y_ref, f32[2,256,1024]{2,1,0:T(8,128)} %collective-permute-done.1.far_ref, bf16[256,768]{1,0:T(8,128)(2,1)} %pad_maximum_fusion.7.a_ref, bf16[256,768]{1,0:T(8,128)(2,1)} %pad_maximum_fusion.8.ab_ref, ...), custom_call_target="tpu_custom_call" | custom-call | flops 3000000000 | bytes 10000000 | tf_op jit(solution)/shard_map/odd_0/pallas_call | solution.py:372
  215.9 0.0 collective-permute-done.3.far_ref
  215.9 11.1 %odd_1.1.refs_3_ = f32[8,128,512]{2,1,0:T(8,128)} custom-call(s32[2]{0:T(128)} %get-tuple-element.23.ints_ref, f32[8,256,512]{2,1,0:T(8,128)} %bitcast.1.y_ref, f32[2,256,1024]{2,1,0:T(8,128)} %collective-permute-done.3.far_ref, bf16[256,768]{1,0:T(8,128)(2,1)} %pad_maximum_fusion.9.a_ref, bf16[256,768]{1,0:T(8,128)(2,1)} %pad_maximum_fusion.8.ab_ref, ...), custom_call_target="tpu_custom_call" | custom-call | flops 3000000000 | bytes 10000000 | tf_op jit(solution)/shard_map/odd_1/pallas_call | solution.py:372
  227.0 17.4 %collective-permute-done.far_ref = f32[2,256,1024]{2,1,0:T(8,128)} collective-permute-done((f32[2,256,1024]{2,1,0:T(8,128)}, f32[2,256,1024]{2,1,0:T(8,128)}, u32[]{:S(2)}, u32[]{:S(2)}) %collective-permute-start) | collective-permute-done | bytes 2097184 | tf_op jit(solution)/shard_map/ppermute | solution.py:395
  244.4 12.8 %even_0.1 = f32[128,1024]{1,0:T(8,128)} custom-call(s32[2]{0:T(128)} %get-tuple-element.19.ints_ref, f32[8,256,512]{2,1,0:T(8,128)} %bitcast.9.y_ref, f32[2,256,1024]{2,1,0:T(8,128)} %collective-permute-done.far_ref, bf16[256,768]{1,0:T(8,128)(2,1)} %pad_maximum_fusion.7.a_ref, bf16[256,768]{1,0:T(8,128)(2,1)} %pad_maximum_fusion.8.ab_ref, ...), custom_call_target="tpu_custom_call" | custom-call | flops 3000000000 | bytes 10000000 | tf_op jit(solution)/shard_map/even_0/pallas_call | solution.py:372
  257.2 0.0 copy-start
  257.2 0.0 collective-permute-done.2.far_ref
  257.2 0.0 copy-start.2
  257.2 1.3 copy-done.2
  258.5 13.0 %even_1.1 = f32[128,1024]{1,0:T(8,128)} custom-call(s32[2]{0:T(128)} %get-tuple-element.23.ints_ref, f32[8,256,512]{2,1,0:T(8,128)} %bitcast.9.y_ref, f32[2,256,1024]{2,1,0:T(8,128)} %copy-done.2, bf16[256,768]{1,0:T(8,128)(2,1)} %pad_maximum_fusion.9.a_ref, bf16[256,768]{1,0:T(8,128)(2,1)} %pad_maximum_fusion.8.ab_ref, ...), custom_call_target="tpu_custom_call" | custom-call | flops 3000000000 | bytes 10000000 | tf_op jit(solution)/shard_map/even_1/pallas_call | solution.py:372
  271.5 0.0 copy-done
  271.5 2.7 fusion.1
  (11 shorter events, 0.2 us)
Async XLA Ops:
  14.5 5.5 %copy-start.1 = (s32[2,2,1]{1,2,0:T(1,128)S(1)}, s32[2,2,1]{1,2,0:T(1,128)}, u32[]{:S(2)}) copy-start(s32[2,2,1]{1,2,0:T(1,128)} %param.7) | copy-start | bytes 52
  14.5 54.9 %all-to-all-start = ((f32[4,2,256,512]{3,2,1,0:T(8,128)}), f32[4,2,256,512]{3,2,1,0:T(8,128)}, u32[]{:S(2)}, u32[]{:S(2)}) async-start(f32[4,2,256,512]{3,2,1,0:T(8,128)} %along_odd.1), calls=%async_computation | async-start | bytes 8388608 | tf_op jit(solution)/shard_map/all_to_all | solution.py:434
  69.4 120.6 %all-to-all-start.1 = ((f32[4,2,256,512]{3,2,1,0:T(8,128)}), f32[4,2,256,512]{3,2,1,0:T(8,128)}, u32[]{:S(2)}, u32[]{:S(2)}) async-start(f32[4,2,256,512]{3,2,1,0:T(8,128)} %along_even.1), calls=%async_computation.1 | async-start | bytes 8388608 | tf_op jit(solution)/shard_map/all_to_all | solution.py:434
  85.0 119.8 %collective-permute-start.1 = (f32[2,256,1024]{2,1,0:T(8,128)}, f32[2,256,1024]{2,1,0:T(8,128)}, u32[]{:S(2)}, u32[]{:S(2)}) collective-permute-start(f32[2,256,1024]{2,1,0:T(8,128)} %get-tuple-element.22), channel_id=1, source_target_pairs={{1,0},{2,1},{3,2},{4,3},{5,4},{6,5},{8,7},{9,8},{10,9},{11,10},{12... | collective-permute-start | bytes 6291464 | tf_op jit(solution)/shard_map/ppermute | solution.py:395
  87.1 128.8 %collective-permute-start.3 = (f32[2,256,1024]{2,1,0:T(8,128)}, f32[2,256,1024]{2,1,0:T(8,128)}, u32[]{:S(2)}, u32[]{:S(2)}) collective-permute-start(f32[2,256,1024]{2,1,0:T(8,128)} %get-tuple-element.25), channel_id=1, source_target_pairs={{7,0},{8,1},{9,2},{10,3},{11,4},{12,5},{13,6},{14,7},{15,8},{16,9}... | collective-permute-start | bytes 6291464 | tf_op jit(solution)/shard_map/ppermute | solution.py:395
  196.5 47.9 %collective-permute-start = (f32[2,256,1024]{2,1,0:T(8,128)}, f32[2,256,1024]{2,1,0:T(8,128)}, u32[]{:S(2)}, u32[]{:S(2)}) collective-permute-start(f32[2,256,1024]{2,1,0:T(8,128)} %get-tuple-element.20), channel_id=1, source_target_pairs={{1,0},{2,1},{3,2},{4,3},{5,4},{6,5},{8,7},{9,8},{10,9},{11,10},{12... | collective-permute-start | bytes 6291464 | tf_op jit(solution)/shard_map/ppermute | solution.py:395
  197.9 59.3 %collective-permute-start.2 = (f32[2,256,1024]{2,1,0:T(8,128)}, f32[2,256,1024]{2,1,0:T(8,128)S(1)}, u32[]{:S(2)}, u32[]{:S(2)}) collective-permute-start(f32[2,256,1024]{2,1,0:T(8,128)} %get-tuple-element.24), channel_id=1, source_target_pairs={{7,0},{8,1},{9,2},{10,3},{11,4},{12,5},{13,6},{14,7},{15,8},{16,9}... | collective-permute-start | bytes 6291464 | tf_op jit(solution)/shard_map/ppermute | solution.py:395
  257.2 14.3 %copy-start = (f32[128,1024]{1,0:T(8,128)S(1)}, f32[128,1024]{1,0:T(8,128)}, u32[]{:S(2)}) copy-start(f32[128,1024]{1,0:T(8,128)} %even_0.1) | copy-start | bytes 1572868
  257.2 1.3 copy-start.2

commit v3 on v2

--- a/solution.py
+++ b/solution.py
@@ -181,34 +181,33 @@
     return [cadd(even[k], odd[k]) for k in range(4)] + [csub(even[k], odd[k]) for k in range(4)]
 
 
-def odd_kernel(order_ref, x_ref, w_ref, out_ref):
+def odd_kernel(x_ref, w_ref, out_ref):
     x = x_ref[0].reshape(512, L)
     out_ref[0] = dot3_left(x[:, :512] - x[:, 512:], w_ref[...]).reshape(2, 256, 512)
 
 
-def even_kernel(order_ref, x_ref, w0_ref, w2_ref, out_ref):
+def even_kernel(x_ref, w0_ref, w2_ref, out_ref):
     x = x_ref[0].reshape(512, L)
     y = x[:, :512] + x[:, 512:]
     out_ref[0, :, :, :256] = dot3_left(y[:, :256] + y[:, 256:], w0_ref[...]).reshape(2, 256, 256)
     out_ref[0, :, :, 256:] = dot3_left(y[:, :256] - y[:, 256:], w2_ref[...]).reshape(2, 256, 256)
 
 
-def along(kernel, name, stored, order, tables, interpret=False):
+def along(kernel, name, stored, tables, interpret=False):
     tiles, planes = stored.shape[:2]
     return pl.pallas_call(
         kernel,
         out_shape=jax.ShapeDtypeStruct((tiles, planes, 256, 512), F32),
-        grid_spec=pltpu.PrefetchScalarGridSpec(
-            num_scalar_prefetch=1,
+        grid_spec=pl.GridSpec(
             grid=(tiles,),
-            in_specs=[pl.BlockSpec((1, planes, 256, L), lambda i, order: (order[i], 0, 0, 0))]
+            in_specs=[pl.BlockSpec((1, planes, 256, L), lambda i: (i, 0, 0, 0))]
             + [whole(t.shape) for t in tables],
-            out_specs=pl.BlockSpec((1, planes, 256, 512), lambda i, order: (i, 0, 0, 0)),
+            out_specs=pl.BlockSpec((1, planes, 256, 512), lambda i: (i, 0, 0, 0)),
         ),
         cost_estimate=pl.CostEstimate(flops=3_200_000_000, bytes_accessed=14_000_000, transcendentals=0),
         interpret=interpret,
         name=name,
-    )(order, stored, *tables)
+    )(stored, *tables)
 
 
 def across(y_ref, first, count, offset, table):
@@ -219,52 +218,68 @@
     return dot3_right(table, jnp.concatenate((real, imag), axis=0))
 
 
-def send_kernel(off_ref, y_ref, a_ref, g0_ref, g1_ref):
-    for out_ref, k in ((g0_ref, 0), (g1_ref, 1)):
-        out_ref[0] = across(y_ref, 0, 4, off_ref[k], a_ref[k])
-
-
-def spectra(y, offs, mats, interpret=False):
-    shape = jax.ShapeDtypeStruct((2, 256, Z * 128), F32)
-    block = pl.BlockSpec((1, 256, 512), lambda w, h, *_: (w, 0, h))
+def send_kernel(off_ref, x_ref, a_ref, out_ref):
+    tile = pl.program_id(0)
+    rnd = pl.program_id(1)
+    later = lax.broadcasted_iota(jnp.int32, (A, 256), 0) >= off_ref[rnd, tile]
+    picked = [
+        jnp.where(later, x_ref[0, p, :A, cols], x_ref[0, p, A:, cols])
+        for p in range(2)
+        for cols in (slice(0, 256), slice(256, 512))
+    ]
+    real = jnp.concatenate([p[:, :128] for p in picked], axis=1)
+    imag = jnp.concatenate([p[:, 128:] for p in picked], axis=1)
+    spec = dot3_right(a_ref[0, 0], jnp.concatenate((real, imag), axis=0))
+    for k in range(4):
+        out_ref[0, 0, k // 2, k % 2] = spec[:, k * 128 : (k + 1) * 128]
+
+
+def spectra(x, offs, mats, interpret=False):
+    tiles = x.shape[0]
     return pl.pallas_call(
         send_kernel,
-        out_shape=(shape, shape),
+        out_shape=jax.ShapeDtypeStruct((tiles, ROUNDS, 2, 2, 256, 128), F32),
         grid_spec=pltpu.PrefetchScalarGridSpec(
             num_scalar_prefetch=1,
-            grid=(2, 2),
-            in_specs=[pl.BlockSpec((4, 256, 256), lambda w, h, *_: (h, 0, w)), whole((2, 256, 768))],
-            out_specs=(block, block),
+            grid=(tiles, ROUNDS),
+            in_specs=[
+                pl.BlockSpec((1, 2, 256, 512), lambda t, r, *_: (t, 0, 0, 0)),
+                pl.BlockSpec((1, 1, 256, 768), lambda t, r, *_: (r, t, 0, 0)),
+            ],
+            out_specs=pl.BlockSpec(
+                (1, 1, 2, 2, 256, 128),
+                lambda t, r, *_: (lax.rem(t + 3 - 2 * r, tiles), r, 0, 0, 0, 0),
+            ),
         ),
-        cost_estimate=pl.CostEstimate(flops=1_600_000_000, bytes_accessed=8_000_000, transcendentals=0),
+        cost_estimate=pl.CostEstimate(flops=1_600_000_000, bytes_accessed=12_000_000, transcendentals=0),
         interpret=interpret,
         name="spectra",
-    )(offs, y, mats)
+    )(offs, x, mats)
 
 
 def normalized(p, q, sign):
     real = p[0] * q[0] + p[1] * q[1]
     imag = p[1] * q[0] - p[0] * q[1]
-    scale = lax.rsqrt(jnp.maximum(real * real + imag * imag, FLOOR * FLOOR))
-    return (real * scale, imag * (scale * sign))
-
-
-def to_lanes(ref, part):
+    scale = lax.rsqrt(jnp.maximum(real * real + imag * imag, FLOOR * FLOOR)) * sign
+    return (real * scale, imag * scale)
+
+
+def to_lanes(block_of, part):
     lane = lax.broadcasted_iota(jnp.int32, (A, 128), 1)
     out = jnp.zeros((A, 128), F32)
     for z in range(Z):
-        block = ref[part * A : (part + 1) * A, z * 128 : (z + 1) * 128]
+        block = block_of(z, slice(part * A, (part + 1) * A))
         if z:
             block = pltpu.roll(block, z, 1)
         out = jnp.where(lane == z, block, out)
     return out
 
 
-def edge_fix(own_ref, far_ref, r_ref, ef_ref, er_ref, flip_ref, sign):
+def edge_fix(own_of, far_of, r_ref, ef_ref, er_ref, flip_ref, sign):
     high = lax.Precision.HIGHEST
 
-    def edge(ref):
-        packed = jnp.concatenate([to_lanes(ref, part) for part in range(2)], axis=1)
+    def edge(block_of):
+        packed = jnp.concatenate([to_lanes(block_of, part) for part in range(2)], axis=1)
         here = jnp.dot(packed, ef_ref[...], precision=high, preferred_element_type=F32)
         turned = jnp.dot(packed, er_ref[...], precision=high, preferred_element_type=F32)
         there = jnp.dot(flip_ref[...], turned, precision=high, preferred_element_type=F32)
@@ -272,8 +287,8 @@
         tr, ti = there[:, :128], there[:, 128:]
         return ((hr + tr) * 0.5, (hi - ti) * 0.5), ((hi + ti) * 0.5, (tr - hr) * 0.5)
 
-    own_zero, own_last = edge(own_ref)
-    far_zero, far_last = edge(far_ref)
+    own_zero, own_last = edge(own_of)
+    far_zero, far_last = edge(far_of)
     zero = normalized(own_zero, far_zero, sign)
     last = normalized(own_last, far_last, sign)
     both = jnp.concatenate((zero[0] - last[1], zero[1] + last[0]), axis=1)
@@ -297,15 +312,18 @@
     for half in range(2):
         own_ref[:, half * 512 : (half + 1) * 512] = across(y_ref, half * 4, 4, ints_ref[0], a_ref[...])
 
+    def own_of(z, rows):
+        return own_ref[rows, z * 128 : (z + 1) * 128]
+
+    def far_of(z, rows):
+        return far_ref[z // 2, 0, z % 2, 0, rows, :]
+
     def chunk(i, _):
         up = pl.ds(pl.multiple_of(i * 8, 8), 8)
         down = pl.ds(pl.multiple_of(i * 8 + A, 8), 8)
 
-        def load(ref):
-            return [(ref[up, z * 128 : (z + 1) * 128], ref[down, z * 128 : (z + 1) * 128]) for z in range(Z)]
-
-        own = dft8(load(own_ref), -1.0)
-        far = dft8(load(far_ref.at[0]), -1.0)
+        own = dft8([(own_of(z, up), own_of(z, down)) for z in range(Z)], -1.0)
+        far = dft8([(far_of(z, up), far_of(z, down)) for z in range(Z)], -1.0)
         back = dft8([normalized(own[u], far[u], sign) for u in range(Z)], 1.0)
         for z in range(Z):
             r_ref[up, z * 128 : (z + 1) * 128] = back[z][0]
@@ -317,7 +335,7 @@
     if even:
         @pl.when(step == 0)
         def _():
-            edge_fix(own_ref, far_ref.at[0], r_ref, ef_ref, er_ref, flip_ref, sign)
+            edge_fix(own_of, far_of, r_ref, ef_ref, er_ref, flip_ref, sign)
 
     def parts():
         for half in range(2):
@@ -357,7 +375,7 @@
     args = [y, far, mat, ab, back]
     in_specs = [
         pl.BlockSpec((Z, 256, 256), lambda w, *_: (0, 0, w)),
-        pl.BlockSpec((1, 256, Z * 128), lambda w, *_: (w, 0, 0)),
+        pl.BlockSpec((4, 1, 2, 1, 256, 128), lambda w, *_: (0, rnd if far.shape[1] > 1 else 0, 0, w, 0, 0)),
         whole((256, 768)),
         whole((256, 768)),
         pl.BlockSpec((1, 768, back.shape[2]), lambda w, *_: (w, 0, 0)),
@@ -385,85 +403,73 @@
     )(ints, *args)
 
 
-SLAB_OF = [t % 4 for t in range(128)]
-TURN_ROW = [False] * 19
-TURN_COLUMN = [False] * 7
-MOVED = False
-
-
-def moved(x, pairs):
-    return lax.ppermute(x, ("tile", "slab"), pairs)
-
-
-def lookup(table, place):
-    return jnp.asarray(table, dtype=jnp.int32)[place]
-
-
-def plan(size, slabs):
-    home = list(range(size))
-    at = [slabs * (t // slabs) + SLAB_OF[t] for t in home]
-    holds = [0] * size
-    for t in home:
-        holds[at[t]] = t
-    order = [holds[p] % slabs for p in home]
-    turned = [[TURN_ROW[t // GC] for t in home], [TURN_COLUMN[t % GC] for t in home]]
-    travel, result = [], []
-    for rnd, step in enumerate((1, GC)):
-        go, out = [], []
-        for t in home:
-            if t + step >= size or (rnd == 0 and t % GC == GC - 1):
-                continue
-            near, far = at[t], at[t + step]
-            go.append((near, far) if turned[rnd][t] else (far, near))
-            out.append((far if turned[rnd][t] else near, t))
-        travel.append(go)
-        result.append(out)
-    return at, holds, order, turned, travel, result
+def from_next(x, step, groups):
+    return lax.ppermute(x, "tile", [(g + step, g) for g in range(groups - step)])
+
+
+def after(first, second):
+    return lax.optimization_barrier((first, second))
 
 
 def on_device(stored, offsets):
     size = lax.axis_size(("tile", "slab"))
+    groups = lax.axis_size("tile")
     slabs = lax.axis_size("slab")
     place = lax.axis_index(("tile", "slab"))
-    at, holds, order, turned, travel, result = plan(size, slabs)
-    group = place // slabs
-    sequence = jnp.asarray(order, dtype=jnp.int32).reshape(-1, slabs)[group]
-    tile = lookup(holds, place)
 
     def gather(x):
-        y = lax.all_to_all(x, "slab", split_axis=0, concat_axis=1, tiled=True)
-        return y.reshape(Z, 256, 512)
-
-    odd_src = along(odd_kernel, "along_odd", stored, sequence, (odd_tables(),))
+        return lax.all_to_all(x, "slab", split_axis=0, concat_axis=1, tiled=True)[0]
+
+    def collect(x):
+        return lax.all_to_all(x, "slab", split_axis=0, concat_axis=0, tiled=True)
+
+    odd_src = along(odd_kernel, "along_odd", stored, (odd_tables(),))
     odd_all = gather(odd_src)
-    offs = moved(offsets[:, :, 0], [(t, at[t]) for t in range(size)]) if MOVED else offsets[:, :, 0]
-    turn = [lookup([int(f) for f in turned[r]], tile) for r in range(ROUNDS)]
-    keep = [jnp.where(turn[r] == 1, offs[r, 1], offs[r, 0]) for r in range(ROUNDS)]
-    send = [jnp.where(turn[r] == 1, offs[r, 0], offs[r, 1]) for r in range(ROUNDS)]
-    ints = [jnp.stack((keep[r], 1 - 2 * turn[r])) for r in range(ROUNDS)]
-    sends = jnp.stack(send)
-    send_mats = jnp.stack([across_forward(o) for o in send])
-    even_src = along(even_kernel, "along_even", stored, sequence, even_tables())
-    odd_all, even_src, sends, send_mats = lax.optimization_barrier((odd_all, even_src, sends, send_mats))
+    mine = offsets[:, 1, 0]
+    turns = [mine] + [
+        lax.ppermute(mine, "slab", [((i + k) % slabs, i) for i in range(slabs)]) for k in range(1, slabs)
+    ]
+    given = jnp.roll(jnp.stack(turns, axis=1), lax.axis_index("slab"), axis=1)
+    mats = jnp.stack([jnp.stack([across_forward(given[r, j]) for j in range(slabs)]) for r in range(ROUNDS)])
+
+    def shifted(src):
+        made = spectra(src, given, mats)
+        near = from_next(jnp.stack((made[3, 0], made[0, 1])), 1, groups)
+        far = from_next(made[1:, 1], 2, groups)
+        zero = [made[0, 0], made[1, 0], made[2, 0], near[0]]
+        one = [near[1], far[0], far[1], far[2]]
+        return zero, one
+
+    odd_sent = jnp.stack([x for pair_of in zip(*shifted(odd_src)) for x in pair_of]).reshape(slabs, ROUNDS, 2, 2, 256, 128)
+    even_src = along(even_kernel, "along_even", stored, even_tables())
+    even_sent = [jnp.stack(x)[:, None] for x in shifted(even_src)]
+    odd_all, even_src = after(odd_all, even_src)
     even_all = gather(even_src)
-    odd_sent = spectra(odd_all, sends, send_mats)
-    odd_far = [moved(odd_sent[r], travel[r]) for r in range(ROUNDS)]
-    keep_mats = [across_forward(o) for o in keep]
+    valid = (
+        jnp.logical_and(place % GC != GC - 1, place + 1 < size),
+        place + GC < size,
+    )
+    own = [offsets[r, 0, 0] for r in range(ROUNDS)]
+    ints = [jnp.stack((own[r], valid[r].astype(jnp.int32))) for r in range(ROUNDS)]
+    own_mats = [across_forward(o) for o in own]
     ab = across_back()
     edges = edge_tables()
     back_odd = odd_back()
     back_even = even_back()
-    even_sent = spectra(even_all, sends, send_mats)
-    even_sent, ints = lax.optimization_barrier((even_sent, ints))
-    even_far = [moved(even_sent[r], travel[r]) for r in range(ROUNDS)]
+    even_all, odd_sent = after(even_all, odd_sent)
+    odd_far = collect(odd_sent)
+    odd_far, even_zero = after(odd_far, even_sent[0])
+    zero_far = collect(even_zero)
     odd = [
-        pair(r, False, ints[r], odd_all, odd_far[r], keep_mats[r], ab, back_odd, None, None)
+        pair(r, False, ints[r], odd_all, odd_far, own_mats[r], ab, back_odd, None, None)
         for r in range(ROUNDS)
     ]
-    surfaces = []
-    for r in range(ROUNDS):
-        top = pair(r, True, ints[r], even_all, even_far[r], keep_mats[r], ab, back_even, edges, odd[r])
-        surfaces.append(moved(top, result[r]) if MOVED else top)
+    zero_far, odd, even_one = lax.optimization_barrier((zero_far, odd, even_sent[1]))
+    even_far = [zero_far, collect(even_one)]
+    surfaces = [
+        pair(r, True, ints[r], even_all, even_far[r], own_mats[r], ab, back_even, edges, odd[r])
+        for r in range(ROUNDS)
+    ]
     surface = jnp.stack(surfaces)[:, None]
     peak = jnp.max(surface, axis=(2, 3))
     return surface, peak

time: 275 us -> 265 us (0.964)
  the two profiles are of different devices: /device:TPU:22 before, /device:TPU:56 now
where the time goes in v3:
time: 265 us; the launch traced here: 262 us
  Pallas kernels  81.5 us (31%)
  waiting for transfers between devices  72 us (27%)
  other arithmetic  43.8 us (17%)
  starting transfers between devices  42.3 us (16%)
  local copies, waits for them, and re-layouts  21.4 us (8%)
    pallas_call x4, Pallas kernels, pair(): pl.pallas_call(functools.partial(pair_kernel, even), out_shape=jax.ShapeD...  46.3 us
    ppermute x4, waiting for transfers between devices, from_next(): lax.ppermute(x, 'tile', [(g + step, g) for g in range(groups - step)])  34.2 us
    all_to_all x2, waiting for transfers between devices, gather(): return lax.all_to_all(x, 'slab', split_axis=0, concat_axis=1, tiled=True)[0]  20.3 us
    pallas_call x2, Pallas kernels, spectra(): pl.pallas_call(send_kernel, out_shape=jax.ShapeDtypeStruct((tiles, ROUNDS...  20 us
    all_to_all x3, waiting for transfers between devices, collect(): return lax.all_to_all(x, 'slab', split_axis=0, concat_axis=0, tiled=True)  17.4 us
    all_to_all x3, starting transfers between devices, collect(): return lax.all_to_all(x, 'slab', split_axis=0, concat_axis=0, tiled=True)  16.2 us
    pallas_call x2, Pallas kernels, along(): pl.pallas_call(kernel, out_shape=jax.ShapeDtypeStruct((tiles, planes, 256...  15.2 us
    all_to_all x2, starting transfers between devices, gather(): return lax.all_to_all(x, 'slab', split_axis=0, concat_axis=1, tiled=True)[0]  11.3 us
  transfers between devices with their start and end apart: 12, of which 7 were waited for; matrix products, arithmetic and copies ran while one was open for 23% of the time, Pallas kernels for 26%

profile of v3, /device:TPU:56, one launch (start us, length us, event | category | flops | bytes accessed | tf_op | source)
XLA Modules:
  0.0 262.1 jit_solution(1809575053178802843)
XLA Ops:
  0.6 0.9 slice_reduce_fusion
  1.7 3.3 %collective-permute-start.1 = (s32[2]{0:T(128)S(1)}, s32[2]{0:T(128)S(1)}, u32[]{:S(2)}, u32[]{:S(2)}) collective-permute-start(s32[2]{0:T(128)S(1)} %get-tuple-element.144), channel_id=1, source_target_pairs={{2,0},{3,1},{0,2},{1,3},{6,4},{7,5},{4,6},{5,7},{10,8},{11,9},{8,1... | collective-permute-start | bytes 32 | tf_op jit(solution)/shard_map/ppermute | solution.py:430
  4.9 2.2 collective-permute-start.2
  7.2 2.1 fusion.34
  9.6 1.3 pad_maximum_fusion.1.w_ref
  10.9 8.2 %along_odd.1.x_ref = f32[4,2,256,512]{3,2,1,0:T(8,128)} custom-call(f32[4,2,256,1024]{3,2,1,0:T(8,128)} %x_ref.3, bf16[1536,512]{1,0:T(8,128)(2,1)} %pad_maximum_fusion.1.w_ref), custom_call_target="tpu_custom_call" | custom-call | flops 3200000000 | bytes 14000000 | tf_op jit(solution)/shard_map/along_odd/pallas_call | solution.py:198
  19.1 5.0 %all-to-all-start = ((f32[4,2,256,512]{3,2,1,0:T(8,128)}), f32[4,2,256,512]{3,2,1,0:T(8,128)}, u32[]{:S(2)}, u32[]{:S(2)}) async-start(f32[4,2,256,512]{3,2,1,0:T(8,128)} %along_odd.1.x_ref), calls=%async_computation | async-start | bytes 8388608 | tf_op jit(solution)/shard_map/all_to_all | solution.py:421
  27.0 6.9 %subtract_add_fusion = (s32[128]{0:T(128)S(1)}, s32[128]{0:T(128)}, s32[128]{0:T(128)S(1)}, s32[128]{0:T(128)S(1)}, s32[128]{0:T(128)S(1)}, /*index=5*/s32[128]{...) fusion(s32[128]{0:T(128)S(1)} %iota.8, ...), kind=kLoop, calls=%fused_computation.340 | loop fusion | flops 2816 | bytes 6696 | tf_op jit(solution)/shard_map/add | solution.py:106
  34.0 4.0 %fusion.122 = (f32[128,128]{1,0:T(8,128)}, f32[128,128]{1,0:T(8,128)}, f32[128,128]{1,0:T(8,128)}, f32[128,128]{1,0:T(8,128)}, f32[128,128]{1,0:T(8,128)S(1)}, /...) fusion(s32[128]{0:T(128)S(1)} %iota.8, ...), kind=kLoop, calls=%fused_computation.328 | loop fusion | flops 2932736 | bytes 2365056 | tf_op jit(solution)/shard_map/neg | solution.py:130
  38.5 0.7 reduce-precision_convert_fusion.7
  39.7 1.9 pad_maximum_fusion.a_ref
  41.6 10.0 %spectra.2 = f32[4,2,2,2,256,128]{5,4,3,2,1,0:T(8,128)} custom-call(s32[2,4]{1,0:T(2,128)} %copy-done.12, f32[4,2,256,512]{3,2,1,0:T(8,128)} %along_odd.1.x_ref, bf16[2,4,256,768]{3,2,1,0:T(8,128)(2,1)} %pad_maximum_fusion.a_ref), custom_call_target="tpu_custom_call" | custom-call | flops 1600000000 | bytes 12000000 | tf_op jit(solution)/shard_map/spectra/pallas_call | solution.py:239
  51.6 1.5 slice_bitcast_fusion.1
  53.2 2.7 %collective-permute-start.4 = (f32[3,2,2,256,128]{4,3,2,1,0:T(8,128)S(1)}, f32[3,2,2,256,128]{4,3,2,1,0:T(8,128)S(1)}, u32[]{:S(2)}, u32[]{:S(2)}) collective-permute-start(f32[3,2,2,256,128]{4,3,2,1,0:T(8,128)S(1)} %slice_bitcast_fusion.1), channel_id=1, source_target_pairs={{8,0},{12,4},{16,8},{20,12},{24,16},{28,20},{32,24},{36,28},{40,32... | collective-permute-start | bytes 4718600 | tf_op jit(solution)/shard_map/ppermute | solution.py:407
  55.9 1.1 fusion.86
  57.1 0.8 pad_maximum_fusion.8.w2_ref
  57.9 0.8 pad_maximum_fusion.7.w0_ref
  58.6 6.9 %along_even.1.x_ref = f32[4,2,256,512]{3,2,1,0:T(8,128)} custom-call(f32[4,2,256,1024]{3,2,1,0:T(8,128)} %x_ref.3, bf16[768,256]{1,0:T(8,128)(2,1)} %pad_maximum_fusion.7.w0_ref, bf16[768,256]{1,0:T(8,128)(2,1)} %pad_maximum_fusion.8.w2_ref), custom_call_target="tpu_custom_call" | custom-call | flops 3200000000 | bytes 14000000 | tf_op jit(solution)/shard_map/along_even/pallas_call | solution.py:198
  65.6 5.2 %all-to-all-done = f32[4,2,256,512]{3,2,1,0:T(8,128)} async-done(((f32[4,2,256,512]{3,2,1,0:T(8,128)}), f32[4,2,256,512]{3,2,1,0:T(8,128)}, u32[]{:S(2)}, u32[]{:S(2)}) %all-to-all-start) | async-done | bytes 4194336 | tf_op jit(solution)/shard_map/all_to_all | solution.py:421
  70.8 6.3 %all-to-all-start.1 = ((f32[4,2,256,512]{3,2,1,0:T(8,128)}), f32[4,2,256,512]{3,2,1,0:T(8,128)}, u32[]{:S(2)}, u32[]{:S(2)}) async-start(f32[4,2,256,512]{3,2,1,0:T(8,128)} %along_even.1.x_ref), calls=%async_computation.1 | async-start | bytes 8388608 | tf_op jit(solution)/shard_map/all_to_all | solution.py:421
  77.1 1.3 slice_bitcast_fusion.10
  78.4 1.9 collective-permute-start.3
  80.3 1.9 fusion.13
  82.2 17.6 %collective-permute-done.3 = f32[2,2,2,256,128]{4,3,2,1,0:T(8,128)S(1)} collective-permute-done((f32[2,2,2,256,128]{4,3,2,1,0:T(8,128)S(1)}, f32[2,2,2,256,128]{4,3,2,1,0:T(8,128)S(1)}, u32[]{:S(2)}, u32[]{:S(2)}) %collective-permute-start.3) | collective-permute-done | bytes 1048608 | tf_op jit(solution)/shard_map/ppermute | solution.py:407
  99.9 0.8 slice_dynamic-update-slice_fusion.4
  100.7 1.9 fusion.12
  102.6 0.9 slice_dynamic-update-slice_fusion.3
  103.4 1.9 fusion.11
  105.3 0.9 slice_dynamic-update-slice_fusion.2
  106.2 0.9 slice_dynamic-update-slice_fusion.1
  107.0 0.9 slice_dynamic-update-slice_fusion
  107.9 15.2 %all-to-all-done.1 = f32[4,2,256,512]{3,2,1,0:T(8,128)} async-done(((f32[4,2,256,512]{3,2,1,0:T(8,128)}), f32[4,2,256,512]{3,2,1,0:T(8,128)}, u32[]{:S(2)}, u32[]{:S(2)}) %all-to-all-start.1) | async-done | bytes 4194336 | tf_op jit(solution)/shard_map/all_to_all | solution.py:421
  123.1 6.4 %all-to-all-start.2 = ((f32[4,2,2,2,256,128]{5,4,3,2,1,0:T(8,128)}), f32[4,2,2,2,256,128]{5,4,3,2,1,0:T(8,128)}, u32[]{:S(2)}, u32[]{:S(2)}) async-start(f32[4,2,2,2,256,128]{5,4,3,2,1,0:T(8,128)} %bitcast.32), calls=%async_computation.2 | async-start | bytes 8388608 | tf_op jit(solution)/shard_map/all_to_all | solution.py:424
  129.5 2.1 fusion.32
  131.6 10.0 %spectra.3 = f32[4,2,2,2,256,128]{5,4,3,2,1,0:T(8,128)} custom-call(s32[2,4]{1,0:T(2,128)} %copy-done.12, f32[4,2,256,512]{3,2,1,0:T(8,128)} %along_even.1.x_ref, bf16[2,4,256,768]{3,2,1,0:T(8,128)(2,1)} %pad_maximum_fusion.a_ref), custom_call_target="tpu_custom_call" | custom-call | flops 1600000000 | bytes 12000000 | tf_op jit(solution)/shard_map/spectra/pallas_call | solution.py:239
  141.6 1.9 slice_bitcast_fusion.6
  143.6 1.9 collective-permute-start.5
  145.5 1.3 pad_add_fusion.1.ints_ref
  147.0 2.7 %slice_bitcast_fusion = f32[3,2,2,256,128]{4,3,2,1,0:T(8,128)} fusion(f32[4,2,2,2,256,128]{5,4,3,2,1,0:T(8,128)} %spectra.3), kind=kLoop, calls=%fused_computation.3 | loop fusion | bytes 3145728 | tf_op jit(solution)/shard_map/squeeze | solution.py:438
  149.7 2.6 %collective-permute-start.6 = (f32[3,2,2,256,128]{4,3,2,1,0:T(8,128)}, f32[3,2,2,256,128]{4,3,2,1,0:T(8,128)}, u32[]{:S(2)}, u32[]{:S(2)}) collective-permute-start(f32[3,2,2,256,128]{4,3,2,1,0:T(8,128)} %slice_bitcast_fusion), channel_id=1, source_target_pairs={{8,0},{12,4},{16,8},{20,12},{24,16},{28,20},{32,24},{36,28},{40,32... | collective-permute-start | bytes 4718600 | tf_op jit(solution)/shard_map/ppermute | solution.py:407
  152.3 0.9 reduce-precision_convert_fusion.1
  153.3 9.2 %collective-permute-done.5 = f32[2,2,2,256,128]{4,3,2,1,0:T(8,128)S(1)} collective-permute-done((f32[2,2,2,256,128]{4,3,2,1,0:T(8,128)S(1)}, f32[2,2,2,256,128]{4,3,2,1,0:T(8,128)S(1)}, u32[]{:S(2)}, u32[]{:S(2)}) %collective-permute-start.5) | collective-permute-done | bytes 1048608 | tf_op jit(solution)/shard_map/ppermute | solution.py:407
  162.6 1.5 maximum_bitcast_fusion
  164.0 10.6 %all-to-all-done.2.far_ref = f32[4,2,2,2,256,128]{5,4,3,2,1,0:T(8,128)} async-done(((f32[4,2,2,2,256,128]{5,4,3,2,1,0:T(8,128)}), f32[4,2,2,2,256,128]{5,4,3,2,1,0:T(8,128)}, u32[]{:S(2)}, u32[]{:S(2)}) %all-to-all-start.2) | async-done | bytes 4194336 | tf_op jit(solution)/shard_map/all_to_all | solution.py:424
  174.7 5.0 %all-to-all-start.3 = ((f32[4,1,2,2,256,128]{5,4,3,2,1,0:T(8,128)}), f32[4,1,2,2,256,128]{5,4,3,2,1,0:T(8,128)S(1)}, u32[]{:S(2)}, u32[]{:S(2)}) async-start(f32[4,1,2,2,256,128]{5,4,3,2,1,0:T(8,128)} %bitcast.39), calls=%async_computation.3 | async-start | bytes 4194304 | tf_op jit(solution)/shard_map/all_to_all | solution.py:424
  179.7 1.2 pad_add_fusion.ints_ref
  180.9 1.2 maximum_bitcast_fusion.5
  182.2 1.3 pad_maximum_fusion.2.v_ref
  183.6 0.8 pad_maximum_fusion.11.a_ref
  184.4 0.8 pad_maximum_fusion.10.ab_ref
  185.2 0.8 pad_maximum_fusion.9.a_ref
  185.9 7.3 %collective-permute-done.6 = f32[3,2,2,256,128]{4,3,2,1,0:T(8,128)} collective-permute-done((f32[3,2,2,256,128]{4,3,2,1,0:T(8,128)}, f32[3,2,2,256,128]{4,3,2,1,0:T(8,128)}, u32[]{:S(2)}, u32[]{:S(2)}) %collective-permute-start.6) | collective-permute-done | bytes 1572896 | tf_op jit(solution)/shard_map/ppermute | solution.py:407
  193.3 2.9 %maximum_bitcast_fusion.1 = f32[4,1,2,2,256,128]{5,4,3,2,1,0:T(8,128)} fusion(f32[3,2,2,256,128]{4,3,2,1,0:T(8,128)} %collective-permute-done.6, f32[1,2,2,256,128]{4,3,2,1,0:T(8,128)S(1)} %get-tuple-element.39), kind=kLoop, calls=%fused_computation.2 | loop fusion | flops 524288 | bytes 4194304 | tf_op jit(solution)/shard_map/broadcast_in_dim | solution.py:445
  196.2 10.7 %odd_1.1.refs_3_ = f32[8,128,512]{2,1,0:T(8,128)} custom-call(s32[2]{0:T(128)} %pad_add_fusion.1.ints_ref, f32[8,256,512]{2,1,0:T(8,128)} %bitcast.2.y_ref, f32[4,2,2,2,256,128]{5,4,3,2,1,0:T(8,128)} %all-to-all-done.2.far_ref, bf16[256,768]{1,0:T(8,128)(2,1)} %pad_maximum_fusion.11.a_ref, bf16[256,768]{1,0:T(8,128)(2,1)} %pad_maximum_fusion.10.ab_ref, ...), custom_call_target="tpu_custom_call" | custom-call | flops 3000000000 | bytes 10000000 | tf_op jit(solution)/shard_map/odd_1/pallas_call | solution.py:390
  206.9 10.7 %odd_0.1.refs_3_ = f32[8,128,512]{2,1,0:T(8,128)} custom-call(s32[2]{0:T(128)} %pad_add_fusion.ints_ref, f32[8,256,512]{2,1,0:T(8,128)} %bitcast.2.y_ref, f32[4,2,2,2,256,128]{5,4,3,2,1,0:T(8,128)} %all-to-all-done.2.far_ref, bf16[256,768]{1,0:T(8,128)(2,1)} %pad_maximum_fusion.9.a_ref, bf16[256,768]{1,0:T(8,128)(2,1)} %pad_maximum_fusion.10.ab_ref, ...), custom_call_target="tpu_custom_call" | custom-call | flops 3000000000 | bytes 10000000 | tf_op jit(solution)/shard_map/odd_0/pallas_call | solution.py:390
  217.6 1.4 copy-done
  219.0 4.8 %all-to-all-start.4 = ((f32[4,1,2,2,256,128]{5,4,3,2,1,0:T(8,128)}), f32[4,1,2,2,256,128]{5,4,3,2,1,0:T(8,128)}, u32[]{:S(2)}, u32[]{:S(2)}) async-start(f32[4,1,2,2,256,128]{5,4,3,2,1,0:T(8,128)} %maximum_bitcast_fusion.1), calls=%async_computation.4 | async-start | bytes 4194304 | tf_op jit(solution)/shard_map/all_to_all | solution.py:424
  224.5 1.1 multiply_select_fusion.7
  225.8 0.9 fusion.15
  226.7 0.9 pad_maximum_fusion.6.v_ref
  227.6 12.5 %even_0.1 = f32[128,1024]{1,0:T(8,128)} custom-call(s32[2]{0:T(128)} %pad_add_fusion.ints_ref, f32[8,256,512]{2,1,0:T(8,128)} %bitcast.3.y_ref, f32[4,1,2,2,256,128]{5,4,3,2,1,0:T(8,128)} %copy-done, bf16[256,768]{1,0:T(8,128)(2,1)} %pad_maximum_fusion.9.a_ref, bf16[256,768]{1,0:T(8,128)(2,1)} %pad_maximum_fusion.10.ab_ref, ...), custom_call_target="tpu_custom_call" | custom-call | flops 3000000000 | bytes 10000000 | tf_op jit(solution)/shard_map/even_0/pallas_call | solution.py:390
  240.1 6.8 %all-to-all-done.4.far_ref = f32[4,1,2,2,256,128]{5,4,3,2,1,0:T(8,128)} async-done(((f32[4,1,2,2,256,128]{5,4,3,2,1,0:T(8,128)}), f32[4,1,2,2,256,128]{5,4,3,2,1,0:T(8,128)}, u32[]{:S(2)}, u32[]{:S(2)}) %all-to-all-start.4) | async-done | bytes 2097184 | tf_op jit(solution)/shard_map/all_to_all | solution.py:424
  246.9 12.5 %even_1.1 = f32[128,1024]{1,0:T(8,128)} custom-call(s32[2]{0:T(128)} %pad_add_fusion.1.ints_ref, f32[8,256,512]{2,1,0:T(8,128)} %bitcast.3.y_ref, f32[4,1,2,2,256,128]{5,4,3,2,1,0:T(8,128)} %all-to-all-done.4.far_ref, bf16[256,768]{1,0:T(8,128)(2,1)} %pad_maximum_fusion.11.a_ref, bf16[256,768]{1,0:T(8,128)(2,1)} %pad_maximum_fusion.10.ab_ref, ...), custom_call_target="tpu_custom_call" | custom-call | flops 3000000000 | bytes 10000000 | tf_op jit(solution)/shard_map/even_1/pallas_call | solution.py:390
  259.4 2.7 %fusion.1 = (f32[2]{0:T(128)}, f32[2,1,128,1024]{3,2,1,0:T(8,128)}) fusion(f32[1,128,1024]{2,1,0:T(8,128)} %bitcast.96, f32[1,128,1024]{2,1,0:T(8,128)S(1)} %bitcast.95), kind=kLoop, calls=%fused_computation.22 | loop fusion | flops 524286 | bytes 2097160 | tf_op jit(solution)/shard_map/reduce_max | solution.py:474
  (94 shorter events, 5.7 us)
Async XLA Ops:
  1.5 24.4 %collective-permute-start = (s32[2]{0:T(128)S(1)}, s32[2]{0:T(128)S(1)}, u32[]{:S(2)}, u32[]{:S(2)}) collective-permute-start(s32[2]{0:T(128)S(1)} %get-tuple-element.144), channel_id=1, source_target_pairs={{1,0},{2,1},{3,2},{0,3},{5,4},{6,5},{7,6},{4,7},{9,8},{10,9},{11,1... | collective-permute-start | bytes 32 | tf_op jit(solution)/shard_map/ppermute | solution.py:430
  1.7 24.3 %collective-permute-start.1 = (s32[2]{0:T(128)S(1)}, s32[2]{0:T(128)S(1)}, u32[]{:S(2)}, u32[]{:S(2)}) collective-permute-start(s32[2]{0:T(128)S(1)} %get-tuple-element.144), channel_id=1, source_target_pairs={{2,0},{3,1},{0,2},{1,3},{6,4},{7,5},{4,6},{5,7},{10,8},{11,9},{8,1... | collective-permute-start | bytes 32 | tf_op jit(solution)/shard_map/ppermute | solution.py:430
  4.9 21.1 %collective-permute-start.2 = (s32[2]{0:T(128)S(1)}, s32[2]{0:T(128)S(1)}, u32[]{:S(2)}, u32[]{:S(2)}) collective-permute-start(s32[2]{0:T(128)S(1)} %get-tuple-element.144), channel_id=1, source_target_pairs={{3,0},{0,1},{1,2},{2,3},{7,4},{4,5},{5,6},{6,7},{11,8},{8,9},{9,10... | collective-permute-start | bytes 32 | tf_op jit(solution)/shard_map/ppermute | solution.py:430
  7.2 2.1 copy-start.13
  19.1 5.0 %copy-start.21 = (s32[2,2,1]{1,2,0:T(1,128)S(1)}, s32[2,2,1]{1,2,0:T(1,128)}, u32[]{:S(2)}) copy-start(s32[2,2,1]{1,2,0:T(1,128)} %param.3) | copy-start | bytes 52
  19.1 51.7 %all-to-all-start = ((f32[4,2,256,512]{3,2,1,0:T(8,128)}), f32[4,2,256,512]{3,2,1,0:T(8,128)}, u32[]{:S(2)}, u32[]{:S(2)}) async-start(f32[4,2,256,512]{3,2,1,0:T(8,128)} %along_odd.1.x_ref), calls=%async_computation | async-start | bytes 8388608 | tf_op jit(solution)/shard_map/all_to_all | solution.py:421
  26.3 11.8 %copy-start.12 = (s32[2,4]{1,0:T(2,128)}, s32[2,4]{1,0:T(2,128)S(1)}, u32[]{:S(2)}) copy-start(s32[2,4]{1,0:T(2,128)S(1)} %constant_dynamic-slice_fusion.off_ref) | copy-start | bytes 100
  51.6 4.2 %copy-start.15 = (s32[128]{0:T(128)S(1)}, s32[128]{0:T(128)}, u32[]{:S(2)}) copy-start(s32[128]{0:T(128)} %get-tuple-element.184) | copy-start | bytes 1540
  51.6 4.2 %copy-start.17 = (s32[128]{0:T(128)S(1)}, s32[128]{0:T(128)}, u32[]{:S(2)}) copy-start(s32[128]{0:T(128)} %get-tuple-element.194) | copy-start | bytes 1540
  51.6 4.2 %copy-start.20 = (f32[256]{0:T(256)S(1)}, f32[256]{0:T(256)}, u32[]{:S(2)}) copy-start(f32[256]{0:T(256)} %get-tuple-element.29) | copy-start | bytes 3076
  51.6 4.2 %copy-start.22 = (pred[128]{0:T(512)(128)(4,1)S(1)}, pred[128]{0:T(512)(128)(4,1)}, u32[]{:S(2)}) copy-start(pred[128]{0:T(512)(128)(4,1)} %get-tuple-element.182) | copy-start | bytes 388
  53.2 49.4 %collective-permute-start.4 = (f32[3,2,2,256,128]{4,3,2,1,0:T(8,128)S(1)}, f32[3,2,2,256,128]{4,3,2,1,0:T(8,128)S(1)}, u32[]{:S(2)}, u32[]{:S(2)}) collective-permute-start(f32[3,2,2,256,128]{4,3,2,1,0:T(8,128)S(1)} %slice_bitcast_fusion.1), channel_id=1, source_target_pairs={{8,0},{12,4},{16,8},{20,12},{24,16},{28,20},{32,24},{36,28},{40,32... | collective-permute-start | bytes 4718600 | tf_op jit(solution)/shard_map/ppermute | solution.py:407
  70.8 52.3 %all-to-all-start.1 = ((f32[4,2,256,512]{3,2,1,0:T(8,128)}), f32[4,2,256,512]{3,2,1,0:T(8,128)}, u32[]{:S(2)}, u32[]{:S(2)}) async-start(f32[4,2,256,512]{3,2,1,0:T(8,128)} %along_even.1.x_ref), calls=%async_computation.1 | async-start | bytes 8388608 | tf_op jit(solution)/shard_map/all_to_all | solution.py:421
  78.4 21.4 %collective-permute-start.3 = (f32[2,2,2,256,128]{4,3,2,1,0:T(8,128)S(1)}, f32[2,2,2,256,128]{4,3,2,1,0:T(8,128)S(1)}, u32[]{:S(2)}, u32[]{:S(2)}) collective-permute-start(f32[2,2,2,256,128]{4,3,2,1,0:T(8,128)S(1)} %pad_maximum_fusion.3), channel_id=1, source_target_pairs={{4,0},{8,4},{12,8},{16,12},{20,16},{24,20},{28,24},{32,28},{36,32}... | collective-permute-start | bytes 3145736 | tf_op jit(solution)/shard_map/ppermute | solution.py:407
  123.1 6.4 %copy-start.14 = (s32[256]{0:T(256)S(1)}, s32[256]{0:T(256)}, u32[]{:S(2)}) copy-start(s32[256]{0:T(256)} %copy-done.13) | copy-start | bytes 3076
  123.1 51.6 %all-to-all-start.2 = ((f32[4,2,2,2,256,128]{5,4,3,2,1,0:T(8,128)}), f32[4,2,2,2,256,128]{5,4,3,2,1,0:T(8,128)}, u32[]{:S(2)}, u32[]{:S(2)}) async-start(f32[4,2,2,2,256,128]{5,4,3,2,1,0:T(8,128)} %bitcast.32), calls=%async_computation.2 | async-start | bytes 8388608 | tf_op jit(solution)/shard_map/all_to_all | solution.py:424
  143.6 18.9 %collective-permute-start.5 = (f32[2,2,2,256,128]{4,3,2,1,0:T(8,128)S(1)}, f32[2,2,2,256,128]{4,3,2,1,0:T(8,128)S(1)}, u32[]{:S(2)}, u32[]{:S(2)}) collective-permute-start(f32[2,2,2,256,128]{4,3,2,1,0:T(8,128)S(1)} %pad_maximum_fusion.4), channel_id=1, source_target_pairs={{4,0},{8,4},{12,8},{16,12},{20,16},{24,20},{28,24},{32,28},{36,32}... | collective-permute-start | bytes 3145736 | tf_op jit(solution)/shard_map/ppermute | solution.py:407
  149.7 43.6 %collective-permute-start.6 = (f32[3,2,2,256,128]{4,3,2,1,0:T(8,128)}, f32[3,2,2,256,128]{4,3,2,1,0:T(8,128)}, u32[]{:S(2)}, u32[]{:S(2)}) collective-permute-start(f32[3,2,2,256,128]{4,3,2,1,0:T(8,128)} %slice_bitcast_fusion), channel_id=1, source_target_pairs={{8,0},{12,4},{16,8},{20,12},{24,16},{28,20},{32,24},{36,28},{40,32... | collective-permute-start | bytes 4718600 | tf_op jit(solution)/shard_map/ppermute | solution.py:407
  174.7 42.9 %all-to-all-start.3 = ((f32[4,1,2,2,256,128]{5,4,3,2,1,0:T(8,128)}), f32[4,1,2,2,256,128]{5,4,3,2,1,0:T(8,128)S(1)}, u32[]{:S(2)}, u32[]{:S(2)}) async-start(f32[4,1,2,2,256,128]{5,4,3,2,1,0:T(8,128)} %bitcast.39), calls=%async_computation.3 | async-start | bytes 4194304 | tf_op jit(solution)/shard_map/all_to_all | solution.py:424
  180.9 2.6 copy-start.3
  180.9 2.6 copy-start.4
  180.9 2.6 copy-start.5
  180.9 2.6 copy-start.6
  180.9 2.6 copy-start.7
  180.9 2.6 copy-start.8
  182.1 3.0 %copy-start.2 = (bf16[256,256]{1,0:T(8,128)(2,1)S(1)}, bf16[256,256]{1,0:T(8,128)(2,1)}, u32[]{:S(2)}) copy-start(bf16[256,256]{1,0:T(8,128)(2,1)} %get-tuple-element.70) | copy-start | bytes 393220
  217.6 6.9 %copy-start.16 = (s32[128]{0:T(128)S(1)}, s32[128]{0:T(128)}, u32[]{:S(2)}) copy-start(s32[128]{0:T(128)} %get-tuple-element.184) | copy-start | bytes 1540
  217.6 6.9 %copy-start.18 = (s32[128]{0:T(128)S(1)}, s32[128]{0:T(128)}, u32[]{:S(2)}) copy-start(s32[128]{0:T(128)} %get-tuple-element.194) | copy-start | bytes 1540
  217.6 6.9 %copy-start.19 = (f32[256]{0:T(256)S(1)}, f32[256]{0:T(256)}, u32[]{:S(2)}) copy-start(f32[256]{0:T(256)} %get-tuple-element.28) | copy-start | bytes 3076
  217.6 6.9 %copy-start.23 = (pred[128]{0:T(512)(128)(4,1)S(1)}, pred[128]{0:T(512)(128)(4,1)}, u32[]{:S(2)}) copy-start(pred[128]{0:T(512)(128)(4,1)} %get-tuple-element.182) | copy-start | bytes 388
  217.6 1.4 copy-start
  219.0 28.0 %all-to-all-start.4 = ((f32[4,1,2,2,256,128]{5,4,3,2,1,0:T(8,128)}), f32[4,1,2,2,256,128]{5,4,3,2,1,0:T(8,128)}, u32[]{:S(2)}, u32[]{:S(2)}) async-start(f32[4,1,2,2,256,128]{5,4,3,2,1,0:T(8,128)} %maximum_bitcast_fusion.1), calls=%async_computation.4 | async-start | bytes 4194304 | tf_op jit(solution)/shard_map/all_to_all | solution.py:424
  223.8 2.0 copy-start.9
  223.8 2.0 copy-start.10
  223.8 2.1 copy-start.11
  240.1 19.3 %copy-start.1 = (f32[128,1024]{1,0:T(8,128)S(1)}, f32[128,1024]{1,0:T(8,128)}, u32[]{:S(2)}) copy-start(f32[128,1024]{1,0:T(8,128)} %even_0.1) | copy-start | bytes 1572868

commit v4 on v3

v4 whole, which is shorter than its diff:
```python
import functools
import math

import jax
import jax.numpy as jnp
from jax import lax
from jax.experimental import pallas as pl
from jax.experimental.pallas import tpu as pltpu
from jax.sharding import PartitionSpec as P


GC = 7
ROUNDS = 2
A = 128
L = 1024
Z = 8
FLOOR = 0.25
BF = jnp.bfloat16
F32 = jnp.float32
HALF = math.sqrt(0.5)


def split(x):
    hi = x.astype(BF)
    lo = (x - hi.astype(F32)).astype(BF)
    return hi, lo


def split_table(x):
    hi = lax.reduce_precision(x, exponent_bits=8, mantissa_bits=7)
    return hi.astype(BF), (x - hi).astype(BF)


def three_rows(x):
    hi, lo = split_table(x)
    return jnp.concatenate((hi, hi, lo), axis=0)


def three_cols(x):
    hi, lo = split_table(x)
    return jnp.concatenate((hi, hi, lo), axis=1)


def trig(index, total):
    angle = (index % total).astype(F32) * (2.0 * math.pi / total)
    return jnp.cos(angle), jnp.sin(angle)


def iota(length):
    return lax.optimization_barrier(jnp.arange(length, dtype=jnp.int32))


def odd_table():
    rows = iota(512)[:, None]
    m = iota(256)[None, :]
    c, s = trig(rows * (2 * m + 1), L)
    scale = 1.0 / L
    return three_rows(
        scale * jnp.concatenate((c[:, :128], -s[:, :128], c[:, 128:], -s[:, 128:]), axis=1)
    )


def fours_table():
    n = iota(256)[:, None]
    m = iota(A)[None, :]
    c, s = trig(n * (4 * m), L)
    last = (1 - 2 * (n % 2)).astype(F32)
    return three_rows((1.0 / L) * jnp.concatenate((c, jnp.where(m == 0, last, -s)), axis=1))


def twos_table():
    n = iota(256)[:, None]
    m = iota(A)[None, :]
    c, s = trig(n * (4 * m + 2), L)
    return three_rows((1.0 / L) * jnp.concatenate((c, -s), axis=1))


def odd_back():
    cols = iota(512)[None, :]
    m = iota(256)[:, None]
    c, s = trig(cols * (2 * m + 1), L)
    scale = 2.0 / L
    return jnp.stack(
        [three_rows(scale * jnp.concatenate((c[b : b + A], -s[b : b + A]), axis=0)) for b in (0, A)]
    )


def fours_back():
    cols = iota(256)[None, :]
    m = iota(A)[:, None]
    c, s = trig(cols * (4 * m), L)
    last = (1 - 2 * (cols % 2)).astype(F32)
    scale = 2.0 / L
    real = jnp.where(m == 0, 0.5 * scale, scale * c)
    imag = jnp.where(m == 0, 0.5 * scale * last, -scale * s)
    return three_rows(jnp.concatenate((real, imag), axis=0))


def twos_back():
    cols = iota(256)[None, :]
    m = iota(A)[:, None]
    c, s = trig(cols * (4 * m + 2), L)
    return three_rows((2.0 / L) * jnp.concatenate((c, -s), axis=0))


def across_base():
    v = iota(A)
    return trig(v[:, None] * v[None, :], A)


def across_forward(offset, base):
    c0, s0 = base
    cv, sv = trig(offset * iota(A)[:, None], A)
    c = c0 * cv + s0 * sv
    s = s0 * cv - c0 * sv
    top = jnp.concatenate((c, s), axis=1)
    low = jnp.concatenate((-s, c), axis=1)
    return three_cols(jnp.concatenate((top, low), axis=0))


def across_back():
    v = iota(A)[None, :]
    a = iota(A)[:, None]
    c, s = trig(a * v, A)
    top = jnp.concatenate((c, -s), axis=1)
    low = jnp.concatenate((s, c), axis=1)
    return three_cols(jnp.concatenate((top, low), axis=0))


def edge_tables():
    lane = iota(A)
    i = lane[:, None]
    j = lane[None, :]
    inside = jnp.logical_and(i < Z, j < Z)
    c, s = trig(i * j, Z)
    c = jnp.where(inside, c, 0.0)
    s = jnp.where(inside, s, 0.0)
    fwd = jnp.concatenate(
        (jnp.concatenate((c, -s), axis=1), jnp.concatenate((s, c), axis=1)), axis=0
    )
    rev = jnp.concatenate(
        (jnp.concatenate((c, s), axis=1), jnp.concatenate((-s, c), axis=1)), axis=0
    )
    flip = ((i + j) % A == 0).astype(F32)
    return fwd, rev, flip


def dot3_left(x, table):
    hi, lo = split(x)
    return jnp.dot(jnp.concatenate((hi, lo, hi), axis=1), table, preferred_element_type=F32)


def dot3_right(table, x):
    hi, lo = split(x)
    return jnp.dot(table, jnp.concatenate((hi, lo, hi), axis=0), preferred_element_type=F32)


def whole(shape):
    return pl.BlockSpec(shape, lambda *_: (0,) * len(shape))


def times_i(x, sign):
    return (-sign * x[1], sign * x[0])


def cadd(x, y):
    return (x[0] + y[0], x[1] + y[1])


def csub(x, y):
    return (x[0] - y[0], x[1] - y[1])


def eighth(x, sign):
    return ((x[0] - sign * x[1]) * HALF, (x[1] + sign * x[0]) * HALF)


def dft4(x, sign):
    a = cadd(x[0], x[2])
    b = csub(x[0], x[2])
    c = cadd(x[1], x[3])
    d = times_i(csub(x[1], x[3]), sign)
    return [cadd(a, c), cadd(b, d), csub(a, c), csub(b, d)]


def dft8(x, sign):
    even = dft4([x[0], x[2], x[4], x[6]], sign)
    odd = dft4([x[1], x[3], x[5], x[7]], sign)
    odd = [odd[0], eighth(odd[1], sign), times_i(odd[2], sign), times_i(eighth(odd[3], sign), sign)]
    return [cadd(even[k], odd[k]) for k in range(4)] + [csub(even[k], odd[k]) for k in range(4)]


def large_kernel(x_ref, w1_ref, w0_ref, out_ref):
    x = x_ref[0].reshape(512, L)
    out_ref[0, :, :, :512] = dot3_left(x[:, :512] - x[:, 512:], w1_ref[...]).reshape(2, 256, 512)
    y = x[:, :512] + x[:, 512:]
    out_ref[0, :, :, 512:] = dot3_left(y[:, :256] + y[:, 256:], w0_ref[...]).reshape(2, 256, 256)


def small_kernel(x_ref, w2_ref, out_ref):
    x = x_ref[0].reshape(512, L)
    y = x[:, :512] + x[:, 512:]
    out_ref[0] = dot3_left(y[:, :256] - y[:, 256:], w2_ref[...]).reshape(2, 256, 256)


def along(kernel, stored, tables, columns, interpret=False):
    tiles, planes = stored.shape[:2]
    return pl.pallas_call(
        kernel,
        out_shape=jax.ShapeDtypeStruct((tiles, planes, 256, columns), F32),
        grid_spec=pl.GridSpec(
            grid=(tiles,),
            in_specs=[pl.BlockSpec((1, planes, 256, L), lambda i: (i, 0, 0, 0))]
            + [whole(t.shape) for t in tables],
            out_specs=pl.BlockSpec((1, planes, 256, columns), lambda i: (i, 0, 0, 0)),
        ),
        cost_estimate=pl.CostEstimate(flops=6_000_000 * columns, bytes_accessed=14_000_000, transcendentals=0),
        interpret=interpret,
    )(stored, *tables)


def across(y_ref, first, count, offset, table):
    later = lax.broadcasted_iota(jnp.int32, (A, 256), 0) >= offset
    picked = [jnp.where(later, y_ref[first + k, :A, :], y_ref[first + k, A:, :]) for k in range(count)]
    real = jnp.concatenate([p[:, :128] for p in picked], axis=1)
    imag = jnp.concatenate([p[:, 128:] for p in picked], axis=1)
    return dot3_right(table, jnp.concatenate((real, imag), axis=0))


def send_kernel(blocks, off_ref, x_ref, a_ref, out_ref):
    tile = pl.program_id(0)
    rnd = pl.program_id(1)
    later = lax.broadcasted_iota(jnp.int32, (A, 256), 0) >= off_ref[rnd, tile]
    picked = [
        jnp.where(later, x_ref[0, p, :A, w * 256 : (w + 1) * 256], x_ref[0, p, A:, w * 256 : (w + 1) * 256])
        for p in range(2)
        for w in range(blocks)
    ]
    real = jnp.concatenate([p[:, :128] for p in picked], axis=1)
    imag = jnp.concatenate([p[:, 128:] for p in picked], axis=1)
    spec = dot3_right(a_ref[0, 0], jnp.concatenate((real, imag), axis=0))
    for k in range(2 * blocks):
        out_ref[0, 0, k // blocks, k % blocks] = spec[:, k * 128 : (k + 1) * 128]


def spectra(x, offs, mats, interpret=False):
    tiles = x.shape[0]
    blocks = x.shape[3] // 256
    return pl.pallas_call(
        functools.partial(send_kernel, blocks),
        out_shape=jax.ShapeDtypeStruct((tiles, ROUNDS, 2, blocks, 256, 128), F32),
        grid_spec=pltpu.PrefetchScalarGridSpec(
            num_scalar_prefetch=1,
            grid=(tiles, ROUNDS),
            in_specs=[
                pl.BlockSpec((1, 2, 256, 256 * blocks), lambda t, r, *_: (t, 0, 0, 0)),
                pl.BlockSpec((1, 1, 256, 768), lambda t, r, *_: (r, t, 0, 0)),
            ],
            out_specs=pl.BlockSpec(
                (1, 1, 2, blocks, 256, 128),
                lambda t, r, *_: (lax.rem(t + 3 - 2 * r, tiles), r, 0, 0, 0, 0),
            ),
        ),
        cost_estimate=pl.CostEstimate(flops=800_000_000 * blocks, bytes_accessed=6_000_000 * blocks, transcendentals=0),
        interpret=interpret,
        name="spectra",
    )(offs, x, mats)


def normalized(p, q, sign):
    real = p[0] * q[0] + p[1] * q[1]
    imag = p[1] * q[0] - p[0] * q[1]
    scale = lax.rsqrt(jnp.maximum(real * real + imag * imag, FLOOR * FLOOR)) * sign
    return (real * scale, imag * scale)


def to_lanes(block_of, part):
    lane = lax.broadcasted_iota(jnp.int32, (A, 128), 1)
    out = jnp.zeros((A, 128), F32)
    for z in range(Z):
        block = block_of(z, slice(part * A, (part + 1) * A))
        if z:
            block = pltpu.roll(block, z, 1)
        out = jnp.where(lane == z, block, out)
    return out


def edge_fix(own_of, far_of, r_ref, ef_ref, er_ref, flip_ref, sign):
    high = lax.Precision.HIGHEST

    def edge(block_of):
        packed = jnp.concatenate([to_lanes(block_of, part) for part in range(2)], axis=1)
        here = jnp.dot(packed, ef_ref[...], precision=high, preferred_element_type=F32)
        turned = jnp.dot(packed, er_ref[...], precision=high, preferred_element_type=F32)
        there = jnp.dot(flip_ref[...], turned, precision=high, preferred_element_type=F32)
        hr, hi = here[:, :128], here[:, 128:]
        tr, ti = there[:, :128], there[:, 128:]
        return ((hr + tr) * 0.5, (hi - ti) * 0.5), ((hi + ti) * 0.5, (tr - hr) * 0.5)

    own_zero, own_last = edge(own_of)
    far_zero, far_last = edge(far_of)
    zero = normalized(own_zero, far_zero, sign)
    last = normalized(own_last, far_last, sign)
    both = jnp.concatenate((zero[0] - last[1], zero[1] + last[0]), axis=1)
    field = jnp.dot(both, er_ref[...], precision=high, preferred_element_type=F32)
    lane = lax.broadcasted_iota(jnp.int32, (A, 128), 1)
    for part in range(2):
        source = field[:, part * 128 : (part + 1) * 128]
        for z in range(Z):
            moved = pltpu.roll(source, 128 - z, 1) if z else source
            place = (slice(part * A, (part + 1) * A), slice(z * 128, (z + 1) * 128))
            r_ref[place] = jnp.where(lane == 0, moved, r_ref[place])


def pair_core(ints_ref, y_ref, far_ref, a_ref, own_ref, r_ref, valid):
    for half in range(2):
        own_ref[:, half * 512 : (half + 1) * 512] = across(y_ref, half * 4, 4, ints_ref[0], a_ref[...])

    def own_of(z, rows):
        return own_ref[rows, z * 128 : (z + 1) * 128]

    def far_of(z, rows):
        return far_ref[z // 2, 0, z % 2, 0, rows, :]

    def chunk(i, _):
        up = pl.ds(pl.multiple_of(i * 8, 8), 8)
        down = pl.ds(pl.multiple_of(i * 8 + A, 8), 8)
        own = dft8([(own_of(z, up), own_of(z, down)) for z in range(Z)], -1.0)
        far = dft8([(far_of(z, up), far_of(z, down)) for z in range(Z)], -1.0)
        back = dft8([normalized(own[u], far[u], valid) for u in range(Z)], 1.0)
        for z in range(Z):
            r_ref[up, z * 128 : (z + 1) * 128] = back[z][0]
            r_ref[down, z * 128 : (z + 1) * 128] = back[z][1]
        return 0

    lax.fori_loop(0, A // 8, chunk, 0)
    return own_of, far_of


def parts(ab_ref, r_ref, v_ref):
    for half in range(2):
        q = dot3_right(ab_ref[...], r_ref[:, half * 512 : (half + 1) * 512])
        for k in range(0, 4, 2):
            rows = [
                jnp.concatenate((q[:A, j * 128 : (j + 1) * 128], q[A:, j * 128 : (j + 1) * 128]), axis=1)
                for j in (k, k + 1)
            ]
            yield half * 4 + k, dot3_left(jnp.concatenate(rows, axis=0), v_ref[...])


def large_pair_kernel(
    ints_ref, y_ref, far_ref, a_ref, ab_ref, v1_ref, v0_ref, ef_ref, er_ref, flip_ref,
    odd_ref, fours_ref, own_ref, r_ref,
):
    step = pl.program_id(0)
    valid = ints_ref[1].astype(F32)
    own_of, far_of = pair_core(ints_ref, y_ref, far_ref, a_ref, own_ref, r_ref, valid)

    @pl.when(step == 0)
    def _():
        for z, part in parts(ab_ref, r_ref, v1_ref.at[0]):
            odd_ref[z : z + 2] = part.reshape(2, A, 512)

    @pl.when(step == 1)
    def _():
        for z, part in parts(ab_ref, r_ref, v1_ref.at[0]):
            odd_ref[z : z + 2] += part.reshape(2, A, 512)

    @pl.when(step == 2)
    def _():
        edge_fix(own_of, far_of, r_ref, ef_ref, er_ref, flip_ref, valid)
        for z, part in parts(ab_ref, r_ref, v0_ref):
            fours_ref[z : z + 2] = part.reshape(2, A, 256)


def small_pair_kernel(ints_ref, y_ref, far_ref, a_ref, ab_ref, v2_ref, odd_ref, fours_ref, *refs):
    surf_ref, peak_ref, own_ref, r_ref = refs[-4:]
    valid = ints_ref[1].astype(F32)
    pair_core(ints_ref, y_ref, far_ref, a_ref, own_ref, r_ref, valid)
    for z, part in parts(ab_ref, r_ref, v2_ref):
        first = fours_ref[z : z + 2].reshape(2 * A, 256)
        odd = odd_ref[z : z + 2].reshape(2 * A, 512)
        y = jnp.concatenate((first + part, first - part), axis=1)
        x = jnp.concatenate((y + odd, y - odd), axis=1)
        x = jnp.maximum(x[:A], x[A:])
        if z == 0:
            surf_ref[0, 0] = x
        else:
            surf_ref[0, 0] = jnp.maximum(surf_ref[0, 0], x)
    peak_ref[0] = jnp.broadcast_to(jnp.max(surf_ref[0, 0]), (8, 128))


SCRATCH = [pltpu.VMEM((256, Z * 128), F32), pltpu.VMEM((256, Z * 128), F32)]


def large_pair(ints, y, far, mat, ab, back1, back0, edges, interpret=False):
    return pl.pallas_call(
        large_pair_kernel,
        out_shape=(jax.ShapeDtypeStruct((Z, A, 512), F32), jax.ShapeDtypeStruct((Z, A, 256), F32)),
        grid_spec=pltpu.PrefetchScalarGridSpec(
            num_scalar_prefetch=1,
            grid=(3,),
            in_specs=[
                pl.BlockSpec((Z, 256, 256), lambda w, *_: (0, 0, w)),
                pl.BlockSpec((4, 1, 2, 1, 256, 128), lambda w, *_: (0, 0, 0, w, 0, 0)),
                whole((256, 768)),
                whole((256, 768)),
                pl.BlockSpec((1, 768, 512), lambda w, *_: (jnp.minimum(w, 1), 0, 0)),
                whole((768, 256)),
                whole((256, 256)),
                whole((256, 256)),
                whole((128, 128)),
            ],
            out_specs=(whole((Z, A, 512)), whole((Z, A, 256))),
            scratch_shapes=SCRATCH,
        ),
        cost_estimate=pl.CostEstimate(flops=6_000_000_000, bytes_accessed=16_000_000, transcendentals=500_000),
        interpret=interpret,
    )(ints, y, far, mat, ab, back1, back0, *edges)


def small_pair(rnd, ints, y, far, mat, ab, back2, odd, fours, before, interpret=False):
    args = [y, far, mat, ab, back2, odd, fours]
    pick = rnd if far.shape[1] > 1 else 0
    in_specs = [
        whole((Z, 256, 256)),
        pl.BlockSpec((4, 1, 2, 1, 256, 128), lambda w, *_: (0, pick, 0, 0, 0, 0)),
        whole((256, 768)),
        whole((256, 768)),
        whole((768, 256)),
        whole((Z, A, 512)),
        whole((Z, A, 256)),
    ]
    aliases = {}
    if before is not None:
        aliases = {len(args) + 1: 0, len(args) + 2: 1}
        args += list(before)
        in_specs += [pl.BlockSpec(memory_space=pl.ANY)] * 2
    return pl.pallas_call(
        small_pair_kernel,
        out_shape=(
            jax.ShapeDtypeStruct((ROUNDS, 1, A, L), F32),
            jax.ShapeDtypeStruct((ROUNDS, 8, 128), F32),
        ),
        grid_spec=pltpu.PrefetchScalarGridSpec(
            num_scalar_prefetch=1,
            grid=(1,),
            in_specs=in_specs,
            out_specs=(
                pl.BlockSpec((1, 1, A, L), lambda w, *_: (rnd, 0, 0, 0)),
                pl.BlockSpec((1, 8, 128), lambda w, *_: (rnd, 0, 0)),
            ),
            scratch_shapes=SCRATCH,
        ),
        input_output_aliases=aliases,
        cost_estimate=pl.CostEstimate(flops=2_000_000_000, bytes_accessed=10_000_000, transcendentals=300_000),
        interpret=interpret,
    )(ints, *args)


def from_next(x, step, groups):
    return lax.ppermute(x, "tile", [(g + step, g) for g in range(groups - step)])


def after(*values):
    return lax.optimization_barrier(values)


def register(stored, offsets):
    size = lax.axis_size(("tile", "slab"))
    groups = lax.axis_size("tile")
    slabs = lax.axis_size("slab")
    place = lax.axis_index(("tile", "slab"))

    def gather(x):
        return lax.all_to_all(x, "slab", split_axis=0, concat_axis=1, tiled=True)[0]

    def collect(x):
        return lax.all_to_all(x, "slab", split_axis=0, concat_axis=0, tiled=True)

    small_src = along(small_kernel, stored, (twos_table(),), 256)
    small_all = gather(small_src)
    small_src, table = after(small_src, odd_table())
    large_src = along(large_kernel, stored, (table, fours_table()), 768)
    large_src, mine = after(large_src, offsets[:, 1, 0])
    turns = [mine] + [
        lax.ppermute(mine, "slab", [((i + k) % slabs, i) for i in range(slabs)]) for k in range(1, slabs)
    ]
    base = lax.optimization_barrier(across_base())
    given = jnp.roll(jnp.stack(turns, axis=1), lax.axis_index("slab"), axis=1)
    mats = jnp.stack([jnp.stack([across_forward(given[r, j], base) for j in range(slabs)]) for r in range(ROUNDS)])
    small_all, large_src = after(small_all, large_src)
    large_all = gather(large_src)

    def shifted(src):
        made = spectra(src, given, mats)
        near = from_next(jnp.stack((made[3, 0], made[0, 1])), 1, groups)
        far = from_next(made[1:, 1], 2, groups)
        zero = [made[0, 0], made[1, 0], made[2, 0], near[0]]
        one = [near[1], far[0], far[1], far[2]]
        return zero, one

    large_zero, large_one = [jnp.stack(x)[:, None] for x in shifted(large_src)]
    both = zip(*shifted(small_src), strict=True)
    small_sent = jnp.stack([x for two in both for x in two]).reshape(slabs, ROUNDS, 2, 1, 256, 128)
    valid = (
        jnp.logical_and(place % GC != GC - 1, place + 1 < size),
        place + GC < size,
    )
    own = [offsets[r, 0, 0] for r in range(ROUNDS)]
    ints = [jnp.stack((own[r], valid[r].astype(jnp.int32))) for r in range(ROUNDS)]
    own_mats = [across_forward(o, base) for o in own]
    ab = across_back()
    edges = edge_tables()
    back1, back0, back2 = odd_back(), fours_back(), twos_back()
    large_all, large_zero, small_sent, large_one, own_mats, ab, edges, back1, back0, back2 = after(
        large_all, large_zero, small_sent, large_one, own_mats, ab, edges, back1, back0, back2
    )
    far_zero = collect(large_zero)
    far_zero, large_one = after(far_zero, large_one)
    far_one = collect(large_one)
    first = large_pair(ints[0], large_all, far_zero, own_mats[0], ab, back1, back0, edges)
    far_one, first, small_sent = after(far_one, first, small_sent)
    small_far = collect(small_sent)
    second = large_pair(ints[1], large_all, far_one, own_mats[1], ab, back1, back0, edges)
    out = small_pair(0, ints[0], small_all, small_far, own_mats[0], ab, back2, *first, None)
    surface, peak = small_pair(1, ints[1], small_all, small_far, own_mats[1], ab, back2, *second, out)
    return surface, peak[:, 0, :1]


def solution(mesh):
    return jax.shard_map(
        register,
        mesh=mesh,
        in_specs=(P("tile", "slab", None, None), P(None, None, ("tile", "slab"))),
        out_specs=(P(None, ("tile", "slab"), None, None), P(None, ("tile", "slab"))),
        check_vma=False,
    )
```

time: 265 us -> 309 us (1.17)
  blocking collectives: 0 us -> 40.7 us
  waiting for transfers between devices: 72 us -> 88.6 us
  starting transfers between devices: 42.3 us -> 34.7 us
  other arithmetic: 43.8 us -> 38.4 us
    all_to_all x0 -> x1, blocking collectives: none -> 40.7 us  [collect(): return lax.all_to_all(x, 'slab', split_axis=0, concat_axis=0, tiled=True)]
    ppermute x4, waiting for transfers between devices: 34.2 us -> 60.9 us  [from_next(): lax.ppermute(x, 'tile', [(g + step, g) for g in range(groups - step)])]
    all_to_all x2, waiting for transfers between devices: 20.3 us -> 0.01 us  [gather(): return lax.all_to_all(x, 'slab', split_axis=0, concat_axis=1, tiled=True)[0]]
    all_to_all x3 -> x2, waiting for transfers between devices: 17.4 us -> 27.7 us  [collect(): return lax.all_to_all(x, 'slab', split_axis=0, concat_axis=0, tiled=True)]
    cos x3 -> x5, other arithmetic: 5.35 us -> 13.9 us  [trig(): return (jnp.cos(angle), jnp.sin(angle))]
    add x2 -> x1, other arithmetic: 6.94 us -> 0.01 us  [odd_table(): c, s = trig(rows * (2 * m + 1), L)]
    all_to_all x3 -> x2, starting transfers between devices: 16.2 us -> 11.1 us  [collect(): return lax.all_to_all(x, 'slab', split_axis=0, concat_axis=0, tiled=True)]
    unnamed x55 -> x35, local copies, waits for them, and re-layouts: 10.5 us -> 6.87 us
  transfers between devices with their start and end apart: 12 -> 11, of which waited for: 7 -> 4; matrix products, arithmetic and copies ran while one was open for 23% -> 15% of each run, Pallas kernels for 26% -> 17%
where the time goes in v4:
time: 309 us; the launch traced here: 305 us
  waiting for transfers between devices  88.6 us (29%)
  Pallas kernels  82.9 us (27%)
  blocking collectives  40.7 us (13%)
  other arithmetic  38.4 us (12%)
  starting transfers between devices  34.7 us (11%)
  local copies, waits for them, and re-layouts  18.6 us (6%)
    ppermute x4, waiting for transfers between devices, from_next(): lax.ppermute(x, 'tile', [(g + step, g) for g in range(groups - step)])  60.9 us
    all_to_all x1, blocking collectives, collect(): return lax.all_to_all(x, 'slab', split_axis=0, concat_axis=0, tiled=True)  40.7 us
    pallas_call x2, Pallas kernels, large_pair(): pl.pallas_call(large_pair_kernel, out_shape=(jax.ShapeDtypeStruct((Z, A,...  32.5 us
    all_to_all x2, waiting for transfers between devices, collect(): return lax.all_to_all(x, 'slab', split_axis=0, concat_axis=0, tiled=True)  27.7 us
    pallas_call x2, Pallas kernels, spectra(): pl.pallas_call(functools.partial(send_kernel, blocks), out_shape=jax.Shap...  19.9 us
    pallas_call x2, Pallas kernels, small_pair(): pl.pallas_call(small_pair_kernel, out_shape=(jax.ShapeDtypeStruct((ROUNDS...  15.3 us
    pallas_call x2, Pallas kernels, along(): pl.pallas_call(kernel, out_shape=jax.ShapeDtypeStruct((tiles, planes, 256...  15.2 us
    cos x5, other arithmetic, trig(): return (jnp.cos(angle), jnp.sin(angle))  13.9 us
  transfers between devices with their start and end apart: 11, of which 4 were waited for; matrix products, arithmetic and copies ran while one was open for 15% of the time, Pallas kernels for 17%

profile of v4, /device:TPU:56, one launch (start us, length us, event | category | flops | bytes accessed | tf_op | source)
XLA Modules:
  0.0 305.2 jit_solution(3807166496379265469)
XLA Ops:
  0.7 1.1 fusion.54
  1.9 0.8 pad_maximum_fusion.5.w2_ref
  2.7 6.0 %shard_map.41.x_ref = f32[4,2,256,256]{3,2,1,0:T(8,128)} custom-call(f32[4,2,256,1024]{3,2,1,0:T(8,128)} %x_ref.3, bf16[768,256]{1,0:T(8,128)(2,1)} %pad_maximum_fusion.5.w2_ref), custom_call_target="tpu_custom_call" | custom-call | flops 1536000000 | bytes 14000000 | tf_op jit(solution)/shard_map/pallas_call | solution.py:208
  8.7 2.1 fusion.32
  11.0 1.3 pad_maximum_fusion.1.w1_ref
  12.5 0.8 pad_maximum_fusion.6.w0_ref
  13.3 9.2 %shard_map.42.x_ref = f32[4,2,256,768]{3,2,1,0:T(8,128)} custom-call(f32[4,2,256,1024]{3,2,1,0:T(8,128)} %x_ref.3, bf16[1536,512]{1,0:T(8,128)(2,1)} %pad_maximum_fusion.1.w1_ref, bf16[768,256]{1,0:T(8,128)(2,1)} %pad_maximum_fusion.6.w0_ref), custom_call_target="tpu_custom_call" | custom-call | flops 4608000000 | bytes 14000000 | tf_op jit(solution)/shard_map/pallas_call | solution.py:208
  22.6 3.3 %collective-permute-start.1 = (s32[2]{0:T(128)S(1)}, s32[2]{0:T(128)}, u32[]{:S(2)}, u32[]{:S(2)}) collective-permute-start(s32[2]{0:T(128)S(1)} %slice_reduce_fusion.1), channel_id=1, source_target_pairs={{2,0},{3,1},{0,2},{1,3},{6,4},{7,5},{4,6},{5,7},{10,8},{11,9},{8,1... | collective-permute-start | bytes 32 | tf_op jit(solution)/shard_map/ppermute | solution.py:487
  25.9 2.2 collective-permute-start.2
  28.1 3.8 %all-to-all-start = ((f32[4,2,256,256]{3,2,1,0:T(8,128)}), f32[4,2,256,256]{3,2,1,0:T(8,128)S(1)}, u32[]{:S(2)}, u32[]{:S(2)}) async-start(f32[4,2,256,256]{3,2,1,0:T(8,128)} %shard_map.41.x_ref), calls=%async_computation | async-start | bytes 4194304 | tf_op jit(solution)/shard_map/all_to_all | solution.py:476
  31.9 0.6 fusion.129
  32.5 2.1 fusion.30
  34.7 0.7 fusion.56.flip_ref
  35.5 1.3 fusion.60
  36.8 1.9 fusion.53
  38.7 1.2 reduce-precision_convert_fusion.3
  39.9 0.8 pad_maximum_fusion.10.v0_ref
  40.7 0.8 pad_maximum_fusion.11.v2_ref
  41.9 1.3 pad_maximum_fusion.3.v1_ref
  43.2 0.8 pad_maximum_fusion.9.ab_ref
  44.0 0.9 fusion.10
  44.9 0.7 copy.37
  45.6 0.8 copy.38
  46.7 0.7 fusion.130
  47.3 6.6 %fusion.97 = (f32[128]{0:T(128)S(1)}, f32[128]{0:T(128)S(1)}, f32[128]{0:T(128)S(1)}, f32[128]{0:T(128)S(1)}, f32[128]{0:T(128)S(1)}, /*index=5*/f32[128]{0:T(12...) fusion(s32[128]{0:T(128)S(1)} %iota.7, ...), kind=kLoop, calls=%fused_computation.314 | loop fusion | flops 17920 | bytes 10792 | tf_op jit(solution)/shard_map/cos | solution.py:46
  54.7 1.1 fusion.96
  56.3 0.2 maximum_bitcast_fusion.2
  56.7 2.0 pad_maximum_fusion.a_ref
  58.7 8.1 %spectra.3 = f32[4,2,2,1,256,128]{5,4,3,2,1,0:T(8,128)} custom-call(s32[2,4]{1,0:T(2,128)} %copy-done.12, f32[4,2,256,256]{3,2,1,0:T(8,128)} %shard_map.41.x_ref, bf16[2,4,256,768]{3,2,1,0:T(8,128)(2,1)} %pad_maximum_fusion.a_ref), custom_call_target="tpu_custom_call" | custom-call | flops 800000000 | bytes 6000000 | tf_op jit(solution)/shard_map/spectra/pallas_call | solution.py:249
  66.8 1.3 copy-done
  68.1 5.3 %all-to-all-start.1 = ((f32[4,2,256,768]{3,2,1,0:T(8,128)}), f32[4,2,256,768]{3,2,1,0:T(8,128)}, u32[]{:S(2)}, u32[]{:S(2)}) async-start(f32[4,2,256,768]{3,2,1,0:T(8,128)} %shard_map.42.x_ref), calls=%async_computation.1 | async-start | bytes 12582912 | tf_op jit(solution)/shard_map/all_to_all | solution.py:476
  73.4 1.2 slice_bitcast_fusion.10
  74.7 0.8 pad_maximum_fusion.4
  75.5 1.9 collective-permute-start.4
  77.5 2.7 collective-permute-start.5
  80.2 0.8 pad_maximum_fusion.8.a_ref
  81.0 0.8 pad_maximum_fusion.7.a_ref
  81.8 0.7 fusion.28
  82.5 11.8 %spectra.2 = f32[4,2,2,3,256,128]{5,4,3,2,1,0:T(8,128)} custom-call(s32[2,4]{1,0:T(2,128)} %copy-done.12, f32[4,2,256,768]{3,2,1,0:T(8,128)} %shard_map.42.x_ref, bf16[2,4,256,768]{3,2,1,0:T(8,128)(2,1)} %pad_maximum_fusion.a_ref), custom_call_target="tpu_custom_call" | custom-call | flops 2400000000 | bytes 18000000 | tf_op jit(solution)/shard_map/spectra/pallas_call | solution.py:249
  94.3 1.9 slice_bitcast_fusion
  96.2 2.4 collective-permute-start.6
  98.5 2.5 slice_bitcast_fusion.6
  101.2 2.1 collective-permute-start.3
  103.3 2.4 collective-permute-done.5
  105.7 1.0 slice_dynamic-update-slice_fusion.3
  106.7 1.0 slice_dynamic-update-slice_fusion.2
  107.7 1.0 slice_dynamic-update-slice_fusion
  108.7 1.4 copy-done.4
  110.1 58.5 %collective-permute-done.3 = f32[2,2,3,256,128]{4,3,2,1,0:T(8,128)S(1)} collective-permute-done((f32[2,2,3,256,128]{4,3,2,1,0:T(8,128)S(1)}, f32[2,2,3,256,128]{4,3,2,1,0:T(8,128)S(1)}, u32[]{:S(2)}, u32[]{:S(2)}) %collective-permute-start.3) | collective-permute-done | bytes 1572896 | tf_op jit(solution)/shard_map/ppermute | solution.py:462
  168.7 2.0 maximum_bitcast_fusion
  170.6 2.0 maximum_bitcast_fusion.1
  172.6 40.7 %all_to_all.33.far_ref = f32[4,1,2,3,256,128]{5,4,3,2,1,0:T(8,128)} all-to-all(f32[4,1,2,3,256,128]{5,4,3,2,1,0:T(8,128)} %bitcast.88), channel_id=1, replica_groups=mesh['tile'=32,'slab'=4] {'slab'}, dimensions={0} | all-to-all | bytes 6291456 | tf_op jit(solution)/shard_map/all_to_all | solution.py:479
  213.3 6.1 %all-to-all-start.3 = ((f32[4,1,2,3,256,128]{5,4,3,2,1,0:T(8,128)}), f32[4,1,2,3,256,128]{5,4,3,2,1,0:T(8,128)}, u32[]{:S(2)}, u32[]{:S(2)}) async-start(f32[4,1,2,3,256,128]{5,4,3,2,1,0:T(8,128)} %maximum_bitcast_fusion.1), calls=%async_computation.3 | async-start | bytes 6291456 | tf_op jit(solution)/shard_map/all_to_all | solution.py:479
  219.4 1.3 pad_add_fusion.1.ints_ref
  220.7 16.2 %shard_map.43 = (f32[8,128,512]{2,1,0:T(8,128)}, f32[8,128,256]{2,1,0:T(8,128)}) custom-call(s32[2]{0:T(128)} %pad_add_fusion.1.ints_ref, f32[8,256,768]{2,1,0:T(8,128)} %bitcast.3.y_ref, f32[4,1,2,3,256,128]{5,4,3,2,1,0:T(8,128)} %all_to_all.33.far_ref, bf16[256,768]{1,0:T(8,128)(2,1)} %pad_maximum_fusion.7.a_ref, ...), custom_call_target="tpu_custom_call" | custom-call | flops 6000000000 | bytes 16000000 | tf_op jit(solution)/shard_map/pallas_call | solution.py:397
  236.9 19.2 %all-to-all-done.3.far_ref = f32[4,1,2,3,256,128]{5,4,3,2,1,0:T(8,128)} async-done(((f32[4,1,2,3,256,128]{5,4,3,2,1,0:T(8,128)}), f32[4,1,2,3,256,128]{5,4,3,2,1,0:T(8,128)}, u32[]{:S(2)}, u32[]{:S(2)}) %all-to-all-start.3) | async-done | bytes 3145760 | tf_op jit(solution)/shard_map/all_to_all | solution.py:479
  256.1 5.0 %all-to-all-start.4 = ((f32[4,2,2,1,256,128]{5,4,3,2,1,0:T(8,128)}), f32[4,2,2,1,256,128]{5,4,3,2,1,0:T(8,128)S(1)}, u32[]{:S(2)}, u32[]{:S(2)}) async-start(f32[4,2,2,1,256,128]{5,4,3,2,1,0:T(8,128)} %bitcast.92), calls=%async_computation.4 | async-start | bytes 4194304 | tf_op jit(solution)/shard_map/all_to_all | solution.py:479
  261.2 1.3 pad_add_fusion.ints_ref
  262.5 16.2 %shard_map.44 = (f32[8,128,512]{2,1,0:T(8,128)}, f32[8,128,256]{2,1,0:T(8,128)}) custom-call(s32[2]{0:T(128)} %pad_add_fusion.ints_ref, f32[8,256,768]{2,1,0:T(8,128)} %bitcast.3.y_ref, f32[4,1,2,3,256,128]{5,4,3,2,1,0:T(8,128)} %all-to-all-done.3.far_ref, bf16[256,768]{1,0:T(8,128)(2,1)} %pad_maximum_fusion.8.a_ref, ...), custom_call_target="tpu_custom_call" | custom-call | flops 6000000000 | bytes 16000000 | tf_op jit(solution)/shard_map/pallas_call | solution.py:397
  278.7 8.4 %all-to-all-done.4.far_ref = f32[4,2,2,1,256,128]{5,4,3,2,1,0:T(8,128)S(1)} async-done(((f32[4,2,2,1,256,128]{5,4,3,2,1,0:T(8,128)}), f32[4,2,2,1,256,128]{5,4,3,2,1,0:T(8,128)S(1)}, u32[]{:S(2)}, u32[]{:S(2)}) %all-to-all-start.4) | async-done | bytes 2097184 | tf_op jit(solution)/shard_map/all_to_all | solution.py:479
  287.2 1.4 copy-done.1
  288.6 7.7 %shard_map.45 = (f32[2,1,128,1024]{3,2,1,0:T(8,128)}, f32[2,8,128]{2,1,0:T(8,128)}) custom-call(s32[2]{0:T(128)} %pad_add_fusion.1.ints_ref, f32[8,256,256]{2,1,0:T(8,128)} %bitcast.86, f32[4,2,2,1,256,128]{5,4,3,2,1,0:T(8,128)} %copy-done.1, bf16[256,768]{1,0:T(8,128)(2,1)} %pad_maximum_fusion.7.a_ref, bf16[256,768]{1,0:T(8,128)(2,1)} %pad_maximum_fusion.9.ab_ref, ...), custom_call_target="tpu_custom_call" | custom-call | flops 2000000000 | bytes 10000000 | tf_op jit(solution)/shard_map/pallas_call | solution.py:439
  296.2 7.6 %shard_map.46 = (f32[2,1,128,1024]{3,2,1,0:T(8,128)}, f32[2,8,128]{2,1,0:T(8,128)}) custom-call(s32[2]{0:T(128)} %pad_add_fusion.ints_ref, f32[8,256,256]{2,1,0:T(8,128)} %bitcast.87, f32[4,2,2,1,256,128]{5,4,3,2,1,0:T(8,128)} %copy-done.1, bf16[256,768]{1,0:T(8,128)(2,1)} %pad_maximum_fusion.8.a_ref, ...), custom_call_target="tpu_custom_call", output_to_operand_aliasing={{0}: (8, {}), {1}: (9, {})} | custom-call | flops 2000000000 | bytes 10000000 | tf_op jit(solution)/shard_map/pallas_call | solution.py:439
  303.9 1.3 slice_reduce_fusion
  (91 shorter events, 3.1 us)
Async XLA Ops:
  10.9 1.5 copy-start.13
  22.5 22.3 %collective-permute-start = (s32[2]{0:T(128)S(1)}, s32[2]{0:T(128)}, u32[]{:S(2)}, u32[]{:S(2)}) collective-permute-start(s32[2]{0:T(128)S(1)} %slice_reduce_fusion.1), channel_id=1, source_target_pairs={{1,0},{2,1},{3,2},{0,3},{5,4},{6,5},{7,6},{4,7},{9,8},{10,9},{11,1... | collective-permute-start | bytes 32 | tf_op jit(solution)/shard_map/ppermute | solution.py:487
  22.6 23.0 %collective-permute-start.1 = (s32[2]{0:T(128)S(1)}, s32[2]{0:T(128)}, u32[]{:S(2)}, u32[]{:S(2)}) collective-permute-start(s32[2]{0:T(128)S(1)} %slice_reduce_fusion.1), channel_id=1, source_target_pairs={{2,0},{3,1},{0,2},{1,3},{6,4},{7,5},{4,6},{5,7},{10,8},{11,9},{8,1... | collective-permute-start | bytes 32 | tf_op jit(solution)/shard_map/ppermute | solution.py:487
  25.9 20.5 %collective-permute-start.2 = (s32[2]{0:T(128)S(1)}, s32[2]{0:T(128)S(1)}, u32[]{:S(2)}, u32[]{:S(2)}) collective-permute-start(s32[2]{0:T(128)S(1)} %slice_reduce_fusion.1), channel_id=1, source_target_pairs={{3,0},{0,1},{1,2},{2,3},{7,4},{4,5},{5,6},{6,7},{11,8},{8,9},{9,10... | collective-permute-start | bytes 32 | tf_op jit(solution)/shard_map/ppermute | solution.py:487
  28.1 38.6 %all-to-all-start = ((f32[4,2,256,256]{3,2,1,0:T(8,128)}), f32[4,2,256,256]{3,2,1,0:T(8,128)S(1)}, u32[]{:S(2)}, u32[]{:S(2)}) async-start(f32[4,2,256,256]{3,2,1,0:T(8,128)} %shard_map.41.x_ref), calls=%async_computation | async-start | bytes 4194304 | tf_op jit(solution)/shard_map/all_to_all | solution.py:476
  41.9 2.1 copy-start.5
  41.9 2.1 copy-start.6
  41.9 2.1 copy-start.7
  46.7 9.2 %copy-start.12 = (s32[2,4]{1,0:T(2,128)}, s32[2,4]{1,0:T(2,128)S(1)}, u32[]{:S(2)}) copy-start(s32[2,4]{1,0:T(2,128)S(1)} %constant_dynamic-slice_fusion.off_ref) | copy-start | bytes 100
  66.8 1.3 copy-start
  68.1 104.5 %all-to-all-start.1 = ((f32[4,2,256,768]{3,2,1,0:T(8,128)}), f32[4,2,256,768]{3,2,1,0:T(8,128)}, u32[]{:S(2)}, u32[]{:S(2)}) async-start(f32[4,2,256,768]{3,2,1,0:T(8,128)} %shard_map.42.x_ref), calls=%async_computation.1 | async-start | bytes 12582912 | tf_op jit(solution)/shard_map/all_to_all | solution.py:476
  73.4 4.0 %copy-start.2 = (f32[4,2,2,1,256,128]{5,4,3,2,1,0:T(8,128)S(1)}, f32[4,2,2,1,256,128]{5,4,3,2,1,0:T(8,128)}, u32[]{:S(2)}) copy-start(f32[4,2,2,1,256,128]{5,4,3,2,1,0:T(8,128)} %spectra.3) | copy-start | bytes 6291460
  73.4 6.7 %copy-start.9 = (f32[128,128]{1,0:T(8,128)S(1)}, f32[128,128]{1,0:T(8,128)}, u32[]{:S(2)}) copy-start(f32[128,128]{1,0:T(8,128)} %get-tuple-element.74) | copy-start | bytes 196612
  73.4 6.7 %copy-start.10 = (f32[128,128]{1,0:T(8,128)S(1)}, f32[128,128]{1,0:T(8,128)}, u32[]{:S(2)}) copy-start(f32[128,128]{1,0:T(8,128)} %get-tuple-element.75) | copy-start | bytes 196612
  73.4 6.7 %copy-start.11 = (f32[128,128]{1,0:T(8,128)S(1)}, f32[128,128]{1,0:T(8,128)}, u32[]{:S(2)}) copy-start(f32[128,128]{1,0:T(8,128)} %get-tuple-element.169) | copy-start | bytes 196612
  73.4 6.8 %copy-start.8 = (f32[128,128]{1,0:T(8,128)S(1)}, f32[128,128]{1,0:T(8,128)}, u32[]{:S(2)}) copy-start(f32[128,128]{1,0:T(8,128)} %get-tuple-element.181) | copy-start | bytes 196612
  75.5 27.7 %collective-permute-start.4 = (f32[2,2,1,256,128]{4,3,1,2,0:T(8,128)}, f32[2,2,1,256,128]{4,3,1,2,0:T(8,128)S(1)}, u32[]{:S(2)}, u32[]{:S(2)}) collective-permute-start(f32[2,2,1,256,128]{4,3,1,2,0:T(8,128)} %pad_maximum_fusion.4), channel_id=1, source_target_pairs={{4,0},{8,4},{12,8},{16,12},{20,16},{24,20},{28,24},{32,28},{36,32}... | collective-permute-start | bytes 1572872 | tf_op jit(solution)/shard_map/ppermute | solution.py:462
  77.5 28.3 %collective-permute-start.5 = (f32[3,2,1,256,128]{4,3,1,2,0:T(8,128)S(1)}, f32[3,2,1,256,128]{4,3,1,2,0:T(8,128)}, u32[]{:S(2)}, u32[]{:S(2)}) collective-permute-start(f32[3,2,1,256,128]{4,3,1,2,0:T(8,128)S(1)} %slice_bitcast_fusion.1), channel_id=1, source_target_pairs={{8,0},{12,4},{16,8},{20,12},{24,16},{28,20},{32,24},{36,28},{40,32... | collective-permute-start | bytes 2359304 | tf_op jit(solution)/shard_map/ppermute | solution.py:462
  96.2 74.5 %collective-permute-start.6 = (f32[3,2,3,256,128]{4,3,2,1,0:T(8,128)S(1)}, f32[3,2,3,256,128]{4,3,2,1,0:T(8,128)S(1)}, u32[]{:S(2)}, u32[]{:S(2)}) collective-permute-start(f32[3,2,3,256,128]{4,3,2,1,0:T(8,128)S(1)} %slice_bitcast_fusion), channel_id=1, source_target_pairs={{8,0},{12,4},{16,8},{20,12},{24,16},{28,20},{32,24},{36,28},{40,32... | collective-permute-start | bytes 7077896 | tf_op jit(solution)/shard_map/ppermute | solution.py:462
  101.0 2.2 copy-start.3
  101.2 67.4 %collective-permute-start.3 = (f32[2,2,3,256,128]{4,3,2,1,0:T(8,128)S(1)}, f32[2,2,3,256,128]{4,3,2,1,0:T(8,128)S(1)}, u32[]{:S(2)}, u32[]{:S(2)}) collective-permute-start(f32[2,2,3,256,128]{4,3,2,1,0:T(8,128)S(1)} %pad_maximum_fusion.2), channel_id=1, source_target_pairs={{4,0},{8,4},{12,8},{16,12},{20,16},{24,20},{28,24},{32,28},{36,32}... | collective-permute-start | bytes 4718600 | tf_op jit(solution)/shard_map/ppermute | solution.py:462
  108.7 1.4 copy-start.4
  213.3 42.8 %all-to-all-start.3 = ((f32[4,1,2,3,256,128]{5,4,3,2,1,0:T(8,128)}), f32[4,1,2,3,256,128]{5,4,3,2,1,0:T(8,128)}, u32[]{:S(2)}, u32[]{:S(2)}) async-start(f32[4,1,2,3,256,128]{5,4,3,2,1,0:T(8,128)} %maximum_bitcast_fusion.1), calls=%async_computation.3 | async-start | bytes 6291456 | tf_op jit(solution)/shard_map/all_to_all | solution.py:479
  256.1 31.1 %all-to-all-start.4 = ((f32[4,2,2,1,256,128]{5,4,3,2,1,0:T(8,128)}), f32[4,2,2,1,256,128]{5,4,3,2,1,0:T(8,128)S(1)}, u32[]{:S(2)}, u32[]{:S(2)}) async-start(f32[4,2,2,1,256,128]{5,4,3,2,1,0:T(8,128)} %bitcast.92), calls=%async_computation.4 | async-start | bytes 4194304 | tf_op jit(solution)/shard_map/all_to_all | solution.py:479
  287.2 1.4 copy-start.1

commit v5 on v4

--- a/solution.py
+++ b/solution.py
@@ -46,8 +46,11 @@
     return jnp.cos(angle), jnp.sin(angle)
 
 
+SEEDS = []
+
+
 def iota(length):
-    return lax.optimization_barrier(jnp.arange(length, dtype=jnp.int32))
+    return lax.optimization_barrier((jnp.arange(length, dtype=jnp.int32), *SEEDS))[0]
 
 
 def odd_table():
@@ -480,42 +483,40 @@
 
     small_src = along(small_kernel, stored, (twos_table(),), 256)
     small_all = gather(small_src)
-    small_src, table = after(small_src, odd_table())
-    large_src = along(large_kernel, stored, (table, fours_table()), 768)
-    large_src, mine = after(large_src, offsets[:, 1, 0])
-    turns = [mine] + [
-        lax.ppermute(mine, "slab", [((i + k) % slabs, i) for i in range(slabs)]) for k in range(1, slabs)
-    ]
+    mine = offsets[:, 1, 0]
+    turns = [mine] + [lax.ppermute(mine, "slab", [((i + k) % slabs, i) for i in range(slabs)]) for k in range(1, slabs)]
+    large_src = along(large_kernel, stored, (odd_table(), fours_table()), 768)
     base = lax.optimization_barrier(across_base())
     given = jnp.roll(jnp.stack(turns, axis=1), lax.axis_index("slab"), axis=1)
     mats = jnp.stack([jnp.stack([across_forward(given[r, j], base) for j in range(slabs)]) for r in range(ROUNDS)])
-    small_all, large_src = after(small_all, large_src)
-    large_all = gather(large_src)
-
-    def shifted(src):
-        made = spectra(src, given, mats)
+    small_all, band_src = after(small_all, large_src)
+    large_all = gather(band_src)
+
+    def shifted(made):
         near = from_next(jnp.stack((made[3, 0], made[0, 1])), 1, groups)
         far = from_next(made[1:, 1], 2, groups)
         zero = [made[0, 0], made[1, 0], made[2, 0], near[0]]
         one = [near[1], far[0], far[1], far[2]]
         return zero, one
 
-    large_zero, large_one = [jnp.stack(x)[:, None] for x in shifted(large_src)]
-    both = zip(*shifted(small_src), strict=True)
+    large_made = spectra(large_src, given, mats)
+    large_zero, large_one = [jnp.stack(x)[:, None] for x in shifted(large_made)]
+    small_made = spectra(small_src, given, mats)
+    both = zip(*shifted(small_made), strict=True)
     small_sent = jnp.stack([x for two in both for x in two]).reshape(slabs, ROUNDS, 2, 1, 256, 128)
     valid = (
         jnp.logical_and(place % GC != GC - 1, place + 1 < size),
         place + GC < size,
     )
+    SEEDS.append(small_made)
     own = [offsets[r, 0, 0] for r in range(ROUNDS)]
     ints = [jnp.stack((own[r], valid[r].astype(jnp.int32))) for r in range(ROUNDS)]
     own_mats = [across_forward(o, base) for o in own]
     ab = across_back()
     edges = edge_tables()
     back1, back0, back2 = odd_back(), fours_back(), twos_back()
-    large_all, large_zero, small_sent, large_one, own_mats, ab, edges, back1, back0, back2 = after(
-        large_all, large_zero, small_sent, large_one, own_mats, ab, edges, back1, back0, back2
-    )
+    SEEDS.clear()
+    large_all, large_zero = after(large_all, large_zero)
     far_zero = collect(large_zero)
     far_zero, large_one = after(far_zero, large_one)
     far_one = collect(large_one)

time: 309 us -> 259 us (0.84)
  blocking collectives: 40.7 us -> 0 us
  waiting for transfers between devices: 88.6 us -> 65.5 us
  local copies, waits for them, and re-layouts: 18.6 us -> 25.9 us
  starting transfers between devices: 34.7 us -> 38.5 us
    all_to_all x1 -> x0, blocking collectives: 40.7 us -> none  [collect(): return lax.all_to_all(x, 'slab', split_axis=0, concat_axis=0, tiled=True)]
    all_to_all x2 -> x3, waiting for transfers between devices: 27.7 us -> 15.6 us  [collect(): return lax.all_to_all(x, 'slab', split_axis=0, concat_axis=0, tiled=True)]
    ppermute x4, waiting for transfers between devices: 60.9 us -> 49.8 us  [from_next(): lax.ppermute(x, 'tile', [(g + step, g) for g in range(groups - step)])]
    unnamed x35 -> x31, local copies, waits for them, and re-layouts: 6.87 us -> 11.8 us
    all_to_all x2 -> x3, starting transfers between devices: 11.1 us -> 14.6 us  [collect(): return lax.all_to_all(x, 'slab', split_axis=0, concat_axis=0, tiled=True)]
    cos x5 -> x6, other arithmetic: 13.9 us -> 13.1 us  [trig(): return (jnp.cos(angle), jnp.sin(angle))]
  transfers between devices with their start and end apart: 11 -> 12, of which waited for: 4 -> 4; matrix products, arithmetic and copies ran while one was open for 15% -> 24% of each run, Pallas kernels for 17% -> 26%
where the time goes in v5:
time: 259 us; the launch traced here: 255 us
  Pallas kernels  82.8 us (32%)
  waiting for transfers between devices  65.5 us (25%)
  other arithmetic  41.4 us (16%)
  starting transfers between devices  38.5 us (15%)
  local copies, waits for them, and re-layouts  25.9 us (10%)
    ppermute x4, waiting for transfers between devices, from_next(): lax.ppermute(x, 'tile', [(g + step, g) for g in range(groups - step)])  49.8 us
    pallas_call x2, Pallas kernels, large_pair(): pl.pallas_call(large_pair_kernel, out_shape=(jax.ShapeDtypeStruct((Z, A,...  32.5 us
    pallas_call x2, Pallas kernels, spectra(): pl.pallas_call(functools.partial(send_kernel, blocks), out_shape=jax.Shap...  19.9 us
    all_to_all x3, waiting for transfers between devices, collect(): return lax.all_to_all(x, 'slab', split_axis=0, concat_axis=0, tiled=True)  15.6 us
    pallas_call x2, Pallas kernels, small_pair(): pl.pallas_call(small_pair_kernel, out_shape=(jax.ShapeDtypeStruct((ROUNDS...  15.3 us
    pallas_call x2, Pallas kernels, along(): pl.pallas_call(kernel, out_shape=jax.ShapeDtypeStruct((tiles, planes, 256...  15.1 us
    all_to_all x3, starting transfers between devices, collect(): return lax.all_to_all(x, 'slab', split_axis=0, concat_axis=0, tiled=True)  14.6 us
    cos x6, other arithmetic, trig(): return (jnp.cos(angle), jnp.sin(angle))  13.1 us
  transfers between devices with their start and end apart: 12, of which 4 were waited for; matrix products, arithmetic and copies ran while one was open for 24% of the time, Pallas kernels for 26%

profile of v5, /device:TPU:56, one launch (start us, length us, event | category | flops | bytes accessed | tf_op | source)
XLA Modules:
  0.0 255.2 jit_solution(17340920484924370629)
XLA Ops:
  0.6 0.9 slice_reduce_fusion.1
  1.7 3.3 %collective-permute-start.1 = (s32[2]{0:T(128)S(1)}, s32[2]{0:T(128)S(1)}, u32[]{:S(2)}, u32[]{:S(2)}) collective-permute-start(s32[2]{0:T(128)S(1)} %get-tuple-element.204), channel_id=1, source_target_pairs={{2,0},{3,1},{0,2},{1,3},{6,4},{7,5},{4,6},{5,7},{10,8},{11,9},{8,1... | collective-permute-start | bytes 32 | tf_op jit(solution)/shard_map/ppermute | solution.py:487
  4.9 2.2 collective-permute-start.2
  7.2 1.1 fusion.57
  8.4 0.8 pad_maximum_fusion.5.w2_ref
  9.2 5.9 %shard_map.41.x_ref = f32[4,2,256,256]{3,2,1,0:T(8,128)} custom-call(f32[4,2,256,1024]{3,2,1,0:T(8,128)} %x_ref.3, bf16[768,256]{1,0:T(8,128)(2,1)} %pad_maximum_fusion.5.w2_ref), custom_call_target="tpu_custom_call" | custom-call | flops 1536000000 | bytes 14000000 | tf_op jit(solution)/shard_map/pallas_call | solution.py:211
  15.1 3.7 %all-to-all-start = ((f32[4,2,256,256]{3,2,1,0:T(8,128)}), f32[4,2,256,256]{3,2,1,0:T(8,128)S(1)}, u32[]{:S(2)}, u32[]{:S(2)}) async-start(f32[4,2,256,256]{3,2,1,0:T(8,128)} %shard_map.41.x_ref), calls=%async_computation | async-start | bytes 4194304 | tf_op jit(solution)/shard_map/all_to_all | solution.py:479
  19.8 0.8 pad_maximum_fusion.6.w0_ref
  20.6 2.1 fusion.32
  22.9 1.3 pad_maximum_fusion.1.w1_ref
  24.2 9.2 %shard_map.42.x_ref = f32[4,2,256,768]{3,2,1,0:T(8,128)} custom-call(f32[4,2,256,1024]{3,2,1,0:T(8,128)} %x_ref.3, bf16[1536,512]{1,0:T(8,128)(2,1)} %pad_maximum_fusion.1.w1_ref, bf16[768,256]{1,0:T(8,128)(2,1)} %pad_maximum_fusion.6.w0_ref), custom_call_target="tpu_custom_call" | custom-call | flops 4608000000 | bytes 14000000 | tf_op jit(solution)/shard_map/pallas_call | solution.py:211
  33.4 1.2 pad_add_fusion.1.ints_ref
  35.8 5.3 %fusion.112 = (f32[128]{0:T(128)S(1)}, f32[128]{0:T(128)S(1)}, f32[128]{0:T(128)S(1)}, f32[128]{0:T(128)S(1)}, f32[128]{0:T(128)S(1)}, /*index=5*/f32[128]{0:T(1...) fusion(s32[128]{0:T(128)S(1)} %iota.13, ...), kind=kLoop, calls=%fused_computation.339 | loop fusion | flops 14336 | bytes 8736 | tf_op jit(solution)/shard_map/cos | solution.py:46
  42.3 0.7 reduce-precision_convert_fusion.8
  43.1 1.4 maximum_bitcast_fusion.2
  44.4 1.3 copy-done
  45.8 5.2 %all-to-all-start.1 = ((f32[4,2,256,768]{3,2,1,0:T(8,128)}), f32[4,2,256,768]{3,2,1,0:T(8,128)}, u32[]{:S(2)}, u32[]{:S(2)}) async-start(f32[4,2,256,768]{3,2,1,0:T(8,128)} %shard_map.42.x_ref), calls=%async_computation.1 | async-start | bytes 12582912 | tf_op jit(solution)/shard_map/all_to_all | solution.py:479
  51.0 1.1 maximum_bitcast_fusion.13
  52.5 2.0 pad_maximum_fusion.a_ref
  54.5 8.1 %spectra.3 = f32[4,2,2,1,256,128]{5,4,3,2,1,0:T(8,128)} custom-call(s32[2,4]{1,0:T(2,128)} %copy-done.10, f32[4,2,256,256]{3,2,1,0:T(8,128)} %shard_map.41.x_ref, bf16[2,4,256,768]{3,2,1,0:T(8,128)(2,1)} %pad_maximum_fusion.a_ref), custom_call_target="tpu_custom_call" | custom-call | flops 800000000 | bytes 6000000 | tf_op jit(solution)/shard_map/spectra/pallas_call | solution.py:252
  62.6 1.2 slice_bitcast_fusion.10
  63.8 0.8 pad_maximum_fusion.4
  64.6 1.9 collective-permute-start.5
  66.6 0.9 slice_bitcast_fusion.1
  67.5 2.6 %collective-permute-start.6 = (f32[3,2,1,256,128]{4,3,1,2,0:T(8,128)}, f32[3,2,1,256,128]{4,3,1,2,0:T(8,128)}, u32[]{:S(2)}, u32[]{:S(2)}) collective-permute-start(f32[3,2,1,256,128]{4,3,1,2,0:T(8,128)} %slice_bitcast_fusion.1), channel_id=1, source_target_pairs={{8,0},{12,4},{16,8},{20,12},{24,16},{28,20},{32,24},{36,28},{40,32... | collective-permute-start | bytes 2359304 | tf_op jit(solution)/shard_map/ppermute | solution.py:465
  70.2 1.4 fusion.106
  71.6 11.8 %spectra.2 = f32[4,2,2,3,256,128]{5,4,3,2,1,0:T(8,128)} custom-call(s32[2,4]{1,0:T(2,128)} %copy-done.10, f32[4,2,256,768]{3,2,1,0:T(8,128)} %shard_map.42.x_ref, bf16[2,4,256,768]{3,2,1,0:T(8,128)(2,1)} %pad_maximum_fusion.a_ref), custom_call_target="tpu_custom_call" | custom-call | flops 2400000000 | bytes 18000000 | tf_op jit(solution)/shard_map/spectra/pallas_call | solution.py:252
  83.4 2.5 slice_bitcast_fusion.6
  86.0 2.2 collective-permute-start.3
  88.2 3.3 %slice_bitcast_fusion = f32[3,2,3,256,128]{4,3,2,1,0:T(8,128)} fusion(f32[4,2,2,3,256,128]{5,4,3,2,1,0:T(8,128)} %spectra.2), kind=kLoop, calls=%fused_computation.3 | loop fusion | bytes 4718592 | tf_op jit(solution)/shard_map/squeeze | solution.py:497
  91.6 2.5 collective-permute-start.4
  94.1 1.1 fusion.56
  95.3 1.3 fusion.65
  96.6 0.8 pad_maximum_fusion.9.v0_ref
  97.4 0.8 pad_maximum_fusion.8.ab_ref
  98.2 21.7 %collective-permute-done.3 = f32[2,2,3,256,128]{4,3,2,1,0:T(8,128)S(1)} collective-permute-done((f32[2,2,3,256,128]{4,3,2,1,0:T(8,128)S(1)}, f32[2,2,3,256,128]{4,3,2,1,0:T(8,128)S(1)}, u32[]{:S(2)}, u32[]{:S(2)}) %collective-permute-start.3) | collective-permute-done | bytes 1572896 | tf_op jit(solution)/shard_map/ppermute | solution.py:465
  120.0 2.0 maximum_bitcast_fusion
  122.0 4.7 %all-to-all-start.2 = ((f32[4,1,2,3,256,128]{5,4,3,2,1,0:T(8,128)}), f32[4,1,2,3,256,128]{5,4,3,2,1,0:T(8,128)}, u32[]{:S(2)}, u32[]{:S(2)}) async-start(f32[4,1,2,3,256,128]{5,4,3,2,1,0:T(8,128)} %bitcast.88), calls=%async_computation.2 | async-start | bytes 6291456 | tf_op jit(solution)/shard_map/all_to_all | solution.py:482
  126.7 2.1 fusion.30
  129.2 1.4 pad_maximum_fusion.3.v1_ref
  132.0 0.8 fusion.105
  132.8 28.2 %collective-permute-done.4 = f32[3,2,3,256,128]{4,3,2,1,0:T(8,128)} collective-permute-done((f32[3,2,3,256,128]{4,3,2,1,0:T(8,128)}, f32[3,2,3,256,128]{4,3,2,1,0:T(8,128)}, u32[]{:S(2)}, u32[]{:S(2)}) %collective-permute-start.4) | collective-permute-done | bytes 2359328 | tf_op jit(solution)/shard_map/ppermute | solution.py:465
  161.0 3.6 %maximum_bitcast_fusion.1 = f32[4,1,2,3,256,128]{5,4,3,2,1,0:T(8,128)} fusion(f32[3,2,3,256,128]{4,3,2,1,0:T(8,128)} %collective-permute-done.4, f32[1,2,3,256,128]{4,3,2,1,0:T(8,128)S(1)} %get-tuple-element.95), kind=kLoop, calls=%fused_computation.2 | loop fusion | flops 786432 | bytes 6291456 | tf_op jit(solution)/shard_map/broadcast_in_dim | solution.py:503
  164.7 4.8 %all-to-all-start.3 = ((f32[4,1,2,3,256,128]{5,4,3,2,1,0:T(8,128)}), f32[4,1,2,3,256,128]{5,4,3,2,1,0:T(8,128)}, u32[]{:S(2)}, u32[]{:S(2)}) async-start(f32[4,1,2,3,256,128]{5,4,3,2,1,0:T(8,128)} %maximum_bitcast_fusion.1), calls=%async_computation.3 | async-start | bytes 6291456 | tf_op jit(solution)/shard_map/all_to_all | solution.py:482
  169.5 0.8 pad_maximum_fusion.7.a_ref
  170.3 0.9 fusion.10
  171.1 1.7 slice_dynamic-update-slice_fusion.4
  172.8 0.7 fusion.27
  173.6 1.7 slice_dynamic-update-slice_fusion.3
  176.0 1.7 slice_dynamic-update-slice_fusion.2
  177.6 1.7 slice_dynamic-update-slice_fusion.1
  179.3 1.7 slice_dynamic-update-slice_fusion
  181.0 16.2 %shard_map.43 = (f32[8,128,512]{2,1,0:T(8,128)}, f32[8,128,256]{2,1,0:T(8,128)}) custom-call(s32[2]{0:T(128)} %pad_add_fusion.1.ints_ref, f32[8,256,768]{2,1,0:T(8,128)} %bitcast.3.y_ref, f32[4,1,2,3,256,128]{5,4,3,2,1,0:T(8,128)} %all-to-all-done.2.far_ref, bf16[256,768]{1,0:T(8,128)(2,1)} %pad_maximum_fusion.7.a_ref, ...), custom_call_target="tpu_custom_call" | custom-call | flops 6000000000 | bytes 16000000 | tf_op jit(solution)/shard_map/pallas_call | solution.py:400
  197.2 9.7 %all-to-all-done.3.far_ref = f32[4,1,2,3,256,128]{5,4,3,2,1,0:T(8,128)} async-done(((f32[4,1,2,3,256,128]{5,4,3,2,1,0:T(8,128)}), f32[4,1,2,3,256,128]{5,4,3,2,1,0:T(8,128)}, u32[]{:S(2)}, u32[]{:S(2)}) %all-to-all-start.3) | async-done | bytes 3145760 | tf_op jit(solution)/shard_map/all_to_all | solution.py:482
  206.9 5.2 %all-to-all-start.4 = ((f32[4,2,2,1,256,128]{5,4,3,2,1,0:T(8,128)}), f32[4,2,2,1,256,128]{5,4,3,2,1,0:T(8,128)S(1)}, u32[]{:S(2)}, u32[]{:S(2)}) async-start(f32[4,2,2,1,256,128]{5,4,3,2,1,0:T(8,128)} %bitcast.92), calls=%async_computation.4 | async-start | bytes 4194304 | tf_op jit(solution)/shard_map/all_to_all | solution.py:482
  212.0 1.3 pad_add_fusion.ints_ref
  213.4 0.8 pad_maximum_fusion.11.v2_ref
  214.2 0.8 pad_maximum_fusion.10.a_ref
  215.0 16.3 %shard_map.44 = (f32[8,128,512]{2,1,0:T(8,128)}, f32[8,128,256]{2,1,0:T(8,128)}) custom-call(s32[2]{0:T(128)} %pad_add_fusion.ints_ref, f32[8,256,768]{2,1,0:T(8,128)} %bitcast.3.y_ref, f32[4,1,2,3,256,128]{5,4,3,2,1,0:T(8,128)} %all-to-all-done.3.far_ref, bf16[256,768]{1,0:T(8,128)(2,1)} %pad_maximum_fusion.10.a_ref, ...), custom_call_target="tpu_custom_call" | custom-call | flops 6000000000 | bytes 16000000 | tf_op jit(solution)/shard_map/pallas_call | solution.py:400
  231.3 6.0 %all-to-all-done.4.far_ref = f32[4,2,2,1,256,128]{5,4,3,2,1,0:T(8,128)S(1)} async-done(((f32[4,2,2,1,256,128]{5,4,3,2,1,0:T(8,128)}), f32[4,2,2,1,256,128]{5,4,3,2,1,0:T(8,128)S(1)}, u32[]{:S(2)}, u32[]{:S(2)}) %all-to-all-start.4) | async-done | bytes 2097184 | tf_op jit(solution)/shard_map/all_to_all | solution.py:482
  237.3 1.3 copy-done.1
  238.6 7.7 %shard_map.45 = (f32[2,1,128,1024]{3,2,1,0:T(8,128)}, f32[2,8,128]{2,1,0:T(8,128)}) custom-call(s32[2]{0:T(128)} %pad_add_fusion.1.ints_ref, f32[8,256,256]{2,1,0:T(8,128)} %bitcast.86, f32[4,2,2,1,256,128]{5,4,3,2,1,0:T(8,128)} %copy-done.1, bf16[256,768]{1,0:T(8,128)(2,1)} %pad_maximum_fusion.7.a_ref, bf16[256,768]{1,0:T(8,128)(2,1)} %pad_maximum_fusion.8.ab_ref, ...), custom_call_target="tpu_custom_call" | custom-call | flops 2000000000 | bytes 10000000 | tf_op jit(solution)/shard_map/pallas_call | solution.py:442
  246.3 7.6 %shard_map.46 = (f32[2,1,128,1024]{3,2,1,0:T(8,128)}, f32[2,8,128]{2,1,0:T(8,128)}) custom-call(s32[2]{0:T(128)} %pad_add_fusion.ints_ref, f32[8,256,256]{2,1,0:T(8,128)} %bitcast.87, f32[4,2,2,1,256,128]{5,4,3,2,1,0:T(8,128)} %copy-done.1, bf16[256,768]{1,0:T(8,128)(2,1)} %pad_maximum_fusion.10.a_ref, ...), custom_call_target="tpu_custom_call", output_to_operand_aliasing={{0}: (8, {}), {1}: (9, {})} | custom-call | flops 2000000000 | bytes 10000000 | tf_op jit(solution)/shard_map/pallas_call | solution.py:442
  253.9 1.3 slice_reduce_fusion
  (93 shorter events, 7.1 us)
Async XLA Ops:
  1.5 33.2 %collective-permute-start = (s32[2]{0:T(128)S(1)}, s32[2]{0:T(128)S(1)}, u32[]{:S(2)}, u32[]{:S(2)}) collective-permute-start(s32[2]{0:T(128)S(1)} %get-tuple-element.204), channel_id=1, source_target_pairs={{1,0},{2,1},{3,2},{0,3},{5,4},{6,5},{7,6},{4,7},{9,8},{10,9},{11,1... | collective-permute-start | bytes 32 | tf_op jit(solution)/shard_map/ppermute | solution.py:487
  1.7 33.1 %collective-permute-start.1 = (s32[2]{0:T(128)S(1)}, s32[2]{0:T(128)S(1)}, u32[]{:S(2)}, u32[]{:S(2)}) collective-permute-start(s32[2]{0:T(128)S(1)} %get-tuple-element.204), channel_id=1, source_target_pairs={{2,0},{3,1},{0,2},{1,3},{6,4},{7,5},{4,6},{5,7},{10,8},{11,9},{8,1... | collective-permute-start | bytes 32 | tf_op jit(solution)/shard_map/ppermute | solution.py:487
  4.9 29.9 %collective-permute-start.2 = (s32[2]{0:T(128)S(1)}, s32[2]{0:T(128)S(1)}, u32[]{:S(2)}, u32[]{:S(2)}) collective-permute-start(s32[2]{0:T(128)S(1)} %get-tuple-element.204), channel_id=1, source_target_pairs={{3,0},{0,1},{1,2},{2,3},{7,4},{4,5},{5,6},{6,7},{11,8},{8,9},{9,10... | collective-permute-start | bytes 32 | tf_op jit(solution)/shard_map/ppermute | solution.py:487
  15.1 4.1 %copy-start.11 = (s32[2,2,1]{1,2,0:T(1,128)S(1)}, s32[2,2,1]{1,2,0:T(1,128)}, u32[]{:S(2)}) copy-start(s32[2,2,1]{1,2,0:T(1,128)} %param.3) | copy-start | bytes 52
  15.1 29.4 %all-to-all-start = ((f32[4,2,256,256]{3,2,1,0:T(8,128)}), f32[4,2,256,256]{3,2,1,0:T(8,128)S(1)}, u32[]{:S(2)}, u32[]{:S(2)}) async-start(f32[4,2,256,256]{3,2,1,0:T(8,128)} %shard_map.41.x_ref), calls=%async_computation | async-start | bytes 4194304 | tf_op jit(solution)/shard_map/all_to_all | solution.py:479
  35.1 6.9 %copy-start.10 = (s32[2,4]{1,0:T(2,128)}, s32[2,4]{1,0:T(2,128)S(1)}, u32[]{:S(2)}) copy-start(s32[2,4]{1,0:T(2,128)S(1)} %constant_dynamic-slice_fusion.off_ref) | copy-start | bytes 100
  44.4 1.3 copy-start
  45.8 76.2 %all-to-all-start.1 = ((f32[4,2,256,768]{3,2,1,0:T(8,128)}), f32[4,2,256,768]{3,2,1,0:T(8,128)}, u32[]{:S(2)}, u32[]{:S(2)}) async-start(f32[4,2,256,768]{3,2,1,0:T(8,128)} %shard_map.42.x_ref), calls=%async_computation.1 | async-start | bytes 12582912 | tf_op jit(solution)/shard_map/all_to_all | solution.py:479
  51.0 1.5 copy-start.3
  62.6 4.0 %copy-start.2 = (f32[4,2,2,1,256,128]{5,4,3,2,1,0:T(8,128)S(1)}, f32[4,2,2,1,256,128]{5,4,3,2,1,0:T(8,128)}, u32[]{:S(2)}) copy-start(f32[4,2,2,1,256,128]{5,4,3,2,1,0:T(8,128)} %spectra.3) | copy-start | bytes 6291460
  64.6 106.5 %collective-permute-start.5 = (f32[2,2,1,256,128]{4,3,1,2,0:T(8,128)}, f32[2,2,1,256,128]{4,3,1,2,0:T(8,128)}, u32[]{:S(2)}, u32[]{:S(2)}) collective-permute-start(f32[2,2,1,256,128]{4,3,1,2,0:T(8,128)} %pad_maximum_fusion.4), channel_id=1, source_target_pairs={{4,0},{8,4},{12,8},{16,12},{20,16},{24,20},{28,24},{32,28},{36,32}... | collective-permute-start | bytes 1572872 | tf_op jit(solution)/shard_map/ppermute | solution.py:465
  67.5 106.1 %collective-permute-start.6 = (f32[3,2,1,256,128]{4,3,1,2,0:T(8,128)}, f32[3,2,1,256,128]{4,3,1,2,0:T(8,128)}, u32[]{:S(2)}, u32[]{:S(2)}) collective-permute-start(f32[3,2,1,256,128]{4,3,1,2,0:T(8,128)} %slice_bitcast_fusion.1), channel_id=1, source_target_pairs={{8,0},{12,4},{16,8},{20,12},{24,16},{28,20},{32,24},{36,28},{40,32... | collective-permute-start | bytes 2359304 | tf_op jit(solution)/shard_map/ppermute | solution.py:465
  86.0 33.8 %collective-permute-start.3 = (f32[2,2,3,256,128]{4,3,2,1,0:T(8,128)S(1)}, f32[2,2,3,256,128]{4,3,2,1,0:T(8,128)S(1)}, u32[]{:S(2)}, u32[]{:S(2)}) collective-permute-start(f32[2,2,3,256,128]{4,3,2,1,0:T(8,128)S(1)} %pad_maximum_fusion.2), channel_id=1, source_target_pairs={{4,0},{8,4},{12,8},{16,12},{20,16},{24,20},{28,24},{32,28},{36,32}... | collective-permute-start | bytes 4718600 | tf_op jit(solution)/shard_map/ppermute | solution.py:465
  91.6 69.4 %collective-permute-start.4 = (f32[3,2,3,256,128]{4,3,2,1,0:T(8,128)}, f32[3,2,3,256,128]{4,3,2,1,0:T(8,128)}, u32[]{:S(2)}, u32[]{:S(2)}) collective-permute-start(f32[3,2,3,256,128]{4,3,2,1,0:T(8,128)} %slice_bitcast_fusion), channel_id=1, source_target_pairs={{8,0},{12,4},{16,8},{20,12},{24,16},{28,20},{32,24},{36,28},{40,32... | collective-permute-start | bytes 7077896 | tf_op jit(solution)/shard_map/ppermute | solution.py:465
  122.0 42.7 %all-to-all-start.2 = ((f32[4,1,2,3,256,128]{5,4,3,2,1,0:T(8,128)}), f32[4,1,2,3,256,128]{5,4,3,2,1,0:T(8,128)}, u32[]{:S(2)}, u32[]{:S(2)}) async-start(f32[4,1,2,3,256,128]{5,4,3,2,1,0:T(8,128)} %bitcast.88), calls=%async_computation.2 | async-start | bytes 6291456 | tf_op jit(solution)/shard_map/all_to_all | solution.py:482
  164.6 5.6 %copy-start.7 = (f32[128,128]{1,0:T(8,128)S(1)}, f32[128,128]{1,0:T(8,128)}, u32[]{:S(2)}) copy-start(f32[128,128]{1,0:T(8,128)} %get-tuple-element.191) | copy-start | bytes 196612
  164.6 5.6 %copy-start.8 = (f32[128,128]{1,0:T(8,128)S(1)}, f32[128,128]{1,0:T(8,128)}, u32[]{:S(2)}) copy-start(f32[128,128]{1,0:T(8,128)} %get-tuple-element.192) | copy-start | bytes 196612
  164.6 5.6 %copy-start.9 = (f32[128,128]{1,0:T(8,128)S(1)}, f32[128,128]{1,0:T(8,128)}, u32[]{:S(2)}) copy-start(f32[128,128]{1,0:T(8,128)} %get-tuple-element.193) | copy-start | bytes 196612
  164.7 42.2 %all-to-all-start.3 = ((f32[4,1,2,3,256,128]{5,4,3,2,1,0:T(8,128)}), f32[4,1,2,3,256,128]{5,4,3,2,1,0:T(8,128)}, u32[]{:S(2)}, u32[]{:S(2)}) async-start(f32[4,1,2,3,256,128]{5,4,3,2,1,0:T(8,128)} %maximum_bitcast_fusion.1), calls=%async_computation.3 | async-start | bytes 6291456 | tf_op jit(solution)/shard_map/all_to_all | solution.py:482
  206.9 6.5 %copy-start.4 = (f32[128,128]{1,0:T(8,128)S(1)}, f32[128,128]{1,0:T(8,128)}, u32[]{:S(2)}) copy-start(f32[128,128]{1,0:T(8,128)} %get-tuple-element.48) | copy-start | bytes 196612
  206.9 6.5 %copy-start.5 = (f32[128,128]{1,0:T(8,128)S(1)}, f32[128,128]{1,0:T(8,128)}, u32[]{:S(2)}) copy-start(f32[128,128]{1,0:T(8,128)} %get-tuple-element.49) | copy-start | bytes 196612
  206.9 6.5 %copy-start.6 = (f32[128,128]{1,0:T(8,128)S(1)}, f32[128,128]{1,0:T(8,128)}, u32[]{:S(2)}) copy-start(f32[128,128]{1,0:T(8,128)} %get-tuple-element.143) | copy-start | bytes 196612
  206.9 30.4 %all-to-all-start.4 = ((f32[4,2,2,1,256,128]{5,4,3,2,1,0:T(8,128)}), f32[4,2,2,1,256,128]{5,4,3,2,1,0:T(8,128)S(1)}, u32[]{:S(2)}, u32[]{:S(2)}) async-start(f32[4,2,2,1,256,128]{5,4,3,2,1,0:T(8,128)} %bitcast.92), calls=%async_computation.4 | async-start | bytes 4194304 | tf_op jit(solution)/shard_map/all_to_all | solution.py:482
  237.3 1.3 copy-start.1

commit v6 on v5

--- a/solution.py
+++ b/solution.py
@@ -230,10 +230,9 @@
     return dot3_right(table, jnp.concatenate((real, imag), axis=0))
 
 
-def send_kernel(blocks, off_ref, x_ref, a_ref, out_ref):
-    tile = pl.program_id(0)
-    rnd = pl.program_id(1)
-    later = lax.broadcasted_iota(jnp.int32, (A, 256), 0) >= off_ref[rnd, tile]
+def send_kernel(blocks, tile_ref, round_ref, off_ref, x_ref, a_ref, near_ref, far_ref, keep_ref):
+    i = pl.program_id(0)
+    later = lax.broadcasted_iota(jnp.int32, (A, 256), 0) >= off_ref[round_ref[i], tile_ref[i]]
     picked = [
         jnp.where(later, x_ref[0, p, :A, w * 256 : (w + 1) * 256], x_ref[0, p, A:, w * 256 : (w + 1) * 256])
         for p in range(2)
@@ -242,32 +241,55 @@
     real = jnp.concatenate([p[:, :128] for p in picked], axis=1)
     imag = jnp.concatenate([p[:, 128:] for p in picked], axis=1)
     spec = dot3_right(a_ref[0, 0], jnp.concatenate((real, imag), axis=0))
-    for k in range(2 * blocks):
-        out_ref[0, 0, k // blocks, k % blocks] = spec[:, k * 128 : (k + 1) * 128]
+
+    def put(ref):
+        for k in range(2 * blocks):
+            ref[0, k // blocks, k % blocks] = spec[:, k * 128 : (k + 1) * 128]
+
+    @pl.when(i < 2)
+    def _():
+        put(near_ref)
+
+    @pl.when(jnp.logical_and(i >= 2, i < 5))
+    def _():
+        put(far_ref)
+
+    @pl.when(i >= 5)
+    def _():
+        put(keep_ref)
+
+
+SEND_TILE = (0, 3, 0, 1, 2, 1, 2, 3)
+SEND_ROUND = (0, 1, 1, 1, 1, 0, 0, 0)
 
 
 def spectra(x, offs, mats, interpret=False):
-    tiles = x.shape[0]
     blocks = x.shape[3] // 256
+
+    def out(count, first):
+        shape = (2, blocks, 256, 128)
+        return (
+            jax.ShapeDtypeStruct((count, *shape), F32),
+            pl.BlockSpec((1, *shape), lambda i, *_: (jnp.clip(i - first, 0, count - 1), 0, 0, 0, 0)),
+        )
+
+    outs = (out(2, 0), out(3, 2), out(3, 5))
     return pl.pallas_call(
         functools.partial(send_kernel, blocks),
-        out_shape=jax.ShapeDtypeStruct((tiles, ROUNDS, 2, blocks, 256, 128), F32),
+        out_shape=tuple(o[0] for o in outs),
         grid_spec=pltpu.PrefetchScalarGridSpec(
-            num_scalar_prefetch=1,
-            grid=(tiles, ROUNDS),
+            num_scalar_prefetch=3,
+            grid=(8,),
             in_specs=[
-                pl.BlockSpec((1, 2, 256, 256 * blocks), lambda t, r, *_: (t, 0, 0, 0)),
-                pl.BlockSpec((1, 1, 256, 768), lambda t, r, *_: (r, t, 0, 0)),
+                pl.BlockSpec((1, 2, 256, 256 * blocks), lambda i, t, r, o: (t[i], 0, 0, 0)),
+                pl.BlockSpec((1, 1, 256, 768), lambda i, t, r, o: (r[i], t[i], 0, 0)),
             ],
-            out_specs=pl.BlockSpec(
-                (1, 1, 2, blocks, 256, 128),
-                lambda t, r, *_: (lax.rem(t + 3 - 2 * r, tiles), r, 0, 0, 0, 0),
-            ),
+            out_specs=tuple(o[1] for o in outs),
         ),
         cost_estimate=pl.CostEstimate(flops=800_000_000 * blocks, bytes_accessed=6_000_000 * blocks, transcendentals=0),
         interpret=interpret,
         name="spectra",
-    )(offs, x, mats)
+    )(jnp.asarray(SEND_TILE, jnp.int32), jnp.asarray(SEND_ROUND, jnp.int32), offs, x, mats)
 
 
 def normalized(p, q, sign):
@@ -315,9 +337,9 @@
             r_ref[place] = jnp.where(lane == 0, moved, r_ref[place])
 
 
-def pair_core(ints_ref, y_ref, far_ref, a_ref, own_ref, r_ref, valid):
+def pair_core(offset, y_ref, far_ref, a_ref, own_ref, r_ref, valid):
     for half in range(2):
-        own_ref[:, half * 512 : (half + 1) * 512] = across(y_ref, half * 4, 4, ints_ref[0], a_ref[...])
+        own_ref[:, half * 512 : (half + 1) * 512] = across(y_ref, half * 4, 4, offset, a_ref[...])
 
     def own_of(z, rows):
         return own_ref[rows, z * 128 : (z + 1) * 128]
@@ -352,37 +374,40 @@
 
 
 def large_pair_kernel(
-    ints_ref, y_ref, far_ref, a_ref, ab_ref, v1_ref, v0_ref, ef_ref, er_ref, flip_ref,
-    odd_ref, fours_ref, own_ref, r_ref,
+    ints_ref, y_ref, far_ref, a_ref, ab_ref, v1_ref, v0_ref, ef_ref, er_ref, flip_ref, *refs
 ):
+    odd_ref, fours_ref, own_ref, r_ref = refs[-4:]
     step = pl.program_id(0)
     valid = ints_ref[1].astype(F32)
-    own_of, far_of = pair_core(ints_ref, y_ref, far_ref, a_ref, own_ref, r_ref, valid)
+    own_of, far_of = pair_core(ints_ref[0], y_ref, far_ref, a_ref, own_ref, r_ref, valid)
 
     @pl.when(step == 0)
     def _():
         for z, part in parts(ab_ref, r_ref, v1_ref.at[0]):
-            odd_ref[z : z + 2] = part.reshape(2, A, 512)
+            odd_ref[0, z : z + 2] = part.reshape(2, A, 512)
 
     @pl.when(step == 1)
     def _():
         for z, part in parts(ab_ref, r_ref, v1_ref.at[0]):
-            odd_ref[z : z + 2] += part.reshape(2, A, 512)
+            odd_ref[0, z : z + 2] += part.reshape(2, A, 512)
 
     @pl.when(step == 2)
     def _():
         edge_fix(own_of, far_of, r_ref, ef_ref, er_ref, flip_ref, valid)
         for z, part in parts(ab_ref, r_ref, v0_ref):
-            fours_ref[z : z + 2] = part.reshape(2, A, 256)
-
-
-def small_pair_kernel(ints_ref, y_ref, far_ref, a_ref, ab_ref, v2_ref, odd_ref, fours_ref, *refs):
-    surf_ref, peak_ref, own_ref, r_ref = refs[-4:]
-    valid = ints_ref[1].astype(F32)
-    pair_core(ints_ref, y_ref, far_ref, a_ref, own_ref, r_ref, valid)
+            fours_ref[0, z : z + 2] = part.reshape(2, A, 256)
+
+
+def small_pair_kernel(
+    own_off_ref, valid_ref, y_ref, far_ref, a_ref, ab_ref, v2_ref, odd_ref, fours_ref,
+    surf_ref, peak_ref, own_ref, r_ref,
+):
+    rnd = pl.program_id(0)
+    valid = valid_ref[rnd].astype(F32)
+    pair_core(own_off_ref[rnd], y_ref, far_ref, a_ref.at[0], own_ref, r_ref, valid)
     for z, part in parts(ab_ref, r_ref, v2_ref):
-        first = fours_ref[z : z + 2].reshape(2 * A, 256)
-        odd = odd_ref[z : z + 2].reshape(2 * A, 512)
+        first = fours_ref[0, z : z + 2].reshape(2 * A, 256)
+        odd = odd_ref[0, z : z + 2].reshape(2 * A, 512)
         y = jnp.concatenate((first + part, first - part), axis=1)
         x = jnp.concatenate((y + odd, y - odd), axis=1)
         x = jnp.maximum(x[:A], x[A:])
@@ -396,43 +421,18 @@
 SCRATCH = [pltpu.VMEM((256, Z * 128), F32), pltpu.VMEM((256, Z * 128), F32)]
 
 
-def large_pair(ints, y, far, mat, ab, back1, back0, edges, interpret=False):
-    return pl.pallas_call(
-        large_pair_kernel,
-        out_shape=(jax.ShapeDtypeStruct((Z, A, 512), F32), jax.ShapeDtypeStruct((Z, A, 256), F32)),
-        grid_spec=pltpu.PrefetchScalarGridSpec(
-            num_scalar_prefetch=1,
-            grid=(3,),
-            in_specs=[
-                pl.BlockSpec((Z, 256, 256), lambda w, *_: (0, 0, w)),
-                pl.BlockSpec((4, 1, 2, 1, 256, 128), lambda w, *_: (0, 0, 0, w, 0, 0)),
-                whole((256, 768)),
-                whole((256, 768)),
-                pl.BlockSpec((1, 768, 512), lambda w, *_: (jnp.minimum(w, 1), 0, 0)),
-                whole((768, 256)),
-                whole((256, 256)),
-                whole((256, 256)),
-                whole((128, 128)),
-            ],
-            out_specs=(whole((Z, A, 512)), whole((Z, A, 256))),
-            scratch_shapes=SCRATCH,
-        ),
-        cost_estimate=pl.CostEstimate(flops=6_000_000_000, bytes_accessed=16_000_000, transcendentals=500_000),
-        interpret=interpret,
-    )(ints, y, far, mat, ab, back1, back0, *edges)
-
-
-def small_pair(rnd, ints, y, far, mat, ab, back2, odd, fours, before, interpret=False):
-    args = [y, far, mat, ab, back2, odd, fours]
-    pick = rnd if far.shape[1] > 1 else 0
+def large_pair(rnd, ints, y, far, mat, ab, back1, back0, edges, before, interpret=False):
+    args = [y, far, mat, ab, back1, back0, *edges]
     in_specs = [
-        whole((Z, 256, 256)),
-        pl.BlockSpec((4, 1, 2, 1, 256, 128), lambda w, *_: (0, pick, 0, 0, 0, 0)),
+        pl.BlockSpec((Z, 256, 256), lambda w, *_: (0, 0, w)),
+        pl.BlockSpec((4, 1, 2, 1, 256, 128), lambda w, *_: (0, 0, 0, w, 0, 0)),
         whole((256, 768)),
         whole((256, 768)),
+        pl.BlockSpec((1, 768, 512), lambda w, *_: (jnp.minimum(w, 1), 0, 0)),
         whole((768, 256)),
-        whole((Z, A, 512)),
-        whole((Z, A, 256)),
+        whole((256, 256)),
+        whole((256, 256)),
+        whole((128, 128)),
     ]
     aliases = {}
     if before is not None:
@@ -440,25 +440,56 @@
         args += list(before)
         in_specs += [pl.BlockSpec(memory_space=pl.ANY)] * 2
     return pl.pallas_call(
+        large_pair_kernel,
+        out_shape=(
+            jax.ShapeDtypeStruct((ROUNDS, Z, A, 512), F32),
+            jax.ShapeDtypeStruct((ROUNDS, Z, A, 256), F32),
+        ),
+        grid_spec=pltpu.PrefetchScalarGridSpec(
+            num_scalar_prefetch=1,
+            grid=(3,),
+            in_specs=in_specs,
+            out_specs=(
+                pl.BlockSpec((1, Z, A, 512), lambda w, *_: (rnd, 0, 0, 0)),
+                pl.BlockSpec((1, Z, A, 256), lambda w, *_: (rnd, 0, 0, 0)),
+            ),
+            scratch_shapes=SCRATCH,
+        ),
+        input_output_aliases=aliases,
+        cost_estimate=pl.CostEstimate(flops=6_000_000_000, bytes_accessed=16_000_000, transcendentals=500_000),
+        interpret=interpret,
+    )(ints, *args)
+
+
+def small_pair(own, valid, y, far, mats, ab, back2, odd, fours, interpret=False):
+    return pl.pallas_call(
         small_pair_kernel,
         out_shape=(
             jax.ShapeDtypeStruct((ROUNDS, 1, A, L), F32),
             jax.ShapeDtypeStruct((ROUNDS, 8, 128), F32),
         ),
         grid_spec=pltpu.PrefetchScalarGridSpec(
-            num_scalar_prefetch=1,
-            grid=(1,),
-            in_specs=in_specs,
+            num_scalar_prefetch=2,
+            grid=(ROUNDS,),
+            in_specs=[
+                whole((Z, 256, 256)),
+                pl.BlockSpec((4, 1, 2, 1, 256, 128), lambda r, *_: (0, r, 0, 0, 0, 0)),
+                pl.BlockSpec((1, 256, 768), lambda r, *_: (r, 0, 0)),
+                whole((256, 768)),
+                whole((768, 256)),
+                pl.BlockSpec((1, Z, A, 512), lambda r, *_: (r, 0, 0, 0)),
+                pl.BlockSpec((1, Z, A, 256), lambda r, *_: (r, 0, 0, 0)),
+            ],
             out_specs=(
-                pl.BlockSpec((1, 1, A, L), lambda w, *_: (rnd, 0, 0, 0)),
-                pl.BlockSpec((1, 8, 128), lambda w, *_: (rnd, 0, 0)),
+                pl.BlockSpec((1, 1, A, L), lambda r, *_: (r, 0, 0, 0)),
+                pl.BlockSpec((1, 8, 128), lambda r, *_: (r, 0, 0)),
             ),
             scratch_shapes=SCRATCH,
         ),
-        input_output_aliases=aliases,
-        cost_estimate=pl.CostEstimate(flops=2_000_000_000, bytes_accessed=10_000_000, transcendentals=300_000),
+        cost_estimate=pl.CostEstimate(flops=4_000_000_000, bytes_accessed=16_000_000, transcendentals=500_000),
         interpret=interpret,
-    )(ints, *args)
+        name="small_pairs",
+    )(own, valid, y, far, mats, ab, back2, odd, fours)
 
 
 def from_next(x, step, groups):
@@ -488,27 +519,27 @@
     large_src = along(large_kernel, stored, (odd_table(), fours_table()), 768)
     base = lax.optimization_barrier(across_base())
     given = jnp.roll(jnp.stack(turns, axis=1), lax.axis_index("slab"), axis=1)
-    mats = jnp.stack([jnp.stack([across_forward(given[r, j], base) for j in range(slabs)]) for r in range(ROUNDS)])
+    mats = jnp.stack(
+        [jnp.stack([across_forward(given[r, j], base) for j in range(slabs)]) for r in range(ROUNDS)]
+    )
     small_all, band_src = after(small_all, large_src)
     large_all = gather(band_src)
 
     def shifted(made):
-        near = from_next(jnp.stack((made[3, 0], made[0, 1])), 1, groups)
-        far = from_next(made[1:, 1], 2, groups)
-        zero = [made[0, 0], made[1, 0], made[2, 0], near[0]]
-        one = [near[1], far[0], far[1], far[2]]
-        return zero, one
+        near, far, keep = made
+        near = from_next(near, 1, groups)
+        far = from_next(far, 2, groups)
+        return jnp.concatenate((keep, near[:1])), jnp.concatenate((near[1:], far))
 
     large_made = spectra(large_src, given, mats)
-    large_zero, large_one = [jnp.stack(x)[:, None] for x in shifted(large_made)]
+    large_zero, large_one = [x[:, None] for x in shifted(large_made)]
     small_made = spectra(small_src, given, mats)
-    both = zip(*shifted(small_made), strict=True)
-    small_sent = jnp.stack([x for two in both for x in two]).reshape(slabs, ROUNDS, 2, 1, 256, 128)
+    small_sent = jnp.stack(shifted(small_made), axis=1)
     valid = (
         jnp.logical_and(place % GC != GC - 1, place + 1 < size),
         place + GC < size,
     )
-    SEEDS.append(small_made)
+    SEEDS.append(small_made[0])
     own = [offsets[r, 0, 0] for r in range(ROUNDS)]
     ints = [jnp.stack((own[r], valid[r].astype(jnp.int32))) for r in range(ROUNDS)]
     own_mats = [across_forward(o, base) for o in own]
@@ -520,12 +551,21 @@
     far_zero = collect(large_zero)
     far_zero, large_one = after(far_zero, large_one)
     far_one = collect(large_one)
-    first = large_pair(ints[0], large_all, far_zero, own_mats[0], ab, back1, back0, edges)
+    first = large_pair(0, ints[0], large_all, far_zero, own_mats[0], ab, back1, back0, edges, None)
     far_one, first, small_sent = after(far_one, first, small_sent)
     small_far = collect(small_sent)
-    second = large_pair(ints[1], large_all, far_one, own_mats[1], ab, back1, back0, edges)
-    out = small_pair(0, ints[0], small_all, small_far, own_mats[0], ab, back2, *first, None)
-    surface, peak = small_pair(1, ints[1], small_all, small_far, own_mats[1], ab, back2, *second, out)
+    odd, fours = large_pair(1, ints[1], large_all, far_one, own_mats[1], ab, back1, back0, edges, first)
+    surface, peak = small_pair(
+        jnp.stack(own),
+        jnp.stack([v.astype(jnp.int32) for v in valid]),
+        small_all,
+        small_far,
+        jnp.stack(own_mats),
+        ab,
+        back2,
+        odd,
+        fours,
+    )
     return surface, peak[:, 0, :1]
 
 

time: 259 us -> 242 us (0.934)
  local copies, waits for them, and re-layouts: 25.9 us -> 11.3 us
  waiting for transfers between devices: 65.5 us -> 59.1 us
  other arithmetic: 41.4 us -> 47.1 us
  starting transfers between devices: 38.5 us -> 41.6 us
  Pallas kernels: 82.8 us -> 79.8 us
    ppermute x4, waiting for transfers between devices: 49.8 us -> 16.1 us  [from_next(): lax.ppermute(x, 'tile', [(g + step, g) for g in range(groups - step)])]
    all_to_all x2, waiting for transfers between devices: 0.01 us -> 28.8 us  [gather(): return lax.all_to_all(x, 'slab', split_axis=0, concat_axis=1, tiled=True)[0]]
    unnamed x31 -> x28, local copies, waits for them, and re-layouts: 11.8 us -> 4.46 us
    another operation x2 -> x6, other arithmetic: 0.94 us -> 6.46 us  [the longest x3 2.84 us: register(): small_sent = jnp.stack(shifted(small_made), axis=1)]
    another operation x3 -> x0, local copies, waits for them, and re-layouts: 5.36 us -> none  [the longest x1 2.47 us: register(): large_zero, large_one = [jnp.stack(x)[:, None] for x in shifted(large_made)]]
    squeeze x2 -> x0, local copies, waits for them, and re-layouts: 4.28 us -> none  [shifted(): far = from_next(made[1:, 1], 2, groups)]
    pallas_call x2 -> x1, Pallas kernels: 15.3 us -> 11.1 us  [small_pair(): pl.pallas_call(small_pair_kernel, out_shape=(jax.ShapeDtypeStruct((ROUNDS...]
  transfers between devices with their start and end apart: 12 -> 12, of which waited for: 4 -> 6; matrix products, arithmetic and copies ran while one was open for 24% -> 22% of each run, Pallas kernels for 26% -> 29%
where the time goes in v6:
time: 242 us; the launch traced here: 240 us
  Pallas kernels  79.8 us (33%)
  waiting for transfers between devices  59.1 us (24%)
  other arithmetic  47.1 us (19%)
  starting transfers between devices  41.6 us (17%)
  local copies, waits for them, and re-layouts  11.3 us (5%)
    pallas_call x2, Pallas kernels, large_pair(): pl.pallas_call(large_pair_kernel, out_shape=(jax.ShapeDtypeStruct((ROUNDS...  32.6 us
    all_to_all x2, waiting for transfers between devices, gather(): return lax.all_to_all(x, 'slab', split_axis=0, concat_axis=1, tiled=True)[0]  28.8 us
    pallas_call x2, Pallas kernels, spectra(): pl.pallas_call(functools.partial(send_kernel, blocks), out_shape=tuple((o...  21 us
    all_to_all x3, starting transfers between devices, collect(): return lax.all_to_all(x, 'slab', split_axis=0, concat_axis=0, tiled=True)  16.4 us
    ppermute x4, waiting for transfers between devices, from_next(): lax.ppermute(x, 'tile', [(g + step, g) for g in range(groups - step)])  16.1 us
    pallas_call x2, Pallas kernels, along(): pl.pallas_call(kernel, out_shape=jax.ShapeDtypeStruct((tiles, planes, 256...  15.1 us
    cos x6, other arithmetic, trig(): return (jnp.cos(angle), jnp.sin(angle))  14.3 us
    all_to_all x3, waiting for transfers between devices, collect(): return lax.all_to_all(x, 'slab', split_axis=0, concat_axis=0, tiled=True)  14.2 us
  transfers between devices with their start and end apart: 12, of which 6 were waited for; matrix products, arithmetic and copies ran while one was open for 22% of the time, Pallas kernels for 29%

profile of v6, /device:TPU:56, one launch (start us, length us, event | category | flops | bytes accessed | tf_op | source)
XLA Modules:
  0.0 240.0 jit_solution(5247535984964892070)
XLA Ops:
  0.6 0.9 slice_reduce_fusion.1
  1.7 3.3 %collective-permute-start.1 = (s32[2]{0:T(128)S(1)}, s32[2]{0:T(128)S(1)}, u32[]{:S(2)}, u32[]{:S(2)}) collective-permute-start(s32[2]{0:T(128)S(1)} %get-tuple-element.209), channel_id=1, source_target_pairs={{2,0},{3,1},{0,2},{1,3},{6,4},{7,5},{4,6},{5,7},{10,8},{11,9},{8,1... | collective-permute-start | bytes 32 | tf_op jit(solution)/shard_map/ppermute | solution.py:518
  4.9 2.2 collective-permute-start.2
  7.2 1.1 fusion.54
  8.4 0.8 pad_maximum_fusion.5.w2_ref
  9.2 5.9 %shard_map.77.x_ref = f32[4,2,256,256]{3,2,1,0:T(8,128)} custom-call(f32[4,2,256,1024]{3,2,1,0:T(8,128)} %x_ref.3, bf16[768,256]{1,0:T(8,128)(2,1)} %pad_maximum_fusion.5.w2_ref), custom_call_target="tpu_custom_call" | custom-call | flops 1536000000 | bytes 14000000 | tf_op jit(solution)/shard_map/pallas_call | solution.py:211
  15.1 3.6 %all-to-all-start = ((f32[4,2,256,256]{3,2,1,0:T(8,128)}), f32[4,2,256,256]{3,2,1,0:T(8,128)S(1)}, u32[]{:S(2)}, u32[]{:S(2)}) async-start(f32[4,2,256,256]{3,2,1,0:T(8,128)} %shard_map.77.x_ref), calls=%async_computation | async-start | bytes 4194304 | tf_op jit(solution)/shard_map/all_to_all | solution.py:510
  19.1 0.8 pad_maximum_fusion.6.w0_ref
  19.8 2.1 fusion.29
  22.2 1.3 pad_maximum_fusion.2.w1_ref
  23.5 9.2 %shard_map.78.x_ref = f32[4,2,256,768]{3,2,1,0:T(8,128)} custom-call(f32[4,2,256,1024]{3,2,1,0:T(8,128)} %x_ref.3, bf16[1536,512]{1,0:T(8,128)(2,1)} %pad_maximum_fusion.2.w1_ref, bf16[768,256]{1,0:T(8,128)(2,1)} %pad_maximum_fusion.6.w0_ref), custom_call_target="tpu_custom_call" | custom-call | flops 4608000000 | bytes 14000000 | tf_op jit(solution)/shard_map/pallas_call | solution.py:211
  33.2 0.7 fusion.138
  33.8 8.9 %all-to-all-done = f32[4,2,256,256]{3,2,1,0:T(8,128)S(1)} async-done(((f32[4,2,256,256]{3,2,1,0:T(8,128)}), f32[4,2,256,256]{3,2,1,0:T(8,128)S(1)}, u32[]{:S(2)}, u32[]{:S(2)}) %all-to-all-start) | async-done | bytes 2097184 | tf_op jit(solution)/shard_map/all_to_all | solution.py:510
  42.8 1.3 copy-done.4
  44.1 6.7 %all-to-all-start.1 = ((f32[4,2,256,768]{3,2,1,0:T(8,128)}), f32[4,2,256,768]{3,2,1,0:T(8,128)}, u32[]{:S(2)}, u32[]{:S(2)}) async-start(f32[4,2,256,768]{3,2,1,0:T(8,128)} %shard_map.78.x_ref), calls=%async_computation.1 | async-start | bytes 12582912 | tf_op jit(solution)/shard_map/all_to_all | solution.py:510
  50.8 5.2 %fusion.111 = (f32[128]{0:T(128)S(1)}, f32[128]{0:T(128)S(1)}, f32[128]{0:T(128)S(1)}, f32[128]{0:T(128)S(1)}, f32[128]{0:T(128)S(1)}, /*index=5*/f32[128]{0:T(1...) fusion(s32[128]{0:T(128)S(1)} %iota.13, ...), kind=kLoop, calls=%fused_computation.325 | loop fusion | flops 14336 | bytes 8736 | tf_op jit(solution)/shard_map/cos | solution.py:46
  57.7 2.0 pad_maximum_fusion.a_ref
  59.6 12.4 %spectra.2 = (f32[2,2,3,256,128]{4,3,2,1,0:T(8,128)}, f32[3,2,3,256,128]{4,3,2,1,0:T(8,128)}, f32[3,2,3,256,128]{4,3,2,1,0:T(8,128)}) custom-call(s32[8]{0:T(128)} %constant.241.clone.tile_ref, s32[8]{0:T(128)} %constant.242.clone.round_ref, s32[2,4]{1,0:T(2,128)} %copy-done.9, f32[4,2,256,768]{3,2,1,0:T(8,128)} %shard_map.78.x_ref, ...), custom_call_target="tpu_custom_call" | custom-call | flops 2400000000 | bytes 18000000 | tf_op jit(solution)/shard_map/spectra/pallas_call | solution.py:277
  72.1 1.9 collective-permute-start.3
  74.6 1.2 pad_add_fusion.2.ints_ref
  75.8 8.6 %spectra.3 = (f32[2,2,1,256,128]{4,3,2,1,0:T(8,128)}, f32[3,2,1,256,128]{4,3,2,1,0:T(8,128)}, f32[3,2,1,256,128]{4,3,2,1,0:T(8,128)}) custom-call(s32[8]{0:T(128)} %constant.241.clone.tile_ref, s32[8]{0:T(128)} %constant.242.clone.round_ref, s32[2,4]{1,0:T(2,128)} %copy-done.9, f32[4,2,256,256]{3,2,1,0:T(8,128)} %shard_map.77.x_ref, ...), custom_call_target="tpu_custom_call" | custom-call | flops 800000000 | bytes 6000000 | tf_op jit(solution)/shard_map/spectra/pallas_call | solution.py:277
  84.4 2.6 %collective-permute-start.4 = (f32[3,2,3,256,128]{4,3,2,1,0:T(8,128)}, f32[3,2,3,256,128]{4,3,2,1,0:T(8,128)}, u32[]{:S(2)}, u32[]{:S(2)}) collective-permute-start(f32[3,2,3,256,128]{4,3,2,1,0:T(8,128)} %get-tuple-element.36), channel_id=1, source_target_pairs={{8,0},{12,4},{16,8},{20,12},{24,16},{28,20},{32,24},{36,28},{40,32... | collective-permute-start | bytes 7077896 | tf_op jit(solution)/shard_map/ppermute | solution.py:496
  87.1 1.9 fusion.53
  89.0 7.6 %collective-permute-done.3 = f32[2,2,3,256,128]{4,3,2,1,0:T(8,128)S(1)} collective-permute-done((f32[2,2,3,256,128]{4,3,2,1,0:T(8,128)}, f32[2,2,3,256,128]{4,3,2,1,0:T(8,128)S(1)}, u32[]{:S(2)}, u32[]{:S(2)}) %collective-permute-start.3) | collective-permute-done | bytes 1572896 | tf_op jit(solution)/shard_map/ppermute | solution.py:496
  96.5 1.0 fusion.134
  97.5 1.9 maximum_bitcast_fusion
  99.4 19.9 %all-to-all-done.1 = f32[4,2,256,768]{3,2,1,0:T(8,128)} async-done(((f32[4,2,256,768]{3,2,1,0:T(8,128)}), f32[4,2,256,768]{3,2,1,0:T(8,128)}, u32[]{:S(2)}, u32[]{:S(2)}) %all-to-all-start.1) | async-done | bytes 6291488 | tf_op jit(solution)/shard_map/all_to_all | solution.py:510
  119.3 5.1 %all-to-all-start.2 = ((f32[4,1,2,3,256,128]{5,4,3,2,1,0:T(8,128)}), f32[4,1,2,3,256,128]{5,4,3,2,1,0:T(8,128)S(1)}, u32[]{:S(2)}, u32[]{:S(2)}) async-start(f32[4,1,2,3,256,128]{5,4,3,2,1,0:T(8,128)} %maximum_bitcast_fusion), calls=%async_computation.2 | async-start | bytes 6291456 | tf_op jit(solution)/shard_map/all_to_all | solution.py:513
  124.4 1.9 fusion.105
  126.2 0.6 sin.79
  126.8 1.9 collective-permute-start.5
  128.7 2.8 %collective-permute-start.6 = (f32[3,2,1,256,128]{4,3,1,0,2:T(8,128)}, f32[3,2,1,256,128]{4,3,1,0,2:T(8,128)}, u32[]{:S(2)}, u32[]{:S(2)}) collective-permute-start(f32[3,2,1,256,128]{4,3,1,0,2:T(8,128)} %bitcast.64), channel_id=1, source_target_pairs={{8,0},{12,4},{16,8},{20,12},{24,16},{28,20},{32,24},{36,28},{40,32... | collective-permute-start | bytes 2359304 | tf_op jit(solution)/shard_map/ppermute | solution.py:496
  131.6 0.6 fusion.62
  132.2 0.8 reduce-precision_convert_fusion.6
  133.0 0.8 pad_maximum_fusion.9.v0_ref
  133.8 2.1 fusion.27
  136.1 0.8 reduce-precision_convert_fusion.1
  136.9 0.9 fusion.10
  137.8 0.9 maximum_bitcast_fusion.6
  138.7 8.6 %collective-permute-done.4 = f32[3,2,3,256,128]{4,3,2,1,0:T(8,128)} collective-permute-done((f32[3,2,3,256,128]{4,3,2,1,0:T(8,128)}, f32[3,2,3,256,128]{4,3,2,1,0:T(8,128)}, u32[]{:S(2)}, u32[]{:S(2)}) %collective-permute-start.4) | collective-permute-done | bytes 2359328 | tf_op jit(solution)/shard_map/ppermute | solution.py:496
  147.3 3.6 %maximum_bitcast_fusion.1 = f32[4,1,2,3,256,128]{5,4,3,2,1,0:T(8,128)} fusion(f32[3,2,3,256,128]{4,3,2,1,0:T(8,128)} %collective-permute-done.4, f32[1,2,3,256,128]{4,3,2,1,0:T(8,128)S(1)} %copy-done.1), kind=kLoop, calls=%fused_computation.2 | loop fusion | flops 786432 | bytes 6291456 | tf_op jit(solution)/shard_map/broadcast_in_dim | solution.py:535
  151.0 7.3 %all-to-all-done.2.far_ref = f32[4,1,2,3,256,128]{5,4,3,2,1,0:T(8,128)S(1)} async-done(((f32[4,1,2,3,256,128]{5,4,3,2,1,0:T(8,128)}), f32[4,1,2,3,256,128]{5,4,3,2,1,0:T(8,128)S(1)}, u32[]{:S(2)}, u32[]{:S(2)}) %all-to-all-start.2) | async-done | bytes 3145760 | tf_op jit(solution)/shard_map/all_to_all | solution.py:513
  158.2 1.7 copy-done
  159.9 6.1 %all-to-all-start.3 = ((f32[4,1,2,3,256,128]{5,4,3,2,1,0:T(8,128)}), f32[4,1,2,3,256,128]{5,4,3,2,1,0:T(8,128)}, u32[]{:S(2)}, u32[]{:S(2)}) async-start(f32[4,1,2,3,256,128]{5,4,3,2,1,0:T(8,128)} %maximum_bitcast_fusion.1), calls=%async_computation.3 | async-start | bytes 6291456 | tf_op jit(solution)/shard_map/all_to_all | solution.py:513
  166.1 1.8 pad_maximum_fusion.8.ab_ref
  167.9 1.1 maximum_bitcast_fusion.7
  169.2 0.8 fusion.103
  170.0 1.3 pad_maximum_fusion.3.v1_ref
  171.3 0.7 fusion.56.flip_ref
  172.0 1.1 fusion.135
  173.2 1.2 maximum_bitcast_fusion.5
  174.4 1.6 pad_maximum_fusion.1
  176.0 16.2 %shard_map.79 = (f32[2,8,128,512]{3,2,1,0:T(8,128)}, f32[2,8,128,256]{3,2,1,0:T(8,128)}) custom-call(s32[2]{0:T(128)} %pad_add_fusion.2.ints_ref, f32[8,256,768]{2,1,0:T(8,128)} %bitcast.5.y_ref, f32[4,1,2,3,256,128]{5,4,3,2,1,0:T(8,128)} %copy-done, bf16[256,768]{1,0:T(8,128)(2,1)} %get-tuple-element.119.a_ref, bf16[256,768]{1,0:T(8,128)(2,1)} %pad_maximum_fusion.8.ab_ref, ...), custom_call_target="tpu_custom_call" | custom-call | flops 6000000000 | bytes 16000000 | tf_op jit(solution)/shard_map/pallas_call | solution.py:442
  192.2 6.9 %all-to-all-done.3.far_ref = f32[4,1,2,3,256,128]{5,4,3,2,1,0:T(8,128)} async-done(((f32[4,1,2,3,256,128]{5,4,3,2,1,0:T(8,128)}), f32[4,1,2,3,256,128]{5,4,3,2,1,0:T(8,128)}, u32[]{:S(2)}, u32[]{:S(2)}) %all-to-all-start.3) | async-done | bytes 3145760 | tf_op jit(solution)/shard_map/all_to_all | solution.py:513
  199.1 5.2 %all-to-all-start.4 = ((f32[4,2,2,1,256,128]{5,4,3,2,1,0:T(8,128)}), f32[4,2,2,1,256,128]{5,4,3,2,1,0:T(8,128)S(1)}, u32[]{:S(2)}, u32[]{:S(2)}) async-start(f32[4,2,2,1,256,128]{5,4,3,2,1,0:T(8,128)} %pad_maximum_fusion.1), calls=%async_computation.4 | async-start | bytes 4194304 | tf_op jit(solution)/shard_map/all_to_all | solution.py:513
  204.3 1.1 pad_add_fusion.3.ints_ref
  205.4 1.9 pad_add_fusion
  207.4 0.8 pad_maximum_fusion.10
  208.2 0.8 pad_maximum_fusion.11.v2_ref
  208.9 1.0 pad_maximum_fusion.4.a_ref
  209.9 16.3 %shard_map.80 = (f32[2,8,128,512]{3,2,1,0:T(8,128)}, f32[2,8,128,256]{3,2,1,0:T(8,128)}) custom-call(s32[2]{0:T(128)} %pad_add_fusion.3.ints_ref, f32[8,256,768]{2,1,0:T(8,128)} %bitcast.5.y_ref, f32[4,1,2,3,256,128]{5,4,3,2,1,0:T(8,128)} %all-to-all-done.3.far_ref, ...), custom_call_target="tpu_custom_call", output_to_operand_aliasing={{0}: (10, {}), {1}: (11, {})} | custom-call | flops 6000000000 | bytes 16000000 | tf_op jit(solution)/shard_map/pallas_call | solution.py:442
  226.2 1.4 copy-done.5
  227.6 11.1 %small_pairs.1 = (f32[2,1,128,1024]{3,2,1,0:T(8,128)}, f32[2,8,128]{2,1,0:T(8,128)}) custom-call(s32[2]{0:T(128)} %get-tuple-element.256.own_off_ref, s32[2]{0:T(128)} %get-tuple-element.257.valid_ref, f32[8,256,256]{2,1,0:T(8,128)} %bitcast.60, f32[4,2,2,1,256,128]{5,4,3,2,1,0:T(8,128)} %copy-done.5, bf16[2,256,768]{2,1,0:T(8,128)(2,1)} %pad_maximum_fusion.4.a_ref, ...), custom_call_target="tpu_custom_call" | custom-call | flops 4000000000 | bytes 16000000 | tf_op jit(solution)/shard_map/small_pairs/pallas_call | solution.py:465
  238.7 1.3 slice_reduce_fusion
  (88 shorter events, 4.1 us)
Async XLA Ops:
  1.5 31.2 %collective-permute-start = (s32[2]{0:T(128)S(1)}, s32[2]{0:T(128)S(1)}, u32[]{:S(2)}, u32[]{:S(2)}) collective-permute-start(s32[2]{0:T(128)S(1)} %get-tuple-element.209), channel_id=1, source_target_pairs={{1,0},{2,1},{3,2},{0,3},{5,4},{6,5},{7,6},{4,7},{9,8},{10,9},{11,1... | collective-permute-start | bytes 32 | tf_op jit(solution)/shard_map/ppermute | solution.py:518
  1.7 31.1 %collective-permute-start.1 = (s32[2]{0:T(128)S(1)}, s32[2]{0:T(128)S(1)}, u32[]{:S(2)}, u32[]{:S(2)}) collective-permute-start(s32[2]{0:T(128)S(1)} %get-tuple-element.209), channel_id=1, source_target_pairs={{2,0},{3,1},{0,2},{1,3},{6,4},{7,5},{4,6},{5,7},{10,8},{11,9},{8,1... | collective-permute-start | bytes 32 | tf_op jit(solution)/shard_map/ppermute | solution.py:518
  4.9 27.9 %collective-permute-start.2 = (s32[2]{0:T(128)S(1)}, s32[2]{0:T(128)S(1)}, u32[]{:S(2)}, u32[]{:S(2)}) collective-permute-start(s32[2]{0:T(128)S(1)} %get-tuple-element.209), channel_id=1, source_target_pairs={{3,0},{0,1},{1,2},{2,3},{7,4},{4,5},{5,6},{6,7},{11,8},{8,9},{9,10... | collective-permute-start | bytes 32 | tf_op jit(solution)/shard_map/ppermute | solution.py:518
  15.1 27.7 %all-to-all-start = ((f32[4,2,256,256]{3,2,1,0:T(8,128)}), f32[4,2,256,256]{3,2,1,0:T(8,128)S(1)}, u32[]{:S(2)}, u32[]{:S(2)}) async-start(f32[4,2,256,256]{3,2,1,0:T(8,128)} %shard_map.77.x_ref), calls=%async_computation | async-start | bytes 4194304 | tf_op jit(solution)/shard_map/all_to_all | solution.py:510
  33.2 9.6 %copy-start.9 = (s32[2,4]{1,0:T(2,128)}, s32[2,4]{1,0:T(2,128)S(1)}, u32[]{:S(2)}) copy-start(s32[2,4]{1,0:T(2,128)S(1)} %constant_dynamic-slice_fusion.off_ref) | copy-start | bytes 100
  42.8 1.3 copy-start.4
  44.1 75.2 %all-to-all-start.1 = ((f32[4,2,256,768]{3,2,1,0:T(8,128)}), f32[4,2,256,768]{3,2,1,0:T(8,128)}, u32[]{:S(2)}, u32[]{:S(2)}) async-start(f32[4,2,256,768]{3,2,1,0:T(8,128)} %shard_map.78.x_ref), calls=%async_computation.1 | async-start | bytes 12582912 | tf_op jit(solution)/shard_map/all_to_all | solution.py:510
  59.6 14.4 %copy-start.10 = (s32[2,2,1]{1,2,0:T(1,128)S(1)}, s32[2,2,1]{1,2,0:T(1,128)}, u32[]{:S(2)}) copy-start(s32[2,2,1]{1,2,0:T(1,128)} %param.7) | copy-start | bytes 52
  72.1 24.4 %collective-permute-start.3 = (f32[2,2,3,256,128]{4,3,2,1,0:T(8,128)}, f32[2,2,3,256,128]{4,3,2,1,0:T(8,128)S(1)}, u32[]{:S(2)}, u32[]{:S(2)}) collective-permute-start(f32[2,2,3,256,128]{4,3,2,1,0:T(8,128)} %get-tuple-element.34), channel_id=1, source_target_pairs={{4,0},{8,4},{12,8},{16,12},{20,16},{24,20},{28,24},{32,28},{36,32}... | collective-permute-start | bytes 4718600 | tf_op jit(solution)/shard_map/ppermute | solution.py:496
  84.4 62.9 %collective-permute-start.4 = (f32[3,2,3,256,128]{4,3,2,1,0:T(8,128)}, f32[3,2,3,256,128]{4,3,2,1,0:T(8,128)}, u32[]{:S(2)}, u32[]{:S(2)}) collective-permute-start(f32[3,2,3,256,128]{4,3,2,1,0:T(8,128)} %get-tuple-element.36), channel_id=1, source_target_pairs={{8,0},{12,4},{16,8},{20,12},{24,16},{28,20},{32,24},{36,28},{40,32... | collective-permute-start | bytes 7077896 | tf_op jit(solution)/shard_map/ppermute | solution.py:496
  89.0 8.5 %copy-start.3 = (f32[3,2,3,256,128]{4,3,2,1,0:T(8,128)S(1)}, f32[3,2,3,256,128]{4,3,2,1,0:T(8,128)}, u32[]{:S(2)}) copy-start(f32[3,2,3,256,128]{4,3,2,1,0:T(8,128)} %get-tuple-element.33) | copy-start | bytes 7077892
  119.3 39.0 %all-to-all-start.2 = ((f32[4,1,2,3,256,128]{5,4,3,2,1,0:T(8,128)}), f32[4,1,2,3,256,128]{5,4,3,2,1,0:T(8,128)S(1)}, u32[]{:S(2)}, u32[]{:S(2)}) async-start(f32[4,1,2,3,256,128]{5,4,3,2,1,0:T(8,128)} %maximum_bitcast_fusion), calls=%async_computation.2 | async-start | bytes 6291456 | tf_op jit(solution)/shard_map/all_to_all | solution.py:513
  126.8 45.2 %collective-permute-start.5 = (f32[2,2,1,256,128]{4,3,1,0,2:T(8,128)}, f32[2,2,1,256,128]{4,3,1,0,2:T(8,128)}, u32[]{:S(2)}, u32[]{:S(2)}) collective-permute-start(f32[2,2,1,256,128]{4,3,1,0,2:T(8,128)} %bitcast.65), channel_id=1, source_target_pairs={{4,0},{8,4},{12,8},{16,12},{20,16},{24,20},{28,24},{32,28},{36,32}... | collective-permute-start | bytes 1572872 | tf_op jit(solution)/shard_map/ppermute | solution.py:496
  128.7 44.5 %collective-permute-start.6 = (f32[3,2,1,256,128]{4,3,1,0,2:T(8,128)}, f32[3,2,1,256,128]{4,3,1,0,2:T(8,128)}, u32[]{:S(2)}, u32[]{:S(2)}) collective-permute-start(f32[3,2,1,256,128]{4,3,1,0,2:T(8,128)} %bitcast.64), channel_id=1, source_target_pairs={{8,0},{12,4},{16,8},{20,12},{24,16},{28,20},{32,24},{36,28},{40,32... | collective-permute-start | bytes 2359304 | tf_op jit(solution)/shard_map/ppermute | solution.py:496
  136.1 11.2 %copy-start.1 = (f32[1,2,3,256,128]{4,3,2,1,0:T(8,128)S(1)}, f32[1,2,3,256,128]{4,3,2,1,0:T(8,128)}, u32[]{:S(2)}) copy-start(f32[1,2,3,256,128]{4,3,2,1,0:T(8,128)} %get-tuple-element.96) | copy-start | bytes 2359300
  151.0 15.1 %copy-start.12 = (f32[128]{0:T(128)S(1)}, f32[128]{0:T(128)}, u32[]{:S(2)}) copy-start(f32[128]{0:T(128)} %get-tuple-element.59) | copy-start | bytes 1540
  158.2 1.7 copy-start
  159.9 39.2 %all-to-all-start.3 = ((f32[4,1,2,3,256,128]{5,4,3,2,1,0:T(8,128)}), f32[4,1,2,3,256,128]{5,4,3,2,1,0:T(8,128)}, u32[]{:S(2)}, u32[]{:S(2)}) async-start(f32[4,1,2,3,256,128]{5,4,3,2,1,0:T(8,128)} %maximum_bitcast_fusion.1), calls=%async_computation.3 | async-start | bytes 6291456 | tf_op jit(solution)/shard_map/all_to_all | solution.py:513
  166.0 3.0 %copy-start.11 = (f32[128]{0:T(128)S(1)}, f32[128]{0:T(128)}, u32[]{:S(2)}) copy-start(f32[128]{0:T(128)} %get-tuple-element.219) | copy-start | bytes 1540
  166.0 3.0 %copy-start.13 = (f32[128]{0:T(128)S(1)}, f32[128]{0:T(128)}, u32[]{:S(2)}) copy-start(f32[128]{0:T(128)} %sin.79) | copy-start | bytes 1540
  167.9 2.1 copy-start.2
  170.0 3.1 %copy-start.6 = (f32[3,2,1,256,128]{4,3,2,1,0:T(8,128)S(1)}, f32[3,2,1,256,128]{4,3,2,1,0:T(8,128)}, u32[]{:S(2)}) copy-start(f32[3,2,1,256,128]{4,3,2,1,0:T(8,128)} %get-tuple-element.46) | copy-start | bytes 2359300
  199.1 8.2 %copy-start.7 = (f32[128,256]{1,0:T(8,128)S(1)}, f32[128,256]{1,0:T(8,128)}, u32[]{:S(2)}) copy-start(f32[128,256]{1,0:T(8,128)} %get-tuple-element.190) | copy-start | bytes 393220
  199.1 8.2 %copy-start.8 = (f32[128,256]{1,0:T(8,128)S(1)}, f32[128,256]{1,0:T(8,128)}, u32[]{:S(2)}) copy-start(f32[128,256]{1,0:T(8,128)} %get-tuple-element.191) | copy-start | bytes 393220
  199.1 27.1 %all-to-all-start.4 = ((f32[4,2,2,1,256,128]{5,4,3,2,1,0:T(8,128)}), f32[4,2,2,1,256,128]{5,4,3,2,1,0:T(8,128)S(1)}, u32[]{:S(2)}, u32[]{:S(2)}) async-start(f32[4,2,2,1,256,128]{5,4,3,2,1,0:T(8,128)} %pad_maximum_fusion.1), calls=%async_computation.4 | async-start | bytes 4194304 | tf_op jit(solution)/shard_map/all_to_all | solution.py:513
  226.2 1.4 copy-start.5

commit v7 on v6

--- a/solution.py
+++ b/solution.py
@@ -230,66 +230,55 @@
     return dot3_right(table, jnp.concatenate((real, imag), axis=0))
 
 
-def send_kernel(blocks, tile_ref, round_ref, off_ref, x_ref, a_ref, near_ref, far_ref, keep_ref):
+def send_kernel(count, steps, src_ref, round_ref, tile_ref, off_ref, *refs):
+    x_refs, a_ref, outs = refs[:count], refs[count], refs[count + 1 :]
     i = pl.program_id(0)
     later = lax.broadcasted_iota(jnp.int32, (A, 256), 0) >= off_ref[round_ref[i], tile_ref[i]]
-    picked = [
-        jnp.where(later, x_ref[0, p, :A, w * 256 : (w + 1) * 256], x_ref[0, p, A:, w * 256 : (w + 1) * 256])
-        for p in range(2)
-        for w in range(blocks)
-    ]
-    real = jnp.concatenate([p[:, :128] for p in picked], axis=1)
-    imag = jnp.concatenate([p[:, 128:] for p in picked], axis=1)
-    spec = dot3_right(a_ref[0, 0], jnp.concatenate((real, imag), axis=0))
-
-    def put(ref):
-        for k in range(2 * blocks):
-            ref[0, k // blocks, k % blocks] = spec[:, k * 128 : (k + 1) * 128]
-
-    @pl.when(i < 2)
-    def _():
-        put(near_ref)
-
-    @pl.when(jnp.logical_and(i >= 2, i < 5))
-    def _():
-        put(far_ref)
-
-    @pl.when(i >= 5)
-    def _():
-        put(keep_ref)
-
-
-SEND_TILE = (0, 3, 0, 1, 2, 1, 2, 3)
-SEND_ROUND = (0, 1, 1, 1, 1, 0, 0, 0)
-
-
-def spectra(x, offs, mats, interpret=False):
-    blocks = x.shape[3] // 256
-
-    def out(count, first):
-        shape = (2, blocks, 256, 128)
-        return (
-            jax.ShapeDtypeStruct((count, *shape), F32),
-            pl.BlockSpec((1, *shape), lambda i, *_: (jnp.clip(i - first, 0, count - 1), 0, 0, 0, 0)),
-        )
-
-    outs = (out(2, 0), out(3, 2), out(3, 5))
+    first = 0
+    for x_ref in x_refs:
+        blocks = x_ref.shape[3] // 256
+        picked = [
+            jnp.where(later, x_ref[0, p, :A, w * 256 : (w + 1) * 256], x_ref[0, p, A:, w * 256 : (w + 1) * 256])
+            for p in range(2)
+            for w in range(blocks)
+        ]
+        real = jnp.concatenate([p[:, :128] for p in picked], axis=1)
+        imag = jnp.concatenate([p[:, 128:] for p in picked], axis=1)
+        spec = dot3_right(a_ref[0, 0], jnp.concatenate((real, imag), axis=0))
+        for step in range(steps):
+            @pl.when(i == step)
+            def _(step=step, first=first, spec=spec, blocks=blocks):
+                for k in range(2 * blocks):
+                    outs[step][k // blocks, first + k % blocks] = spec[:, k * 128 : (k + 1) * 128]
+
+        first += blocks
+
+
+def spectra(xs, sources, rounds, tiles, offs, mats, interpret=False):
+    steps = len(sources)
+    blocks = sum(x.shape[3] for x in xs) // 256
+    shape = (2, blocks, 256, 128)
+
+    def array(values):
+        return jnp.stack([jnp.asarray(v, jnp.int32) for v in values])
+
     return pl.pallas_call(
-        functools.partial(send_kernel, blocks),
-        out_shape=tuple(o[0] for o in outs),
+        functools.partial(send_kernel, len(xs), steps),
+        out_shape=(jax.ShapeDtypeStruct(shape, F32),) * steps,
         grid_spec=pltpu.PrefetchScalarGridSpec(
-            num_scalar_prefetch=3,
-            grid=(8,),
+            num_scalar_prefetch=4,
+            grid=(steps,),
             in_specs=[
-                pl.BlockSpec((1, 2, 256, 256 * blocks), lambda i, t, r, o: (t[i], 0, 0, 0)),
-                pl.BlockSpec((1, 1, 256, 768), lambda i, t, r, o: (r[i], t[i], 0, 0)),
-            ],
-            out_specs=tuple(o[1] for o in outs),
-        ),
-        cost_estimate=pl.CostEstimate(flops=800_000_000 * blocks, bytes_accessed=6_000_000 * blocks, transcendentals=0),
+                pl.BlockSpec((1, 2, 256, x.shape[3]), lambda i, s, r, t, o: (s[i], 0, 0, 0)) for x in xs
+            ]
+            + [pl.BlockSpec((1, 1, 256, 768), lambda i, s, r, t, o: (r[i], t[i], 0, 0))],
+            out_specs=(whole(shape),) * steps,
+        ),
+        cost_estimate=pl.CostEstimate(
+            flops=100_000_000 * blocks * steps, bytes_accessed=800_000 * blocks * steps, transcendentals=0
+        ),
         interpret=interpret,
-        name="spectra",
-    )(jnp.asarray(SEND_TILE, jnp.int32), jnp.asarray(SEND_ROUND, jnp.int32), offs, x, mats)
+    )(array(sources), array(rounds), array(tiles), offs, *xs, mats)
 
 
 def normalized(p, q, sign):
@@ -337,7 +326,10 @@
             r_ref[place] = jnp.where(lane == 0, moved, r_ref[place])
 
 
-def pair_core(offset, y_ref, far_ref, a_ref, own_ref, r_ref, valid):
+def pair_core(offset, slab, y_ref, far_refs, a_ref, own_ref, r_ref, far_scr, valid):
+    for turn in range(4):
+        target = lax.rem(slab + turn, 4)
+        far_scr[pl.ds(target, 1)] = far_refs[turn][:, 0][None]
     for half in range(2):
         own_ref[:, half * 512 : (half + 1) * 512] = across(y_ref, half * 4, 4, offset, a_ref[...])
 
@@ -345,7 +337,7 @@
         return own_ref[rows, z * 128 : (z + 1) * 128]
 
     def far_of(z, rows):
-        return far_ref[z // 2, 0, z % 2, 0, rows, :]
+        return far_scr[z // 2, z % 2, rows, :]
 
     def chunk(i, _):
         up = pl.ds(pl.multiple_of(i * 8, 8), 8)
@@ -374,12 +366,14 @@
 
 
 def large_pair_kernel(
-    ints_ref, y_ref, far_ref, a_ref, ab_ref, v1_ref, v0_ref, ef_ref, er_ref, flip_ref, *refs
+    ints_ref, y_ref, f0_ref, f1_ref, f2_ref, f3_ref, a_ref, ab_ref, v1_ref, v0_ref, ef_ref, er_ref, flip_ref, *refs
 ):
-    odd_ref, fours_ref, own_ref, r_ref = refs[-4:]
+    odd_ref, fours_ref, own_ref, r_ref, far_scr = refs[-5:]
     step = pl.program_id(0)
     valid = ints_ref[1].astype(F32)
-    own_of, far_of = pair_core(ints_ref[0], y_ref, far_ref, a_ref, own_ref, r_ref, valid)
+    own_of, far_of = pair_core(
+        ints_ref[0], ints_ref[2], y_ref, (f0_ref, f1_ref, f2_ref, f3_ref), a_ref, own_ref, r_ref, far_scr, valid
+    )
 
     @pl.when(step == 0)
     def _():
@@ -399,12 +393,13 @@
 
 
 def small_pair_kernel(
-    own_off_ref, valid_ref, y_ref, far_ref, a_ref, ab_ref, v2_ref, odd_ref, fours_ref,
-    surf_ref, peak_ref, own_ref, r_ref,
+    ints_ref, y_ref, f0_ref, f1_ref, f2_ref, f3_ref, a_ref, ab_ref, v2_ref, odd_ref, fours_ref, *refs
 ):
-    rnd = pl.program_id(0)
-    valid = valid_ref[rnd].astype(F32)
-    pair_core(own_off_ref[rnd], y_ref, far_ref, a_ref.at[0], own_ref, r_ref, valid)
+    surf_ref, peak_ref, own_ref, r_ref, far_scr = refs[-5:]
+    valid = ints_ref[1].astype(F32)
+    pair_core(
+        ints_ref[0], ints_ref[2], y_ref, (f0_ref, f1_ref, f2_ref, f3_ref), a_ref, own_ref, r_ref, far_scr, valid
+    )
     for z, part in parts(ab_ref, r_ref, v2_ref):
         first = fours_ref[0, z : z + 2].reshape(2 * A, 256)
         odd = odd_ref[0, z : z + 2].reshape(2 * A, 512)
@@ -418,14 +413,14 @@
     peak_ref[0] = jnp.broadcast_to(jnp.max(surf_ref[0, 0]), (8, 128))
 
 
-SCRATCH = [pltpu.VMEM((256, Z * 128), F32), pltpu.VMEM((256, Z * 128), F32)]
+SCRATCH = [pltpu.VMEM((256, Z * 128), F32)] * 2 + [pltpu.VMEM((4, 2, 256, 128), F32)]
 
 
 def large_pair(rnd, ints, y, far, mat, ab, back1, back0, edges, before, interpret=False):
-    args = [y, far, mat, ab, back1, back0, *edges]
+    args = [y, *far, mat, ab, back1, back0, *edges]
     in_specs = [
         pl.BlockSpec((Z, 256, 256), lambda w, *_: (0, 0, w)),
-        pl.BlockSpec((4, 1, 2, 1, 256, 128), lambda w, *_: (0, 0, 0, w, 0, 0)),
+        *[pl.BlockSpec((2, 1, 256, 128), lambda w, *_: (0, w, 0, 0))] * 4,
         whole((256, 768)),
         whole((256, 768)),
         pl.BlockSpec((1, 768, 512), lambda w, *_: (jnp.minimum(w, 1), 0, 0)),
@@ -461,7 +456,22 @@
     )(ints, *args)
 
 
-def small_pair(own, valid, y, far, mats, ab, back2, odd, fours, interpret=False):
+def small_pair(rnd, ints, y, far, mat, ab, back2, odd, fours, before, interpret=False):
+    args = [y, *far, mat, ab, back2, odd, fours]
+    in_specs = [
+        whole((Z, 256, 256)),
+        *[pl.BlockSpec((2, 1, 256, 128), lambda r, *_, last=x.shape[1] - 1: (0, last, 0, 0)) for x in far],
+        whole((256, 768)),
+        whole((256, 768)),
+        whole((768, 256)),
+        pl.BlockSpec((1, Z, A, 512), lambda r, *_: (rnd, 0, 0, 0)),
+        pl.BlockSpec((1, Z, A, 256), lambda r, *_: (rnd, 0, 0, 0)),
+    ]
+    aliases = {}
+    if before is not None:
+        aliases = {len(args) + 1: 0, len(args) + 2: 1}
+        args += list(before)
+        in_specs += [pl.BlockSpec(memory_space=pl.ANY)] * 2
     return pl.pallas_call(
         small_pair_kernel,
         out_shape=(
@@ -469,103 +479,110 @@
             jax.ShapeDtypeStruct((ROUNDS, 8, 128), F32),
         ),
         grid_spec=pltpu.PrefetchScalarGridSpec(
-            num_scalar_prefetch=2,
-            grid=(ROUNDS,),
-            in_specs=[
-                whole((Z, 256, 256)),
-                pl.BlockSpec((4, 1, 2, 1, 256, 128), lambda r, *_: (0, r, 0, 0, 0, 0)),
-                pl.BlockSpec((1, 256, 768), lambda r, *_: (r, 0, 0)),
-                whole((256, 768)),
-                whole((768, 256)),
-                pl.BlockSpec((1, Z, A, 512), lambda r, *_: (r, 0, 0, 0)),
-                pl.BlockSpec((1, Z, A, 256), lambda r, *_: (r, 0, 0, 0)),
-            ],
+            num_scalar_prefetch=1,
+            grid=(1,),
+            in_specs=in_specs,
             out_specs=(
-                pl.BlockSpec((1, 1, A, L), lambda r, *_: (r, 0, 0, 0)),
-                pl.BlockSpec((1, 8, 128), lambda r, *_: (r, 0, 0)),
+                pl.BlockSpec((1, 1, A, L), lambda r, *_: (rnd, 0, 0, 0)),
+                pl.BlockSpec((1, 8, 128), lambda r, *_: (rnd, 0, 0)),
             ),
             scratch_shapes=SCRATCH,
         ),
-        cost_estimate=pl.CostEstimate(flops=4_000_000_000, bytes_accessed=16_000_000, transcendentals=500_000),
+        input_output_aliases=aliases,
+        cost_estimate=pl.CostEstimate(flops=2_000_000_000, bytes_accessed=10_000_000, transcendentals=300_000),
         interpret=interpret,
-        name="small_pairs",
-    )(own, valid, y, far, mats, ab, back2, odd, fours)
-
-
-def from_next(x, step, groups):
-    return lax.ppermute(x, "tile", [(g + step, g) for g in range(groups - step)])
+    )(ints, *args)
 
 
 def after(*values):
     return lax.optimization_barrier(values)
+
+
+DIRECT = (0, 1, 3)
+
+
+def routes(groups, slabs, rnd, tile_of):
+    pairs = []
+    for g in range(groups):
+        for s in range(slabs):
+            i = tile_of(s)
+            if rnd == 0:
+                to, j = g - (i == 0), (i - 1) % slabs
+            else:
+                to, j = g - (1 if i == slabs - 1 else 2), (i + 1) % slabs
+            if to >= 0:
+                pairs.append((slabs * g + s, slabs * to + j))
+    return pairs
 
 
 def register(stored, offsets):
     size = lax.axis_size(("tile", "slab"))
     groups = lax.axis_size("tile")
     slabs = lax.axis_size("slab")
+    slab = lax.axis_index("slab")
     place = lax.axis_index(("tile", "slab"))
 
     def gather(x):
         return lax.all_to_all(x, "slab", split_axis=0, concat_axis=1, tiled=True)[0]
 
-    def collect(x):
-        return lax.all_to_all(x, "slab", split_axis=0, concat_axis=0, tiled=True)
-
-    small_src = along(small_kernel, stored, (twos_table(),), 256)
-    small_all = gather(small_src)
+    def send(x, rnd, tile_of):
+        return lax.ppermute(x, ("tile", "slab"), routes(groups, slabs, rnd, tile_of))
+
+    large_src = along(large_kernel, stored, (odd_table(), fours_table()), 768)
+    large_all = gather(large_src)
     mine = offsets[:, 1, 0]
     turns = [mine] + [lax.ppermute(mine, "slab", [((i + k) % slabs, i) for i in range(slabs)]) for k in range(1, slabs)]
-    large_src = along(large_kernel, stored, (odd_table(), fours_table()), 768)
+    small_src = along(small_kernel, stored, (twos_table(),), 256)
     base = lax.optimization_barrier(across_base())
-    given = jnp.roll(jnp.stack(turns, axis=1), lax.axis_index("slab"), axis=1)
+    given = jnp.roll(jnp.stack(turns, axis=1), slab, axis=1)
     mats = jnp.stack(
         [jnp.stack([across_forward(given[r, j], base) for j in range(slabs)]) for r in range(ROUNDS)]
     )
-    small_all, band_src = after(small_all, large_src)
-    large_all = gather(band_src)
-
-    def shifted(made):
-        near, far, keep = made
-        near = from_next(near, 1, groups)
-        far = from_next(far, 2, groups)
-        return jnp.concatenate((keep, near[:1])), jnp.concatenate((near[1:], far))
-
-    large_made = spectra(large_src, given, mats)
-    large_zero, large_one = [x[:, None] for x in shifted(large_made)]
-    small_made = spectra(small_src, given, mats)
-    small_sent = jnp.stack(shifted(small_made), axis=1)
+
+    def shift_of(rnd, k):
+        return 1 - k if rnd == 0 else -1 - k
+
+    plan = [(r, k) for r in range(ROUNDS) for k in DIRECT]
+    tiles = [(slab + shift_of(r, k) + slabs) % slabs for r, k in plan]
+    made = spectra([large_src, small_src], tiles, [r for r, _ in plan], tiles, given, mats)
+    far = [[None] * slabs for _ in range(ROUNDS)]
+    for (r, k), x in zip(plan, made, strict=True):
+        far[r][k] = send(x, r, lambda s, r=r, k=k: (s + shift_of(r, k)) % slabs)
+    SEEDS.append(made[0])
     valid = (
         jnp.logical_and(place % GC != GC - 1, place + 1 < size),
         place + GC < size,
     )
-    SEEDS.append(small_made[0])
     own = [offsets[r, 0, 0] for r in range(ROUNDS)]
-    ints = [jnp.stack((own[r], valid[r].astype(jnp.int32))) for r in range(ROUNDS)]
+    ints = [jnp.stack((own[r], valid[r].astype(jnp.int32), slab)) for r in range(ROUNDS)]
     own_mats = [across_forward(o, base) for o in own]
     ab = across_back()
     edges = edge_tables()
     back1, back0, back2 = odd_back(), fours_back(), twos_back()
     SEEDS.clear()
-    large_all, large_zero = after(large_all, large_zero)
-    far_zero = collect(large_zero)
-    far_zero, large_one = after(far_zero, large_one)
-    far_one = collect(large_one)
-    first = large_pair(0, ints[0], large_all, far_zero, own_mats[0], ab, back1, back0, edges, None)
-    far_one, first, small_sent = after(far_one, first, small_sent)
-    small_far = collect(small_sent)
-    odd, fours = large_pair(1, ints[1], large_all, far_one, own_mats[1], ab, back1, back0, edges, first)
-    surface, peak = small_pair(
-        jnp.stack(own),
-        jnp.stack([v.astype(jnp.int32) for v in valid]),
-        small_all,
-        small_far,
-        jnp.stack(own_mats),
-        ab,
-        back2,
-        odd,
-        fours,
-    )
+    large_all, band_src = after(large_all, small_src)
+    small_all = gather(band_src)
+
+    def relayed(x):
+        whole_band = x.reshape(slabs, 2, 256, x.shape[2])
+        both = spectra(
+            [whole_band], [(slab + 1) % slabs, (slab + slabs - 1) % slabs], [0, 1], [slab, slab], given, mats
+        )
+        return [send(both[r], r, lambda s: s) for r in range(ROUNDS)]
+
+    large_two = relayed(large_all)
+    small_two = relayed(small_all)
+
+    def around(r, two):
+        return [far[r][0], far[r][1], two[r], far[r][3]]
+
+    sums = None
+    for r in range(ROUNDS):
+        sums = large_pair(r, ints[r], large_all, around(r, large_two), own_mats[r], ab, back1, back0, edges, sums)
+    out = None
+    for r in range(ROUNDS):
+        out = small_pair(r, ints[r], small_all, around(r, small_two), own_mats[r], ab, back2, *sums, out)
+    surface, peak = out
     return surface, peak[:, 0, :1]
 
 

time: 242 us -> 257 us (1.062)
  the two profiles are of different devices: /device:TPU:56 before, /device:TPU:6 now
where the time goes in v7:
time: 257 us; the launch traced here: 256 us
  Pallas kernels  84.3 us (33%)
  waiting for transfers between devices  71.4 us (28%)
  starting transfers between devices  53.6 us (21%)
  other arithmetic  36.8 us (14%)
  local copies, waits for them, and re-layouts  8.25 us (3%)
    ppermute x10, waiting for transfers between devices, send(): lax.ppermute(x, ('tile', 'slab'), routes(groups, slabs, rnd, tile_of))  48.1 us
    ppermute x10, starting transfers between devices, send(): lax.ppermute(x, ('tile', 'slab'), routes(groups, slabs, rnd, tile_of))  38.1 us
    pallas_call x2, Pallas kernels, large_pair(): pl.pallas_call(large_pair_kernel, out_shape=(jax.ShapeDtypeStruct((ROUNDS...  33 us
    all_to_all x2, waiting for transfers between devices, gather(): return lax.all_to_all(x, 'slab', split_axis=0, concat_axis=1, tiled=True)[0]  23.3 us
    pallas_call x3, Pallas kernels, spectra(): pl.pallas_call(functools.partial(send_kernel, len(xs), steps), out_shape=...  20.7 us
    pallas_call x2, Pallas kernels, small_pair(): pl.pallas_call(small_pair_kernel, out_shape=(jax.ShapeDtypeStruct((ROUNDS...  15.4 us
    pallas_call x2, Pallas kernels, along(): pl.pallas_call(kernel, out_shape=jax.ShapeDtypeStruct((tiles, planes, 256...  15.2 us
    cos x5, other arithmetic, trig(): return (jnp.cos(angle), jnp.sin(angle))  11.9 us
  transfers between devices with their start and end apart: 15, of which 3 were waited for; matrix products, arithmetic and copies ran while one was open for 16% of the time, Pallas kernels for 30%

profile of v7, /device:TPU:6, one launch (start us, length us, event | category | flops | bytes accessed | tf_op | source)
XLA Modules:
  0.0 255.7 jit_solution(8966932929835372290)
XLA Ops:
  0.6 0.9 slice_reduce_fusion.1
  1.5 2.0 collective-permute-start.2
  3.5 3.6 %collective-permute-start.1 = (s32[2]{0:T(128)S(1)}, s32[2]{0:T(128)S(1)}, u32[]{:S(2)}, u32[]{:S(2)}) collective-permute-start(s32[2]{0:T(128)S(1)} %get-tuple-element.199), channel_id=1, source_target_pairs={{2,0},{3,1},{0,2},{1,3},{6,4},{7,5},{4,6},{5,7},{10,8},{11,9},{8,1... | collective-permute-start | bytes 32 | tf_op jit(solution)/shard_map/ppermute | solution.py:534
  7.1 1.0 collective-permute-start
  8.1 1.1 fusion.54
  9.3 0.8 pad_maximum_fusion.3.w0_ref
  10.1 2.1 fusion.29
  12.5 1.3 pad_maximum_fusion.1.w1_ref
  13.8 9.2 %shard_map.41.refs_0_ = f32[4,2,256,768]{3,2,1,0:T(8,128)} custom-call(f32[4,2,256,1024]{3,2,1,0:T(8,128)} %x_ref.3, bf16[1536,512]{1,0:T(8,128)(2,1)} %pad_maximum_fusion.1.w1_ref, bf16[768,256]{1,0:T(8,128)(2,1)} %pad_maximum_fusion.3.w0_ref), custom_call_target="tpu_custom_call" | custom-call | flops 4608000000 | bytes 14000000 | tf_op jit(solution)/shard_map/pallas_call | solution.py:211
  23.0 5.4 %all-to-all-start = ((f32[4,2,256,768]{3,2,1,0:T(8,128)}), f32[4,2,256,768]{3,2,1,0:T(8,128)}, u32[]{:S(2)}, u32[]{:S(2)}) async-start(f32[4,2,256,768]{3,2,1,0:T(8,128)} %shard_map.41.refs_0_), calls=%async_computation | async-start | bytes 12582912 | tf_op jit(solution)/shard_map/all_to_all | solution.py:526
  28.5 0.6 fusion.134
  29.4 0.8 pad_maximum_fusion.4.w2_ref
  30.2 5.9 %shard_map.42.refs_1_ = f32[4,2,256,256]{3,2,1,0:T(8,128)} custom-call(f32[4,2,256,1024]{3,2,1,0:T(8,128)} %x_ref.3, bf16[768,256]{1,0:T(8,128)(2,1)} %pad_maximum_fusion.4.w2_ref), custom_call_target="tpu_custom_call" | custom-call | flops 1536000000 | bytes 14000000 | tf_op jit(solution)/shard_map/pallas_call | solution.py:211
  36.2 0.7 pad_add_fusion
  36.8 1.2 add_add_fusion.1.ints_ref
  38.0 1.3 add_add_fusion.ints_ref
  39.3 0.6 stack.133.src_ref.tile_ref
  40.3 0.7 fusion.135
  41.0 5.2 %fusion.109 = (f32[128]{0:T(128)S(1)}, f32[128]{0:T(128)S(1)}, f32[128]{0:T(128)S(1)}, f32[128]{0:T(128)S(1)}, f32[128]{0:T(128)S(1)}, /*index=5*/f32[128]{0:T(1...) fusion(s32[128]{0:T(128)S(1)} %iota.19, ...), kind=kLoop, calls=%fused_computation.317 | loop fusion | flops 14336 | bytes 8736 | tf_op jit(solution)/shard_map/cos | solution.py:46
  48.0 2.0 pad_maximum_fusion.refs_2_.refs_1_
  49.9 12.9 %shard_map.43 = (f32[2,4,256,128]{3,2,1,0:T(8,128)}, f32[2,4,256,128]{3,2,1,0:T(8,128)}, f32[2,4,256,128]{3,2,1,0:T(8,128)}, f32[2,4,256,128]{3,2,1,0:T(8,128)},...) custom-call(s32[6]{0:T(128)} %stack.133.src_ref.tile_ref, s32[6]{0:T(128)} %constant.274.clone.1.round_ref, ...), custom_call_target="tpu_custom_call" | custom-call | flops 2400000000 | bytes 19200000 | tf_op jit(solution)/shard_map/pallas_call | solution.py:265
  62.8 1.9 collective-permute-start.8
  64.7 1.4 fusion.103
  66.2 3.8 %collective-permute-start.3 = (f32[2,4,256,128]{3,2,1,0:T(8,128)}, f32[2,4,256,128]{3,2,1,0:T(8,128)}, u32[]{:S(2)}, u32[]{:S(2)}) collective-permute-start(f32[2,4,256,128]{3,2,1,0:T(8,128)} %get-tuple-element.30), channel_id=1, source_target_pairs={{4,0},{8,4},{9,1},{10,2},{11,3},{12,8},{13,5},{14,6},{15,7},{16,12... | collective-permute-start | bytes 3145736 | tf_op jit(solution)/shard_map/ppermute | solution.py:529
  70.0 6.5 %collective-permute-start.9 = (f32[2,4,256,128]{3,2,1,0:T(8,128)}, f32[2,4,256,128]{3,2,1,0:T(8,128)}, u32[]{:S(2)}, u32[]{:S(2)}) collective-permute-start(f32[2,4,256,128]{3,2,1,0:T(8,128)} %get-tuple-element.40), channel_id=1, source_target_pairs={{1,0},{2,1},{3,2},{4,3},{5,4},{6,5},{7,6},{8,7},{9,8},{10,9},{11,1... | collective-permute-start | bytes 3145736 | tf_op jit(solution)/shard_map/ppermute | solution.py:529
  76.5 2.1 collective-permute-start.11
  78.8 0.6 fusion.62
  79.4 0.8 pad_maximum_fusion.9.a_ref
  80.2 0.8 pad_maximum_fusion.5.a_ref
  81.0 2.1 fusion.27
  83.2 0.8 reduce-precision_convert_fusion.2
  84.0 0.9 reduce-precision_convert_fusion.1
  84.9 0.8 pad_maximum_fusion.6.ab_ref
  85.7 1.9 multiply_select_fusion.7
  87.6 0.7 reduce-precision_convert_fusion.4
  88.3 0.8 fusion.10
  89.1 23.3 %all-to-all-done = f32[4,2,256,768]{3,2,1,0:T(8,128)} async-done(((f32[4,2,256,768]{3,2,1,0:T(8,128)}), f32[4,2,256,768]{3,2,1,0:T(8,128)}, u32[]{:S(2)}, u32[]{:S(2)}) %all-to-all-start) | async-done | bytes 6291488 | tf_op jit(solution)/shard_map/all_to_all | solution.py:526
  112.5 3.6 %all-to-all-start.1 = ((f32[4,2,256,256]{3,2,1,0:T(8,128)}), f32[4,2,256,256]{3,2,1,0:T(8,128)S(1)}, u32[]{:S(2)}, u32[]{:S(2)}) async-start(f32[4,2,256,256]{3,2,1,0:T(8,128)} %shard_map.42.refs_1_), calls=%async_computation.1 | async-start | bytes 4194304 | tf_op jit(solution)/shard_map/all_to_all | solution.py:526
  116.1 1.8 pad_maximum_fusion.8.v0_ref
  117.9 0.5 iota.23.round_ref
  118.4 4.5 %shard_map.45 = (f32[2,3,256,128]{3,2,1,0:T(8,128)}, f32[2,3,256,128]{3,2,1,0:T(8,128)}) custom-call(s32[2]{0:T(128)} %get-tuple-element.244.src_ref, s32[2]{0:T(128)} %iota.23.round_ref, s32[2]{0:T(128)} %get-tuple-element.245.tile_ref, s32[2,4]{1,0:T(2,128)} %copy-done.6, f32[4,2,256,768]{3,2,1,0:T(8,128)} %bitcast.34.refs_0_, ...), custom_call_target="tpu_custom_call" | custom-call | flops 600000000 | bytes 4800000 | tf_op jit(solution)/shard_map/pallas_call | solution.py:265
  122.9 3.4 %collective-permute-start.10 = (f32[2,3,256,128]{3,2,1,0:T(8,128)}, f32[2,3,256,128]{3,2,1,0:T(8,128)}, u32[]{:S(2)}, u32[]{:S(2)}) collective-permute-start(f32[2,3,256,128]{3,2,1,0:T(8,128)} %get-tuple-element.41), channel_id=1, source_target_pairs={{1,0},{2,1},{3,2},{4,3},{5,4},{6,5},{7,6},{8,7},{9,8},{10,9},{11,1... | collective-permute-start | bytes 2359304 | tf_op jit(solution)/shard_map/ppermute | solution.py:529
  126.3 0.9 reduce-precision_convert_fusion.5
  127.3 1.0 maximum_bitcast_fusion.2
  128.4 5.0 %collective-permute-done.9.f1_ref = f32[2,4,256,128]{3,2,1,0:T(8,128)} collective-permute-done((f32[2,4,256,128]{3,2,1,0:T(8,128)}, f32[2,4,256,128]{3,2,1,0:T(8,128)}, u32[]{:S(2)}, u32[]{:S(2)}) %collective-permute-start.9) | collective-permute-done | bytes 1048608 | tf_op jit(solution)/shard_map/ppermute | solution.py:529
  133.4 2.3 collective-permute-start.4
  135.7 3.8 %collective-permute-start.6 = (f32[2,4,256,128]{3,2,1,0:T(8,128)}, f32[2,4,256,128]{3,2,1,0:T(8,128)}, u32[]{:S(2)}, u32[]{:S(2)}) collective-permute-start(f32[2,4,256,128]{3,2,1,0:T(8,128)} %get-tuple-element.33), channel_id=1, source_target_pairs={{7,0},{8,1},{9,2},{10,3},{11,4},{12,5},{13,6},{14,7},{15,8},{16,9}... | collective-permute-start | bytes 3145736 | tf_op jit(solution)/shard_map/ppermute | solution.py:529
  139.5 0.8 pad_maximum_fusion.7.v2_ref
  140.3 1.3 pad_maximum_fusion.2.v1_ref
  141.6 4.0 %collective-permute-start.7 = (f32[2,3,256,128]{3,2,1,0:T(8,128)}, f32[2,3,256,128]{3,2,1,0:T(8,128)}, u32[]{:S(2)}, u32[]{:S(2)}) collective-permute-start(f32[2,3,256,128]{3,2,1,0:T(8,128)} %get-tuple-element.38), channel_id=1, source_target_pairs={{7,0},{8,1},{9,2},{10,3},{11,4},{12,5},{13,6},{14,7},{15,8},{16,9}... | collective-permute-start | bytes 2359304 | tf_op jit(solution)/shard_map/ppermute | solution.py:529
  145.6 0.7 fusion.56.flip_ref
  146.3 43.1 %collective-permute-done.10.f2_ref = f32[2,3,256,128]{3,2,1,0:T(8,128)} collective-permute-done((f32[2,3,256,128]{3,2,1,0:T(8,128)}, f32[2,3,256,128]{3,2,1,0:T(8,128)}, u32[]{:S(2)}, u32[]{:S(2)}) %collective-permute-start.10) | collective-permute-done | bytes 786464 | tf_op jit(solution)/shard_map/ppermute | solution.py:529
  189.4 16.4 %shard_map.46 = (f32[2,8,128,512]{3,2,1,0:T(8,128)}, f32[2,8,128,256]{3,2,1,0:T(8,128)}) custom-call(s32[3]{0:T(128)} %add_add_fusion.1.ints_ref, f32[8,256,768]{2,1,0:T(8,128)} %bitcast.3.y_ref, f32[2,4,256,128]{3,2,1,0:T(8,128)} %copy-done.1, f32[2,4,256,128]{3,2,1,0:T(8,128)} %collective-permute-done.9.f1_ref, ...), custom_call_target="tpu_custom_call" | custom-call | flops 6000000000 | bytes 16000000 | tf_op jit(solution)/shard_map/pallas_call | solution.py:437
  205.8 0.6 iota.20.round_ref
  206.4 0.8 copy-done
  207.2 3.3 %shard_map.44 = (f32[2,1,256,128]{3,2,1,0:T(8,128)}, f32[2,1,256,128]{3,2,1,0:T(8,128)}) custom-call(s32[2]{0:T(128)} %get-tuple-element.244.src_ref, s32[2]{0:T(128)} %iota.20.round_ref, s32[2]{0:T(128)} %get-tuple-element.245.tile_ref, s32[2,4]{1,0:T(2,128)} %copy-done.6, f32[4,2,256,256]{3,2,1,0:T(8,128)} %copy-done, ...), custom_call_target="tpu_custom_call" | custom-call | flops 200000000 | bytes 1600000 | tf_op jit(solution)/shard_map/pallas_call | solution.py:265
  210.5 4.8 %collective-permute-start.5 = (f32[2,1,256,128]{3,2,1,0:T(8,128)}, f32[2,1,256,128]{3,2,1,0:T(8,128)S(1)}, u32[]{:S(2)}, u32[]{:S(2)}) collective-permute-start(f32[2,1,256,128]{3,2,1,0:T(8,128)} %get-tuple-element.32), channel_id=1, source_target_pairs={{7,0},{8,1},{9,2},{10,3},{11,4},{12,5},{13,6},{14,7},{15,8},{16,9}... | collective-permute-start | bytes 786440 | tf_op jit(solution)/shard_map/ppermute | solution.py:529
  215.3 5.5 %collective-permute-start.12 = (f32[2,1,256,128]{3,2,1,0:T(8,128)}, f32[2,1,256,128]{3,2,1,0:T(8,128)S(1)}, u32[]{:S(2)}, u32[]{:S(2)}) collective-permute-start(f32[2,1,256,128]{3,2,1,0:T(8,128)} %get-tuple-element.47), channel_id=1, source_target_pairs={{1,0},{2,1},{3,2},{4,3},{5,4},{6,5},{7,6},{8,7},{9,8},{10,9},{11,1... | collective-permute-start | bytes 786440 | tf_op jit(solution)/shard_map/ppermute | solution.py:529
  220.9 16.6 %shard_map.47 = (f32[2,8,128,512]{3,2,1,0:T(8,128)}, f32[2,8,128,256]{3,2,1,0:T(8,128)}) custom-call(s32[3]{0:T(128)} %add_add_fusion.ints_ref, f32[8,256,768]{2,1,0:T(8,128)} %bitcast.3.y_ref, f32[2,4,256,128]{3,2,1,0:T(8,128)} %collective-permute-done.3.f0_ref, ...), custom_call_target="tpu_custom_call", output_to_operand_aliasing={{0}: (13, {}), {1}: (14, {})} | custom-call | flops 6000000000 | bytes 16000000 | tf_op jit(solution)/shard_map/pallas_call | solution.py:437
  237.5 0.7 copy-done.5
  238.2 7.7 %shard_map.48 = (f32[2,1,128,1024]{3,2,1,0:T(8,128)}, f32[2,8,128]{2,1,0:T(8,128)}) custom-call(s32[3]{0:T(128)} %add_add_fusion.1.ints_ref, f32[8,256,256]{2,1,0:T(8,128)} %bitcast.53, f32[2,4,256,128]{3,2,1,0:T(8,128)} %copy-done.1, f32[2,4,256,128]{3,2,1,0:T(8,128)} %collective-permute-done.9.f1_ref, f32[2,1,256,128]{3,2,1,0:T(8,128)} %copy-done.5, ...), custom_call_target="tpu_custom_call" | custom-call | flops 2000000000 | bytes 10000000 | tf_op jit(solution)/shard_map/pallas_call | solution.py:475
  245.9 0.7 copy-done.4
  246.6 7.7 %shard_map.49 = (f32[2,1,128,1024]{3,2,1,0:T(8,128)}, f32[2,8,128]{2,1,0:T(8,128)}) custom-call(s32[3]{0:T(128)} %add_add_fusion.ints_ref, f32[8,256,256]{2,1,0:T(8,128)} %bitcast.54, f32[2,4,256,128]{3,2,1,0:T(8,128)} %collective-permute-done.3.f0_ref, ...), custom_call_target="tpu_custom_call", output_to_operand_aliasing={{0}: (11, {}), {1}: (12, {})} | custom-call | flops 2000000000 | bytes 10000000 | tf_op jit(solution)/shard_map/pallas_call | solution.py:475
  254.3 1.3 slice_reduce_fusion
  (79 shorter events, 3.3 us)
Async XLA Ops:
  1.5 38.4 %collective-permute-start.2 = (s32[2]{0:T(128)S(1)}, s32[2]{0:T(128)S(1)}, u32[]{:S(2)}, u32[]{:S(2)}) collective-permute-start(s32[2]{0:T(128)S(1)} %get-tuple-element.199), channel_id=1, source_target_pairs={{3,0},{0,1},{1,2},{2,3},{7,4},{4,5},{5,6},{6,7},{11,8},{8,9},{9,10... | collective-permute-start | bytes 32 | tf_op jit(solution)/shard_map/ppermute | solution.py:534
  3.5 36.5 %collective-permute-start.1 = (s32[2]{0:T(128)S(1)}, s32[2]{0:T(128)S(1)}, u32[]{:S(2)}, u32[]{:S(2)}) collective-permute-start(s32[2]{0:T(128)S(1)} %get-tuple-element.199), channel_id=1, source_target_pairs={{2,0},{3,1},{0,2},{1,3},{6,4},{7,5},{4,6},{5,7},{10,8},{11,9},{8,1... | collective-permute-start | bytes 32 | tf_op jit(solution)/shard_map/ppermute | solution.py:534
  7.1 33.0 %collective-permute-start = (s32[2]{0:T(128)S(1)}, s32[2]{0:T(128)S(1)}, u32[]{:S(2)}, u32[]{:S(2)}) collective-permute-start(s32[2]{0:T(128)S(1)} %get-tuple-element.199), channel_id=1, source_target_pairs={{1,0},{2,1},{3,2},{0,3},{5,4},{6,5},{7,6},{4,7},{9,8},{10,9},{11,1... | collective-permute-start | bytes 32 | tf_op jit(solution)/shard_map/ppermute | solution.py:534
  23.0 5.5 %copy-start.7 = (s32[2,2,1]{1,2,0:T(1,128)S(1)}, s32[2,2,1]{1,2,0:T(1,128)}, u32[]{:S(2)}) copy-start(s32[2,2,1]{1,2,0:T(1,128)} %param.3) | copy-start | bytes 52
  23.0 89.5 %all-to-all-start = ((f32[4,2,256,768]{3,2,1,0:T(8,128)}), f32[4,2,256,768]{3,2,1,0:T(8,128)}, u32[]{:S(2)}, u32[]{:S(2)}) async-start(f32[4,2,256,768]{3,2,1,0:T(8,128)} %shard_map.41.refs_0_), calls=%async_computation | async-start | bytes 12582912 | tf_op jit(solution)/shard_map/all_to_all | solution.py:526
  40.3 6.7 %copy-start.6 = (s32[2,4]{1,0:T(2,128)}, s32[2,4]{1,0:T(2,128)S(1)}, u32[]{:S(2)}) copy-start(s32[2,4]{1,0:T(2,128)S(1)} %constant_dynamic-slice_fusion.off_ref) | copy-start | bytes 100
  62.8 78.8 %collective-permute-start.8 = (f32[2,4,256,128]{3,2,1,0:T(8,128)}, f32[2,4,256,128]{3,2,1,0:T(8,128)S(1)}, u32[]{:S(2)}, u32[]{:S(2)}) collective-permute-start(f32[2,4,256,128]{3,2,1,0:T(8,128)} %get-tuple-element.34), channel_id=1, source_target_pairs={{0,0},{1,1},{2,2},{4,4},{5,5},{6,6},{7,3},{8,8},{9,9},{10,10},{11,... | collective-permute-start | bytes 3145736 | tf_op jit(solution)/shard_map/ppermute | solution.py:529
  66.2 149.2 %collective-permute-start.3 = (f32[2,4,256,128]{3,2,1,0:T(8,128)}, f32[2,4,256,128]{3,2,1,0:T(8,128)}, u32[]{:S(2)}, u32[]{:S(2)}) collective-permute-start(f32[2,4,256,128]{3,2,1,0:T(8,128)} %get-tuple-element.30), channel_id=1, source_target_pairs={{4,0},{8,4},{9,1},{10,2},{11,3},{12,8},{13,5},{14,6},{15,7},{16,12... | collective-permute-start | bytes 3145736 | tf_op jit(solution)/shard_map/ppermute | solution.py:529
  70.0 63.4 %collective-permute-start.9 = (f32[2,4,256,128]{3,2,1,0:T(8,128)}, f32[2,4,256,128]{3,2,1,0:T(8,128)}, u32[]{:S(2)}, u32[]{:S(2)}) collective-permute-start(f32[2,4,256,128]{3,2,1,0:T(8,128)} %get-tuple-element.40), channel_id=1, source_target_pairs={{1,0},{2,1},{3,2},{4,3},{5,4},{6,5},{7,6},{8,7},{9,8},{10,9},{11,1... | collective-permute-start | bytes 3145736 | tf_op jit(solution)/shard_map/ppermute | solution.py:529
  76.5 59.2 %collective-permute-start.11 = (f32[2,4,256,128]{3,2,1,0:T(8,128)}, f32[2,4,256,128]{3,2,1,0:T(8,128)}, u32[]{:S(2)}, u32[]{:S(2)}) collective-permute-start(f32[2,4,256,128]{3,2,1,0:T(8,128)} %get-tuple-element.42), channel_id=1, source_target_pairs={{0,1},{1,2},{3,0},{4,5},{5,6},{6,3},{7,4},{8,9},{9,10},{10,7},{11,... | collective-permute-start | bytes 3145736 | tf_op jit(solution)/shard_map/ppermute | solution.py:529
  112.5 93.4 %all-to-all-start.1 = ((f32[4,2,256,256]{3,2,1,0:T(8,128)}), f32[4,2,256,256]{3,2,1,0:T(8,128)S(1)}, u32[]{:S(2)}, u32[]{:S(2)}) async-start(f32[4,2,256,256]{3,2,1,0:T(8,128)} %shard_map.42.refs_1_), calls=%async_computation.1 | async-start | bytes 4194304 | tf_op jit(solution)/shard_map/all_to_all | solution.py:526
  122.9 5.4 %copy-start.2 = (bf16[256,512]{1,0:T(8,128)(2,1)S(1)}, bf16[256,512]{1,0:T(8,128)(2,1)}, u32[]{:S(2)}) copy-start(bf16[256,512]{1,0:T(8,128)(2,1)} %get-tuple-element.100) | copy-start | bytes 786436
  122.9 5.4 %copy-start.3 = (bf16[256,512]{1,0:T(8,128)(2,1)S(1)}, bf16[256,512]{1,0:T(8,128)(2,1)}, u32[]{:S(2)}) copy-start(bf16[256,512]{1,0:T(8,128)(2,1)} %get-tuple-element.101) | copy-start | bytes 786436
  122.9 66.5 %collective-permute-start.10 = (f32[2,3,256,128]{3,2,1,0:T(8,128)}, f32[2,3,256,128]{3,2,1,0:T(8,128)}, u32[]{:S(2)}, u32[]{:S(2)}) collective-permute-start(f32[2,3,256,128]{3,2,1,0:T(8,128)} %get-tuple-element.41), channel_id=1, source_target_pairs={{1,0},{2,1},{3,2},{4,3},{5,4},{6,5},{7,6},{8,7},{9,8},{10,9},{11,1... | collective-permute-start | bytes 2359304 | tf_op jit(solution)/shard_map/ppermute | solution.py:529
  133.4 87.5 %collective-permute-start.4 = (f32[2,4,256,128]{3,2,1,0:T(8,128)}, f32[2,4,256,128]{3,2,1,0:T(8,128)}, u32[]{:S(2)}, u32[]{:S(2)}) collective-permute-start(f32[2,4,256,128]{3,2,1,0:T(8,128)} %get-tuple-element.31), channel_id=1, source_target_pairs={{5,0},{8,3},{9,4},{10,1},{11,2},{12,7},{13,8},{14,5},{15,6},{16,11... | collective-permute-start | bytes 3145736 | tf_op jit(solution)/shard_map/ppermute | solution.py:529
  135.7 85.2 %collective-permute-start.6 = (f32[2,4,256,128]{3,2,1,0:T(8,128)}, f32[2,4,256,128]{3,2,1,0:T(8,128)}, u32[]{:S(2)}, u32[]{:S(2)}) collective-permute-start(f32[2,4,256,128]{3,2,1,0:T(8,128)} %get-tuple-element.33), channel_id=1, source_target_pairs={{7,0},{8,1},{9,2},{10,3},{11,4},{12,5},{13,6},{14,7},{15,8},{16,9}... | collective-permute-start | bytes 3145736 | tf_op jit(solution)/shard_map/ppermute | solution.py:529
  141.6 47.8 %copy-start.1 = (f32[2,4,256,128]{3,2,1,0:T(8,128)}, f32[2,4,256,128]{3,2,1,0:T(8,128)S(1)}, u32[]{:S(2)}) copy-start(f32[2,4,256,128]{3,2,1,0:T(8,128)S(1)} %collective-permute-done.8.f0_ref) | copy-start | bytes 3145732
  141.6 79.3 %collective-permute-start.7 = (f32[2,3,256,128]{3,2,1,0:T(8,128)}, f32[2,3,256,128]{3,2,1,0:T(8,128)}, u32[]{:S(2)}, u32[]{:S(2)}) collective-permute-start(f32[2,3,256,128]{3,2,1,0:T(8,128)} %get-tuple-element.38), channel_id=1, source_target_pairs={{7,0},{8,1},{9,2},{10,3},{11,4},{12,5},{13,6},{14,7},{15,8},{16,9}... | collective-permute-start | bytes 2359304 | tf_op jit(solution)/shard_map/ppermute | solution.py:529
  205.8 1.4 copy-start
  210.5 35.4 %collective-permute-start.5 = (f32[2,1,256,128]{3,2,1,0:T(8,128)}, f32[2,1,256,128]{3,2,1,0:T(8,128)S(1)}, u32[]{:S(2)}, u32[]{:S(2)}) collective-permute-start(f32[2,1,256,128]{3,2,1,0:T(8,128)} %get-tuple-element.32), channel_id=1, source_target_pairs={{7,0},{8,1},{9,2},{10,3},{11,4},{12,5},{13,6},{14,7},{15,8},{16,9}... | collective-permute-start | bytes 786440 | tf_op jit(solution)/shard_map/ppermute | solution.py:529
  215.3 22.2 %collective-permute-start.12 = (f32[2,1,256,128]{3,2,1,0:T(8,128)}, f32[2,1,256,128]{3,2,1,0:T(8,128)S(1)}, u32[]{:S(2)}, u32[]{:S(2)}) collective-permute-start(f32[2,1,256,128]{3,2,1,0:T(8,128)} %get-tuple-element.47), channel_id=1, source_target_pairs={{1,0},{2,1},{3,2},{4,3},{5,4},{6,5},{7,6},{8,7},{9,8},{10,9},{11,1... | collective-permute-start | bytes 786440 | tf_op jit(solution)/shard_map/ppermute | solution.py:529
  237.5 0.7 copy-start.5
  245.9 0.7 copy-start.4

commit v8 on v7

--- a/solution.py
+++ b/solution.py
@@ -326,10 +326,15 @@
             r_ref[place] = jnp.where(lane == 0, moved, r_ref[place])
 
 
-def pair_core(offset, slab, y_ref, far_refs, a_ref, own_ref, r_ref, far_scr, valid):
+def arrange(slab, far_refs, far_scr):
     for turn in range(4):
         target = lax.rem(slab + turn, 4)
         far_scr[pl.ds(target, 1)] = far_refs[turn][:, 0][None]
+
+
+def pair_core(offset, slab, y_ref, far_refs, a_ref, own_ref, r_ref, far_scr, valid):
+    if far_refs is not None:
+        arrange(slab, far_refs, far_scr)
     for half in range(2):
         own_ref[:, half * 512 : (half + 1) * 512] = across(y_ref, half * 4, 4, offset, a_ref[...])
 
@@ -392,14 +397,21 @@
             fours_ref[0, z : z + 2] = part.reshape(2, A, 256)
 
 
-def small_pair_kernel(
-    ints_ref, y_ref, f0_ref, f1_ref, f2_ref, f3_ref, a_ref, ab_ref, v2_ref, odd_ref, fours_ref, *refs
-):
-    surf_ref, peak_ref, own_ref, r_ref, far_scr = refs[-5:]
-    valid = ints_ref[1].astype(F32)
-    pair_core(
-        ints_ref[0], ints_ref[2], y_ref, (f0_ref, f1_ref, f2_ref, f3_ref), a_ref, own_ref, r_ref, far_scr, valid
-    )
+def small_pair_kernel(own_ref_s, valid_ref, slab_ref, y_ref, *refs):
+    zero_refs, one_refs = refs[:4], refs[4:8]
+    a_ref, ab_ref, v2_ref, odd_ref, fours_ref, surf_ref, peak_ref, own_ref, r_ref, far_scr = refs[8:]
+    rnd = pl.program_id(0)
+    valid = valid_ref[rnd].astype(F32)
+
+    @pl.when(rnd == 0)
+    def _():
+        arrange(slab_ref[0], zero_refs, far_scr)
+
+    @pl.when(rnd == 1)
+    def _():
+        arrange(slab_ref[0], one_refs, far_scr)
+
+    pair_core(own_ref_s[rnd], None, y_ref, None, a_ref.at[0], own_ref, r_ref, far_scr, valid)
     for z, part in parts(ab_ref, r_ref, v2_ref):
         first = fours_ref[0, z : z + 2].reshape(2 * A, 256)
         odd = odd_ref[0, z : z + 2].reshape(2 * A, 512)
@@ -410,7 +422,7 @@
             surf_ref[0, 0] = x
         else:
             surf_ref[0, 0] = jnp.maximum(surf_ref[0, 0], x)
-    peak_ref[0] = jnp.broadcast_to(jnp.max(surf_ref[0, 0]), (8, 128))
+    peak_ref[rnd, 0] = jnp.max(surf_ref[0, 0])
 
 
 SCRATCH = [pltpu.VMEM((256, Z * 128), F32)] * 2 + [pltpu.VMEM((4, 2, 256, 128), F32)]
@@ -456,42 +468,36 @@
     )(ints, *args)
 
 
-def small_pair(rnd, ints, y, far, mat, ab, back2, odd, fours, before, interpret=False):
-    args = [y, *far, mat, ab, back2, odd, fours]
-    in_specs = [
-        whole((Z, 256, 256)),
-        *[pl.BlockSpec((2, 1, 256, 128), lambda r, *_, last=x.shape[1] - 1: (0, last, 0, 0)) for x in far],
-        whole((256, 768)),
-        whole((256, 768)),
-        whole((768, 256)),
-        pl.BlockSpec((1, Z, A, 512), lambda r, *_: (rnd, 0, 0, 0)),
-        pl.BlockSpec((1, Z, A, 256), lambda r, *_: (rnd, 0, 0, 0)),
-    ]
-    aliases = {}
-    if before is not None:
-        aliases = {len(args) + 1: 0, len(args) + 2: 1}
-        args += list(before)
-        in_specs += [pl.BlockSpec(memory_space=pl.ANY)] * 2
+def small_pair(own, valid, slab, y, far, mats, ab, back2, odd, fours, interpret=False):
+    flat = [*far[0], *far[1]]
     return pl.pallas_call(
         small_pair_kernel,
         out_shape=(
             jax.ShapeDtypeStruct((ROUNDS, 1, A, L), F32),
-            jax.ShapeDtypeStruct((ROUNDS, 8, 128), F32),
+            jax.ShapeDtypeStruct((ROUNDS, 1), F32),
         ),
         grid_spec=pltpu.PrefetchScalarGridSpec(
-            num_scalar_prefetch=1,
-            grid=(1,),
-            in_specs=in_specs,
+            num_scalar_prefetch=3,
+            grid=(ROUNDS,),
+            in_specs=[
+                whole((Z, 256, 256)),
+                *[pl.BlockSpec((2, 1, 256, 128), lambda r, *_, last=x.shape[1] - 1: (0, last, 0, 0)) for x in flat],
+                pl.BlockSpec((1, 256, 768), lambda r, *_: (r, 0, 0)),
+                whole((256, 768)),
+                whole((768, 256)),
+                pl.BlockSpec((1, Z, A, 512), lambda r, *_: (r, 0, 0, 0)),
+                pl.BlockSpec((1, Z, A, 256), lambda r, *_: (r, 0, 0, 0)),
+            ],
             out_specs=(
-                pl.BlockSpec((1, 1, A, L), lambda r, *_: (rnd, 0, 0, 0)),
-                pl.BlockSpec((1, 8, 128), lambda r, *_: (rnd, 0, 0)),
+                pl.BlockSpec((1, 1, A, L), lambda r, *_: (r, 0, 0, 0)),
+                pl.BlockSpec(memory_space=pltpu.SMEM),
             ),
             scratch_shapes=SCRATCH,
         ),
-        input_output_aliases=aliases,
-        cost_estimate=pl.CostEstimate(flops=2_000_000_000, bytes_accessed=10_000_000, transcendentals=300_000),
+        cost_estimate=pl.CostEstimate(flops=4_000_000_000, bytes_accessed=16_000_000, transcendentals=500_000),
         interpret=interpret,
-    )(ints, *args)
+        name="small_pairs",
+    )(own, valid, slab, y, *flat, mats, ab, back2, odd, fours)
 
 
 def after(*values):
@@ -542,12 +548,12 @@
     def shift_of(rnd, k):
         return 1 - k if rnd == 0 else -1 - k
 
-    plan = [(r, k) for r in range(ROUNDS) for k in DIRECT]
-    tiles = [(slab + shift_of(r, k) + slabs) % slabs for r, k in plan]
-    made = spectra([large_src, small_src], tiles, [r for r, _ in plan], tiles, given, mats)
     far = [[None] * slabs for _ in range(ROUNDS)]
-    for (r, k), x in zip(plan, made, strict=True):
-        far[r][k] = send(x, r, lambda s, r=r, k=k: (s + shift_of(r, k)) % slabs)
+    for r in range(ROUNDS):
+        tiles = [(slab + shift_of(r, k) + slabs) % slabs for k in DIRECT]
+        made = spectra([large_src, small_src], tiles, [r] * 3, tiles, given, mats)
+        for k, x in zip(DIRECT, made, strict=True):
+            far[r][k] = send(x, r, lambda s, r=r, k=k: (s + shift_of(r, k)) % slabs)
     SEEDS.append(made[0])
     valid = (
         jnp.logical_and(place % GC != GC - 1, place + 1 < size),
@@ -579,11 +585,17 @@
     sums = None
     for r in range(ROUNDS):
         sums = large_pair(r, ints[r], large_all, around(r, large_two), own_mats[r], ab, back1, back0, edges, sums)
-    out = None
-    for r in range(ROUNDS):
-        out = small_pair(r, ints[r], small_all, around(r, small_two), own_mats[r], ab, back2, *sums, out)
-    surface, peak = out
-    return surface, peak[:, 0, :1]
+    return small_pair(
+        jnp.stack(own),
+        jnp.stack([v.astype(jnp.int32) for v in valid]),
+        jnp.stack([slab]),
+        small_all,
+        [around(r, small_two) for r in range(ROUNDS)],
+        jnp.stack(own_mats),
+        ab,
+        back2,
+        *sums,
+    )
 
 
 def solution(mesh):

time: 257 us -> 251 us (0.977)
  waiting for transfers between devices: 71.4 us -> 48.8 us
  starting transfers between devices: 53.6 us -> 67.2 us
  other arithmetic: 36.8 us -> 40.6 us
    ppermute x10, starting transfers between devices: 38.1 us -> 51.6 us  [send(): lax.ppermute(x, ('tile', 'slab'), routes(groups, slabs, rnd, tile_of))]
    all_to_all x2, waiting for transfers between devices: 23.3 us -> 10.3 us  [gather(): return lax.all_to_all(x, 'slab', split_axis=0, concat_axis=1, tiled=True)[0]]
    ppermute x10, waiting for transfers between devices: 48.1 us -> 38.5 us  [send(): lax.ppermute(x, ('tile', 'slab'), routes(groups, slabs, rnd, tile_of))]
    pallas_call x2 -> x1, Pallas kernels: 15.4 us -> 11.5 us  [small_pair(): pl.pallas_call(small_pair_kernel, out_shape=(jax.ShapeDtypeStruct((ROUNDS...]
    another operation x0 -> x2, other arithmetic: none -> 2.93 us  [the longest x1 1.97 us: register(): jnp.stack(own)]
    pallas_call x3 -> x4, Pallas kernels: 20.7 us -> 23.2 us  [spectra(): pl.pallas_call(functools.partial(send_kernel, len(xs), steps), out_shape=...]
  transfers between devices with their start and end apart: 15 -> 15, of which waited for: 3 -> 2; matrix products, arithmetic and copies ran while one was open for 16% -> 18% of each run, Pallas kernels for 30% -> 29%
where the time goes in v8:
time: 251 us; the launch traced here: 250 us
  Pallas kernels  82.8 us (33%)
  starting transfers between devices  67.2 us (27%)
  waiting for transfers between devices  48.8 us (19%)
  other arithmetic  40.6 us (16%)
  local copies, waits for them, and re-layouts  8.98 us (4%)
    ppermute x10, starting transfers between devices, send(): lax.ppermute(x, ('tile', 'slab'), routes(groups, slabs, rnd, tile_of))  51.6 us
    ppermute x10, waiting for transfers between devices, send(): lax.ppermute(x, ('tile', 'slab'), routes(groups, slabs, rnd, tile_of))  38.5 us
    pallas_call x2, Pallas kernels, large_pair(): pl.pallas_call(large_pair_kernel, out_shape=(jax.ShapeDtypeStruct((ROUNDS...  32.9 us
    pallas_call x4, Pallas kernels, spectra(): pl.pallas_call(functools.partial(send_kernel, len(xs), steps), out_shape=...  23.2 us
    pallas_call x2, Pallas kernels, along(): pl.pallas_call(kernel, out_shape=jax.ShapeDtypeStruct((tiles, planes, 256...  15.1 us
    cos x5, other arithmetic, trig(): return (jnp.cos(angle), jnp.sin(angle))  11.9 us
    pallas_call x1, Pallas kernels, small_pair(): pl.pallas_call(small_pair_kernel, out_shape=(jax.ShapeDtypeStruct((ROUNDS...  11.5 us
    all_to_all x2, waiting for transfers between devices, gather(): return lax.all_to_all(x, 'slab', split_axis=0, concat_axis=1, tiled=True)[0]  10.3 us
  transfers between devices with their start and end apart: 15, of which 2 were waited for; matrix products, arithmetic and copies ran while one was open for 18% of the time, Pallas kernels for 29%

profile of v8, /device:TPU:6, one launch (start us, length us, event | category | flops | bytes accessed | tf_op | source)
XLA Modules:
  0.0 249.6 jit_solution(9395288459660124805)
XLA Ops:
  0.6 0.9 slice_reduce_fusion
  1.5 2.0 collective-permute-start.2
  3.5 3.6 %collective-permute-start.1 = (s32[2]{0:T(128)S(1)}, s32[2]{0:T(128)S(1)}, u32[]{:S(2)}, u32[]{:S(2)}) collective-permute-start(s32[2]{0:T(128)S(1)} %get-tuple-element.197), channel_id=1, source_target_pairs={{2,0},{3,1},{0,2},{1,3},{6,4},{7,5},{4,6},{5,7},{10,8},{11,9},{8,1... | collective-permute-start | bytes 32 | tf_op jit(solution)/shard_map/ppermute | solution.py:540
  7.1 1.0 collective-permute-start
  8.1 1.1 fusion.54
  9.3 0.8 pad_maximum_fusion.4.w0_ref
  10.1 2.1 fusion.29
  12.5 1.3 pad_maximum_fusion.1.w1_ref
  13.8 9.2 %shard_map.41.refs_0_ = f32[4,2,256,768]{3,2,1,0:T(8,128)} custom-call(f32[4,2,256,1024]{3,2,1,0:T(8,128)} %x_ref.3, bf16[1536,512]{1,0:T(8,128)(2,1)} %pad_maximum_fusion.1.w1_ref, bf16[768,256]{1,0:T(8,128)(2,1)} %pad_maximum_fusion.4.w0_ref), custom_call_target="tpu_custom_call" | custom-call | flops 4608000000 | bytes 14000000 | tf_op jit(solution)/shard_map/pallas_call | solution.py:211
  23.0 5.4 %all-to-all-start = ((f32[4,2,256,768]{3,2,1,0:T(8,128)}), f32[4,2,256,768]{3,2,1,0:T(8,128)}, u32[]{:S(2)}, u32[]{:S(2)}) async-start(f32[4,2,256,768]{3,2,1,0:T(8,128)} %shard_map.41.refs_0_), calls=%async_computation | async-start | bytes 12582912 | tf_op jit(solution)/shard_map/all_to_all | solution.py:532
  28.5 0.6 fusion.137
  29.1 1.2 add_add_fusion.1.ints_ref
  30.3 1.3 add_add_fusion.ints_ref
  31.6 2.0 pad_add_fusion
  34.0 0.8 pad_maximum_fusion.5.w2_ref
  34.7 5.9 %shard_map.42.refs_1_ = f32[4,2,256,256]{3,2,1,0:T(8,128)} custom-call(f32[4,2,256,1024]{3,2,1,0:T(8,128)} %x_ref.3, bf16[768,256]{1,0:T(8,128)(2,1)} %pad_maximum_fusion.5.w2_ref), custom_call_target="tpu_custom_call" | custom-call | flops 1536000000 | bytes 14000000 | tf_op jit(solution)/shard_map/pallas_call | solution.py:211
  40.6 0.6 pad_add_fusion.3
  41.2 0.7 pad_add_fusion.2
  42.4 0.7 fusion.136
  43.0 5.2 %fusion.111 = (f32[128]{0:T(128)S(1)}, f32[128]{0:T(128)S(1)}, f32[128]{0:T(128)S(1)}, f32[128]{0:T(128)S(1)}, f32[128]{0:T(128)S(1)}, /*index=5*/f32[128]{0:T(1...) fusion(s32[128]{0:T(128)S(1)} %iota.19, ...), kind=kLoop, calls=%fused_computation.323 | loop fusion | flops 14336 | bytes 8736 | tf_op jit(solution)/shard_map/cos | solution.py:46
  50.0 2.0 pad_maximum_fusion.refs_2_.refs_1_
  52.5 7.7 %shard_map.45 = (f32[2,4,256,128]{3,2,1,0:T(8,128)}, f32[2,4,256,128]{3,2,1,0:T(8,128)}, f32[2,4,256,128]{3,2,1,0:T(8,128)}) custom-call(s32[3]{0:T(128)} %get-tuple-element.237.src_ref.tile_ref, s32[3]{0:T(128)} %broadcast_35_round_ref.2.round_ref, s32[3]{0:T(128)} %get-tuple-element.237.src_ref.tile_ref, s32[2,4]{1,0:T(2,128)} %copy-done.6, ...), custom_call_target="tpu_custom_call" | custom-call | flops 1200000000 | bytes 9600000 | tf_op jit(solution)/shard_map/pallas_call | solution.py:265
  60.2 3.8 %collective-permute-start.7 = (f32[2,4,256,128]{3,2,1,0:T(8,128)}, f32[2,4,256,128]{3,2,1,0:T(8,128)S(1)}, u32[]{:S(2)}, u32[]{:S(2)}) collective-permute-start(f32[2,4,256,128]{3,2,1,0:T(8,128)} %get-tuple-element.30), channel_id=1, source_target_pairs={{4,0},{8,4},{9,1},{10,2},{11,3},{12,8},{13,5},{14,6},{15,7},{16,12... | collective-permute-start | bytes 3145736 | tf_op jit(solution)/shard_map/ppermute | solution.py:535
  64.0 1.4 fusion.105
  66.0 7.7 %shard_map.43 = (f32[2,4,256,128]{3,2,1,0:T(8,128)}, f32[2,4,256,128]{3,2,1,0:T(8,128)}, f32[2,4,256,128]{3,2,1,0:T(8,128)}) custom-call(s32[3]{0:T(128)} %get-tuple-element.236.src_ref.tile_ref, s32[3]{0:T(128)} %broadcast_36_round_ref.2.round_ref, s32[3]{0:T(128)} %get-tuple-element.236.src_ref.tile_ref, s32[2,4]{1,0:T(2,128)} %copy-done.6, ...), custom_call_target="tpu_custom_call" | custom-call | flops 1200000000 | bytes 9600000 | tf_op jit(solution)/shard_map/pallas_call | solution.py:265
  73.7 9.4 %collective-permute-start.3 = (f32[2,4,256,128]{3,2,1,0:T(8,128)}, f32[2,4,256,128]{3,2,1,0:T(8,128)}, u32[]{:S(2)}, u32[]{:S(2)}) collective-permute-start(f32[2,4,256,128]{3,2,1,0:T(8,128)} %get-tuple-element.26), channel_id=1, source_target_pairs={{0,0},{1,1},{2,2},{4,4},{5,5},{6,6},{7,3},{8,8},{9,9},{10,10},{11,... | collective-permute-start | bytes 3145736 | tf_op jit(solution)/shard_map/ppermute | solution.py:535
  83.2 1.9 collective-permute-start.4
  85.1 5.4 %collective-permute-start.6 = (f32[2,4,256,128]{3,2,1,0:T(8,128)}, f32[2,4,256,128]{3,2,1,0:T(8,128)}, u32[]{:S(2)}, u32[]{:S(2)}) collective-permute-start(f32[2,4,256,128]{3,2,1,0:T(8,128)} %get-tuple-element.29), channel_id=1, source_target_pairs={{0,1},{1,2},{3,0},{4,5},{5,6},{6,3},{7,4},{8,9},{9,10},{10,7},{11,... | collective-permute-start | bytes 3145736 | tf_op jit(solution)/shard_map/ppermute | solution.py:535
  90.7 0.6 fusion.62
  91.3 0.8 pad_maximum_fusion.8.ab_ref.refs_9_
  92.1 0.8 pad_maximum_fusion.7
  93.0 0.8 pad_maximum_fusion.6
  93.8 2.1 fusion.27
  96.0 0.8 reduce-precision_convert_fusion.2
  96.8 0.9 reduce-precision_convert_fusion.1
  97.7 0.8 fusion.10
  98.6 1.9 multiply_select_fusion.7
  100.5 0.7 reduce-precision_convert_fusion.3
  101.2 1.0 pad_maximum_fusion.3.refs_8_
  102.2 10.3 %all-to-all-done = f32[4,2,256,768]{3,2,1,0:T(8,128)} async-done(((f32[4,2,256,768]{3,2,1,0:T(8,128)}), f32[4,2,256,768]{3,2,1,0:T(8,128)}, u32[]{:S(2)}, u32[]{:S(2)}) %all-to-all-start) | async-done | bytes 6291488 | tf_op jit(solution)/shard_map/all_to_all | solution.py:532
  112.5 3.6 %all-to-all-start.1 = ((f32[4,2,256,256]{3,2,1,0:T(8,128)}), f32[4,2,256,256]{3,2,1,0:T(8,128)S(1)}, u32[]{:S(2)}, u32[]{:S(2)}) async-start(f32[4,2,256,256]{3,2,1,0:T(8,128)} %shard_map.42.refs_1_), calls=%async_computation.1 | async-start | bytes 4194304 | tf_op jit(solution)/shard_map/all_to_all | solution.py:532
  116.1 1.8 pad_maximum_fusion.10.v0_ref
  118.4 4.5 %shard_map.46 = (f32[2,3,256,128]{3,2,1,0:T(8,128)}, f32[2,3,256,128]{3,2,1,0:T(8,128)}) custom-call(s32[2]{0:T(128)} %get-tuple-element.246.src_ref, s32[2]{0:T(128)} %iota.23.round_ref, s32[2]{0:T(128)} %get-tuple-element.247.tile_ref, s32[2,4]{1,0:T(2,128)} %copy-done.6, f32[4,2,256,768]{3,2,1,0:T(8,128)} %bitcast.39.refs_0_, ...), custom_call_target="tpu_custom_call" | custom-call | flops 600000000 | bytes 4800000 | tf_op jit(solution)/shard_map/pallas_call | solution.py:265
  122.9 3.4 %collective-permute-start.12 = (f32[2,3,256,128]{3,2,1,0:T(8,128)}, f32[2,3,256,128]{3,2,1,0:T(8,128)}, u32[]{:S(2)}, u32[]{:S(2)}) collective-permute-start(f32[2,3,256,128]{3,2,1,0:T(8,128)} %get-tuple-element.39), channel_id=1, source_target_pairs={{1,0},{2,1},{3,2},{4,3},{5,4},{6,5},{7,6},{8,7},{9,8},{10,9},{11,1... | collective-permute-start | bytes 2359304 | tf_op jit(solution)/shard_map/ppermute | solution.py:535
  126.3 0.9 reduce-precision_convert_fusion.4
  127.3 1.0 maximum_bitcast_fusion.2
  128.4 7.3 %collective-permute-start.8 = (f32[2,4,256,128]{3,2,1,0:T(8,128)}, f32[2,4,256,128]{3,2,1,0:T(8,128)}, u32[]{:S(2)}, u32[]{:S(2)}) collective-permute-start(f32[2,4,256,128]{3,2,1,0:T(8,128)} %get-tuple-element.31), channel_id=1, source_target_pairs={{5,0},{8,3},{9,4},{10,1},{11,2},{12,7},{13,8},{14,5},{15,6},{16,11... | collective-permute-start | bytes 3145736 | tf_op jit(solution)/shard_map/ppermute | solution.py:535
  135.7 3.0 %collective-permute-start.10 = (f32[2,4,256,128]{3,2,1,0:T(8,128)}, f32[2,4,256,128]{3,2,1,0:T(8,128)}, u32[]{:S(2)}, u32[]{:S(2)}) collective-permute-start(f32[2,4,256,128]{3,2,1,0:T(8,128)} %get-tuple-element.33), channel_id=1, source_target_pairs={{7,0},{8,1},{9,2},{10,3},{11,4},{12,5},{13,6},{14,7},{15,8},{16,9}... | collective-permute-start | bytes 3145736 | tf_op jit(solution)/shard_map/ppermute | solution.py:535
  138.7 0.8 pad_maximum_fusion.9.refs_10_
  139.5 1.3 pad_maximum_fusion.2.v1_ref
  140.8 1.9 collective-permute-start.11
  142.7 0.7 fusion.56.flip_ref
  143.4 38.5 %collective-permute-done.12.f2_ref = f32[2,3,256,128]{3,2,1,0:T(8,128)} collective-permute-done((f32[2,3,256,128]{3,2,1,0:T(8,128)}, f32[2,3,256,128]{3,2,1,0:T(8,128)}, u32[]{:S(2)}, u32[]{:S(2)}) %collective-permute-start.12) | collective-permute-done | bytes 786464 | tf_op jit(solution)/shard_map/ppermute | solution.py:535
  181.9 16.4 %shard_map.47 = (f32[2,8,128,512]{3,2,1,0:T(8,128)}, f32[2,8,128,256]{3,2,1,0:T(8,128)}) custom-call(s32[3]{0:T(128)} %add_add_fusion.1.ints_ref, f32[8,256,768]{2,1,0:T(8,128)} %bitcast.5.y_ref, f32[2,4,256,128]{3,2,1,0:T(8,128)} %collective-permute-done.3.f0_ref.refs_0_, f32[2,4,256,128]{3,2,1,0:T(8,128)} %collective-permute-done.4.f1_ref.refs_1_, ...), custom_call_target="tpu_custom_call" | custom-call | flops 6000000000 | bytes 16000000 | tf_op jit(solution)/shard_map/pallas_call | solution.py:449
  198.4 0.6 iota.20.round_ref
  198.9 0.8 copy-done
  199.7 3.3 %shard_map.44 = (f32[2,1,256,128]{3,2,1,0:T(8,128)}, f32[2,1,256,128]{3,2,1,0:T(8,128)}) custom-call(s32[2]{0:T(128)} %get-tuple-element.246.src_ref, s32[2]{0:T(128)} %iota.20.round_ref, s32[2]{0:T(128)} %get-tuple-element.247.tile_ref, s32[2,4]{1,0:T(2,128)} %copy-done.6, f32[4,2,256,256]{3,2,1,0:T(8,128)} %copy-done, ...), custom_call_target="tpu_custom_call" | custom-call | flops 200000000 | bytes 1600000 | tf_op jit(solution)/shard_map/pallas_call | solution.py:265
  203.1 4.3 %collective-permute-start.5 = (f32[2,1,256,128]{3,2,1,0:T(8,128)}, f32[2,1,256,128]{3,2,1,0:T(8,128)S(1)}, u32[]{:S(2)}, u32[]{:S(2)}) collective-permute-start(f32[2,1,256,128]{3,2,1,0:T(8,128)} %get-tuple-element.28), channel_id=1, source_target_pairs={{1,0},{2,1},{3,2},{4,3},{5,4},{6,5},{7,6},{8,7},{9,8},{10,9},{11,1... | collective-permute-start | bytes 786440 | tf_op jit(solution)/shard_map/ppermute | solution.py:535
  207.4 11.2 %collective-permute-start.9 = (f32[2,1,256,128]{3,2,1,0:T(8,128)}, f32[2,1,256,128]{3,2,1,0:T(8,128)S(1)}, u32[]{:S(2)}, u32[]{:S(2)}) collective-permute-start(f32[2,1,256,128]{3,2,1,0:T(8,128)} %get-tuple-element.32), channel_id=1, source_target_pairs={{7,0},{8,1},{9,2},{10,3},{11,4},{12,5},{13,6},{14,7},{15,8},{16,9}... | collective-permute-start | bytes 786440 | tf_op jit(solution)/shard_map/ppermute | solution.py:535
  218.6 1.0 copy-done.1
  219.6 16.5 %shard_map.48 = (f32[2,8,128,512]{3,2,1,0:T(8,128)}, f32[2,8,128,256]{3,2,1,0:T(8,128)}) custom-call(s32[3]{0:T(128)} %add_add_fusion.ints_ref, f32[8,256,768]{2,1,0:T(8,128)} %bitcast.5.y_ref, f32[2,4,256,128]{3,2,1,0:T(8,128)} %copy-done.1, ...), custom_call_target="tpu_custom_call", output_to_operand_aliasing={{0}: (13, {}), {1}: (14, {})} | custom-call | flops 6000000000 | bytes 16000000 | tf_op jit(solution)/shard_map/pallas_call | solution.py:449
  236.1 0.7 copy-done.4
  236.9 11.5 %small_pairs.1 = (f32[2,1,128,1024]{3,2,1,0:T(8,128)}, f32[2,1]{1,0:T(2,128)}) custom-call(s32[2]{0:T(128)} %get-tuple-element.248.own_ref_s, s32[2]{0:T(128)} %get-tuple-element.249.valid_ref, s32[1]{0:T(128)} %bitcast.4.slab_ref, f32[8,256,256]{2,1,0:T(8,128)} %bitcast.56, f32[2,4,256,128]{3,2,1,0:T(8,128)} %collective-permute-done.3.f0_ref.refs_0_, ...), custom_call_target="tpu_custom_call" | custom-call | flops 4000000000 | bytes 16000000 | tf_op jit(solution)/shard_map/small_pairs/pallas_call | solution.py:473
  248.3 1.3 copy.23
  (83 shorter events, 4.9 us)
Async XLA Ops:
  1.5 40.4 %collective-permute-start.2 = (s32[2]{0:T(128)S(1)}, s32[2]{0:T(128)S(1)}, u32[]{:S(2)}, u32[]{:S(2)}) collective-permute-start(s32[2]{0:T(128)S(1)} %get-tuple-element.197), channel_id=1, source_target_pairs={{3,0},{0,1},{1,2},{2,3},{7,4},{4,5},{5,6},{6,7},{11,8},{8,9},{9,10... | collective-permute-start | bytes 32 | tf_op jit(solution)/shard_map/ppermute | solution.py:540
  3.5 38.5 %collective-permute-start.1 = (s32[2]{0:T(128)S(1)}, s32[2]{0:T(128)S(1)}, u32[]{:S(2)}, u32[]{:S(2)}) collective-permute-start(s32[2]{0:T(128)S(1)} %get-tuple-element.197), channel_id=1, source_target_pairs={{2,0},{3,1},{0,2},{1,3},{6,4},{7,5},{4,6},{5,7},{10,8},{11,9},{8,1... | collective-permute-start | bytes 32 | tf_op jit(solution)/shard_map/ppermute | solution.py:540
  7.1 35.0 %collective-permute-start = (s32[2]{0:T(128)S(1)}, s32[2]{0:T(128)S(1)}, u32[]{:S(2)}, u32[]{:S(2)}) collective-permute-start(s32[2]{0:T(128)S(1)} %get-tuple-element.197), channel_id=1, source_target_pairs={{1,0},{2,1},{3,2},{0,3},{5,4},{6,5},{7,6},{4,7},{9,8},{10,9},{11,1... | collective-permute-start | bytes 32 | tf_op jit(solution)/shard_map/ppermute | solution.py:540
  23.0 5.5 %copy-start.7 = (s32[2,2,1]{1,2,0:T(1,128)S(1)}, s32[2,2,1]{1,2,0:T(1,128)}, u32[]{:S(2)}) copy-start(s32[2,2,1]{1,2,0:T(1,128)} %param.3) | copy-start | bytes 52
  23.0 89.5 %all-to-all-start = ((f32[4,2,256,768]{3,2,1,0:T(8,128)}), f32[4,2,256,768]{3,2,1,0:T(8,128)}, u32[]{:S(2)}, u32[]{:S(2)}) async-start(f32[4,2,256,768]{3,2,1,0:T(8,128)} %shard_map.41.refs_0_), calls=%async_computation | async-start | bytes 12582912 | tf_op jit(solution)/shard_map/all_to_all | solution.py:532
  42.4 6.7 %copy-start.6 = (s32[2,4]{1,0:T(2,128)}, s32[2,4]{1,0:T(2,128)S(1)}, u32[]{:S(2)}) copy-start(s32[2,4]{1,0:T(2,128)S(1)} %constant_dynamic-slice_fusion.off_ref) | copy-start | bytes 100
  60.2 158.4 %collective-permute-start.7 = (f32[2,4,256,128]{3,2,1,0:T(8,128)}, f32[2,4,256,128]{3,2,1,0:T(8,128)S(1)}, u32[]{:S(2)}, u32[]{:S(2)}) collective-permute-start(f32[2,4,256,128]{3,2,1,0:T(8,128)} %get-tuple-element.30), channel_id=1, source_target_pairs={{4,0},{8,4},{9,1},{10,2},{11,3},{12,8},{13,5},{14,6},{15,7},{16,12... | collective-permute-start | bytes 3145736 | tf_op jit(solution)/shard_map/ppermute | solution.py:535
  73.7 54.7 %collective-permute-start.3 = (f32[2,4,256,128]{3,2,1,0:T(8,128)}, f32[2,4,256,128]{3,2,1,0:T(8,128)}, u32[]{:S(2)}, u32[]{:S(2)}) collective-permute-start(f32[2,4,256,128]{3,2,1,0:T(8,128)} %get-tuple-element.26), channel_id=1, source_target_pairs={{0,0},{1,1},{2,2},{4,4},{5,5},{6,6},{7,3},{8,8},{9,9},{10,10},{11,... | collective-permute-start | bytes 3145736 | tf_op jit(solution)/shard_map/ppermute | solution.py:535
  83.2 52.5 %collective-permute-start.4 = (f32[2,4,256,128]{3,2,1,0:T(8,128)}, f32[2,4,256,128]{3,2,1,0:T(8,128)}, u32[]{:S(2)}, u32[]{:S(2)}) collective-permute-start(f32[2,4,256,128]{3,2,1,0:T(8,128)} %get-tuple-element.27), channel_id=1, source_target_pairs={{1,0},{2,1},{3,2},{4,3},{5,4},{6,5},{7,6},{8,7},{9,8},{10,9},{11,1... | collective-permute-start | bytes 3145736 | tf_op jit(solution)/shard_map/ppermute | solution.py:535
  85.1 55.7 %collective-permute-start.6 = (f32[2,4,256,128]{3,2,1,0:T(8,128)}, f32[2,4,256,128]{3,2,1,0:T(8,128)}, u32[]{:S(2)}, u32[]{:S(2)}) collective-permute-start(f32[2,4,256,128]{3,2,1,0:T(8,128)} %get-tuple-element.29), channel_id=1, source_target_pairs={{0,1},{1,2},{3,0},{4,5},{5,6},{6,3},{7,4},{8,9},{9,10},{10,7},{11,... | collective-permute-start | bytes 3145736 | tf_op jit(solution)/shard_map/ppermute | solution.py:535
  112.5 85.9 %all-to-all-start.1 = ((f32[4,2,256,256]{3,2,1,0:T(8,128)}), f32[4,2,256,256]{3,2,1,0:T(8,128)S(1)}, u32[]{:S(2)}, u32[]{:S(2)}) async-start(f32[4,2,256,256]{3,2,1,0:T(8,128)} %shard_map.42.refs_1_), calls=%async_computation.1 | async-start | bytes 4194304 | tf_op jit(solution)/shard_map/all_to_all | solution.py:532
  122.9 5.4 %copy-start.2 = (bf16[256,512]{1,0:T(8,128)(2,1)S(1)}, bf16[256,512]{1,0:T(8,128)(2,1)}, u32[]{:S(2)}) copy-start(bf16[256,512]{1,0:T(8,128)(2,1)} %get-tuple-element.96) | copy-start | bytes 786436
  122.9 5.4 %copy-start.3 = (bf16[256,512]{1,0:T(8,128)(2,1)S(1)}, bf16[256,512]{1,0:T(8,128)(2,1)}, u32[]{:S(2)}) copy-start(bf16[256,512]{1,0:T(8,128)(2,1)} %get-tuple-element.97) | copy-start | bytes 786436
  122.9 59.0 %collective-permute-start.12 = (f32[2,3,256,128]{3,2,1,0:T(8,128)}, f32[2,3,256,128]{3,2,1,0:T(8,128)}, u32[]{:S(2)}, u32[]{:S(2)}) collective-permute-start(f32[2,3,256,128]{3,2,1,0:T(8,128)} %get-tuple-element.39), channel_id=1, source_target_pairs={{1,0},{2,1},{3,2},{4,3},{5,4},{6,5},{7,6},{8,7},{9,8},{10,9},{11,1... | collective-permute-start | bytes 2359304 | tf_op jit(solution)/shard_map/ppermute | solution.py:535
  128.4 79.0 %collective-permute-start.8 = (f32[2,4,256,128]{3,2,1,0:T(8,128)}, f32[2,4,256,128]{3,2,1,0:T(8,128)}, u32[]{:S(2)}, u32[]{:S(2)}) collective-permute-start(f32[2,4,256,128]{3,2,1,0:T(8,128)} %get-tuple-element.31), channel_id=1, source_target_pairs={{5,0},{8,3},{9,4},{10,1},{11,2},{12,7},{13,8},{14,5},{15,6},{16,11... | collective-permute-start | bytes 3145736 | tf_op jit(solution)/shard_map/ppermute | solution.py:535
  135.7 82.9 %collective-permute-start.10 = (f32[2,4,256,128]{3,2,1,0:T(8,128)}, f32[2,4,256,128]{3,2,1,0:T(8,128)}, u32[]{:S(2)}, u32[]{:S(2)}) collective-permute-start(f32[2,4,256,128]{3,2,1,0:T(8,128)} %get-tuple-element.33), channel_id=1, source_target_pairs={{7,0},{8,1},{9,2},{10,3},{11,4},{12,5},{13,6},{14,7},{15,8},{16,9}... | collective-permute-start | bytes 3145736 | tf_op jit(solution)/shard_map/ppermute | solution.py:535
  140.8 77.8 %collective-permute-start.11 = (f32[2,3,256,128]{3,2,1,0:T(8,128)}, f32[2,3,256,128]{3,2,1,0:T(8,128)}, u32[]{:S(2)}, u32[]{:S(2)}) collective-permute-start(f32[2,3,256,128]{3,2,1,0:T(8,128)} %get-tuple-element.37), channel_id=1, source_target_pairs={{7,0},{8,1},{9,2},{10,3},{11,4},{12,5},{13,6},{14,7},{15,8},{16,9}... | collective-permute-start | bytes 2359304 | tf_op jit(solution)/shard_map/ppermute | solution.py:535
  198.3 1.4 copy-start
  203.1 33.0 %collective-permute-start.5 = (f32[2,1,256,128]{3,2,1,0:T(8,128)}, f32[2,1,256,128]{3,2,1,0:T(8,128)S(1)}, u32[]{:S(2)}, u32[]{:S(2)}) collective-permute-start(f32[2,1,256,128]{3,2,1,0:T(8,128)} %get-tuple-element.28), channel_id=1, source_target_pairs={{1,0},{2,1},{3,2},{4,3},{5,4},{6,5},{7,6},{8,7},{9,8},{10,9},{11,1... | collective-permute-start | bytes 786440 | tf_op jit(solution)/shard_map/ppermute | solution.py:535
  207.4 28.7 %collective-permute-start.9 = (f32[2,1,256,128]{3,2,1,0:T(8,128)}, f32[2,1,256,128]{3,2,1,0:T(8,128)S(1)}, u32[]{:S(2)}, u32[]{:S(2)}) collective-permute-start(f32[2,1,256,128]{3,2,1,0:T(8,128)} %get-tuple-element.32), channel_id=1, source_target_pairs={{7,0},{8,1},{9,2},{10,3},{11,4},{12,5},{13,6},{14,7},{15,8},{16,9}... | collective-permute-start | bytes 786440 | tf_op jit(solution)/shard_map/ppermute | solution.py:535
  218.6 1.0 copy-start.1
  236.1 0.7 copy-start.4
  236.1 0.8 copy-start.5

commit v9 on v8

--- a/solution.py
+++ b/solution.py
@@ -422,7 +422,7 @@
             surf_ref[0, 0] = x
         else:
             surf_ref[0, 0] = jnp.maximum(surf_ref[0, 0], x)
-    peak_ref[rnd, 0] = jnp.max(surf_ref[0, 0])
+    peak_ref[0, rnd] = jnp.max(surf_ref[0, 0])
 
 
 SCRATCH = [pltpu.VMEM((256, Z * 128), F32)] * 2 + [pltpu.VMEM((4, 2, 256, 128), F32)]
@@ -474,7 +474,7 @@
         small_pair_kernel,
         out_shape=(
             jax.ShapeDtypeStruct((ROUNDS, 1, A, L), F32),
-            jax.ShapeDtypeStruct((ROUNDS, 1), F32),
+            jax.ShapeDtypeStruct((1, ROUNDS), F32),
         ),
         grid_spec=pltpu.PrefetchScalarGridSpec(
             num_scalar_prefetch=3,
@@ -549,6 +549,11 @@
         return 1 - k if rnd == 0 else -1 - k
 
     far = [[None] * slabs for _ in range(ROUNDS)]
+    two_tiles = [(slab + shift_of(r, 2) + slabs) % slabs for r in range(ROUNDS)]
+    made = spectra([small_src], two_tiles, [0, 1], two_tiles, given, mats)
+    small_two = [
+        send(x, r, lambda s, r=r: (s + shift_of(r, 2)) % slabs) for r, x in enumerate(made)
+    ]
     for r in range(ROUNDS):
         tiles = [(slab + shift_of(r, k) + slabs) % slabs for k in DIRECT]
         made = spectra([large_src, small_src], tiles, [r] * 3, tiles, given, mats)
@@ -577,7 +582,6 @@
         return [send(both[r], r, lambda s: s) for r in range(ROUNDS)]
 
     large_two = relayed(large_all)
-    small_two = relayed(small_all)
 
     def around(r, two):
         return [far[r][0], far[r][1], two[r], far[r][3]]
@@ -585,7 +589,7 @@
     sums = None
     for r in range(ROUNDS):
         sums = large_pair(r, ints[r], large_all, around(r, large_two), own_mats[r], ab, back1, back0, edges, sums)
-    return small_pair(
+    surface, peak = small_pair(
         jnp.stack(own),
         jnp.stack([v.astype(jnp.int32) for v in valid]),
         jnp.stack([slab]),
@@ -596,6 +600,7 @@
         back2,
         *sums,
     )
+    return surface, peak.reshape(ROUNDS, 1)
 
 
 def solution(mesh):

time: 251 us -> 236 us (0.940)
  the two profiles are of different devices: /device:TPU:6 before, /device:TPU:28 now
where the time goes in v9:
time: 236 us; the launch traced here: 234 us
  Pallas kernels  82.6 us (35%)
  waiting for transfers between devices  54.5 us (23%)
  starting transfers between devices  51.4 us (22%)
  other arithmetic  37 us (16%)
  local copies, waits for them, and re-layouts  7.37 us (3%)
    ppermute x10, waiting for transfers between devices, send(): lax.ppermute(x, ('tile', 'slab'), routes(groups, slabs, rnd, tile_of))  39.6 us
    ppermute x10, starting transfers between devices, send(): lax.ppermute(x, ('tile', 'slab'), routes(groups, slabs, rnd, tile_of))  35.8 us
    pallas_call x2, Pallas kernels, large_pair(): pl.pallas_call(large_pair_kernel, out_shape=(jax.ShapeDtypeStruct((ROUNDS...  32.9 us
    pallas_call x4, Pallas kernels, spectra(): pl.pallas_call(functools.partial(send_kernel, len(xs), steps), out_shape=...  23.1 us
    pallas_call x2, Pallas kernels, along(): pl.pallas_call(kernel, out_shape=jax.ShapeDtypeStruct((tiles, planes, 256...  15.1 us
    all_to_all x2, waiting for transfers between devices, gather(): return lax.all_to_all(x, 'slab', split_axis=0, concat_axis=1, tiled=True)[0]  14.9 us
    cos x5, other arithmetic, trig(): return (jnp.cos(angle), jnp.sin(angle))  11.7 us
    pallas_call x1, Pallas kernels, small_pair(): pl.pallas_call(small_pair_kernel, out_shape=(jax.ShapeDtypeStruct((ROUNDS...  11.5 us
  transfers between devices with their start and end apart: 15, of which 4 were waited for; matrix products, arithmetic and copies ran while one was open for 18% of the time, Pallas kernels for 30%

profile of v9, /device:TPU:28, one launch (start us, length us, event | category | flops | bytes accessed | tf_op | source)
XLA Modules:
  0.0 234.1 jit_solution(11765352833070888075)
XLA Ops:
  0.6 0.9 slice_reduce_fusion
  1.5 2.0 collective-permute-start.2
  3.5 3.6 %collective-permute-start.1 = (s32[2]{0:T(128)S(1)}, s32[2]{0:T(128)S(1)}, u32[]{:S(2)}, u32[]{:S(2)}) collective-permute-start(s32[2]{0:T(128)S(1)} %get-tuple-element.197), channel_id=1, source_target_pairs={{2,0},{3,1},{0,2},{1,3},{6,4},{7,5},{4,6},{5,7},{10,8},{11,9},{8,1... | collective-permute-start | bytes 32 | tf_op jit(solution)/shard_map/ppermute | solution.py:540
  7.1 1.0 collective-permute-start
  8.1 1.1 fusion.54
  9.3 0.8 pad_maximum_fusion.4.w0_ref
  10.1 2.1 fusion.29
  12.5 1.3 pad_maximum_fusion.1.w1_ref
  13.8 9.2 %shard_map.41.refs_0_ = f32[4,2,256,768]{3,2,1,0:T(8,128)} custom-call(f32[4,2,256,1024]{3,2,1,0:T(8,128)} %x_ref.3, bf16[1536,512]{1,0:T(8,128)(2,1)} %pad_maximum_fusion.1.w1_ref, bf16[768,256]{1,0:T(8,128)(2,1)} %pad_maximum_fusion.4.w0_ref), custom_call_target="tpu_custom_call" | custom-call | flops 4608000000 | bytes 14000000 | tf_op jit(solution)/shard_map/pallas_call | solution.py:211
  23.0 5.4 %all-to-all-start = ((f32[4,2,256,768]{3,2,1,0:T(8,128)}), f32[4,2,256,768]{3,2,1,0:T(8,128)}, u32[]{:S(2)}, u32[]{:S(2)}) async-start(f32[4,2,256,768]{3,2,1,0:T(8,128)} %shard_map.41.refs_0_), calls=%async_computation | async-start | bytes 12582912 | tf_op jit(solution)/shard_map/all_to_all | solution.py:532
  28.4 0.5 fusion.137
  29.0 0.7 pad_add_fusion.6.tile_ref
  29.6 1.3 add_add_fusion.1.ints_ref
  30.9 1.1 add_add_fusion.ints_ref
  32.1 1.9 pad_add_fusion
  34.3 0.8 pad_maximum_fusion.5.w2_ref
  35.1 5.9 %shard_map.42.refs_1_.refs_0_ = f32[4,2,256,256]{3,2,1,0:T(8,128)} custom-call(f32[4,2,256,1024]{3,2,1,0:T(8,128)} %x_ref.3, bf16[768,256]{1,0:T(8,128)(2,1)} %pad_maximum_fusion.5.w2_ref), custom_call_target="tpu_custom_call" | custom-call | flops 1536000000 | bytes 14000000 | tf_op jit(solution)/shard_map/pallas_call | solution.py:211
  41.0 0.6 pad_add_fusion.3
  41.6 0.7 pad_add_fusion.2
  42.7 0.7 fusion.136
  43.4 5.1 %fusion.111 = (f32[128]{0:T(128)S(1)}, f32[128]{0:T(128)S(1)}, f32[128]{0:T(128)S(1)}, f32[128]{0:T(128)S(1)}, f32[128]{0:T(128)S(1)}, /*index=5*/f32[128]{0:T(1...) fusion(s32[128]{0:T(128)S(1)} %iota.19, ...), kind=kLoop, calls=%fused_computation.324 | loop fusion | flops 14336 | bytes 8736 | tf_op jit(solution)/shard_map/cos | solution.py:46
  50.3 2.0 pad_maximum_fusion.refs_2_.refs_1_
  52.8 7.6 %shard_map.45 = (f32[2,4,256,128]{3,2,1,0:T(8,128)}, f32[2,4,256,128]{3,2,1,0:T(8,128)}, f32[2,4,256,128]{3,2,1,0:T(8,128)}) custom-call(s32[3]{0:T(128)} %get-tuple-element.237.src_ref.tile_ref, s32[3]{0:T(128)} %broadcast_35_round_ref.2.round_ref, s32[3]{0:T(128)} %get-tuple-element.237.src_ref.tile_ref, s32[2,4]{1,0:T(2,128)} %copy-done.3, ...), custom_call_target="tpu_custom_call" | custom-call | flops 1200000000 | bytes 9600000 | tf_op jit(solution)/shard_map/pallas_call | solution.py:265
  60.4 1.9 collective-permute-start.7
  62.4 1.3 fusion.105
  63.7 0.5 broadcast_36_round_ref.2.round_ref
  64.2 7.7 %shard_map.43 = (f32[2,4,256,128]{3,2,1,0:T(8,128)}, f32[2,4,256,128]{3,2,1,0:T(8,128)}, f32[2,4,256,128]{3,2,1,0:T(8,128)}) custom-call(s32[3]{0:T(128)} %get-tuple-element.236.src_ref.tile_ref, s32[3]{0:T(128)} %broadcast_36_round_ref.2.round_ref, s32[3]{0:T(128)} %get-tuple-element.236.src_ref.tile_ref, s32[2,4]{1,0:T(2,128)} %copy-done.3, ...), custom_call_target="tpu_custom_call" | custom-call | flops 1200000000 | bytes 9600000 | tf_op jit(solution)/shard_map/pallas_call | solution.py:265
  71.9 9.4 %collective-permute-start.3 = (f32[2,4,256,128]{3,2,1,0:T(8,128)}, f32[2,4,256,128]{3,2,1,0:T(8,128)}, u32[]{:S(2)}, u32[]{:S(2)}) collective-permute-start(f32[2,4,256,128]{3,2,1,0:T(8,128)} %get-tuple-element.28), channel_id=1, source_target_pairs={{0,0},{1,1},{2,2},{4,4},{5,5},{6,6},{7,3},{8,8},{9,9},{10,10},{11,... | collective-permute-start | bytes 3145736 | tf_op jit(solution)/shard_map/ppermute | solution.py:535
  81.4 1.9 collective-permute-start.4
  83.3 4.7 %collective-permute-start.6 = (f32[2,4,256,128]{3,2,1,0:T(8,128)}, f32[2,4,256,128]{3,2,1,0:T(8,128)}, u32[]{:S(2)}, u32[]{:S(2)}) collective-permute-start(f32[2,4,256,128]{3,2,1,0:T(8,128)} %get-tuple-element.31), channel_id=1, source_target_pairs={{0,1},{1,2},{3,0},{4,5},{5,6},{6,3},{7,4},{8,9},{9,10},{10,7},{11,... | collective-permute-start | bytes 3145736 | tf_op jit(solution)/shard_map/ppermute | solution.py:535
  88.1 1.1 multiply_select_fusion.7
  89.4 0.6 fusion.62
  90.1 0.8 pad_maximum_fusion.8.ab_ref.refs_9_
  90.8 0.8 pad_maximum_fusion.10.v0_ref
  91.7 0.8 pad_maximum_fusion.7
  92.5 2.1 fusion.27
  94.9 0.8 pad_maximum_fusion.6
  95.7 0.8 fusion.10
  96.6 1.0 pad_maximum_fusion.3.refs_8_
  97.5 14.9 %all-to-all-done = f32[4,2,256,768]{3,2,1,0:T(8,128)} async-done(((f32[4,2,256,768]{3,2,1,0:T(8,128)}), f32[4,2,256,768]{3,2,1,0:T(8,128)}, u32[]{:S(2)}, u32[]{:S(2)}) %all-to-all-start) | async-done | bytes 6291488 | tf_op jit(solution)/shard_map/all_to_all | solution.py:532
  112.4 0.5 iota.23.round_ref
  113.0 4.5 %shard_map.46 = (f32[2,3,256,128]{3,2,1,0:T(8,128)}, f32[2,3,256,128]{3,2,1,0:T(8,128)}) custom-call(s32[2]{0:T(128)} %get-tuple-element.247.src_ref, s32[2]{0:T(128)} %iota.23.round_ref, s32[2]{0:T(128)} %pad_add_fusion.6.tile_ref, s32[2,4]{1,0:T(2,128)} %copy-done.3, f32[4,2,256,768]{3,2,1,0:T(8,128)} %bitcast.39.refs_0_, ...), custom_call_target="tpu_custom_call" | custom-call | flops 600000000 | bytes 4800000 | tf_op jit(solution)/shard_map/pallas_call | solution.py:265
  117.4 1.9 collective-permute-start.12
  119.5 0.9 maximum_bitcast_fusion.3
  120.4 3.6 %all-to-all-start.1 = ((f32[4,2,256,256]{3,2,1,0:T(8,128)}), f32[4,2,256,256]{3,2,1,0:T(8,128)S(1)}, u32[]{:S(2)}, u32[]{:S(2)}) async-start(f32[4,2,256,256]{3,2,1,0:T(8,128)} %shard_map.42.refs_1_.refs_0_), calls=%async_computation.1 | async-start | bytes 4194304 | tf_op jit(solution)/shard_map/all_to_all | solution.py:532
  124.0 5.3 %collective-permute-start.8 = (f32[2,4,256,128]{3,2,1,0:T(8,128)}, f32[2,4,256,128]{3,2,1,0:T(8,128)}, u32[]{:S(2)}, u32[]{:S(2)}) collective-permute-start(f32[2,4,256,128]{3,2,1,0:T(8,128)} %get-tuple-element.33), channel_id=1, source_target_pairs={{5,0},{8,3},{9,4},{10,1},{11,2},{12,7},{13,8},{14,5},{15,6},{16,11... | collective-permute-start | bytes 3145736 | tf_op jit(solution)/shard_map/ppermute | solution.py:535
  129.3 3.9 %collective-permute-done.4.f1_ref.refs_1_ = f32[2,4,256,128]{3,2,1,0:T(8,128)} collective-permute-done((f32[2,4,256,128]{3,2,1,0:T(8,128)}, f32[2,4,256,128]{3,2,1,0:T(8,128)}, u32[]{:S(2)}, u32[]{:S(2)}) %collective-permute-start.4) | collective-permute-done | bytes 1048608 | tf_op jit(solution)/shard_map/ppermute | solution.py:535
  133.3 1.9 collective-permute-start.10
  135.2 0.8 pad_maximum_fusion.9.refs_10_
  136.0 0.5 iota.20.round_ref
  136.5 3.3 %shard_map.44 = (f32[2,1,256,128]{3,2,1,0:T(8,128)}, f32[2,1,256,128]{3,2,1,0:T(8,128)}) custom-call(s32[2]{0:T(128)} %get-tuple-element.246.src_ref.tile_ref, s32[2]{0:T(128)} %iota.20.round_ref, s32[2]{0:T(128)} %get-tuple-element.246.src_ref.tile_ref, s32[2,4]{1,0:T(2,128)} %copy-done.3, f32[4,2,256,256]{3,2,1,0:T(8,128)} %shard_map.42.refs_1_.refs_0_, ...), custom_call_target="tpu_custom_call" | custom-call | flops 200000000 | bytes 1600000 | tf_op jit(solution)/shard_map/pallas_call | solution.py:265
  139.8 2.4 %pad_maximum_fusion.2.v1_ref = bf16[2,768,512]{2,1,0:T(8,128)(2,1)} fusion(bf16[1,768,512]{2,1,0:T(8,128)(2,1)} %maximum_bitcast_fusion.3, bf16[1,768,512]{2,1,0:T(8,128)(2,1)S(1)} %maximum_bitcast_fusion.2), kind=kLoop, calls=%fused_computation.4 | loop fusion | flops 786432 | bytes 3145728 | tf_op jit(solution)/shard_map/stack | solution.py:86
  142.2 1.9 collective-permute-start.11
  144.1 0.7 fusion.56.flip_ref
  144.8 16.5 %collective-permute-done.12.f2_ref = f32[2,3,256,128]{3,2,1,0:T(8,128)} collective-permute-done((f32[2,3,256,128]{3,2,1,0:T(8,128)}, f32[2,3,256,128]{3,2,1,0:T(8,128)}, u32[]{:S(2)}, u32[]{:S(2)}) %collective-permute-start.12) | collective-permute-done | bytes 786464 | tf_op jit(solution)/shard_map/ppermute | solution.py:535
  161.3 4.7 %collective-permute-start.5 = (f32[2,1,256,128]{3,2,1,0:T(8,128)}, f32[2,1,256,128]{3,2,1,0:T(8,128)S(1)}, u32[]{:S(2)}, u32[]{:S(2)}) collective-permute-start(f32[2,1,256,128]{3,2,1,0:T(8,128)} %get-tuple-element.30), channel_id=1, source_target_pairs={{0,2},{2,0},{3,1},{4,6},{5,3},{6,4},{7,5},{8,10},{9,7},{10,8},{11,... | collective-permute-start | bytes 786440 | tf_op jit(solution)/shard_map/ppermute | solution.py:535
  166.0 16.4 %shard_map.47 = (f32[2,8,128,512]{3,2,1,0:T(8,128)}, f32[2,8,128,256]{3,2,1,0:T(8,128)}) custom-call(s32[3]{0:T(128)} %add_add_fusion.1.ints_ref, f32[8,256,768]{2,1,0:T(8,128)} %bitcast.5.y_ref, f32[2,4,256,128]{3,2,1,0:T(8,128)} %collective-permute-done.3.f0_ref.refs_0_, f32[2,4,256,128]{3,2,1,0:T(8,128)} %collective-permute-done.4.f1_ref.refs_1_, ...), custom_call_target="tpu_custom_call" | custom-call | flops 6000000000 | bytes 16000000 | tf_op jit(solution)/shard_map/pallas_call | solution.py:449
  182.5 19.1 %collective-permute-done.8.f1_ref.refs_5_ = f32[2,4,256,128]{3,2,1,0:T(8,128)} collective-permute-done((f32[2,4,256,128]{3,2,1,0:T(8,128)}, f32[2,4,256,128]{3,2,1,0:T(8,128)}, u32[]{:S(2)}, u32[]{:S(2)}) %collective-permute-start.8) | collective-permute-done | bytes 1048608 | tf_op jit(solution)/shard_map/ppermute | solution.py:535
  201.6 2.1 collective-permute-start.9
  203.7 0.9 copy-done.5
  204.6 16.4 %shard_map.48 = (f32[2,8,128,512]{3,2,1,0:T(8,128)}, f32[2,8,128,256]{3,2,1,0:T(8,128)}) custom-call(s32[3]{0:T(128)} %add_add_fusion.ints_ref, f32[8,256,768]{2,1,0:T(8,128)} %bitcast.5.y_ref, f32[2,4,256,128]{3,2,1,0:T(8,128)} %collective-permute-done.7.f0_ref.refs_4_, ...), custom_call_target="tpu_custom_call", output_to_operand_aliasing={{0}: (13, {}), {1}: (14, {})} | custom-call | flops 6000000000 | bytes 16000000 | tf_op jit(solution)/shard_map/pallas_call | solution.py:449
  221.1 0.6 copy-done.1
  221.9 0.7 copy-done
  222.6 11.5 %small_pairs.1 = (f32[2,1,128,1024]{3,2,1,0:T(8,128)}, f32[1,2]{1,0:T(1,128)}) custom-call(s32[2]{0:T(128)} %get-tuple-element.248.own_ref_s, s32[2]{0:T(128)} %get-tuple-element.249.valid_ref, s32[1]{0:T(128)} %bitcast.4.slab_ref, f32[8,256,256]{2,1,0:T(8,128)} %bitcast.57, f32[2,4,256,128]{3,2,1,0:T(8,128)} %collective-permute-done.3.f0_ref.refs_0_, ...), custom_call_target="tpu_custom_call" | custom-call | flops 4000000000 | bytes 16000000 | tf_op jit(solution)/shard_map/small_pairs/pallas_call | solution.py:473
  (79 shorter events, 4.1 us)
Async XLA Ops:
  1.5 40.8 %collective-permute-start.2 = (s32[2]{0:T(128)S(1)}, s32[2]{0:T(128)S(1)}, u32[]{:S(2)}, u32[]{:S(2)}) collective-permute-start(s32[2]{0:T(128)S(1)} %get-tuple-element.197), channel_id=1, source_target_pairs={{3,0},{0,1},{1,2},{2,3},{7,4},{4,5},{5,6},{6,7},{11,8},{8,9},{9,10... | collective-permute-start | bytes 32 | tf_op jit(solution)/shard_map/ppermute | solution.py:540
  3.5 38.9 %collective-permute-start.1 = (s32[2]{0:T(128)S(1)}, s32[2]{0:T(128)S(1)}, u32[]{:S(2)}, u32[]{:S(2)}) collective-permute-start(s32[2]{0:T(128)S(1)} %get-tuple-element.197), channel_id=1, source_target_pairs={{2,0},{3,1},{0,2},{1,3},{6,4},{7,5},{4,6},{5,7},{10,8},{11,9},{8,1... | collective-permute-start | bytes 32 | tf_op jit(solution)/shard_map/ppermute | solution.py:540
  7.1 35.4 %collective-permute-start = (s32[2]{0:T(128)S(1)}, s32[2]{0:T(128)S(1)}, u32[]{:S(2)}, u32[]{:S(2)}) collective-permute-start(s32[2]{0:T(128)S(1)} %get-tuple-element.197), channel_id=1, source_target_pairs={{1,0},{2,1},{3,2},{0,3},{5,4},{6,5},{7,6},{4,7},{9,8},{10,9},{11,1... | collective-permute-start | bytes 32 | tf_op jit(solution)/shard_map/ppermute | solution.py:540
  23.0 5.5 %copy-start.4 = (s32[2,2,1]{1,2,0:T(1,128)S(1)}, s32[2,2,1]{1,2,0:T(1,128)}, u32[]{:S(2)}) copy-start(s32[2,2,1]{1,2,0:T(1,128)} %param.3) | copy-start | bytes 52
  23.0 89.5 %all-to-all-start = ((f32[4,2,256,768]{3,2,1,0:T(8,128)}), f32[4,2,256,768]{3,2,1,0:T(8,128)}, u32[]{:S(2)}, u32[]{:S(2)}) async-start(f32[4,2,256,768]{3,2,1,0:T(8,128)} %shard_map.41.refs_0_), calls=%async_computation | async-start | bytes 12582912 | tf_op jit(solution)/shard_map/all_to_all | solution.py:532
  42.7 6.6 %copy-start.3 = (s32[2,4]{1,0:T(2,128)}, s32[2,4]{1,0:T(2,128)S(1)}, u32[]{:S(2)}) copy-start(s32[2,4]{1,0:T(2,128)S(1)} %constant_dynamic-slice_fusion.off_ref) | copy-start | bytes 100
  60.4 143.3 %collective-permute-start.7 = (f32[2,4,256,128]{3,2,1,0:T(8,128)}, f32[2,4,256,128]{3,2,1,0:T(8,128)}, u32[]{:S(2)}, u32[]{:S(2)}) collective-permute-start(f32[2,4,256,128]{3,2,1,0:T(8,128)} %get-tuple-element.32), channel_id=1, source_target_pairs={{4,0},{8,4},{9,1},{10,2},{11,3},{12,8},{13,5},{14,6},{15,7},{16,12... | collective-permute-start | bytes 3145736 | tf_op jit(solution)/shard_map/ppermute | solution.py:535
  71.9 52.1 %collective-permute-start.3 = (f32[2,4,256,128]{3,2,1,0:T(8,128)}, f32[2,4,256,128]{3,2,1,0:T(8,128)}, u32[]{:S(2)}, u32[]{:S(2)}) collective-permute-start(f32[2,4,256,128]{3,2,1,0:T(8,128)} %get-tuple-element.28), channel_id=1, source_target_pairs={{0,0},{1,1},{2,2},{4,4},{5,5},{6,6},{7,3},{8,8},{9,9},{10,10},{11,... | collective-permute-start | bytes 3145736 | tf_op jit(solution)/shard_map/ppermute | solution.py:535
  81.4 51.9 %collective-permute-start.4 = (f32[2,4,256,128]{3,2,1,0:T(8,128)}, f32[2,4,256,128]{3,2,1,0:T(8,128)}, u32[]{:S(2)}, u32[]{:S(2)}) collective-permute-start(f32[2,4,256,128]{3,2,1,0:T(8,128)} %get-tuple-element.29), channel_id=1, source_target_pairs={{1,0},{2,1},{3,2},{4,3},{5,4},{6,5},{7,6},{8,7},{9,8},{10,9},{11,1... | collective-permute-start | bytes 3145736 | tf_op jit(solution)/shard_map/ppermute | solution.py:535
  83.3 58.9 %collective-permute-start.6 = (f32[2,4,256,128]{3,2,1,0:T(8,128)}, f32[2,4,256,128]{3,2,1,0:T(8,128)}, u32[]{:S(2)}, u32[]{:S(2)}) collective-permute-start(f32[2,4,256,128]{3,2,1,0:T(8,128)} %get-tuple-element.31), channel_id=1, source_target_pairs={{0,1},{1,2},{3,0},{4,5},{5,6},{6,3},{7,4},{8,9},{9,10},{10,7},{11,... | collective-permute-start | bytes 3145736 | tf_op jit(solution)/shard_map/ppermute | solution.py:535
  117.4 43.9 %collective-permute-start.12 = (f32[2,3,256,128]{3,2,1,0:T(8,128)}, f32[2,3,256,128]{3,2,1,0:T(8,128)}, u32[]{:S(2)}, u32[]{:S(2)}) collective-permute-start(f32[2,3,256,128]{3,2,1,0:T(8,128)} %get-tuple-element.41), channel_id=1, source_target_pairs={{1,0},{2,1},{3,2},{4,3},{5,4},{6,5},{7,6},{8,7},{9,8},{10,9},{11,1... | collective-permute-start | bytes 2359304 | tf_op jit(solution)/shard_map/ppermute | solution.py:535
  120.4 100.7 %all-to-all-start.1 = ((f32[4,2,256,256]{3,2,1,0:T(8,128)}), f32[4,2,256,256]{3,2,1,0:T(8,128)S(1)}, u32[]{:S(2)}, u32[]{:S(2)}) async-start(f32[4,2,256,256]{3,2,1,0:T(8,128)} %shard_map.42.refs_1_.refs_0_), calls=%async_computation.1 | async-start | bytes 4194304 | tf_op jit(solution)/shard_map/all_to_all | solution.py:532
  124.0 77.5 %collective-permute-start.8 = (f32[2,4,256,128]{3,2,1,0:T(8,128)}, f32[2,4,256,128]{3,2,1,0:T(8,128)}, u32[]{:S(2)}, u32[]{:S(2)}) collective-permute-start(f32[2,4,256,128]{3,2,1,0:T(8,128)} %get-tuple-element.33), channel_id=1, source_target_pairs={{5,0},{8,3},{9,4},{10,1},{11,2},{12,7},{13,8},{14,5},{15,6},{16,11... | collective-permute-start | bytes 3145736 | tf_op jit(solution)/shard_map/ppermute | solution.py:535
  133.3 70.4 %collective-permute-start.10 = (f32[2,4,256,128]{3,2,1,0:T(8,128)}, f32[2,4,256,128]{3,2,1,0:T(8,128)}, u32[]{:S(2)}, u32[]{:S(2)}) collective-permute-start(f32[2,4,256,128]{3,2,1,0:T(8,128)} %get-tuple-element.35), channel_id=1, source_target_pairs={{7,0},{8,1},{9,2},{10,3},{11,4},{12,5},{13,6},{14,7},{15,8},{16,9}... | collective-permute-start | bytes 3145736 | tf_op jit(solution)/shard_map/ppermute | solution.py:535
  142.2 61.5 %collective-permute-start.11 = (f32[2,3,256,128]{3,2,1,0:T(8,128)}, f32[2,3,256,128]{3,2,1,0:T(8,128)S(1)}, u32[]{:S(2)}, u32[]{:S(2)}) collective-permute-start(f32[2,3,256,128]{3,2,1,0:T(8,128)} %get-tuple-element.39), channel_id=1, source_target_pairs={{7,0},{8,1},{9,2},{10,3},{11,4},{12,5},{13,6},{14,7},{15,8},{16,9}... | collective-permute-start | bytes 2359304 | tf_op jit(solution)/shard_map/ppermute | solution.py:535
  161.3 59.7 %collective-permute-start.5 = (f32[2,1,256,128]{3,2,1,0:T(8,128)}, f32[2,1,256,128]{3,2,1,0:T(8,128)S(1)}, u32[]{:S(2)}, u32[]{:S(2)}) collective-permute-start(f32[2,1,256,128]{3,2,1,0:T(8,128)} %get-tuple-element.30), channel_id=1, source_target_pairs={{0,2},{2,0},{3,1},{4,6},{5,3},{6,4},{7,5},{8,10},{9,7},{10,8},{11,... | collective-permute-start | bytes 786440 | tf_op jit(solution)/shard_map/ppermute | solution.py:535
  201.6 19.5 %collective-permute-start.9 = (f32[2,1,256,128]{3,2,1,0:T(8,128)}, f32[2,1,256,128]{3,2,1,0:T(8,128)S(1)}, u32[]{:S(2)}, u32[]{:S(2)}) collective-permute-start(f32[2,1,256,128]{3,2,1,0:T(8,128)} %get-tuple-element.34), channel_id=1, source_target_pairs={{6,0},{8,2},{9,3},{10,4},{11,1},{12,6},{13,7},{14,8},{15,5},{16,10... | collective-permute-start | bytes 786440 | tf_op jit(solution)/shard_map/ppermute | solution.py:535
  203.7 0.9 copy-start.5
  221.0 0.7 copy-start.1
  221.1 0.8 copy-start.2
  221.1 1.5 copy-start

commit v10 on v9

--- a/solution.py
+++ b/solution.py
@@ -571,17 +571,20 @@
     edges = edge_tables()
     back1, back0, back2 = odd_back(), fours_back(), twos_back()
     SEEDS.clear()
-    large_all, band_src = after(large_all, small_src)
-    small_all = gather(band_src)
 
     def relayed(x):
         whole_band = x.reshape(slabs, 2, 256, x.shape[2])
         both = spectra(
             [whole_band], [(slab + 1) % slabs, (slab + slabs - 1) % slabs], [0, 1], [slab, slab], given, mats
         )
-        return [send(both[r], r, lambda s: s) for r in range(ROUNDS)]
+        out = []
+        for r in range(ROUNDS):
+            out.append(send(both[r], r, lambda s: s))
+        return out
 
     large_two = relayed(large_all)
+    large_two[0], band_src = after(large_two[0], small_src)
+    small_all = gather(band_src)
 
     def around(r, two):
         return [far[r][0], far[r][1], two[r], far[r][3]]

time: 236 us -> 247 us (1.047)
  the two profiles are of different devices: /device:TPU:28 before, /device:TPU:26 now
where the time goes in v10:
time: 247 us; the launch traced here: 246 us
  Pallas kernels  82.7 us (33%)
  waiting for transfers between devices  63.6 us (26%)
  starting transfers between devices  53.9 us (22%)
  other arithmetic  37.1 us (15%)
  local copies, waits for them, and re-layouts  7.33 us (3%)
    ppermute x10, waiting for transfers between devices, send(): lax.ppermute(x, ('tile', 'slab'), routes(groups, slabs, rnd, tile_of))  46.2 us
    ppermute x10, starting transfers between devices, send(): lax.ppermute(x, ('tile', 'slab'), routes(groups, slabs, rnd, tile_of))  38.3 us
    pallas_call x2, Pallas kernels, large_pair(): pl.pallas_call(large_pair_kernel, out_shape=(jax.ShapeDtypeStruct((ROUNDS...  32.9 us
    pallas_call x4, Pallas kernels, spectra(): pl.pallas_call(functools.partial(send_kernel, len(xs), steps), out_shape=...  23.2 us
    all_to_all x2, waiting for transfers between devices, gather(): return lax.all_to_all(x, 'slab', split_axis=0, concat_axis=1, tiled=True)[0]  17.5 us
    pallas_call x2, Pallas kernels, along(): pl.pallas_call(kernel, out_shape=jax.ShapeDtypeStruct((tiles, planes, 256...  15.1 us
    cos x5, other arithmetic, trig(): return (jnp.cos(angle), jnp.sin(angle))  11.8 us
    pallas_call x1, Pallas kernels, small_pair(): pl.pallas_call(small_pair_kernel, out_shape=(jax.ShapeDtypeStruct((ROUNDS...  11.5 us
  transfers between devices with their start and end apart: 15, of which 6 were waited for; matrix products, arithmetic and copies ran while one was open for 17% of the time, Pallas kernels for 29%

profile of v10, /device:TPU:26, one launch (start us, length us, event | category | flops | bytes accessed | tf_op | source)
XLA Modules:
  0.0 245.9 jit_solution(5549622867653231671)
XLA Ops:
  0.6 0.9 slice_reduce_fusion
  1.5 2.0 collective-permute-start.2
  3.5 3.6 %collective-permute-start.1 = (s32[2]{0:T(128)S(1)}, s32[2]{0:T(128)S(1)}, u32[]{:S(2)}, u32[]{:S(2)}) collective-permute-start(s32[2]{0:T(128)S(1)} %get-tuple-element.201), channel_id=1, source_target_pairs={{2,0},{3,1},{0,2},{1,3},{6,4},{7,5},{4,6},{5,7},{10,8},{11,9},{8,1... | collective-permute-start | bytes 32 | tf_op jit(solution)/shard_map/ppermute | solution.py:540
  7.1 1.0 collective-permute-start
  8.1 1.1 fusion.54
  9.3 0.8 pad_maximum_fusion.4.w0_ref
  10.1 2.1 fusion.29
  12.5 1.3 pad_maximum_fusion.1.w1_ref
  13.8 9.2 %shard_map.41.refs_0_ = f32[4,2,256,768]{3,2,1,0:T(8,128)} custom-call(f32[4,2,256,1024]{3,2,1,0:T(8,128)} %x_ref.3, bf16[1536,512]{1,0:T(8,128)(2,1)} %pad_maximum_fusion.1.w1_ref, bf16[768,256]{1,0:T(8,128)(2,1)} %pad_maximum_fusion.4.w0_ref), custom_call_target="tpu_custom_call" | custom-call | flops 4608000000 | bytes 14000000 | tf_op jit(solution)/shard_map/pallas_call | solution.py:211
  23.0 5.4 %all-to-all-start = ((f32[4,2,256,768]{3,2,1,0:T(8,128)}), f32[4,2,256,768]{3,2,1,0:T(8,128)}, u32[]{:S(2)}, u32[]{:S(2)}) async-start(f32[4,2,256,768]{3,2,1,0:T(8,128)} %shard_map.41.refs_0_), calls=%async_computation | async-start | bytes 12582912 | tf_op jit(solution)/shard_map/all_to_all | solution.py:532
  28.5 0.5 fusion.137
  29.0 0.7 pad_add_fusion.5.src_ref.tile_ref
  29.7 0.6 pad_add_fusion.2
  30.3 1.3 add_add_fusion.1.ints_ref
  31.6 1.2 add_add_fusion.ints_ref
  32.8 1.9 pad_add_fusion
  35.0 0.8 pad_maximum_fusion.5.w2_ref
  35.8 5.9 %shard_map.43.refs_1_.refs_0_ = f32[4,2,256,256]{3,2,1,0:T(8,128)} custom-call(f32[4,2,256,1024]{3,2,1,0:T(8,128)} %x_ref.3, bf16[768,256]{1,0:T(8,128)(2,1)} %pad_maximum_fusion.5.w2_ref), custom_call_target="tpu_custom_call" | custom-call | flops 1536000000 | bytes 14000000 | tf_op jit(solution)/shard_map/pallas_call | solution.py:211
  41.7 0.6 pad_add_fusion.4
  42.8 0.7 fusion.136
  43.5 5.1 %fusion.111 = (f32[128]{0:T(128)S(1)}, f32[128]{0:T(128)S(1)}, f32[128]{0:T(128)S(1)}, f32[128]{0:T(128)S(1)}, f32[128]{0:T(128)S(1)}, /*index=5*/f32[128]{0:T(1...) fusion(s32[128]{0:T(128)S(1)} %iota.20, ...), kind=kLoop, calls=%fused_computation.324 | loop fusion | flops 14336 | bytes 8736 | tf_op jit(solution)/shard_map/cos | solution.py:46
  50.4 2.0 pad_maximum_fusion.refs_1_.refs_2_
  52.9 7.6 %shard_map.46 = (f32[2,4,256,128]{3,2,1,0:T(8,128)}, f32[2,4,256,128]{3,2,1,0:T(8,128)}, f32[2,4,256,128]{3,2,1,0:T(8,128)}) custom-call(s32[3]{0:T(128)} %get-tuple-element.247.src_ref.tile_ref, s32[3]{0:T(128)} %broadcast_35_round_ref.2.round_ref, s32[3]{0:T(128)} %get-tuple-element.247.src_ref.tile_ref, s32[2,4]{1,0:T(2,128)} %copy-done.3, ...), custom_call_target="tpu_custom_call" | custom-call | flops 1200000000 | bytes 9600000 | tf_op jit(solution)/shard_map/pallas_call | solution.py:265
  60.5 1.9 collective-permute-start.8
  62.5 1.3 fusion.105
  63.9 0.5 broadcast_36_round_ref.2.round_ref
  64.4 7.7 %shard_map.44 = (f32[2,4,256,128]{3,2,1,0:T(8,128)}, f32[2,4,256,128]{3,2,1,0:T(8,128)}, f32[2,4,256,128]{3,2,1,0:T(8,128)}) custom-call(s32[3]{0:T(128)} %get-tuple-element.246.src_ref.tile_ref, s32[3]{0:T(128)} %broadcast_36_round_ref.2.round_ref, s32[3]{0:T(128)} %get-tuple-element.246.src_ref.tile_ref, s32[2,4]{1,0:T(2,128)} %copy-done.3, ...), custom_call_target="tpu_custom_call" | custom-call | flops 1200000000 | bytes 9600000 | tf_op jit(solution)/shard_map/pallas_call | solution.py:265
  72.1 9.5 %collective-permute-start.4 = (f32[2,4,256,128]{3,2,1,0:T(8,128)}, f32[2,4,256,128]{3,2,1,0:T(8,128)}, u32[]{:S(2)}, u32[]{:S(2)}) collective-permute-start(f32[2,4,256,128]{3,2,1,0:T(8,128)} %get-tuple-element.29), channel_id=1, source_target_pairs={{0,0},{1,1},{2,2},{4,4},{5,5},{6,6},{7,3},{8,8},{9,9},{10,10},{11,... | collective-permute-start | bytes 3145736 | tf_op jit(solution)/shard_map/ppermute | solution.py:535
  81.6 1.9 collective-permute-start.5
  83.5 4.7 %collective-permute-start.7 = (f32[2,4,256,128]{3,2,1,0:T(8,128)}, f32[2,4,256,128]{3,2,1,0:T(8,128)}, u32[]{:S(2)}, u32[]{:S(2)}) collective-permute-start(f32[2,4,256,128]{3,2,1,0:T(8,128)} %get-tuple-element.32), channel_id=1, source_target_pairs={{0,1},{1,2},{3,0},{4,5},{5,6},{6,3},{7,4},{8,9},{9,10},{10,7},{11,... | collective-permute-start | bytes 3145736 | tf_op jit(solution)/shard_map/ppermute | solution.py:535
  88.3 1.1 multiply_select_fusion.7
  89.6 0.6 fusion.62
  90.3 0.8 pad_maximum_fusion.8.ab_ref.refs_9_
  91.0 0.8 pad_maximum_fusion.10.v0_ref
  91.8 2.1 fusion.27
  94.2 0.8 pad_maximum_fusion.7
  95.0 17.5 %all-to-all-done.refs_0_ = f32[4,2,256,768]{3,2,1,0:T(8,128)} async-done(((f32[4,2,256,768]{3,2,1,0:T(8,128)}), f32[4,2,256,768]{3,2,1,0:T(8,128)}, u32[]{:S(2)}, u32[]{:S(2)}) %all-to-all-start) | async-done | bytes 6291488 | tf_op jit(solution)/shard_map/all_to_all | solution.py:532
  113.0 4.5 %shard_map.42 = (f32[2,3,256,128]{3,2,1,0:T(8,128)}, f32[2,3,256,128]{3,2,1,0:T(8,128)}) custom-call(s32[2]{0:T(128)} %get-tuple-element.244.src_ref, s32[2]{0:T(128)} %iota.17.round_ref, s32[2]{0:T(128)} %get-tuple-element.245.tile_ref, s32[2,4]{1,0:T(2,128)} %copy-done.3, f32[4,2,256,768]{3,2,1,0:T(8,128)} %all-to-all-done.refs_0_, ...), custom_call_target="tpu_custom_call" | custom-call | flops 600000000 | bytes 4800000 | tf_op jit(solution)/shard_map/pallas_call | solution.py:265
  117.5 1.9 collective-permute-start.3
  119.5 0.8 pad_maximum_fusion.6
  120.3 0.8 fusion.10
  121.2 0.9 pad_maximum_fusion.3.refs_8_
  122.2 0.9 maximum_bitcast_fusion.3
  123.1 24.9 %collective-permute-done.3.f2_ref = f32[2,3,256,128]{3,2,1,0:T(8,128)} collective-permute-done((f32[2,3,256,128]{3,2,1,0:T(8,128)}, f32[2,3,256,128]{3,2,1,0:T(8,128)}, u32[]{:S(2)}, u32[]{:S(2)}) %collective-permute-start.3) | collective-permute-done | bytes 786464 | tf_op jit(solution)/shard_map/ppermute | solution.py:535
  148.0 1.9 collective-permute-start.9
  149.9 3.6 %all-to-all-start.1 = ((f32[4,2,256,256]{3,2,1,0:T(8,128)}), f32[4,2,256,256]{3,2,1,0:T(8,128)S(1)}, u32[]{:S(2)}, u32[]{:S(2)}) async-start(f32[4,2,256,256]{3,2,1,0:T(8,128)} %shard_map.43.refs_1_.refs_0_), calls=%async_computation.1 | async-start | bytes 4194304 | tf_op jit(solution)/shard_map/all_to_all | solution.py:532
  153.6 1.9 collective-permute-start.11
  155.5 0.8 pad_maximum_fusion.9.refs_10_
  156.8 3.3 %shard_map.45 = (f32[2,1,256,128]{3,2,1,0:T(8,128)}, f32[2,1,256,128]{3,2,1,0:T(8,128)}) custom-call(s32[2]{0:T(128)} %pad_add_fusion.5.src_ref.tile_ref, s32[2]{0:T(128)} %iota.21.round_ref, s32[2]{0:T(128)} %pad_add_fusion.5.src_ref.tile_ref, s32[2,4]{1,0:T(2,128)} %copy-done.3, f32[4,2,256,256]{3,2,1,0:T(8,128)} %shard_map.43.refs_1_.refs_0_, ...), custom_call_target="tpu_custom_call" | custom-call | flops 200000000 | bytes 1600000 | tf_op jit(solution)/shard_map/pallas_call | solution.py:265
  160.1 2.4 pad_maximum_fusion.2.v1_ref
  162.6 2.3 collective-permute-start.12
  164.9 0.7 fusion.56.flip_ref
  165.6 5.0 %collective-permute-start.6 = (f32[2,1,256,128]{3,2,1,0:T(8,128)}, f32[2,1,256,128]{3,2,1,0:T(8,128)S(1)}, u32[]{:S(2)}, u32[]{:S(2)}) collective-permute-start(f32[2,1,256,128]{3,2,1,0:T(8,128)} %get-tuple-element.31), channel_id=1, source_target_pairs={{0,2},{2,0},{3,1},{4,6},{5,3},{6,4},{7,5},{8,10},{9,7},{10,8},{11,... | collective-permute-start | bytes 786440 | tf_op jit(solution)/shard_map/ppermute | solution.py:535
  170.6 16.5 %shard_map.47 = (f32[2,8,128,512]{3,2,1,0:T(8,128)}, f32[2,8,128,256]{3,2,1,0:T(8,128)}) custom-call(s32[3]{0:T(128)} %add_add_fusion.1.ints_ref, f32[8,256,768]{2,1,0:T(8,128)} %bitcast.38.y_ref, f32[2,4,256,128]{3,2,1,0:T(8,128)} %collective-permute-done.4.f0_ref.refs_0_, f32[2,4,256,128]{3,2,1,0:T(8,128)} %collective-permute-done.5.f1_ref.refs_1_, ...), custom_call_target="tpu_custom_call" | custom-call | flops 6000000000 | bytes 16000000 | tf_op jit(solution)/shard_map/pallas_call | solution.py:449
  187.1 7.2 %collective-permute-start.10 = (f32[2,1,256,128]{3,2,1,0:T(8,128)}, f32[2,1,256,128]{3,2,1,0:T(8,128)S(1)}, u32[]{:S(2)}, u32[]{:S(2)}) collective-permute-start(f32[2,1,256,128]{3,2,1,0:T(8,128)} %get-tuple-element.35), channel_id=1, source_target_pairs={{6,0},{8,2},{9,3},{10,4},{11,1},{12,6},{13,7},{14,8},{15,5},{16,10... | collective-permute-start | bytes 786440 | tf_op jit(solution)/shard_map/ppermute | solution.py:535
  194.3 9.9 %collective-permute-done.11.f3_ref.refs_7_ = f32[2,4,256,128]{3,2,1,0:T(8,128)} collective-permute-done((f32[2,4,256,128]{3,2,1,0:T(8,128)}, f32[2,4,256,128]{3,2,1,0:T(8,128)}, u32[]{:S(2)}, u32[]{:S(2)}) %collective-permute-start.11) | collective-permute-done | bytes 1048608 | tf_op jit(solution)/shard_map/ppermute | solution.py:535
  204.2 9.0 %collective-permute-done.12.f2_ref = f32[2,3,256,128]{3,2,1,0:T(8,128)S(1)} collective-permute-done((f32[2,3,256,128]{3,2,1,0:T(8,128)}, f32[2,3,256,128]{3,2,1,0:T(8,128)S(1)}, u32[]{:S(2)}, u32[]{:S(2)}) %collective-permute-start.12) | collective-permute-done | bytes 786464 | tf_op jit(solution)/shard_map/ppermute | solution.py:535
  213.1 0.9 copy-done.5
  214.0 16.4 %shard_map.48 = (f32[2,8,128,512]{3,2,1,0:T(8,128)}, f32[2,8,128,256]{3,2,1,0:T(8,128)}) custom-call(s32[3]{0:T(128)} %add_add_fusion.ints_ref, f32[8,256,768]{2,1,0:T(8,128)} %bitcast.38.y_ref, f32[2,4,256,128]{3,2,1,0:T(8,128)} %collective-permute-done.8.f0_ref.refs_4_, ...), custom_call_target="tpu_custom_call", output_to_operand_aliasing={{0}: (13, {}), {1}: (14, {})} | custom-call | flops 6000000000 | bytes 16000000 | tf_op jit(solution)/shard_map/pallas_call | solution.py:449
  230.4 1.1 collective-permute-done.6.refs_2_
  231.5 1.4 collective-permute-done.10.refs_6_
  232.9 0.7 copy-done.2
  233.6 0.7 copy-done
  234.3 11.5 %small_pairs.1 = (f32[2,1,128,1024]{3,2,1,0:T(8,128)}, f32[1,2]{1,0:T(1,128)}) custom-call(s32[2]{0:T(128)} %get-tuple-element.248.own_ref_s, s32[2]{0:T(128)} %get-tuple-element.249.valid_ref, s32[1]{0:T(128)} %bitcast.4.slab_ref, f32[8,256,256]{2,1,0:T(8,128)} %bitcast.56, f32[2,4,256,128]{3,2,1,0:T(8,128)} %collective-permute-done.4.f0_ref.refs_0_, ...), custom_call_target="tpu_custom_call" | custom-call | flops 4000000000 | bytes 16000000 | tf_op jit(solution)/shard_map/small_pairs/pallas_call | solution.py:473
  (79 shorter events, 5.0 us)
Async XLA Ops:
  1.5 40.8 %collective-permute-start.2 = (s32[2]{0:T(128)S(1)}, s32[2]{0:T(128)S(1)}, u32[]{:S(2)}, u32[]{:S(2)}) collective-permute-start(s32[2]{0:T(128)S(1)} %get-tuple-element.201), channel_id=1, source_target_pairs={{3,0},{0,1},{1,2},{2,3},{7,4},{4,5},{5,6},{6,7},{11,8},{8,9},{9,10... | collective-permute-start | bytes 32 | tf_op jit(solution)/shard_map/ppermute | solution.py:540
  3.5 38.9 %collective-permute-start.1 = (s32[2]{0:T(128)S(1)}, s32[2]{0:T(128)S(1)}, u32[]{:S(2)}, u32[]{:S(2)}) collective-permute-start(s32[2]{0:T(128)S(1)} %get-tuple-element.201), channel_id=1, source_target_pairs={{2,0},{3,1},{0,2},{1,3},{6,4},{7,5},{4,6},{5,7},{10,8},{11,9},{8,1... | collective-permute-start | bytes 32 | tf_op jit(solution)/shard_map/ppermute | solution.py:540
  7.1 35.4 %collective-permute-start = (s32[2]{0:T(128)S(1)}, s32[2]{0:T(128)S(1)}, u32[]{:S(2)}, u32[]{:S(2)}) collective-permute-start(s32[2]{0:T(128)S(1)} %get-tuple-element.201), channel_id=1, source_target_pairs={{1,0},{2,1},{3,2},{0,3},{5,4},{6,5},{7,6},{4,7},{9,8},{10,9},{11,1... | collective-permute-start | bytes 32 | tf_op jit(solution)/shard_map/ppermute | solution.py:540
  23.0 5.5 %copy-start.4 = (s32[2,2,1]{1,2,0:T(1,128)S(1)}, s32[2,2,1]{1,2,0:T(1,128)}, u32[]{:S(2)}) copy-start(s32[2,2,1]{1,2,0:T(1,128)} %param.3) | copy-start | bytes 52
  23.0 89.5 %all-to-all-start = ((f32[4,2,256,768]{3,2,1,0:T(8,128)}), f32[4,2,256,768]{3,2,1,0:T(8,128)}, u32[]{:S(2)}, u32[]{:S(2)}) async-start(f32[4,2,256,768]{3,2,1,0:T(8,128)} %shard_map.41.refs_0_), calls=%async_computation | async-start | bytes 12582912 | tf_op jit(solution)/shard_map/all_to_all | solution.py:532
  42.8 6.7 %copy-start.3 = (s32[2,4]{1,0:T(2,128)}, s32[2,4]{1,0:T(2,128)S(1)}, u32[]{:S(2)}) copy-start(s32[2,4]{1,0:T(2,128)S(1)} %constant_dynamic-slice_fusion.off_ref) | copy-start | bytes 100
  60.5 143.6 %collective-permute-start.8 = (f32[2,4,256,128]{3,2,1,0:T(8,128)}, f32[2,4,256,128]{3,2,1,0:T(8,128)}, u32[]{:S(2)}, u32[]{:S(2)}) collective-permute-start(f32[2,4,256,128]{3,2,1,0:T(8,128)} %get-tuple-element.33), channel_id=1, source_target_pairs={{4,0},{8,4},{9,1},{10,2},{11,3},{12,8},{13,5},{14,6},{15,7},{16,12... | collective-permute-start | bytes 3145736 | tf_op jit(solution)/shard_map/ppermute | solution.py:535
  72.1 81.5 %collective-permute-start.4 = (f32[2,4,256,128]{3,2,1,0:T(8,128)}, f32[2,4,256,128]{3,2,1,0:T(8,128)}, u32[]{:S(2)}, u32[]{:S(2)}) collective-permute-start(f32[2,4,256,128]{3,2,1,0:T(8,128)} %get-tuple-element.29), channel_id=1, source_target_pairs={{0,0},{1,1},{2,2},{4,4},{5,5},{6,6},{7,3},{8,8},{9,9},{10,10},{11,... | collective-permute-start | bytes 3145736 | tf_op jit(solution)/shard_map/ppermute | solution.py:535
  81.6 81.0 %collective-permute-start.5 = (f32[2,4,256,128]{3,2,1,0:T(8,128)}, f32[2,4,256,128]{3,2,1,0:T(8,128)}, u32[]{:S(2)}, u32[]{:S(2)}) collective-permute-start(f32[2,4,256,128]{3,2,1,0:T(8,128)} %get-tuple-element.30), channel_id=1, source_target_pairs={{1,0},{2,1},{3,2},{4,3},{5,4},{6,5},{7,6},{8,7},{9,8},{10,9},{11,1... | collective-permute-start | bytes 3145736 | tf_op jit(solution)/shard_map/ppermute | solution.py:535
  83.5 82.1 %collective-permute-start.7 = (f32[2,4,256,128]{3,2,1,0:T(8,128)}, f32[2,4,256,128]{3,2,1,0:T(8,128)}, u32[]{:S(2)}, u32[]{:S(2)}) collective-permute-start(f32[2,4,256,128]{3,2,1,0:T(8,128)} %get-tuple-element.32), channel_id=1, source_target_pairs={{0,1},{1,2},{3,0},{4,5},{5,6},{6,3},{7,4},{8,9},{9,10},{10,7},{11,... | collective-permute-start | bytes 3145736 | tf_op jit(solution)/shard_map/ppermute | solution.py:535
  117.5 30.5 %collective-permute-start.3 = (f32[2,3,256,128]{3,2,1,0:T(8,128)}, f32[2,3,256,128]{3,2,1,0:T(8,128)}, u32[]{:S(2)}, u32[]{:S(2)}) collective-permute-start(f32[2,3,256,128]{3,2,1,0:T(8,128)} %get-tuple-element.27), channel_id=1, source_target_pairs={{1,0},{2,1},{3,2},{4,3},{5,4},{6,5},{7,6},{8,7},{9,8},{10,9},{11,1... | collective-permute-start | bytes 2359304 | tf_op jit(solution)/shard_map/ppermute | solution.py:535
  148.0 39.0 %collective-permute-start.9 = (f32[2,4,256,128]{3,2,1,0:T(8,128)}, f32[2,4,256,128]{3,2,1,0:T(8,128)}, u32[]{:S(2)}, u32[]{:S(2)}) collective-permute-start(f32[2,4,256,128]{3,2,1,0:T(8,128)} %get-tuple-element.34), channel_id=1, source_target_pairs={{5,0},{8,3},{9,4},{10,1},{11,2},{12,7},{13,8},{14,5},{15,6},{16,11... | collective-permute-start | bytes 3145736 | tf_op jit(solution)/shard_map/ppermute | solution.py:535
  149.9 83.0 %all-to-all-start.1 = ((f32[4,2,256,256]{3,2,1,0:T(8,128)}), f32[4,2,256,256]{3,2,1,0:T(8,128)S(1)}, u32[]{:S(2)}, u32[]{:S(2)}) async-start(f32[4,2,256,256]{3,2,1,0:T(8,128)} %shard_map.43.refs_1_.refs_0_), calls=%async_computation.1 | async-start | bytes 4194304 | tf_op jit(solution)/shard_map/all_to_all | solution.py:532
  153.6 50.6 %collective-permute-start.11 = (f32[2,4,256,128]{3,2,1,0:T(8,128)}, f32[2,4,256,128]{3,2,1,0:T(8,128)}, u32[]{:S(2)}, u32[]{:S(2)}) collective-permute-start(f32[2,4,256,128]{3,2,1,0:T(8,128)} %get-tuple-element.36), channel_id=1, source_target_pairs={{7,0},{8,1},{9,2},{10,3},{11,4},{12,5},{13,6},{14,7},{15,8},{16,9}... | collective-permute-start | bytes 3145736 | tf_op jit(solution)/shard_map/ppermute | solution.py:535
  162.6 50.6 %collective-permute-start.12 = (f32[2,3,256,128]{3,2,1,0:T(8,128)}, f32[2,3,256,128]{3,2,1,0:T(8,128)S(1)}, u32[]{:S(2)}, u32[]{:S(2)}) collective-permute-start(f32[2,3,256,128]{3,2,1,0:T(8,128)} %get-tuple-element.39), channel_id=1, source_target_pairs={{7,0},{8,1},{9,2},{10,3},{11,4},{12,5},{13,6},{14,7},{15,8},{16,9}... | collective-permute-start | bytes 2359304 | tf_op jit(solution)/shard_map/ppermute | solution.py:535
  165.6 65.9 %collective-permute-start.6 = (f32[2,1,256,128]{3,2,1,0:T(8,128)}, f32[2,1,256,128]{3,2,1,0:T(8,128)S(1)}, u32[]{:S(2)}, u32[]{:S(2)}) collective-permute-start(f32[2,1,256,128]{3,2,1,0:T(8,128)} %get-tuple-element.31), channel_id=1, source_target_pairs={{0,2},{2,0},{3,1},{4,6},{5,3},{6,4},{7,5},{8,10},{9,7},{10,8},{11,... | collective-permute-start | bytes 786440 | tf_op jit(solution)/shard_map/ppermute | solution.py:535
  187.1 45.8 %collective-permute-start.10 = (f32[2,1,256,128]{3,2,1,0:T(8,128)}, f32[2,1,256,128]{3,2,1,0:T(8,128)S(1)}, u32[]{:S(2)}, u32[]{:S(2)}) collective-permute-start(f32[2,1,256,128]{3,2,1,0:T(8,128)} %get-tuple-element.35), channel_id=1, source_target_pairs={{6,0},{8,2},{9,3},{10,4},{11,1},{12,6},{13,7},{14,8},{15,5},{16,10... | collective-permute-start | bytes 786440 | tf_op jit(solution)/shard_map/ppermute | solution.py:535
  213.1 0.9 copy-start.5
  231.5 1.4 copy-start.1
  232.9 0.7 copy-start.2
  232.9 1.4 copy-start
